TPU v7x, 32 devices: a whole 2x2x4 slice. The times are simulated.
32 devices in a mesh: shadow: 2 (over y), seq: 4 (over x, core), head: 4 (over z).
Axes of the slice: x: 2, y: 2, z: 4, core: 2. Of those that a mesh axis runs over, the one named last changes fastest.
Arguments:
- token_ids: int32 [4096], P(('shadow', 'seq')), parts along dimension 0, may hold values from 0 to 25599
- target_ids: int32 [4096], P(('shadow', 'seq')), parts along dimension 0, may hold values from 0 to 25599
- doc_start: int32 [8], P(('shadow', 'seq')), parts along dimension 0, may hold values from 0 to 512, as said below
- vocab_table: bfloat16 [51200, 2048], P(('shadow', 'head'), 'seq'), parts along dimension 0, may hold values from -2.25 to 2.25
- norm_gain_one: bfloat16 [4096], P('shadow'), parts along dimension 0, may hold values from 0.25 to 1.75
- lin_qkv: bfloat16 [4096, 2560], P('shadow', 'head'), parts along dimension 0, may hold values from -0.125 to 0.125
- lin_head_gain: bfloat16 [4096], P(('shadow', 'head')), parts along dimension 0, may hold values from 0.25 to 1.75
- lin_out: bfloat16 [4096, 2048], P(('shadow', 'head')), parts along dimension 0, may hold values from -0.125 to 0.125
- norm_gain_two: bfloat16 [4096], P('shadow'), parts along dimension 0, may hold values from 0.25 to 1.75
- win_qkv: bfloat16 [4096, 6144], P('shadow', 'head'), parts along dimension 0, may hold values from -4 to 4
- win_out: bfloat16 [4096, 2048], P(('shadow', 'head')), parts along dimension 0, may hold values from -0.125 to 0.125
- final_gain: bfloat16 [4096], P('shadow'), parts along dimension 0, may hold values from 0.25 to 1.75
Outputs:
- loglik: float32 [4096], P(('shadow', 'seq', 'head')), parts along dimension 0
There are 2 independent parts, one for each index of `shadow`. A program takes and returns all parts, laid end to end along the dimension named above; each array names one. Nothing has to cross between parts.
Inputs may be any that keep to these rules, and one draw needn't show every extreme that they name: `doc_start`: in exactly max(1, B // 4) of the B = 4 blocks a document begins, at this offset within the block; every other entry equals 512, and no document begins in that block.
All inputs are finite; a program needn't handle non-finite values.
Results may differ from a plain program's by a relative error of at most 0.005.
Values may be sent and summed in bfloat16 or wider, within the bound.
No kernel may reach another device: no remote copies, remote signals or barrier semaphores. Data moves between devices by JAX's collectives and lax.ppermute only.
A program may use at most 192 MiB of HBM per device.

v0:
```python
import jax
import jax.numpy as jnp
from jax import lax
from jax.sharding import PartitionSpec as P

FEAT = 16
WINDOW = 64
HEAD_DIM = 128


EPSILON = 1e-05
NEGATIVE = -1e30
HIGHEST = lax.Precision.HIGHEST


def carried_in(x, axis, combine, identity):
    length, mine = (lax.axis_size(axis), lax.axis_index(axis))
    everything = jax.tree.map(
        lambda part, kind: lax.all_gather(part.astype(kind), axis),
        x,
        (jnp.bfloat16, jnp.bfloat16, jnp.bfloat16),
    )
    start = jax.tree.map(
        lambda part, zero: jnp.broadcast_to(jnp.asarray(zero, part.dtype), part.shape), x, identity
    )

    def hop(k, before):
        reached = k < mine
        new = combine(
            before, jax.tree.map(lambda part, own: part[k].astype(own.dtype), everything, x)
        )
        return jax.tree.map(lambda a, b: jnp.where(reached, a, b), new, before)

    return lax.fori_loop(0, length, hop, start)


def from_behind(value, axis, steps):
    count = lax.axis_size(axis)
    first, last = (max(0, -steps), min(count, count - steps))
    return lax.ppermute(value, axis, [(source, source + steps) for source in range(first, last)])


def combined_all(part, axis, combine):
    gathered = jax.tree.map(lambda a: lax.all_gather(a, axis), part)

    def take(source):
        return jax.tree.map(lambda a: lax.dynamic_index_in_dim(a, source, 0, False), gathered)

    return lax.fori_loop(
        1, lax.axis_size(axis), lambda source, state: combine(state, take(source)), take(0)
    )


def normed(values, weight_gain):
    widened = values.astype(jnp.float32)
    factor = lax.rsqrt(jnp.mean(widened * widened, axis=-1, keepdims=True) + EPSILON)
    return (widened * factor * weight_gain.astype(jnp.float32)).astype(jnp.bfloat16)


def taylor(projected):
    scaled = projected * FEAT ** (-0.25)
    squares = (scaled[..., :, None] * scaled[..., None, :]).reshape(
        scaled.shape[:-1] + (FEAT * FEAT,)
    ) * 0.5**0.5
    leading = jnp.ones(scaled.shape[:-1] + (1,), jnp.float32)
    return jnp.concatenate([leading, scaled, squares], axis=-1).astype(jnp.bfloat16)


def combine_prefix(earlier, later):
    return (
        earlier[0] * later[0],
        later[0][0] * earlier[1] + later[1],
        later[0][0] * earlier[2] + later[2],
    )


def combine_softmax(first, second):
    highest_value = jnp.maximum(first[0], second[0])
    totals = first[1] * jnp.exp(first[0] - highest_value) + second[1] * jnp.exp(
        second[0] - highest_value
    )
    return (highest_value, totals, jnp.maximum(first[2], second[2]))


def shards(
    token_ids,
    target_ids,
    doc_start,
    vocab_table,
    norm_gain_one,
    lin_qkv,
    lin_head_gain,
    lin_out,
    norm_gain_two,
    win_qkv,
    win_out,
    final_gain,
):
    head_count = lax.axis_size("head")
    head_index = lax.axis_index("head")
    tok_count = token_ids.shape[0]
    own_rows = tok_count // head_count
    vocab_rows = vocab_table.shape[0]
    heads_here = lin_qkv.shape[1] // (2 * FEAT + HEAD_DIM)
    boundary = doc_start[0]
    places = jnp.arange(tok_count, dtype=jnp.int32)
    row_first = head_index * own_rows
    vocab_first = head_index * vocab_rows
    full_table = lax.all_gather(vocab_table, "seq", axis=1, tiled=True)
    local_ids = token_ids - vocab_first
    present = (local_ids >= 0) & (local_ids < vocab_rows)
    looked = jnp.take(full_table, jnp.clip(local_ids, 0, vocab_rows - 1), axis=0)
    looked = jnp.where(present[:, None], looked.astype(jnp.float32), 0.0)
    embedded = lax.psum_scatter(
        looked.astype(jnp.bfloat16), "head", scatter_dimension=0, tiled=True
    )
    units_one = normed(embedded, norm_gain_one)
    projected = jnp.dot(
        lax.all_gather(units_one, "head", axis=0, tiled=True),
        lin_qkv,
        preferred_element_type=jnp.float32,
    )
    projected = projected.reshape(tok_count, heads_here, 2 * FEAT + HEAD_DIM)
    feat_query = taylor(projected[..., :FEAT])
    feat_key = taylor(projected[..., FEAT : 2 * FEAT])
    values_one = projected[..., 2 * FEAT :].astype(jnp.bfloat16)
    after_start = places >= boundary
    no_start = boundary == tok_count
    causal = (places[:, None] >= places[None, :]) & (after_start[:, None] == after_start[None, :])
    weights_one = jnp.einsum(
        "ihf,jhf->hij", feat_query, feat_key, preferred_element_type=jnp.float32
    )
    weights_one = jnp.where(causal[None], weights_one, 0.0)
    numerator = jnp.einsum(
        "hij,jhe->ihe", weights_one, values_one.astype(jnp.float32), precision=HIGHEST
    )
    denominator = jnp.sum(weights_one, axis=-1).T
    kept_rows = (after_start | no_start).astype(jnp.bfloat16)
    kept_keys = feat_key * kept_rows[:, None, None]
    state_here = jnp.einsum(
        "jhf,jhe->hfe", kept_keys, values_one, preferred_element_type=jnp.float32
    )
    total_here = jnp.sum(kept_keys.astype(jnp.float32), axis=0)
    carried_flag = jnp.reshape(no_start.astype(jnp.float32), (1,))
    identity = (jnp.ones((1,), jnp.float32), jnp.zeros_like(state_here), jnp.zeros_like(total_here))
    prefix = carried_in((carried_flag, state_here, total_here), "seq", combine_prefix, identity)
    state_before = prefix[1]
    total_before = prefix[2]
    before = (places < boundary).astype(jnp.float32)
    query_wide = feat_query.astype(jnp.float32)
    numerator = numerator + before[:, None, None] * jnp.einsum(
        "ihf,hfe->ihe", query_wide, state_before, precision=HIGHEST
    )
    denominator = denominator + before[:, None] * jnp.einsum(
        "ihf,hf->ih", query_wide, total_before, precision=HIGHEST
    )
    mixture = numerator / denominator[..., None]
    heads_one = (
        (mixture * lin_head_gain.astype(jnp.float32).reshape(heads_here, HEAD_DIM))
        .astype(jnp.bfloat16)
        .reshape(tok_count, heads_here * HEAD_DIM)
    )
    residual_one = (
        embedded.astype(jnp.float32)
        + lax.psum_scatter(
            jnp.dot(heads_one, lin_out, preferred_element_type=jnp.float32).astype(jnp.bfloat16),
            "head",
            scatter_dimension=0,
            tiled=True,
        ).astype(jnp.float32)
    ).astype(jnp.bfloat16)
    units_two = normed(residual_one, norm_gain_two)
    attend_in = jnp.dot(
        lax.all_gather(units_two, "head", axis=0, tiled=True),
        win_qkv,
        preferred_element_type=jnp.float32,
    ).astype(jnp.bfloat16)
    attend_in = attend_in.reshape(tok_count, heads_here, 3 * HEAD_DIM)
    reach_back = WINDOW - 1
    tail_rows = attend_in[tok_count - reach_back :, :, HEAD_DIM:]
    tail_start = jnp.where(no_start, 0, boundary)
    tail_valid = (places[tok_count - reach_back :] >= tail_start).astype(jnp.bfloat16)
    halo_rows, halo_valid = from_behind((tail_rows, tail_valid), "seq", 1)
    key_rows = jnp.concatenate([halo_rows, attend_in[:, :, HEAD_DIM:]], axis=0)
    key_places = jnp.arange(reach_back + tok_count, dtype=jnp.int32)
    distance = places[:, None] + reach_back - key_places[None, :]
    in_band = (distance >= 0) & (distance < WINDOW)
    key_after = jnp.concatenate([jnp.zeros((reach_back,), jnp.bool_), after_start])
    key_ok = jnp.concatenate([halo_valid > 0, jnp.ones((tok_count,), jnp.bool_)])
    allowed = in_band & (after_start[:, None] == key_after[None, :]) & key_ok[None, :]
    scores = jnp.einsum(
        "ihd,jhd->hij",
        attend_in[..., :HEAD_DIM],
        key_rows[..., :HEAD_DIM],
        preferred_element_type=jnp.float32,
    ) * HEAD_DIM ** (-0.5)
    scores = jnp.where(allowed[None], scores, NEGATIVE)
    highest_score = jnp.max(scores, axis=-1, keepdims=True)
    weights_two = jnp.where(allowed[None], jnp.exp(scores - highest_score), 0.0)
    probabilities = (weights_two / jnp.sum(weights_two, axis=-1, keepdims=True)).astype(
        jnp.bfloat16
    )
    attended = jnp.einsum(
        "hij,jhe->ihe", probabilities, key_rows[..., HEAD_DIM:], preferred_element_type=jnp.float32
    )
    attended = attended.astype(jnp.bfloat16).reshape(tok_count, heads_here * HEAD_DIM)
    residual_two = residual_one.astype(jnp.float32) + lax.psum_scatter(
        jnp.dot(attended, win_out, preferred_element_type=jnp.float32).astype(jnp.bfloat16),
        "head",
        scatter_dimension=0,
        tiled=True,
    ).astype(jnp.float32)
    final_units = normed(residual_two, final_gain)
    every_row = lax.all_gather(final_units, "head", axis=0, tiled=True)
    logits = lax.dot_general(
        every_row, full_table, (((1,), (1,)), ((), ())), preferred_element_type=jnp.float32
    )
    peak_values = jnp.max(logits, axis=-1)
    totals = jnp.sum(jnp.exp(logits - peak_values[:, None]), axis=-1)
    local_goal = target_ids - vocab_first
    has_goal = (local_goal >= 0) & (local_goal < vocab_rows)
    picked = jnp.take_along_axis(logits, jnp.clip(local_goal, 0, vocab_rows - 1)[:, None], axis=1)[
        :, 0
    ]
    picked = jnp.where(has_goal, picked, NEGATIVE)
    peak_values, totals, picked = combined_all(
        (peak_values, totals, picked), "head", combine_softmax
    )
    scored = picked - (peak_values + jnp.log(totals))
    return lax.dynamic_slice_in_dim(scored, row_first, own_rows, 0)


def solution(mesh):
    return jax.shard_map(
        shards,
        mesh=mesh,
        in_specs=(
            P(("shadow", "seq")),
            P(("shadow", "seq")),
            P(("shadow", "seq")),
            P(("shadow", "head"), "seq"),
            P("shadow"),
            P("shadow", "head"),
            P(("shadow", "head")),
            P(("shadow", "head"), None),
            P("shadow"),
            P("shadow", "head"),
            P(("shadow", "head"), None),
            P("shadow"),
        ),
        out_specs=P(("shadow", "seq", "head")),
        check_vma=False,
    )
```

profile of v0, /device:TPU:0, one launch (start us, length us, event | category | flops | bytes accessed | tf_op | source)
XLA Modules:
  0.0 616.8 jit_solution(6773517089864402447)
XLA Ops:
  6.5 0.7 all-gather.15.cloned.1.call-update
  7.4 164.9 %all-gather.15.cloned.1.call-done = bf16[6400,2048]{1,0:T(8,128)(2,1)} async-done(((bf16[6400,512]{1,0:T(8,128)(2,1)}), bf16[6400,2048]{1,0:T(8,128)(2,1)}) %all-gather.15.cloned.1.call-update) | async-done | bytes 26214416 | tf_op jit(solution)/shard_map/all_gather | solution.py:109
  172.3 17.1 %gather_fusion = bf16[512,2048]{1,0:T(8,128)(2,1)} fusion(bf16[6400,2048]{1,0:T(8,128)(2,1)} %all-gather.15.cloned.1.call-done, s32[1024]{0:T(1024)S(1)} %pad_clamp_fusion), kind=kCustom, calls=%fused_computation | custom fusion | bytes 4196352 | tf_op jit(solution)/shard_map/jit(_take)/gather | solution.py:112
  189.3 3.5 select_convert_fusion
  193.5 43.4 %reduce-scatter.4.cloned.1.call-done = bf16[128,2048]{1,0:T(8,128)(2,1)} async-done(((bf16[512,2048]{1,0:T(8,128)(2,1)}), bf16[128,2048]{1,0:T(8,128)(2,1)}) %reduce-scatter.4.cloned.1.call-update) | async-done | bytes 524304 | tf_op jit(solution)/shard_map/reduce_scatter | solution.py:114
  236.9 1.2 fusion.33
  238.1 2.0 fusion.35
  240.9 44.7 %all-gather.17.cloned.1.call-done = bf16[512,2048]{1,0:T(8,128)(2,1)} async-done(((bf16[128,2048]{1,0:T(8,128)(2,1)}), bf16[512,2048]{1,0:T(8,128)(2,1)}) %all-gather.17.cloned.1.call-update) | async-done | bytes 2097168 | tf_op jit(solution)/shard_map/all_gather | solution.py:119
  285.6 3.1 fusion.67
  289.1 0.8 copy-done.5
  289.8 1.4 convolution_convert_fusion.3
  291.9 0.7 dynamic-update-slice
  292.6 6.8 %all-reduce.2 = bf16[4]{0:T(256)(128)(2,1)S(1)} all-reduce(bf16[4]{0:T(256)(128)(2,1)S(1)} %dynamic-update-slice), channel_id=1, replica_groups=mesh['shadow'=2,'seq'=4,'head'=4] {'seq'}, use_global_device_ids=true, to_apply=%add.2 | all-reduce | flops 4 | bytes 16
  300.4 5.4 all-gather.5
  306.0 1.0 copy-done.3
  307.0 3.8 select_reduce_fusion
  310.9 10.1 %while.36 = (s32[]{:T(128)}, f32[4,273,128]{2,1,0:T(8,128)S(1)}, f32[4,273]{1,0:T(4,128)S(1)}, s32[]{:T(128)}, bf16[4,1]{0,1:T(2,128)(2,1)S(1)}, /*index=5*/bf16...) while((s32[]{:T(128)}, f32[4,273,128]{2,1,0:T(8,128)S(1)}, ...), condition=%wide.region_4.5_spmd.clone, body=%wide.region_3.4_spmd.clone.sunk | while | flops 704345 | bytes 1408825 | solution.py:34
  312.1 1.3 fusion.81
  314.6 1.3 fusion.81
  317.1 1.3 fusion.81
  319.7 1.3 fusion.81
  321.0 0.8 fusion.50
  321.8 1.3 convolution_multiply_fusion
  323.2 4.5 fusion.30
  327.7 2.6 convolution_convert_fusion.2
  331.0 41.2 %reduce-scatter.6.cloned.1.call-done = bf16[128,2048]{1,0:T(8,128)(2,1)} async-done(((bf16[512,2048]{1,0:T(8,128)(2,1)}), bf16[128,2048]{1,0:T(8,128)(2,1)}) %reduce-scatter.6.cloned.1.call-update) | async-done | bytes 524304 | tf_op jit(solution)/shard_map/reduce_scatter | solution.py:165
  372.2 1.3 fusion.37
  373.5 1.0 fusion.39
  374.7 1.6 collective-permute-start.1
  376.3 0.7 collective-permute-done.1
  377.1 42.9 %all-gather.19.cloned.1.call-done = bf16[512,2048]{1,0:T(8,128)(2,1)} async-done(((bf16[128,2048]{1,0:T(8,128)(2,1)}), bf16[512,2048]{1,0:T(8,128)(2,1)}) %all-gather.19.cloned.1.call-update) | async-done | bytes 2097168 | tf_op jit(solution)/shard_map/all_gather | solution.py:174
  419.9 8.1 %convolution_convert_fusion.1 = bf16[512,1536]{1,0:T(8,128)(2,1)} fusion(bf16[512,2048]{1,0:T(8,128)(2,1)} %all-gather.19.cloned.1.call-done, bf16[2048,1536]{1,0:T(8,128)(2,1)} %param.25), kind=kOutput, calls=%fused_computation.22 | convolution fusion | flops 3222011904 | bytes 9961472 | tf_op jit(solution)/shard_map/dot_general | solution.py:173
  428.0 3.0 reshape.237
  431.1 2.0 collective-permute-start
  434.2 0.8 fusion.44
  435.0 2.9 fusion.65
  438.6 0.9 copy-done.14
  439.5 2.6 convolution_convert_fusion
  442.8 45.2 %reduce-scatter.8.cloned.1.call-done = bf16[128,2048]{1,0:T(8,128)(2,1)} async-done(((bf16[512,2048]{1,0:T(8,128)(2,1)}), bf16[128,2048]{1,0:T(8,128)(2,1)}) %reduce-scatter.8.cloned.1.call-update) | async-done | bytes 524304 | tf_op jit(solution)/shard_map/reduce_scatter | solution.py:207
  488.0 1.3 multiply_reduce_fusion
  489.3 2.1 multiply_convert_fusion.2
  491.4 45.3 %all-gather.21.cloned.1.call-done = bf16[512,2048]{1,0:T(8,128)(2,1)} async-done(((bf16[128,2048]{1,0:T(8,128)(2,1)}), bf16[512,2048]{1,0:T(8,128)(2,1)}) %all-gather.21.cloned.1.call-update) | async-done | bytes 2097168 | tf_op jit(solution)/shard_map/all_gather | solution.py:214
  536.8 21.8 %fusion.66 = (f32[512]{0:T(512)S(1)}, f32[512,6400]{1,0:T(8,128)}) fusion(bf16[512,2048]{1,0:T(8,128)(2,1)} %all-gather.21.cloned.1.call-done, bf16[6400,2048]{1,0:T(8,128)(2,1)} %all-gather.15.cloned.1.call-done), kind=kOutput, calls=%fused_computation.119 | convolution fusion | flops 13425049600 | bytes 41420800 | tf_op jit(solution)/shard_map/dot_general | solution.py:215
  558.5 8.1 %gather_fusion.1 = f32[512]{0:T(512)S(1)} fusion(f32[512,6400]{1,0:T(8,128)} %get-tuple-element.383, s32[512]{0:T(512)S(1)} %bitcast.91), kind=kCustom, calls=%fused_computation.1 | custom fusion | bytes 8192 | tf_op jit(solution)/shard_map/jit(take_along_axis)/gather | solution.py:222
  566.7 11.9 %all-gather.8 = f32[4,1,512]{2,1,0:T(1,128)S(1)} all-gather(f32[1,1,512]{2,1,0:T(1,128)S(1)} %bitcast.115), channel_id=6, replica_groups=mesh['shadow'=2,'seq'=4,'head'=4] {'head'}, dimensions={0}, use_global_device_ids=true | all-gather | bytes 10240 | tf_op jit(solution)/shard_map/all_gather | solution.py:44
  578.6 6.7 %exponential_reduce_fusion = f32[512]{0:T(512)S(1)} fusion(f32[512,6400]{1,0:T(8,128)} %get-tuple-element.383, f32[512]{0:T(512)S(1)} %get-tuple-element.382), kind=kLoop, calls=%fused_computation.12 | loop fusion | flops 6553088 | bytes 13111296 | tf_op jit(solution)/shard_map/reduce_sum | solution.py:219
  585.3 11.9 %all-gather.7 = f32[4,1,512]{2,1,0:T(1,128)S(1)} all-gather(f32[1,1,512]{2,1,0:T(1,128)S(1)} %bitcast.114), channel_id=5, replica_groups=mesh['shadow'=2,'seq'=4,'head'=4] {'head'}, dimensions={0}, use_global_device_ids=true | all-gather | bytes 10240 | tf_op jit(solution)/shard_map/all_gather | solution.py:44
  597.2 11.9 %all-gather.6 = f32[4,1,512]{2,1,0:T(1,128)S(1)} all-gather(f32[1,1,512]{2,1,0:T(1,128)S(1)} %bitcast.113), channel_id=4, replica_groups=mesh['shadow'=2,'seq'=4,'head'=4] {'head'}, dimensions={0}, use_global_device_ids=true | all-gather | bytes 10240 | tf_op jit(solution)/shard_map/all_gather | solution.py:44
  (115 shorter events, 10.0 us)
Async XLA Ops:
  6.5 279.0 %copy-start = (bf16[2048,640]{1,0:T(8,128)(2,1)S(1)}, bf16[2048,640]{1,0:T(8,128)(2,1)}, u32[]{:S(2)}) copy-start(bf16[2048,640]{1,0:T(8,128)(2,1)} %param.21) | copy-start | bytes 7864324
  6.5 0.8 copy-start.11
  6.5 165.7 %all-gather.15.cloned.1.call-start = ((), (), s32[]{:S(2)}) async-start(), calls=%async_computation.3 | async-start | bytes 32768000 | tf_op jit(solution)/shard_map/all_gather | solution.py:109
  7.3 229.6 %reduce-scatter.4.cloned.1.call-start = ((), (), s32[]{:S(2)}) async-start(), calls=%async_computation.4 | async-start | bytes 2621440 | tf_op jit(solution)/shard_map/reduce_scatter | solution.py:114
  192.8 0.7 copy-start.8
  192.8 92.7 %all-gather.17.cloned.1.call-start = ((), (), s32[]{:S(2)}) async-start(), calls=%async_computation.5 | async-start | bytes 2621440 | tf_op jit(solution)/shard_map/all_gather | solution.py:119
  240.2 70.7 %all-gather.23.cloned.1.call-start = ((), (), s32[]{:S(2)}) async-start(), calls=%async_computation.10 | async-start | bytes 1433600 | tf_op jit(solution)/shard_map/all_gather | solution.py:19
  288.7 1.1 copy-start.5
  289.8 1.4 copy-start.15
  289.8 9.7 %copy-start.12 = (bf16[512]{0:T(512)(128)(2,1)S(1)}, bf16[512]{0:T(512)(128)(2,1)}, u32[]{:S(2)}) copy-start(bf16[512]{0:T(512)(128)(2,1)} %param.22) | copy-start | bytes 3076
  291.2 81.0 %reduce-scatter.6.cloned.1.call-start = ((), (), s32[]{:S(2)}) async-start(), calls=%async_computation.6 | async-start | bytes 2621440 | tf_op jit(solution)/shard_map/reduce_scatter | solution.py:165
  306.0 1.0 copy-start.3
  310.8 10.2 %copy-start.4 = (bf16[512,4,16,16]{0,3,2,1:T(8,128)(2,1)S(1)}, bf16[512,4,16,16]{0,3,2,1:T(8,128)(2,1)}, u32[]{:S(2)}) copy-start(bf16[512,4,16,16]{0,3,2,1:T(8,128)(2,1)} %copy-done.3) | copy-start | bytes 3145732
  321.8 1.3 copy-start.6
  323.2 4.6 copy-start.13
  330.3 0.7 copy-start.9
  330.3 41.8 %copy-start.2 = (bf16[128,2048]{1,0:T(8,128)(2,1)S(1)}, bf16[128,2048]{1,0:T(8,128)(2,1)}, u32[]{:S(2)}) copy-start(bf16[128,2048]{1,0:T(8,128)(2,1)} %reduce-scatter.4.cloned.1.call-done) | copy-start | bytes 1572868
  330.4 89.6 %all-gather.19.cloned.1.call-start = ((), (), s32[]{:S(2)}) async-start(), calls=%async_computation.7 | async-start | bytes 2621440 | tf_op jit(solution)/shard_map/all_gather | solution.py:174
  374.5 113.5 %reduce-scatter.8.cloned.1.call-start = ((), (), s32[]{:S(2)}) async-start(), calls=%async_computation.8 | async-start | bytes 2621440 | tf_op jit(solution)/shard_map/reduce_scatter | solution.py:207
  374.7 2.4 collective-permute-start.1
  431.1 3.1 collective-permute-start
  437.9 1.6 copy-start.14
  442.1 0.7 copy-start.10
  442.1 49.2 %copy-start.7 = (s32[512]{0:T(512)S(1)}, s32[512]{0:T(512)}, u32[]{:S(2)}) copy-start(s32[512]{0:T(512)} %param.17) | copy-start | bytes 6148
  442.1 94.6 %all-gather.21.cloned.1.call-start = ((), (), s32[]{:S(2)}) async-start(), calls=%async_computation.9 | async-start | bytes 2621440 | tf_op jit(solution)/shard_map/all_gather | solution.py:214
  578.6 31.4 %copy-start.1 = (bf16[2048,640]{1,0:T(8,128)(2,1)S(1)}, bf16[2048,640]{1,0:T(8,128)(2,1)}, u32[]{:S(2)}) copy-start(bf16[2048,640]{1,0:T(8,128)(2,1)} %param.21) | copy-start | bytes 7864324
Sparse Core Ops, SparseCore 0:
  8.9 163.2 all-gather.14
  193.0 43.8 reduce-scatter.3
  240.3 45.2 all-gather.16
  291.3 16.0 all-gather.22
  330.5 41.6 reduce-scatter.5
  374.7 45.2 all-gather.18
  442.2 45.6 reduce-scatter.7
  491.5 45.2 all-gather.20
where the time goes:
time: 618 us; the launch traced here: 617 us
  waiting for transfers between devices  429 us (69%)
  matrix products  51.5 us (8%)
  blocking collectives  47.8 us (8%)
  local copies, waits for them, and re-layouts  38 us (6%)
  other arithmetic  29.4 us (5%)
  between operations  14.6 us (2%)
    all_gather x1, waiting for transfers between devices, shards(): full_table = lax.all_gather(vocab_table, 'seq', axis=1, tiled=True)  165 us
    all_gather x1, waiting for transfers between devices, shards(): every_row = lax.all_gather(final_units, 'head', axis=0, tiled=True)  45.3 us
    reduce_scatter x1, waiting for transfers between devices, shards(): lax.psum_scatter(jnp.dot(attended, win_out, preferred_element_type=jnp.fl...  45.2 us
    all_gather x1, waiting for transfers between devices, shards(): lax.all_gather(units_one, 'head', axis=0, tiled=True)  44.7 us
    reduce_scatter x1, waiting for transfers between devices, shards(): lax.psum_scatter(looked.astype(jnp.bfloat16), 'head', scatter_dimension=0...  43.4 us
    all_gather x1, waiting for transfers between devices, shards(): lax.all_gather(units_two, 'head', axis=0, tiled=True)  42.9 us
    reduce_scatter x1, waiting for transfers between devices, shards(): lax.psum_scatter(jnp.dot(heads_one, lin_out, preferred_element_type=jnp.f...  41.2 us
    all_gather x3, blocking collectives, combined_all(): gathered = jax.tree.map(lambda a: lax.all_gather(a, axis), part)  35.6 us
  transfers between devices with their start and end apart: 10, of which 8 were waited for; matrix products, arithmetic and copies ran while one was open for 1% of the time, Pallas kernels for 0%

commit v1 on v0

v1 whole, which is shorter than its diff:
```python
import functools

import jax
import jax.numpy as jnp
import numpy as np
from jax import lax
from jax.experimental import pallas as pl
from jax.experimental.pallas import tpu as pltpu
from jax.sharding import PartitionSpec as P

FEAT = 16
WINDOW = 64
HEAD_DIM = 128
EPSILON = 1e-05
NEGATIVE = -1e30
LANES = 128
WIDE = 256
DISTINCT = 1 + FEAT + FEAT * (FEAT + 1) // 2
STATE_ROWS = 160
BUFFER_ROWS = 176
F32 = jnp.float32
BF16 = jnp.bfloat16
VMEM_BYTES = 56 * 1024 * 1024


def params(**kw):
    return pltpu.CompilerParams(vmem_limit_bytes=VMEM_BYTES, **kw)


def whole():
    return pl.BlockSpec(memory_space=pltpu.VMEM)


def smem():
    return pl.BlockSpec(memory_space=pltpu.SMEM)


def dot(a, b, dims=((1,), (0,))):
    return lax.dot_general(a, b, (dims, ((), ())), preferred_element_type=F32)


def xor_pairs(size, k):
    return [(i, i ^ k) for i in range(size)]


def rms(values, gain):
    factor = lax.rsqrt(jnp.mean(values * values, axis=-1, keepdims=True) + EPSILON)
    return (values * factor * gain.astype(F32)).astype(BF16)


def lookup_kernel(ids_ref, table_ref, out_ref):
    rows = table_ref.shape[0]
    parts, each, width = out_ref.shape[0], out_ref.shape[2], out_ref.shape[3]
    ids = ids_ref[0]
    hot = (lax.broadcasted_iota(jnp.int32, (parts * each, rows), 1) == ids).astype(F32).astype(BF16)
    found = dot(hot, table_ref[...]).astype(BF16)
    for part in range(parts):
        out_ref[part, 0] = found[part * each : (part + 1) * each]


def lookup(local_ids, table, parts):
    blocks, count = local_ids.shape
    rows, width = table.shape
    each = count // parts
    return pl.pallas_call(
        lookup_kernel,
        grid=(blocks,),
        in_specs=[
            pl.BlockSpec((1, count, 1), lambda k: (k, 0, 0)),
            pl.BlockSpec((rows, width), lambda k: (0, 0), pipeline_mode=pl.Buffered(1)),
        ],
        out_specs=pl.BlockSpec((parts, 1, each, width), lambda k: (0, k, 0, 0)),
        out_shape=jax.ShapeDtypeStruct((parts, blocks, each, width), BF16),
        compiler_params=params(),
        name="lookup",
    )(local_ids.reshape(blocks, count, 1), table)


def selectors(heads):
    pairs = [(r, s) for r in range(FEAT) for s in range(r, FEAT)]
    picks = np.zeros((2, heads, 2, LANES, WIDE), np.float32)
    bias = np.zeros((2, WIDE), np.float32)
    scale = 0.5
    bias[:, 0] = 1.0
    for r in range(FEAT):
        bias[1, 1 + r] = 1.0
    for kind in range(2):
        for head in range(heads):
            first = (kind * heads + head) * FEAT
            for r in range(FEAT):
                picks[kind, head, 0, first + r, 1 + r] = scale
            for n, (r, s) in enumerate(pairs):
                picks[kind, head, 0, first + r, 1 + FEAT + n] = scale
                picks[kind, head, 1, first + s, 1 + FEAT + n] = scale
    factor = np.ones((1, WIDE), np.float32)
    for n, (r, s) in enumerate(pairs):
        factor[0, 1 + FEAT + n] = 0.5**0.5 if r == s else 1.0
    doubled = np.concatenate([picks, picks], axis=3)
    return jnp.asarray(doubled, BF16), jnp.asarray(bias), jnp.asarray(factor)


def project_kernel(heads, bound_ref, units_ref, weight_ref, pick_ref, bias_ref, factor_ref, fq_ref, fk_ref, v_ref, state_ref):
    projected = dot(units_ref[...], weight_ref[...])
    count = projected.shape[0]
    width = heads * HEAD_DIM
    values = projected[:, :width].astype(BF16)
    v_ref[...] = values
    narrow = projected[:, width:]
    upper = narrow.astype(BF16)
    lower = (narrow - upper.astype(F32)).astype(BF16)
    both = jnp.concatenate([upper, lower], axis=1)
    bound = bound_ref[0]
    place = lax.broadcasted_iota(jnp.int32, (count, 1), 0)
    kept = ((place >= bound) | (bound == count)).astype(F32)
    ones = jnp.ones((8, count), BF16)
    for head in range(heads):
        feats = []
        for kind in range(2):
            one = dot(both, pick_ref[kind, head, 0]) + bias_ref[0:1]
            two = dot(both, pick_ref[kind, head, 1]) + bias_ref[1:2]
            feats.append(one * two * factor_ref[...])
        fq_ref[head] = feats[0].astype(BF16)
        keys = feats[1].astype(BF16)
        fk_ref[head] = keys
        keys = (keys.astype(F32) * kept).astype(BF16)
        state = dot(keys, values[:, head * HEAD_DIM : (head + 1) * HEAD_DIM], ((0,), (0,)))
        total = dot(ones, keys)
        state_ref[head, 0:STATE_ROWS] = state[0:STATE_ROWS].astype(BF16)
        tail = jnp.concatenate([total[0:1, :LANES], total[0:1, LANES:], jnp.zeros((14, LANES), F32)], axis=0)
        state_ref[head, STATE_ROWS:BUFFER_ROWS] = tail.astype(BF16)


def project(bound, units, weight, heads):
    pick, bias, factor = selectors(heads)
    count = units.shape[0]
    return pl.pallas_call(
        functools.partial(project_kernel, heads),
        in_specs=[smem()] + [whole()] * 5,
        out_specs=[whole()] * 4,
        out_shape=[
            jax.ShapeDtypeStruct((heads, count, WIDE), BF16),
            jax.ShapeDtypeStruct((heads, count, WIDE), BF16),
            jax.ShapeDtypeStruct((count, heads * HEAD_DIM), BF16),
            jax.ShapeDtypeStruct((heads, BUFFER_ROWS, HEAD_DIM), BF16),
        ],
        compiler_params=params(),
        name="project",
    )(bound, units, weight, pick, bias, factor)


def within_kernel(heads, bound_ref, fq_ref, fk_ref, v_ref, num_ref, den_ref):
    count = v_ref.shape[0]
    bound = bound_ref[0]
    step = count // 2
    for first in range(0, count, step):
        reach = first + step
        row = lax.broadcasted_iota(jnp.int32, (step, reach), 0) + first
        col = lax.broadcasted_iota(jnp.int32, (step, reach), 1)
        allowed = (row >= col) & ((row >= bound) == (col >= bound))
        for head in range(heads):
            weights = dot(fq_ref[head, first:reach], fk_ref[head, 0:reach], ((1,), (1,)))
            weights = jnp.where(allowed, weights, 0.0)
            den_ref[head, first:reach] = jnp.broadcast_to(
                jnp.sum(weights, axis=-1, keepdims=True), (step, 8)
            )
            num_ref[head, first:reach] = dot(
                weights.astype(BF16), v_ref[0:reach, head * HEAD_DIM : (head + 1) * HEAD_DIM]
            )


def within(bound, fq, fk, values, heads):
    count = values.shape[0]
    return pl.pallas_call(
        functools.partial(within_kernel, heads),
        in_specs=[smem()] + [whole()] * 3,
        out_specs=[whole()] * 2,
        out_shape=[
            jax.ShapeDtypeStruct((heads, count, HEAD_DIM), F32),
            jax.ShapeDtypeStruct((heads, count, 8), F32),
        ],
        compiler_params=params(),
        name="within",
    )(bound, fq, fk, values)


def across_kernel(heads, earlier, bound_ref, share_ref, fq_ref, num_ref, den_ref, gain_ref, out_ref, *rest):
    states, result_ref = rest[:earlier], rest[earlier]
    count = num_ref.shape[1]
    bound = bound_ref[0]
    before = (lax.broadcasted_iota(jnp.int32, (count, 1), 0) < bound).astype(F32)
    parts = []
    for head in range(heads):
        carried = jnp.zeros((BUFFER_ROWS, HEAD_DIM), F32)
        for n in range(earlier):
            carried = carried + jnp.where(share_ref[n] > 0, states[n][head].astype(F32), 0.0)
        state = jnp.concatenate(
            [carried[0:STATE_ROWS], jnp.zeros((WIDE - STATE_ROWS, HEAD_DIM), F32)], axis=0
        ).astype(BF16)
        total = jnp.concatenate(
            [carried[STATE_ROWS : STATE_ROWS + 1], carried[STATE_ROWS + 1 : STATE_ROWS + 2]], axis=1
        )
        query = fq_ref[head]
        numerator = num_ref[head] + before * dot(query, state)
        more = jnp.sum(query.astype(F32) * total, axis=-1, keepdims=True)
        denominator = den_ref[head][:, 0:1] + before * more
        parts.append(
            (numerator / denominator * gain_ref[:, head * HEAD_DIM : (head + 1) * HEAD_DIM].astype(F32)).astype(BF16)
        )
    mixed = jnp.concatenate(parts, axis=1)
    result_ref[...] = dot(mixed, out_ref[...]).astype(BF16)


def across(bound, share, fq, num, den, gain, weight, states, heads):
    count = num.shape[1]
    return pl.pallas_call(
        functools.partial(across_kernel, heads, len(states)),
        in_specs=[smem(), smem()] + [whole()] * (5 + len(states)),
        out_specs=whole(),
        out_shape=jax.ShapeDtypeStruct((count, weight.shape[1]), BF16),
        compiler_params=params(),
        name="across",
    )(bound, share, fq, num, den, gain, weight, *states)


def matmul_kernel(a_ref, b_ref, o_ref):
    o_ref[...] = dot(a_ref[...], b_ref[...]).astype(BF16)


def matmul(a, b, tile):
    rows, inner = a.shape
    return pl.pallas_call(
        matmul_kernel,
        grid=(b.shape[1] // tile,),
        in_specs=[
            pl.BlockSpec((rows, inner), lambda n: (0, 0), pipeline_mode=pl.Buffered(1)),
            pl.BlockSpec((inner, tile), lambda n: (0, n)),
        ],
        out_specs=pl.BlockSpec((rows, tile), lambda n: (0, n)),
        out_shape=jax.ShapeDtypeStruct((rows, b.shape[1]), BF16),
        compiler_params=params(),
        name="matmul",
    )(a, b)


def window_kernel(heads, bound_ref, qkv_ref, halo_ref, out_ref, result_ref, held):
    count = qkv_ref.shape[0]
    step = 2 * WINDOW
    reach = step + WINDOW
    bound, valid_from = bound_ref[0], bound_ref[1]
    row = lax.broadcasted_iota(jnp.int32, (step, reach), 0)
    col = lax.broadcasted_iota(jnp.int32, (step, reach), 1)
    band = (col > row) & (col <= row + WINDOW)
    for first in range(0, count, step):
        query_place = row + first
        key_place = col + (first - WINDOW)
        allowed = band & ((query_place >= bound) == (key_place >= bound))
        if first == 0:
            allowed = allowed & ((key_place >= 0) | ((key_place + count >= valid_from) & (query_place < bound)))
        for head in range(heads):
            base = head * 3 * HEAD_DIM
            query = qkv_ref[first : first + step, base : base + HEAD_DIM]
            both = []
            for n in (1, 2):
                lanes = slice(base + n * HEAD_DIM, base + (n + 1) * HEAD_DIM)
                if first == 0:
                    both.append(
                        jnp.concatenate([halo_ref[:, lanes], qkv_ref[0:step, lanes]], axis=0)
                    )
                else:
                    both.append(qkv_ref[first - WINDOW : first + step, lanes])
            scores = dot(query, both[0], ((1,), (1,))) * HEAD_DIM ** (-0.5)
            scores = jnp.where(allowed, scores, NEGATIVE)
            peak = jnp.max(scores, axis=-1, keepdims=True)
            weights = jnp.where(allowed, jnp.exp(scores - peak), 0.0)
            probabilities = (weights / jnp.sum(weights, axis=-1, keepdims=True)).astype(BF16)
            held[first : first + step, head * HEAD_DIM : (head + 1) * HEAD_DIM] = dot(
                probabilities, both[1]
            ).astype(BF16)
    result_ref[...] = dot(held[...], out_ref[...]).astype(BF16)


def window(bound, qkv, halo, weight, heads):
    count = qkv.shape[0]
    return pl.pallas_call(
        functools.partial(window_kernel, heads),
        in_specs=[smem()] + [whole()] * 3,
        out_specs=whole(),
        out_shape=jax.ShapeDtypeStruct((count, weight.shape[1]), BF16),
        scratch_shapes=[pltpu.VMEM((count, heads * HEAD_DIM), BF16)],
        compiler_params=params(),
        name="window",
    )(bound, qkv, halo, weight)


def score_kernel(pieces, tile, order_ref, *refs):
    units, tables = refs[:pieces], refs[pieces : 2 * pieces]
    goal_ref, out_ref, peak_ref, total_ref, picked_ref = refs[2 * pieces :]
    step = pl.program_id(0)
    count = goal_ref.shape[0]

    @pl.when(step == 0)
    def _():
        peak_ref[...] = jnp.full_like(peak_ref, NEGATIVE)
        total_ref[...] = jnp.zeros_like(total_ref)
        picked_ref[...] = jnp.zeros_like(picked_ref)

    chunk = 128
    lane = lax.broadcasted_iota(jnp.int32, (chunk, LANES), 1) + step * tile
    for first in range(0, count, chunk):
        rows = slice(first, first + chunk)
        logits = dot(units[0][rows], tables[0][...], ((1,), (1,)))
        for n in range(1, pieces):
            logits = logits + dot(units[n][rows], tables[n][...], ((1,), (1,)))
        goal = goal_ref[rows]
        old = peak_ref[rows]
        peak = old
        for k in range(0, tile, LANES):
            peak = jnp.maximum(peak, logits[:, k : k + LANES])
        total = total_ref[rows] * jnp.exp(old - peak)
        picked = picked_ref[rows]
        for k in range(0, tile, LANES):
            part = logits[:, k : k + LANES]
            total = total + jnp.exp(part - peak)
            picked = picked + jnp.where(lane + k == goal, part, 0.0)
        peak_ref[rows] = peak
        total_ref[rows] = total
        picked_ref[rows] = picked

    @pl.when(step == pl.num_programs(0) - 1)
    def _():
        peak = jnp.max(peak_ref[...], axis=-1, keepdims=True)
        total = jnp.sum(total_ref[...] * jnp.exp(peak_ref[...] - peak), axis=-1, keepdims=True)
        picked = jnp.sum(picked_ref[...], axis=-1, keepdims=True)
        spread = lax.broadcasted_iota(jnp.int32, (count, 8), 1)
        out_ref[...] = jnp.where(spread == 0, peak, jnp.where(spread == 1, total, picked))


def scores(order, units, tables, goal):
    count = units.shape[0]
    pieces = len(tables)
    rows, width = tables[0].shape
    tile = 640
    unit_specs = [
        pl.BlockSpec((count, width), lambda i, order, n=n: (0, order[n]), pipeline_mode=pl.Buffered(1))
        for n in range(pieces)
    ]
    table_specs = [pl.BlockSpec((tile, width), lambda i, order: (i, 0)) for n in range(pieces)]
    return pl.pallas_call(
        functools.partial(score_kernel, pieces, tile),
        grid_spec=pltpu.PrefetchScalarGridSpec(
            num_scalar_prefetch=1,
            grid=(rows // tile,),
            in_specs=unit_specs
            + table_specs
            + [pl.BlockSpec((count, 1), lambda i, order: (0, 0), pipeline_mode=pl.Buffered(1))],
            out_specs=pl.BlockSpec((count, 8), lambda i, order: (0, 0)),
            scratch_shapes=[pltpu.VMEM((count, LANES), F32)] * 3,
        ),
        out_shape=jax.ShapeDtypeStruct((count, 8), F32),
        compiler_params=params(),
        name="scores",
    )(order, *([units] * pieces), *tables, goal)


def shards(
    token_ids,
    target_ids,
    doc_start,
    vocab_table,
    norm_gain_one,
    lin_qkv,
    lin_head_gain,
    lin_out,
    norm_gain_two,
    win_qkv,
    win_out,
    final_gain,
):
    head_count = lax.axis_size("head")
    seq_count = lax.axis_size("seq")
    head_index = lax.axis_index("head")
    seq_index = lax.axis_index("seq")
    tok_count = token_ids.shape[0]
    own_rows = tok_count // head_count
    vocab_rows, table_width = vocab_table.shape
    heads = lin_qkv.shape[1] // (2 * FEAT + HEAD_DIM)
    vocab_first = head_index * vocab_rows

    marks = jnp.concatenate([token_ids, jnp.broadcast_to(doc_start, (LANES,))])
    marks = jnp.stack(
        [marks] + [lax.ppermute(marks, "seq", xor_pairs(seq_count, k)) for k in range(1, seq_count)]
    )
    starts = marks[:, tok_count]
    starts = jnp.stack(
        [lax.dynamic_index_in_dim(starts, seq_index ^ j, 0, False) for j in range(seq_count)]
    )
    bound = doc_start.astype(jnp.int32)
    block = jnp.arange(seq_count, dtype=jnp.int32)

    found = lookup(marks[:, :tok_count] - vocab_first, vocab_table, head_count)
    found = lax.psum_scatter(found, "head", scatter_dimension=0, tiled=True)[0]
    gathered = [found[0]] + [
        lax.ppermute(found[k], "seq", xor_pairs(seq_count, k)) for k in range(1, seq_count)
    ]
    table, gathered = lax.optimization_barrier((vocab_table, gathered))
    gathered = jnp.stack(gathered)
    embedded = jnp.concatenate(
        [lax.dynamic_index_in_dim(gathered, seq_index ^ j, 0, False) for j in range(seq_count)], axis=1
    )

    if seq_count == 4:
        beside = lax.ppermute(table, "seq", xor_pairs(seq_count, 1))
        across_x = lax.ppermute(table, "seq", xor_pairs(seq_count, 2))
        corner = lax.ppermute(across_x, "seq", xor_pairs(seq_count, 1))
        tables = [table, beside, across_x, corner]
        order = seq_index ^ block
    else:
        tables = [lax.all_gather(table, "seq", axis=1, tiled=True)]
        order = jnp.zeros((1,), jnp.int32)

    units_one = rms(embedded.astype(F32), norm_gain_one)
    units_one = lax.all_gather(units_one, "head", axis=0, tiled=True)

    by_head = lin_qkv.reshape(lin_qkv.shape[0], heads, 2 * FEAT + HEAD_DIM)
    pad = LANES - 2 * FEAT * heads
    weight_one = jnp.concatenate(
        [
            by_head[:, :, 2 * FEAT :].reshape(-1, heads * HEAD_DIM),
            by_head[:, :, :FEAT].reshape(-1, heads * FEAT),
            by_head[:, :, FEAT : 2 * FEAT].reshape(-1, heads * FEAT),
            jnp.zeros((lin_qkv.shape[0], pad), BF16),
        ],
        axis=1,
    )
    feat_query, feat_key, values_one, state_here = project(bound, units_one, weight_one, heads)
    states, shares = [], []
    for back in range(1, seq_count):
        states.append(
            lax.ppermute(state_here, "seq", [(i, i + back) for i in range(seq_count - back)])
        )
        between = (block > seq_index - back) & (block < seq_index)
        unbroken = jnp.all(~between | (starts == tok_count))
        shares.append((unbroken & (seq_index >= back)).astype(jnp.int32))
    num, den = within(bound, feat_query, feat_key, values_one, heads)
    partial_one = across(
        bound, jnp.stack(shares), feat_query, num, den, lin_head_gain.reshape(1, -1), lin_out, states, heads
    )
    residual_one = (
        embedded.astype(F32)
        + lax.psum_scatter(partial_one, "head", scatter_dimension=0, tiled=True).astype(F32)
    ).astype(BF16)

    units_two = rms(residual_one.astype(F32), norm_gain_two)
    units_two = lax.all_gather(units_two, "head", axis=0, tiled=True)
    tail = matmul(units_two[tok_count - WINDOW :], win_qkv, 3 * HEAD_DIM)
    halo = lax.ppermute(tail, "seq", [(i, i + 1) for i in range(seq_count - 1)])
    qkv = matmul(units_two, win_qkv, 3 * HEAD_DIM)
    previous = lax.dynamic_index_in_dim(starts, jnp.maximum(seq_index - 1, 0), 0, False)
    valid_from = jnp.where(
        seq_index == 0, tok_count, jnp.where(previous == tok_count, 0, previous)
    ).astype(jnp.int32)
    partial_two = window(
        jnp.concatenate([bound, valid_from.reshape(1)]), qkv, halo, win_out, heads
    )
    residual_two = residual_one.astype(F32) + lax.psum_scatter(
        partial_two, "head", scatter_dimension=0, tiled=True
    ).astype(F32)

    final_units = lax.all_gather(rms(residual_two, final_gain), "head", axis=0, tiled=True)
    found = scores(order, final_units, tables, (target_ids - vocab_first).reshape(tok_count, 1))
    found = found[:, :3].T.reshape(3, head_count, own_rows)

    shares = [lax.dynamic_index_in_dim(found, head_index, 1, False)]
    for step in range(1, head_count):
        leaving = lax.dynamic_index_in_dim(found, (head_index + step) % head_count, 1, False)
        shares.append(
            lax.ppermute(leaving, "head", [(i, (i + step) % head_count) for i in range(head_count)])
        )
    shares = jnp.stack(shares)
    peak = jnp.max(shares[:, 0], axis=0)
    total = jnp.sum(shares[:, 1] * jnp.exp(shares[:, 0] - peak), axis=0)
    return jnp.sum(shares[:, 2], axis=0) - (peak + jnp.log(total))


def solution(mesh):
    return jax.shard_map(
        shards,
        mesh=mesh,
        in_specs=(
            P(("shadow", "seq")),
            P(("shadow", "seq")),
            P(("shadow", "seq")),
            P(("shadow", "head"), "seq"),
            P("shadow"),
            P("shadow", "head"),
            P(("shadow", "head")),
            P(("shadow", "head"), None),
            P("shadow"),
            P("shadow", "head"),
            P(("shadow", "head"), None),
            P("shadow"),
        ),
        out_specs=P(("shadow", "seq", "head")),
        check_vma=False,
    )
```

time: 618 us -> 467 us (0.76)
  waiting for transfers between devices: 429 us -> 262 us
  Pallas kernels: 0 us -> 99.8 us
  matrix products: 51.5 us -> 0 us
  blocking collectives: 47.8 us -> 0 us
  starting transfers between devices: 3.82 us -> 50.7 us
  local copies, waits for them, and re-layouts: 38 us -> 20.6 us
  other arithmetic: 29.4 us -> 15.5 us
    all_gather x5 -> x3, waiting for transfers between devices: 298 us -> 120 us  [the longest x1 45.4 us: shards(): units_two = lax.all_gather(units_two, 'head', axis=0, tiled=True)]
    pallas_call x0 -> x8, Pallas kernels: none -> 99.8 us  [the longest x1 39 us: scores(): pl.pallas_call(functools.partial(score_kernel, pieces, tile), grid_spec=p...]
    dot_general x12 -> x0, matrix products: 51.5 us -> none  [the longest x1 21.8 us: shards(): lax.dot_general(every_row, full_table, (((1,), (1,)), ((), ())), preferre...]
    ppermute x2 -> x16, starting transfers between devices: 3.52 us -> 50.5 us  [the longest x1 33.7 us: shards(): beside = lax.ppermute(table, 'seq', xor_pairs(seq_count, 1))]
    all_gather x4 -> x0, blocking collectives: 41 us -> none  [the longest x3 35.6 us: combined_all(): gathered = jax.tree.map(lambda a: lax.all_gather(a, axis), part)]
    gather x2 -> x0, local copies, waits for them, and re-layouts: 25.2 us -> none  [the longest x1 17.1 us: shards(): jnp.take(full_table, jnp.clip(local_ids, 0, vocab_rows - 1), axis=0)]
    ppermute x2 -> x16, waiting for transfers between devices: 0.72 us -> 12.7 us  [the longest x3 6.4 us: shards(): lax.ppermute(found[k], 'seq', xor_pairs(seq_count, k))]
    reduce_sum x5 -> x4, other arithmetic: 11.2 us -> 2.82 us  [the longest x3 2.79 us: rms(): jnp.mean(values * values, axis=-1, keepdims=True) + EPSILON]
  transfers between devices with their start and end apart: 10 -> 22, of which waited for: 8 -> 13; matrix products, arithmetic and copies ran while one was open for 1% -> 6% of each run, Pallas kernels for 0% -> 6%
where the time goes in v1:
time: 467 us; the launch traced here: 466 us
  waiting for transfers between devices  262 us (56%)
  Pallas kernels  99.8 us (21%)
  starting transfers between devices  50.7 us (11%)
  local copies, waits for them, and re-layouts  20.6 us (4%)
  between operations  17.4 us (4%)
  other arithmetic  15.5 us (3%)
    all_gather x1, waiting for transfers between devices, shards(): units_two = lax.all_gather(units_two, 'head', axis=0, tiled=True)  45.4 us
    reduce_scatter x1, waiting for transfers between devices, shards(): found = lax.psum_scatter(found, 'head', scatter_dimension=0, tiled=True)[0]  44.3 us
    all_gather x1, waiting for transfers between devices, shards(): lax.all_gather(rms(residual_two, final_gain), 'head', axis=0, tiled=True)  44 us
    reduce_scatter x1, waiting for transfers between devices, shards(): lax.psum_scatter(partial_two, 'head', scatter_dimension=0, tiled=True)  43.3 us
    reduce_scatter x1, waiting for transfers between devices, shards(): lax.psum_scatter(partial_one, 'head', scatter_dimension=0, tiled=True)  41.7 us
    pallas_call x1, Pallas kernels, scores(): pl.pallas_call(functools.partial(score_kernel, pieces, tile), grid_spec=p...  39 us
    ppermute x1, starting transfers between devices, shards(): beside = lax.ppermute(table, 'seq', xor_pairs(seq_count, 1))  33.7 us
    all_gather x1, waiting for transfers between devices, shards(): units_one = lax.all_gather(units_one, 'head', axis=0, tiled=True)  30.8 us
  transfers between devices with their start and end apart: 22, of which 13 were waited for; matrix products, arithmetic and copies ran while one was open for 6% of the time, Pallas kernels for 6%

profile of v1, /device:TPU:0, one launch (start us, length us, event | category | flops | bytes accessed | tf_op | source)
XLA Modules:
  0.0 466.3 jit_solution(4109666678722541980)
XLA Ops:
  7.2 0.7 concatenate.12
  8.3 2.5 collective-permute-start.1
  11.0 1.4 collective-permute-done.1
  12.4 1.4 collective-permute-done.2
  13.9 1.3 copy.17.ids_ref
  15.2 18.2 %lookup.1 = bf16[4,4,128,512]{3,2,1,0:T(8,128)(2,1)} custom-call(s32[4,512,1]{2,1,0:T(8,128)} %copy.17.ids_ref, bf16[6400,512]{1,0:T(8,128)(2,1)} %refs_4_), custom_call_target="tpu_custom_call" | custom-call | tf_op jit(solution)/shard_map/lookup/pallas_call | solution.py:65
  33.5 44.3 %reduce-scatter.4.cloned.1.call-done = bf16[1,4,128,512]{3,2,1,0:T(8,128)(2,1)} async-done(((bf16[4,4,128,512]{3,2,1,0:T(8,128)(2,1)}), bf16[1,4,128,512]{3,2,1,0:T(8,128)(2,1)}) %reduce-scatter.4.cloned.1.call-update) | async-done | bytes 524304 | tf_op jit(solution)/shard_map/reduce_scatter | solution.py:401
  77.8 1.1 slice_bitcast_fusion
  79.0 1.5 collective-permute-start.4
  80.9 4.5 collective-permute-done.4
  85.4 1.9 collective-permute-done.5
  87.6 1.0 fusion.2
  88.7 3.0 copy.18
  91.7 1.5 slice.66
  93.2 0.8 fusion.12
  93.9 1.2 copy.20
  95.2 1.0 copy.21
  96.2 2.9 copy.28
  99.7 2.9 pad_maximum_fusion.weight_ref
  103.2 30.8 %all-gather.4.cloned.1.call-done.units_ref = bf16[512,2048]{1,0:T(8,128)(2,1)} async-done(((bf16[128,2048]{1,0:T(8,128)(2,1)}), bf16[512,2048]{1,0:T(8,128)(2,1)}) %all-gather.4.cloned.1.call-update) | async-done | bytes 2097168 | tf_op jit(solution)/shard_map/all_gather | solution.py:422
  134.0 9.1 %project.1 = (bf16[4,512,256]{2,1,0:T(8,128)(2,1)}, bf16[4,512,256]{2,1,0:T(8,128)(2,1)}, bf16[512,512]{1,0:T(8,128)(2,1)}, bf16[4,176,128]{2,1,0:T(8,128)(2,1)}) custom-call(s32[1]{0:T(128)} %copy.32.bound_ref, bf16[512,2048]{1,0:T(8,128)(2,1)} %all-gather.4.cloned.1.call-done.units_ref, bf16[2048,640]{1,0:T(8,128)(2,1)} %pad_maximum_fusion.weight_ref, ...), custom_call_target="tpu_custom_call" | custom-call | tf_op jit(solution)/shard_map/project/pallas_call | solution.py:136
  143.1 1.7 collective-permute-start.6
  144.8 3.6 collective-permute-start.7
  148.4 1.5 collective-permute-start.8
  149.9 3.2 or_reduce_fusion.2
  155.6 4.5 within.1
  161.0 5.8 %across.1 = bf16[512,2048]{1,0:T(8,128)(2,1)} custom-call(s32[1]{0:T(128)} %copy.32.bound_ref, s32[3]{0:T(128)} %add_convert_fusion.share_ref, bf16[4,512,256]{2,1,0:T(8,128)(2,1)} %get-tuple-element.20.fq_ref, f32[4,512,128]{2,1,0:T(8,128)} %get-tuple-element.23.num_ref, f32[4,512,8]{2,1,0:T(8,128)} %get-tuple-element.24.den_ref, ...), custom_call_target="tpu_custom_call" | custom-call | tf_op jit(solution)/shard_map/across/pallas_call | solution.py:215
  167.0 41.7 %reduce-scatter.6.cloned.1.call-done = bf16[128,2048]{1,0:T(8,128)(2,1)} async-done(((bf16[512,2048]{1,0:T(8,128)(2,1)}), bf16[128,2048]{1,0:T(8,128)(2,1)}) %reduce-scatter.6.cloned.1.call-update) | async-done | bytes 524304 | tf_op jit(solution)/shard_map/reduce_scatter | solution.py:450
  208.7 1.3 fusion.4
  210.0 1.0 fusion.6
  211.1 45.4 %all-gather.6.cloned.1.call-done.a_ref = bf16[512,2048]{1,0:T(8,128)(2,1)} async-done(((bf16[128,2048]{1,0:T(8,128)(2,1)}), bf16[512,2048]{1,0:T(8,128)(2,1)}) %all-gather.6.cloned.1.call-update) | async-done | bytes 2097168 | tf_op jit(solution)/shard_map/all_gather | solution.py:454
  256.5 1.7 slice.69.a_ref
  258.2 5.0 %matmul.3 = bf16[64,1536]{1,0:T(8,128)(2,1)} custom-call(bf16[64,2048]{1,0:T(8,128)(2,1)} %slice.69.a_ref, bf16[2048,1536]{1,0:T(8,128)(2,1)} %b_ref.3), custom_call_target="tpu_custom_call" | custom-call | tf_op jit(solution)/shard_map/matmul/pallas_call | solution.py:231
  263.1 1.7 collective-permute-start.9
  267.2 8.3 %matmul.2.qkv_ref = bf16[512,1536]{1,0:T(8,128)(2,1)} custom-call(bf16[512,2048]{1,0:T(8,128)(2,1)} %all-gather.6.cloned.1.call-done.a_ref, bf16[2048,1536]{1,0:T(8,128)(2,1)} %b_ref.3), custom_call_target="tpu_custom_call" | custom-call | tf_op jit(solution)/shard_map/matmul/pallas_call | solution.py:231
  276.2 10.0 %window.1 = bf16[512,2048]{1,0:T(8,128)(2,1)} custom-call(s32[2]{0:T(128)} %pad_add_fusion.3.bound_ref, bf16[512,1536]{1,0:T(8,128)(2,1)} %matmul.2.qkv_ref, bf16[64,1536]{1,0:T(8,128)(2,1)} %copy-done, bf16[512,2048]{1,0:T(8,128)(2,1)} %out_ref.3), custom_call_target="tpu_custom_call" | custom-call | tf_op jit(solution)/shard_map/window/pallas_call | solution.py:284
  286.2 33.7 %collective-permute-start.10 = (bf16[6400,512]{1,0:T(8,128)(2,1)}, bf16[6400,512]{1,0:T(8,128)(2,1)}, u32[]{:S(2)}, u32[]{:S(2)}) collective-permute-start(bf16[6400,512]{1,0:T(8,128)(2,1)} %refs_4_), channel_id=1, source_target_pairs={{0,4},{4,0},{8,12},{12,8},{1,5},{5,1},{9,13},{13,9},{2,6},{6,2},{1... | collective-permute-start | bytes 19660808 | tf_op jit(solution)/shard_map/ppermute | solution.py:412
  320.1 43.3 %reduce-scatter.8.cloned.1.call-done = bf16[128,2048]{1,0:T(8,128)(2,1)} async-done(((bf16[512,2048]{1,0:T(8,128)(2,1)}), bf16[128,2048]{1,0:T(8,128)(2,1)}) %reduce-scatter.8.cloned.1.call-update) | async-done | bytes 524304 | tf_op jit(solution)/shard_map/reduce_scatter | solution.py:465
  363.4 1.3 multiply_reduce_fusion
  364.7 2.1 multiply_convert_fusion
  366.8 0.9 copy.22.refs_8_
  368.2 44.0 %all-gather.8.cloned.1.call-done.refs_0_.refs_1_.refs_2_.refs_3_ = bf16[512,2048]{1,0:T(8,128)(2,1)} async-done(((bf16[128,2048]{1,0:T(8,128)(2,1)}), bf16[512,2048]{1,0:T(8,128)(2,1)}) %all-gather.8.cloned.1.call-update) | async-done | bytes 2097168 | tf_op jit(solution)/shard_map/all_gather | solution.py:469
  412.2 39.0 %scores.1 = f32[512,8]{1,0:T(8,128)} custom-call(s32[4]{0:T(128)} %iota_xor_fusion.order_ref, bf16[512,2048]{1,0:T(8,128)(2,1)} %all-gather.8.cloned.1.call-done.refs_0_.refs_1_.refs_2_.refs_3_, bf16[512,2048]{1,0:T(8,128)(2,1)} %all-gather.8.cloned.1.call-done.refs_0_.refs_1_.refs_2_.refs_3_, ...), custom_call_target="tpu_custom_call" | custom-call | tf_op jit(solution)/shard_map/scores/pallas_call | solution.py:348
  451.2 1.0 constant_dynamic-slice_fusion.3
  452.2 1.2 collective-permute-start.15
  453.4 0.9 collective-permute-start.13
  454.4 1.1 collective-permute-start.14
  455.8 3.0 collective-permute-done.13
  (81 shorter events, 8.1 us)
Async XLA Ops:
  6.5 71.2 %reduce-scatter.4.cloned.1.call-start = ((), (), s32[]{:S(2)}) async-start(), calls=%async_computation.3 | async-start | bytes 2621440 | tf_op jit(solution)/shard_map/reduce_scatter | solution.py:401
  7.9 3.1 collective-permute-start
  8.3 4.1 collective-permute-start.1
  10.8 3.0 collective-permute-start.2
  33.4 47.5 %copy-start.4 = (bf16[2048]{0:T(1024)(128)(2,1)S(1)}, bf16[2048]{0:T(1024)(128)(2,1)}, u32[]{:S(2)}) copy-start(bf16[2048]{0:T(1024)(128)(2,1)} %param.19) | copy-start | bytes 12292
  33.4 100.6 %all-gather.4.cloned.1.call-start = ((), (), s32[]{:S(2)}) async-start(), calls=%async_computation.4 | async-start | bytes 2621440 | tf_op jit(solution)/shard_map/all_gather | solution.py:422
  78.9 1.9 collective-permute-start.3
  79.0 6.4 %collective-permute-start.4 = (bf16[128,512]{1,0:T(8,128)(2,1)S(1)}, bf16[128,512]{1,0:T(8,128)(2,1)S(1)}, u32[]{:S(2)}, u32[]{:S(2)}) collective-permute-start(bf16[128,512]{1,0:T(8,128)(2,1)S(1)} %get-tuple-element.42), channel_id=1, source_target_pairs={{0,8},{4,12},{8,0},{12,4},{1,9},{5,13},{9,1},{13,5},{2,10},{6,14},... | collective-permute-start | bytes 393224 | tf_op jit(solution)/shard_map/ppermute | solution.py:403
  80.5 6.7 %collective-permute-start.5 = (bf16[128,512]{1,0:T(8,128)(2,1)S(1)}, bf16[128,512]{1,0:T(8,128)(2,1)S(1)}, u32[]{:S(2)}, u32[]{:S(2)}) collective-permute-start(bf16[128,512]{1,0:T(8,128)(2,1)S(1)} %get-tuple-element.41), channel_id=1, source_target_pairs={{0,12},{4,8},{8,4},{12,0},{1,13},{5,9},{9,5},{13,1},{2,14},{6,10},... | collective-permute-start | bytes 393224 | tf_op jit(solution)/shard_map/ppermute | solution.py:403
  88.6 120.1 %reduce-scatter.6.cloned.1.call-start = ((), (), s32[]{:S(2)}) async-start(), calls=%async_computation.5 | async-start | bytes 2621440 | tf_op jit(solution)/shard_map/reduce_scatter | solution.py:450
  95.1 4.0 copy-start.8
  143.1 17.1 %collective-permute-start.6 = (bf16[4,176,128]{2,1,0:T(8,128)(2,1)}, bf16[4,176,128]{2,1,0:T(8,128)(2,1)S(1)}, u32[]{:S(2)}, u32[]{:S(2)}) collective-permute-start(bf16[4,176,128]{2,1,0:T(8,128)(2,1)} %get-tuple-element.25), channel_id=1, source_target_pairs={{0,4},{4,8},{8,12},{1,5},{5,9},{9,13},{2,6},{6,10},{10,14},{3,7},{... | collective-permute-start | bytes 540680 | tf_op jit(solution)/shard_map/ppermute | solution.py:439
  144.8 15.3 %collective-permute-start.7 = (bf16[4,176,128]{2,1,0:T(8,128)(2,1)}, bf16[4,176,128]{2,1,0:T(8,128)(2,1)S(1)}, u32[]{:S(2)}, u32[]{:S(2)}) collective-permute-start(bf16[4,176,128]{2,1,0:T(8,128)(2,1)} %get-tuple-element.25), channel_id=1, source_target_pairs={{0,8},{4,12},{1,9},{5,13},{2,10},{6,14},{3,11},{7,15},{16,24},{20,... | collective-permute-start | bytes 540680 | tf_op jit(solution)/shard_map/ppermute | solution.py:439
  148.4 11.8 %collective-permute-start.8 = (bf16[4,176,128]{2,1,0:T(8,128)(2,1)}, bf16[4,176,128]{2,1,0:T(8,128)(2,1)S(1)}, u32[]{:S(2)}, u32[]{:S(2)}) collective-permute-start(bf16[4,176,128]{2,1,0:T(8,128)(2,1)} %get-tuple-element.25), channel_id=1, source_target_pairs={{0,12},{1,13},{2,14},{3,15},{16,28},{17,29},{18,30},{19,31}} | collective-permute-start | bytes 540680 | tf_op jit(solution)/shard_map/ppermute | solution.py:439
  160.2 0.7 copy-start.1
  160.2 0.7 copy-start.2
  160.2 0.8 copy-start.3
  161.0 6.0 %copy-start.5 = (bf16[2048]{0:T(1024)(128)(2,1)S(1)}, bf16[2048]{0:T(1024)(128)(2,1)}, u32[]{:S(2)}) copy-start(bf16[2048]{0:T(1024)(128)(2,1)} %param.23) | copy-start | bytes 12292
  166.8 89.7 %all-gather.6.cloned.1.call-start = ((), (), s32[]{:S(2)}) async-start(), calls=%async_computation.6 | async-start | bytes 2621440 | tf_op jit(solution)/shard_map/all_gather | solution.py:454
  166.9 153.1 %collective-permute-start.11 = (bf16[6400,512]{1,0:T(8,128)(2,1)}, bf16[6400,512]{1,0:T(8,128)(2,1)}, u32[]{:S(2)}, u32[]{:S(2)}) collective-permute-start(bf16[6400,512]{1,0:T(8,128)(2,1)} %refs_4_), channel_id=1, source_target_pairs={{0,8},{4,12},{8,0},{12,4},{1,9},{5,13},{9,1},{13,5},{2,10},{6,14},... | collective-permute-start | bytes 19660808 | tf_op jit(solution)/shard_map/ppermute | solution.py:413
  211.1 152.3 %reduce-scatter.8.cloned.1.call-start = ((), (), s32[]{:S(2)}) async-start(), calls=%async_computation.7 | async-start | bytes 2621440 | tf_op jit(solution)/shard_map/reduce_scatter | solution.py:465
  263.1 12.4 %collective-permute-start.9 = (bf16[64,1536]{1,0:T(8,128)(2,1)}, bf16[64,1536]{1,0:T(8,128)(2,1)S(1)}, u32[]{:S(2)}, u32[]{:S(2)}) collective-permute-start(bf16[64,1536]{1,0:T(8,128)(2,1)} %matmul.3), channel_id=1, source_target_pairs={{0,4},{4,8},{8,12},{1,5},{5,9},{9,13},{2,6},{6,10},{10,14},{3,7},{... | collective-permute-start | bytes 589832 | tf_op jit(solution)/shard_map/ppermute | solution.py:456
  275.5 44.5 %copy-start.6 = (bf16[2048]{0:T(1024)(128)(2,1)S(1)}, bf16[2048]{0:T(1024)(128)(2,1)}, u32[]{:S(2)}) copy-start(bf16[2048]{0:T(1024)(128)(2,1)} %param.26) | copy-start | bytes 12292
  275.5 0.7 copy-start
  286.2 80.6 %copy-start.7 = (s32[512]{0:T(512)S(1)}, s32[512]{0:T(512)}, u32[]{:S(2)}) copy-start(s32[512]{0:T(512)} %param.16) | copy-start | bytes 6148
  286.2 126.0 %all-gather.8.cloned.1.call-start = ((), (), s32[]{:S(2)}) async-start(), calls=%async_computation.8 | async-start | bytes 2621440 | tf_op jit(solution)/shard_map/all_gather | solution.py:469
  286.2 82.0 %collective-permute-start.10 = (bf16[6400,512]{1,0:T(8,128)(2,1)}, bf16[6400,512]{1,0:T(8,128)(2,1)}, u32[]{:S(2)}, u32[]{:S(2)}) collective-permute-start(bf16[6400,512]{1,0:T(8,128)(2,1)} %refs_4_), channel_id=1, source_target_pairs={{0,4},{4,0},{8,12},{12,8},{1,5},{5,1},{9,13},{13,9},{2,6},{6,2},{1... | collective-permute-start | bytes 19660808 | tf_op jit(solution)/shard_map/ppermute | solution.py:412
  320.0 48.3 %collective-permute-start.12 = (bf16[6400,512]{1,0:T(8,128)(2,1)}, bf16[6400,512]{1,0:T(8,128)(2,1)}, u32[]{:S(2)}, u32[]{:S(2)}) collective-permute-start(bf16[6400,512]{1,0:T(8,128)(2,1)} %collective-permute-done.11.refs_6_), channel_id=1, source_target_pairs={{0,4},{4,0},{8,12},{12,8},{1,5},{5,1},{9,13},{13,9},{2,6},{6,2},{1... | collective-permute-start | bytes 19660808 | tf_op jit(solution)/shard_map/ppermute | solution.py:414
  452.2 3.6 collective-permute-start.15
  453.4 5.4 %collective-permute-start.13 = (f32[3,128]{1,0:T(4,128)S(1)}, f32[3,128]{1,0:T(4,128)S(1)}, u32[]{:S(2)}, u32[]{:S(2)}) collective-permute-start(f32[3,128]{1,0:T(4,128)S(1)} %bitcast.72), channel_id=1, source_target_pairs={{0,1},{1,2},{2,3},{3,0},{4,5},{5,6},{6,7},{7,4},{8,9},{9,10},{10,1... | collective-permute-start | bytes 4616 | tf_op jit(solution)/shard_map/ppermute | solution.py:477
  454.4 4.5 collective-permute-start.14
Sparse Core Ops, SparseCore 0:
  33.5 44.2 reduce-scatter.3
  88.7 45.2 all-gather.3
  166.9 41.7 reduce-scatter.5
  211.2 45.2 all-gather.5
  286.3 77.0 reduce-scatter.7
  366.9 45.2 all-gather.7

commit v2 on v1

v2 whole, which is shorter than its diff:
```python
import functools

import jax
import jax.numpy as jnp
import numpy as np
from jax import lax
from jax.experimental import pallas as pl
from jax.experimental.pallas import tpu as pltpu
from jax.sharding import PartitionSpec as P

FEAT = 16
WINDOW = 64
HEAD_DIM = 128
EPSILON = 1e-05
NEGATIVE = -1e30
LANES = 128
WIDE = 256
STATE_ROWS = 160
BUFFER_ROWS = 176
F32 = jnp.float32
BF16 = jnp.bfloat16
VMEM_BYTES = 56 * 1024 * 1024


def params(**kw):
    return pltpu.CompilerParams(vmem_limit_bytes=VMEM_BYTES, **kw)


def whole():
    return pl.BlockSpec(memory_space=pltpu.VMEM)


def smem():
    return pl.BlockSpec(memory_space=pltpu.SMEM)


def dot(a, b, dims=((1,), (0,))):
    return lax.dot_general(a, b, (dims, ((), ())), preferred_element_type=F32)


def xor_pairs(size, k):
    return [(i, i ^ k) for i in range(size)]


def rms(values, gain):
    factor = lax.rsqrt(jnp.mean(values * values, axis=-1, keepdims=True) + EPSILON)
    return (values * factor * gain.astype(F32)).astype(BF16)


def turned(value, step):
    size = lax.axis_size("head")
    return lax.ppermute(value, "head", [(i, (i + step) % size) for i in range(size)])


def gather_rows(own):
    size = lax.axis_size("head")
    if size != 4:
        full = lax.all_gather(own, "head")
        here = lax.axis_index("head")
        return [[own]] + [
            [lax.dynamic_index_in_dim(full, (here + k) % size, 0, False)] for k in range(1, size)
        ]
    half = own.shape[0] // 2
    before, after = turned(own, 1), turned(own, -1)
    return [[own], [after], [turned(before[:half], 1), turned(after[half:], -1)], [before]]


def add_kernel(next_ref, prev_ref, upper_ref, lower_ref, right_ref, left_ref):
    half = upper_ref.shape[0]
    right_ref[0:half] = (next_ref[0:half].astype(F32) + upper_ref[...].astype(F32)).astype(BF16)
    right_ref[half:] = next_ref[half:]
    left_ref[0:half] = prev_ref[0:half]
    left_ref[half:] = (prev_ref[half:].astype(F32) + lower_ref[...].astype(F32)).astype(BF16)


def scatter_rows(far, near):
    size = lax.axis_size("head")
    if size != 4:
        here = lax.axis_index("head")
        full = jnp.stack([near()[0]] + list(far))
        full = jnp.stack(
            [lax.dynamic_index_in_dim(full, (d - here) % size, 0, False) for d in range(size)]
        )
        return [lax.psum_scatter(full, "head", scatter_dimension=0, tiled=True)[0]]
    upper, lower = turned(far[0], 1), turned(far[1], -1)
    own, after, before = near()
    right, left = pl.pallas_call(
        add_kernel,
        in_specs=[whole()] * 4,
        out_specs=[whole()] * 2,
        out_shape=[jax.ShapeDtypeStruct(own.shape, BF16)] * 2,
        compiler_params=params(),
        name="pass_on",
    )(after, before, upper, lower)
    return [own, turned(right, 1), turned(left, -1)]


def chunk_order(size):
    if size == 4:
        return [[0], [1, 3], [2]]
    return [[k] for k in range(size)]


def lookup_kernel(ids_ref, table_ref, *refs):
    outs, total = refs[:-1], refs[-1]
    step = pl.program_id(0)
    tile = table_ref.shape[0]
    count = ids_ref.shape[1]
    ids = jnp.transpose(jnp.broadcast_to(ids_ref[...], (8, count)))[:, 0:1] - step * tile
    hot = (lax.broadcasted_iota(jnp.int32, (count, tile), 1) == ids).astype(F32).astype(BF16)
    found = dot(hot, table_ref[...])

    @pl.when(step == 0)
    def _():
        total[...] = found

    @pl.when(step > 0)
    def _():
        total[...] += found

    @pl.when(step == pl.num_programs(0) - 1)
    def _():
        rows = outs[0].shape[0]
        for n, out in enumerate(outs):
            out[...] = total[n * rows : (n + 1) * rows].astype(BF16)


def lookup(ids, table, pieces):
    count = ids.shape[0]
    rows, width = table.shape
    tile = rows // 5
    return pl.pallas_call(
        lookup_kernel,
        grid=(rows // tile,),
        in_specs=[
            pl.BlockSpec((1, count), lambda i: (0, 0)),
            pl.BlockSpec((tile, width), lambda i: (i, 0)),
        ],
        out_specs=[pl.BlockSpec((count // pieces, width), lambda i: (0, 0))] * pieces,
        out_shape=[jax.ShapeDtypeStruct((count // pieces, width), BF16)] * pieces,
        scratch_shapes=[pltpu.VMEM((count, width), F32)],
        compiler_params=params(),
        name="lookup",
    )(ids.reshape(1, count), table)


def collect_kernel(parts, *refs):
    ins, outs = refs[:parts], refs[parts:]
    rows = outs[0].shape[0]
    for n, out in enumerate(outs):
        span = slice(n * rows, (n + 1) * rows)
        total = ins[0][span].astype(F32)
        for part in ins[1:]:
            total = total + part[span].astype(F32)
        out[...] = total.astype(BF16)


def collect(parts, pieces):
    rows, width = parts[0].shape
    return pl.pallas_call(
        functools.partial(collect_kernel, len(parts)),
        in_specs=[whole()] * len(parts),
        out_specs=[whole()] * pieces,
        out_shape=[jax.ShapeDtypeStruct((rows // pieces, width), BF16)] * pieces,
        compiler_params=params(),
        name="collect",
    )(*parts)


def begin_kernel(pieces, order_ref, gain_ref, *refs):
    ins, (embedded_ref, units_ref, held) = refs[:pieces], refs[pieces:]
    width = ins[0].shape[1]
    for n in range(pieces):
        held[order_ref[n]] = ins[n][...]
    values = jnp.concatenate([held[n] for n in range(pieces)], axis=1)
    embedded_ref[...] = values
    units_ref[...] = rms(values.astype(F32), gain_ref[...])


def begin(order, gain, pieces):
    rows, width = pieces[0].shape
    full = jax.ShapeDtypeStruct((rows, width * len(pieces)), BF16)
    return pl.pallas_call(
        functools.partial(begin_kernel, len(pieces)),
        in_specs=[smem()] + [whole()] * (1 + len(pieces)),
        out_specs=[whole()] * 2,
        out_shape=[full, full],
        scratch_shapes=[pltpu.VMEM((len(pieces), rows, width), BF16)],
        compiler_params=params(),
        name="begin",
    )(order, gain.reshape(1, -1), *pieces)


def finish_kernel(parts, last, residual_ref, gain_ref, *refs):
    total = refs[0][...].astype(F32)
    for part in refs[1:parts]:
        total = total + part[...].astype(F32)
    total = total + residual_ref[...].astype(F32)
    if not last:
        total = total.astype(BF16)
        refs[parts + 1][...] = total
    refs[parts][...] = rms(total.astype(F32), gain_ref[...])


def finish(residual, gain, parts, last):
    full = jax.ShapeDtypeStruct(residual.shape, BF16)
    return pl.pallas_call(
        functools.partial(finish_kernel, len(parts), last),
        in_specs=[whole()] * (2 + len(parts)),
        out_specs=[whole()] * (1 if last else 2),
        out_shape=[full] * (1 if last else 2),
        compiler_params=params(),
        name="finish",
    )(residual, gain.reshape(1, -1), *parts)


def selectors():
    pairs = [(r, s) for r in range(FEAT) for s in range(r, FEAT)]
    picks = np.zeros((2, 2, LANES, WIDE), np.float32)
    extra = np.zeros((3, WIDE), np.float32)
    extra[0:2, 0] = 1.0
    extra[1, 1 : 1 + FEAT] = 1.0
    extra[2] = 1.0
    for kind in range(2):
        first = kind * FEAT
        for r in range(FEAT):
            picks[kind, 0, first + r, 1 + r] = FEAT ** (-0.25)
        for n, (r, s) in enumerate(pairs):
            picks[kind, 0, first + r, 1 + FEAT + n] = FEAT ** (-0.25)
            picks[kind, 1, first + s, 1 + FEAT + n] = FEAT ** (-0.25)
    for n, (r, s) in enumerate(pairs):
        extra[2, 1 + FEAT + n] = 0.5**0.5 if r == s else 1.0
    return jnp.asarray(np.concatenate([picks, picks], axis=2), BF16), jnp.asarray(extra)


def place_column(places_ref, slots, rows):
    inner = lax.broadcasted_iota(jnp.int32, (rows, 1), 0)
    return jnp.concatenate([inner + places_ref[slot] for slot in slots], axis=0)


def place_row(places_ref, slots, rows):
    inner = lax.broadcasted_iota(jnp.int32, (1, rows), 1)
    return jnp.concatenate([inner + places_ref[slot] for slot in slots], axis=1)


def project_kernel(heads, slots, chunk, count, pieces, more, last, bound_ref, places_ref, *refs):
    units = jnp.concatenate([ref[...] for ref in refs[:pieces]], axis=0)
    weight_ref, pick_ref, extra_ref = refs[pieces : pieces + 3]
    fq_ref, fk_ref, v_ref, state_ref = refs[-4:]
    projected = dot(units, weight_ref[...])
    rows, width = projected.shape
    needed = (heads - 1) * LANES + WIDE
    if needed > width:
        projected = jnp.pad(projected, ((0, 0), (0, needed - width)))
    bound = bound_ref[0]
    place = place_column(places_ref, slots, chunk)
    kept = ((place >= bound) | (bound == count)).astype(F32)
    ones = jnp.ones((8, rows), BF16)
    shift = 2 * FEAT
    for head in range(heads):
        part = projected[:, head * LANES : head * LANES + WIDE]
        narrow = part if head == 0 else pltpu.roll(part, WIDE - shift * head, 1)
        narrow = narrow[:, :LANES]
        values = pltpu.roll(part, WIDE - shift * (head + 1), 1)[:, :HEAD_DIM].astype(BF16)
        v_ref[:, head * HEAD_DIM : (head + 1) * HEAD_DIM] = values
        upper = narrow.astype(BF16)
        lower = (narrow - upper.astype(F32)).astype(BF16)
        both = jnp.concatenate([upper, lower], axis=1)
        feats = []
        for kind in range(2):
            one = dot(both, pick_ref[kind, 0]) + extra_ref[0:1]
            two = dot(both, pick_ref[kind, 1]) + extra_ref[1:2]
            feats.append((one * two * extra_ref[2:3]).astype(BF16))
        fq_ref[head] = feats[0]
        fk_ref[head] = feats[1]
        keys = (feats[1].astype(F32) * kept).astype(BF16)
        state = dot(keys, values, ((0,), (0,)))
        total = dot(ones, keys)
        tail = jnp.concatenate([total[0:1, :LANES], total[0:1, LANES:], jnp.zeros((14, LANES), F32)], axis=0)
        state = jnp.concatenate([state[0:STATE_ROWS], tail], axis=0)
        if more:
            state = state + refs[pieces + 3][head]
        state_ref[head] = state.astype(BF16) if last else state


def project(bound, places, slots, chunk, count, pieces, weight, constants, earlier, last, heads):
    rows = sum(piece.shape[0] for piece in pieces)
    extra = [] if earlier is None else [earlier]
    return pl.pallas_call(
        functools.partial(project_kernel, heads, slots, chunk, count, len(pieces), bool(extra), last),
        in_specs=[smem(), smem()] + [whole()] * (len(pieces) + 3 + len(extra)),
        out_specs=[whole()] * 4,
        out_shape=[
            jax.ShapeDtypeStruct((heads, rows, WIDE), BF16),
            jax.ShapeDtypeStruct((heads, rows, WIDE), BF16),
            jax.ShapeDtypeStruct((rows, heads * HEAD_DIM), BF16),
            jax.ShapeDtypeStruct((heads, BUFFER_ROWS, HEAD_DIM), BF16 if last else F32),
        ],
        compiler_params=params(),
        name="project",
    )(bound, places, *pieces, weight, *constants, *extra)


def within_kernel(heads, slots, chunk, sets, bound_ref, places_ref, *refs):
    fqs, fks, vs = refs[:sets], refs[sets : 2 * sets], refs[2 * sets : 3 * sets]
    num_ref, den_ref = refs[3 * sets :]
    bound = bound_ref[0]
    row = place_column(places_ref, slots, chunk)
    col = place_row(places_ref, slots, chunk)
    allowed = (row >= col) & ((row >= bound) == (col >= bound))
    for head in range(heads):
        query = jnp.concatenate([ref[head] for ref in fqs], axis=0)
        keys = jnp.concatenate([ref[head] for ref in fks], axis=0)
        values = jnp.concatenate(
            [ref[:, head * HEAD_DIM : (head + 1) * HEAD_DIM] for ref in vs], axis=0
        )
        weights = dot(query, keys, ((1,), (1,)))
        weights = jnp.where(allowed, weights, 0.0)
        den_ref[head] = jnp.broadcast_to(
            jnp.sum(weights, axis=-1, keepdims=True), (row.shape[0], 8)
        )
        num_ref[head] = dot(weights.astype(BF16), values)


def within(bound, places, slots, chunk, fqs, fks, vs, heads):
    count = len(slots) * chunk
    return pl.pallas_call(
        functools.partial(within_kernel, heads, slots, chunk, len(fqs)),
        in_specs=[smem(), smem()] + [whole()] * (3 * len(fqs)),
        out_specs=[whole()] * 2,
        out_shape=[
            jax.ShapeDtypeStruct((heads, count, HEAD_DIM), F32),
            jax.ShapeDtypeStruct((heads, count, 8), F32),
        ],
        compiler_params=params(),
        name="within",
    )(bound, places, *fqs, *fks, *vs)


def split_store(total, refs):
    rows = refs[0].shape[0]
    for n, ref in enumerate(refs):
        ref[...] = total[n * rows : (n + 1) * rows].astype(BF16)


def across_kernel(heads, slots, chunk, sets, earlier, near, bound_ref, places_ref, share_ref, *refs):
    fqs, refs = refs[:sets], refs[sets:]
    num_ref, den_ref, gain_ref, weight_ref = refs[:4]
    states, refs = refs[4 : 4 + earlier], refs[4 + earlier :]
    mixed_ref, fars = refs[0], refs[1:]
    bound = bound_ref[0]
    before = (place_column(places_ref, slots, chunk) < bound).astype(F32)
    for head in range(heads):
        carried = jnp.zeros((BUFFER_ROWS, HEAD_DIM), F32)
        for n in range(earlier):
            carried = carried + jnp.where(share_ref[n] > 0, states[n][head].astype(F32), 0.0)
        state = jnp.concatenate(
            [carried[0:STATE_ROWS], jnp.zeros((WIDE - STATE_ROWS, HEAD_DIM), F32)], axis=0
        ).astype(BF16)
        total = jnp.concatenate(
            [carried[STATE_ROWS : STATE_ROWS + 1], carried[STATE_ROWS + 1 : STATE_ROWS + 2]], axis=1
        )
        query = jnp.concatenate([ref[head] for ref in fqs], axis=0)
        numerator = num_ref[head] + before * dot(query, state)
        more = jnp.sum(query.astype(F32) * total, axis=-1, keepdims=True)
        denominator = den_ref[head][:, 0:1] + before * more
        lanes = slice(head * HEAD_DIM, (head + 1) * HEAD_DIM)
        mixed_ref[:, lanes] = (numerator / denominator * gain_ref[:, lanes].astype(F32)).astype(BF16)
    split_store(dot(mixed_ref[near * chunk :], weight_ref[...]), fars)


def across(bound, places, share, slots, chunk, near, far, fqs, num, den, gain, weight, states, heads):
    count = len(slots) * chunk
    rows = (count - near * chunk) // far
    return pl.pallas_call(
        functools.partial(across_kernel, heads, slots, chunk, len(fqs), len(states), near),
        in_specs=[smem()] * 3 + [whole()] * (len(fqs) + 4 + len(states)),
        out_specs=[whole()] * (1 + far),
        out_shape=[jax.ShapeDtypeStruct((count, heads * HEAD_DIM), BF16)]
        + [jax.ShapeDtypeStruct((rows, weight.shape[1]), BF16)] * far,
        compiler_params=params(),
        name="across",
    )(bound, places, share, *fqs, num, den, gain, weight, *states)


def near_kernel(chunk, mixed_ref, weight_ref, *outs):
    split_store(dot(mixed_ref[0 : chunk * len(outs)], weight_ref[...]), outs)


def near_chunks(mixed, weight, near, chunk):
    return pl.pallas_call(
        functools.partial(near_kernel, chunk),
        in_specs=[whole()] * 2,
        out_specs=[whole()] * near,
        out_shape=[jax.ShapeDtypeStruct((chunk, weight.shape[1]), BF16)] * near,
        compiler_params=params(),
        name="near",
    )(mixed, weight)


def matmul_kernel(*refs):
    a = jnp.concatenate([ref[...] for ref in refs[:-2]], axis=0)
    refs[-1][...] = dot(a, refs[-2][...]).astype(BF16)


def matmul(pieces, b, tile):
    rows = sum(piece.shape[0] for piece in pieces)
    inner = b.shape[0]
    return pl.pallas_call(
        matmul_kernel,
        grid=(b.shape[1] // tile,),
        in_specs=[
            pl.BlockSpec(piece.shape, lambda n: (0, 0), pipeline_mode=pl.Buffered(1)) for piece in pieces
        ]
        + [pl.BlockSpec((inner, tile), lambda n: (0, n))],
        out_specs=pl.BlockSpec((rows, tile), lambda n: (0, n)),
        out_shape=jax.ShapeDtypeStruct((rows, b.shape[1]), BF16),
        compiler_params=params(),
        name="matmul",
    )(*pieces, b)


def attend(query, keys, values, allowed):
    scores = dot(query, keys, ((1,), (1,))) * HEAD_DIM ** (-0.5)
    scores = jnp.where(allowed, scores, NEGATIVE)
    peak = jnp.max(scores, axis=-1, keepdims=True)
    weights = jnp.where(allowed, jnp.exp(scores - peak), 0.0)
    probabilities = (weights / jnp.sum(weights, axis=-1, keepdims=True)).astype(BF16)
    return dot(probabilities, values).astype(BF16)


def local_kernel(heads, slots, spots, chunk, sets, bound_ref, places_ref, *refs):
    qkvs, (result_ref, first_ref) = refs[:sets], refs[sets:]
    size = len(slots)
    reach = chunk + WINDOW
    bound = bound_ref[0]
    row = lax.broadcasted_iota(jnp.int32, (chunk, reach), 0)
    col = lax.broadcasted_iota(jnp.int32, (chunk, reach), 1)
    band = (col > row) & (col <= row + WINDOW)
    for slot in range(size):
        k = slots[slot]
        mine, at = spots[k]
        theirs, there = spots[(k - 1) % size]
        base = places_ref[slot]
        query_place = row + base
        key_place = col + (base - WINDOW)
        allowed = band & (key_place >= 0) & ((query_place >= bound) == (key_place >= bound))
        rows = slice(at, at + chunk)
        tail = slice(there + chunk - WINDOW, there + chunk)

        @pl.when(base == 0)
        def _():
            first_ref[...] = qkvs[mine][at : at + WINDOW]

        for head in range(heads):
            lane = head * 3 * HEAD_DIM
            keys, values = [
                jnp.concatenate(
                    [
                        qkvs[theirs][tail, lane + n * HEAD_DIM : lane + (n + 1) * HEAD_DIM],
                        qkvs[mine][rows, lane + n * HEAD_DIM : lane + (n + 1) * HEAD_DIM],
                    ],
                    axis=0,
                )
                for n in (1, 2)
            ]
            result_ref[slot * chunk : (slot + 1) * chunk, head * HEAD_DIM : (head + 1) * HEAD_DIM] = attend(
                qkvs[mine][rows, lane : lane + HEAD_DIM], keys, values, allowed
            )


def local_window(bound, places, slots, spots, chunk, qkvs, heads):
    return pl.pallas_call(
        functools.partial(local_kernel, heads, slots, spots, chunk, len(qkvs)),
        in_specs=[smem(), smem()] + [whole()] * len(qkvs),
        out_specs=[whole()] * 2,
        out_shape=[
            jax.ShapeDtypeStruct((len(slots) * chunk, heads * HEAD_DIM), BF16),
            jax.ShapeDtypeStruct((WINDOW, qkvs[0].shape[1]), BF16),
        ],
        compiler_params=params(),
        name="local_window",
    )(bound, places, *qkvs)


def halo_kernel(heads, count, start, info_ref, local_ref, first_ref, halo_ref, weight_ref, result_ref, *fars):
    result_ref[...] = local_ref[...]
    bound, valid_from, spot = info_ref[0], info_ref[1], info_ref[2]
    row = lax.broadcasted_iota(jnp.int32, (WINDOW, 2 * WINDOW), 0)
    col = lax.broadcasted_iota(jnp.int32, (WINDOW, 2 * WINDOW), 1)
    key_place = col - WINDOW
    allowed = (col > row) & (col <= row + WINDOW) & ((row >= bound) == (key_place >= bound))
    allowed = allowed & ((key_place >= 0) | (key_place + count >= valid_from))
    spot = pl.multiple_of(spot, WINDOW)
    for head in range(heads):
        lane = head * 3 * HEAD_DIM
        keys, values = [
            jnp.concatenate(
                [ref[:, lane + n * HEAD_DIM : lane + (n + 1) * HEAD_DIM] for ref in (halo_ref, first_ref)], axis=0
            )
            for n in (1, 2)
        ]
        result_ref[pl.ds(spot, WINDOW), head * HEAD_DIM : (head + 1) * HEAD_DIM] = attend(
            first_ref[:, lane : lane + HEAD_DIM], keys, values, allowed
        )
    split_store(dot(result_ref[start:], weight_ref[...]), fars)


def halo_window(info, near, chunk, far, local, first, halo, weight, heads):
    count = local.shape[0]
    rows = (count - near * chunk) // far
    return pl.pallas_call(
        functools.partial(halo_kernel, heads, count, near * chunk),
        in_specs=[smem()] + [whole()] * 4,
        out_specs=[whole()] * (1 + far),
        out_shape=[jax.ShapeDtypeStruct(local.shape, BF16)]
        + [jax.ShapeDtypeStruct((rows, weight.shape[1]), BF16)] * far,
        compiler_params=params(),
        name="halo_window",
    )(info, local, first, halo, weight)


def score_kernel(units_count, pieces, first, order_ref, *refs):
    units, refs = refs[:units_count], refs[units_count:]
    tables, (goal_ref, before_ref, out_ref, turned_ref) = refs[:pieces], refs[pieces:]
    step = pl.program_id(0)
    tile, width = tables[0].shape

    @pl.when(step == 0)
    def _():
        rows = jnp.concatenate([ref[...] for ref in units], axis=0)
        turned_ref[...] = jnp.transpose(rows)
        out_ref[...] = before_ref[...]

    logits = None
    for n in range(pieces):
        part = turned_ref[pl.ds(pl.multiple_of(order_ref[n] * width, width), width), :]
        more = dot(tables[n][...], part)
        logits = more if logits is None else logits + more
    count = logits.shape[1]
    logits = logits.reshape(tile // 8, 8, count)
    row = lax.broadcasted_iota(jnp.int32, (tile // 8, 8, count), 0) * 8
    row = row + lax.broadcasted_iota(jnp.int32, (tile // 8, 8, count), 1)
    goal = (goal_ref[...] - (step * tile + first)).reshape(1, 1, count)
    old = out_ref[0]
    peak = jnp.maximum(old, jnp.max(logits, axis=0))
    out_ref[0] = peak
    out_ref[1] = out_ref[1] * jnp.exp(old - peak) + jnp.sum(jnp.exp(logits - peak[None]), axis=0)
    out_ref[2] = out_ref[2] + jnp.sum(jnp.where(row == goal, logits, 0.0), axis=0)


def scores(order, units, tables, goal, before, first):
    count = goal.shape[1]
    tile = 640
    rows, width = tables[-1].shape
    skips = [first // tile if table.shape[0] != rows else 0 for table in tables]
    return pl.pallas_call(
        functools.partial(score_kernel, len(units), len(tables), first),
        in_specs=[smem()]
        + [pl.BlockSpec(piece.shape, lambda i: (0, 0), pipeline_mode=pl.Buffered(1)) for piece in units]
        + [pl.BlockSpec((tile, width), lambda i, skip=skip: (i + skip, 0)) for skip in skips]
        + [
            pl.BlockSpec((1, count), lambda i: (0, 0)),
            pl.BlockSpec((3, 8, count), lambda i: (0, 0, 0)),
        ],
        out_specs=pl.BlockSpec((3, 8, count), lambda i: (0, 0, 0)),
        grid=(rows // tile,),
        out_shape=jax.ShapeDtypeStruct((3, 8, count), F32),
        scratch_shapes=[pltpu.VMEM((units[0].shape[1], count), BF16)],
        compiler_params=params(),
        name="scores",
    )(order, *units, *tables, goal, before)


def shards(
    token_ids,
    target_ids,
    doc_start,
    vocab_table,
    norm_gain_one,
    lin_qkv,
    lin_head_gain,
    lin_out,
    norm_gain_two,
    win_qkv,
    win_out,
    final_gain,
):
    head_count = lax.axis_size("head")
    seq_count = lax.axis_size("seq")
    head_index = lax.axis_index("head")
    seq_index = lax.axis_index("seq")
    tok_count = token_ids.shape[0]
    chunk = tok_count // head_count
    vocab_rows = vocab_table.shape[0]
    heads = lin_qkv.shape[1] // (2 * FEAT + HEAD_DIM)
    vocab_first = head_index * vocab_rows
    calls = chunk_order(head_count)
    slots = [k for call in calls for k in call]
    near = 3 if head_count == 4 else 1
    far = 2 if head_count == 4 else head_count - 1
    spots = {}
    for n, call in enumerate(calls):
        for at, k in enumerate(call):
            spots[k] = (n, at * chunk)
    held_at = (head_index + jnp.asarray(slots, jnp.int32)) % head_count
    places = held_at * chunk

    marks = jnp.concatenate([token_ids, jnp.broadcast_to(doc_start, (LANES,))])
    marks = jnp.stack(
        [marks] + [lax.ppermute(marks, "seq", xor_pairs(seq_count, k)) for k in range(1, seq_count)]
    )
    block = jnp.arange(seq_count, dtype=jnp.int32)
    order = seq_index ^ block
    starts = marks[:, tok_count]
    starts = jnp.sum(jnp.where(order[None, :] == block[:, None], starts[None, :], 0), axis=1)
    bound = doc_start.astype(jnp.int32)

    ids = (marks[:, :tok_count] - vocab_first).reshape(seq_count, head_count, chunk)

    def ids_of(k):
        return lax.dynamic_index_in_dim(ids, (head_index + k) % head_count, 1, False).reshape(-1)

    if head_count == 4:
        outer = lookup(ids_of(2), vocab_table, 2)
        inner = lambda: (
            lookup(ids_of(0), vocab_table, 1)
            + lookup(jnp.concatenate([ids_of(1), ids_of(3)]), vocab_table, 2)
        )
    else:
        outer = [lookup(ids_of(k), vocab_table, 1)[0] for k in range(1, head_count)]
        inner = lambda: lookup(ids_of(0), vocab_table, 1)
    found = collect(scatter_rows(outer, inner), seq_count)
    gathered = [found[0]] + [
        lax.ppermute(found[k], "seq", xor_pairs(seq_count, k)) for k in range(1, seq_count)
    ]
    embedded, units = begin(order, norm_gain_one, gathered)
    chunks = gather_rows(units)

    constants = selectors()
    sets, state = [], None
    for n, call in enumerate(calls):
        pieces = [piece for k in call for piece in chunks[k]]
        first = sum(len(c) for c in calls[:n])
        made = project(
            bound,
            places[first : first + len(call)],
            list(range(len(call))),
            chunk,
            tok_count,
            pieces,
            lin_qkv,
            constants,
            state,
            n == len(calls) - 1,
            heads,
        )
        sets.append(made[:3])
        state = made[3]
    fqs, fks, vs = zip(*sets)
    states, shares = [], []
    for back in range(1, seq_count):
        states.append(
            lax.ppermute(state, "seq", [(i, i + back) for i in range(seq_count - back)])
        )
        between = (block > seq_index - back) & (block < seq_index)
        broken = jnp.sum(jnp.where(between & (starts != tok_count), 1, 0))
        shares.append(((broken == 0) & (seq_index >= back)).astype(jnp.int32))
    position = list(range(head_count))
    num, den = within(bound, places, position, chunk, fqs, fks, vs, heads)
    mixed, *outer = across(
        bound,
        places,
        jnp.stack(shares),
        position,
        chunk,
        near,
        far,
        fqs,
        num,
        den,
        lin_head_gain.reshape(1, -1),
        lin_out,
        states,
        heads,
    )
    parts = scatter_rows(outer, lambda: near_chunks(mixed, lin_out, near, chunk))
    units, residual = finish(embedded, norm_gain_two, parts, False)

    if seq_count == 4:
        lots = [vocab_rows * 3 // 5, vocab_rows * 2 // 5]
        early, _ = lax.optimization_barrier((vocab_table[: lots[0]], states))
        early = lax.ppermute(early, "seq", xor_pairs(seq_count, 2))
        early_corner = lax.ppermute(early, "seq", xor_pairs(seq_count, 1))
        beside = lax.ppermute(vocab_table, "seq", xor_pairs(seq_count, 1))

    chunks = gather_rows(units)
    qkvs = []
    for call in calls:
        qkvs.append(matmul([piece for k in call for piece in chunks[k]], win_qkv, 3 * HEAD_DIM))
    tail = jnp.zeros((WINDOW, win_qkv.shape[1]), BF16)
    for slot, k in enumerate(slots):
        n, at = spots[k]
        tail = jnp.where(
            held_at[slot] == head_count - 1, qkvs[n][at + chunk - WINDOW : at + chunk], tail
        )
    halo = lax.ppermute(tail, "seq", [(i, i + 1) for i in range(seq_count - 1)])
    previous = jnp.sum(jnp.where(block == seq_index - 1, starts, 0))
    valid_from = jnp.where(
        seq_index == 0, tok_count, jnp.where(previous == tok_count, 0, previous)
    ).astype(jnp.int32)
    first_spot = jnp.sum(jnp.where(held_at == 0, jnp.arange(head_count) * chunk, 0)).astype(jnp.int32)
    local, first = local_window(bound, places, slots, spots, chunk, qkvs, heads)
    info = jnp.stack([bound[0], valid_from, first_spot])
    mixed, *outer = halo_window(info, near, chunk, far, local, first, halo, win_out, heads)
    parts = scatter_rows(outer, lambda: near_chunks(mixed, win_out, near, chunk))
    units = finish(residual, final_gain, parts, True)[0]

    if seq_count == 4:
        late, _ = lax.optimization_barrier((vocab_table[lots[0] :], halo))
        late = lax.ppermute(late, "seq", xor_pairs(seq_count, 2))
        late_corner = lax.ppermute(late, "seq", xor_pairs(seq_count, 1))
        lots = [
            (0, [vocab_table, beside, early, early_corner]),
            (lots[0], [vocab_table, beside, late, late_corner]),
        ]
    else:
        lots = [(0, [lax.all_gather(vocab_table, "seq", axis=1, tiled=True)])]
        order = jnp.zeros((1,), jnp.int32)
    chunks = gather_rows(units)
    goals = (target_ids - vocab_first).reshape(head_count, chunk)
    found = {}
    for group in [[0, 3], [1, 2]] if head_count == 4 else [[k] for k in range(head_count)]:
        goal = jnp.concatenate(
            [
                lax.dynamic_index_in_dim(goals, (head_index + k) % head_count, 0, False)
                for k in group
            ]
        ).reshape(1, -1)
        state = jnp.zeros((3, 8, goal.shape[1]), F32).at[0].set(NEGATIVE)
        for first, tables in lots:
            state = scores(
                order, [piece for k in group for piece in chunks[k]], tables, goal, state, first
            )
        peak = jnp.max(state[0], axis=0)
        total = jnp.sum(state[1] * jnp.exp(state[0] - peak), axis=0)
        triple = jnp.stack([peak, total, jnp.sum(state[2], axis=0)])
        for at, k in enumerate(group):
            found[k] = triple[:, at * chunk : (at + 1) * chunk]

    shares = jnp.stack([found[0]] + [turned(found[k], k) for k in range(1, head_count)])
    peak = jnp.max(shares[:, 0], axis=0)
    total = jnp.sum(shares[:, 1] * jnp.exp(shares[:, 0] - peak), axis=0)
    return jnp.sum(shares[:, 2], axis=0) - (peak + jnp.log(total))


def solution(mesh):
    return jax.shard_map(
        shards,
        mesh=mesh,
        in_specs=(
            P(("shadow", "seq")),
            P(("shadow", "seq")),
            P(("shadow", "seq")),
            P(("shadow", "head"), "seq"),
            P("shadow"),
            P("shadow", "head"),
            P(("shadow", "head")),
            P(("shadow", "head"), None),
            P("shadow"),
            P("shadow", "head"),
            P(("shadow", "head"), None),
            P("shadow"),
        ),
        out_specs=P(("shadow", "seq", "head")),
        check_vma=False,
    )
```

time: 467 us -> 456 us (0.976)
  waiting for transfers between devices: 262 us -> 199 us
  Pallas kernels: 99.8 us -> 147 us
  starting transfers between devices: 50.7 us -> 70.8 us
  between operations: 17.4 us -> 6.43 us
  other arithmetic: 15.5 us -> 10.2 us
    ppermute x9 -> x35, waiting for transfers between devices: 3.4 us -> 191 us  [the longest x27 134 us: turned(): lax.ppermute(value, 'head', [(i, (i + step) % size) for i in range(size)])]
    reduce_scatter x3 -> x0, waiting for transfers between devices: 129 us -> none  [the longest x1 44.3 us: shards(): found = lax.psum_scatter(found, 'head', scatter_dimension=0, tiled=True)[0]]
    all_gather x3 -> x0, waiting for transfers between devices: 120 us -> none  [the longest x1 45.4 us: shards(): units_two = lax.all_gather(units_two, 'head', axis=0, tiled=True)]
    pallas_call x6 -> x23, Pallas kernels: 86.5 us -> 131 us  [the longest x4 37.5 us: scores(): pl.pallas_call(functools.partial(score_kernel, len(units), len(tables), f...]
    ppermute x9 -> x35, starting transfers between devices: 43.8 us -> 64.6 us  [the longest x27 54.2 us: turned(): lax.ppermute(value, 'head', [(i, (i + step) % size) for i in range(size)])]
    reshape x5 -> x3, local copies, waits for them, and re-layouts: 7.41 us -> 1.8 us  [the longest x2 1.2 us: finish(): gain.reshape(1, -1)]
    pallas_call x2 -> x3, Pallas kernels: 13.3 us -> 16.7 us  [matmul(): pl.pallas_call(matmul_kernel, grid=(b.shape[1] // tile,), in_specs=[pl.Bl...]
  transfers between devices with their start and end apart: 22 -> 42, of which waited for: 13 -> 24; matrix products, arithmetic and copies ran while one was open for 6% -> 4% of each run, Pallas kernels for 6% -> 24%
where the time goes in v2:
time: 456 us; the launch traced here: 454 us
  waiting for transfers between devices  199 us (44%)
  Pallas kernels  147 us (32%)
  starting transfers between devices  70.8 us (16%)
  local copies, waits for them, and re-layouts  20.2 us (4%)
  other arithmetic  10.2 us (2%)
  between operations  6.43 us (1%)
    ppermute x27, waiting for transfers between devices, turned(): lax.ppermute(value, 'head', [(i, (i + step) % size) for i in range(size)])  134 us
    ppermute x1, waiting for transfers between devices, shards(): late = lax.ppermute(late, 'seq', xor_pairs(seq_count, 2))  56.4 us
    ppermute x27, starting transfers between devices, turned(): lax.ppermute(value, 'head', [(i, (i + step) % size) for i in range(size)])  54.2 us
    pallas_call x4, Pallas kernels, scores(): pl.pallas_call(functools.partial(score_kernel, len(units), len(tables), f...  37.5 us
    pallas_call x3, Pallas kernels, lookup(): pl.pallas_call(lookup_kernel, grid=(rows // tile,), in_specs=[pl.BlockSpe...  30.4 us
    pallas_call x3, Pallas kernels, matmul(): pl.pallas_call(matmul_kernel, grid=(b.shape[1] // tile,), in_specs=[pl.Bl...  16.7 us
    pallas_call x3, Pallas kernels, project(): pl.pallas_call(functools.partial(project_kernel, heads, slots, chunk, cou...  15.7 us
  transfers between devices with their start and end apart: 42, of which 24 were waited for; matrix products, arithmetic and copies ran while one was open for 4% of the time, Pallas kernels for 24%

profile of v2, /device:TPU:0, one launch (start us, length us, event | category | flops | bytes accessed | tf_op | source)
XLA Modules:
  0.0 454.1 jit_solution(916003767404600961)
XLA Ops:
  8.0 8.6 %lookup.5 = (bf16[256,512]{1,0:T(8,128)(2,1)}, bf16[256,512]{1,0:T(8,128)(2,1)}) custom-call(s32[1,512]{1,0:T(1,128)} %bitcast.84, bf16[6400,512]{1,0:T(8,128)(2,1)} %refs_3_.6), custom_call_target="tpu_custom_call" | custom-call | tf_op jit(solution)/shard_map/lookup/pallas_call | solution.py:132
  21.0 13.3 %lookup.4 = (bf16[512,512]{1,0:T(8,128)(2,1)}, bf16[512,512]{1,0:T(8,128)(2,1)}) custom-call(s32[1,1024]{1,0:T(1,128)} %bitcast.77, bf16[6400,512]{1,0:T(8,128)(2,1)} %refs_3_.6), custom_call_target="tpu_custom_call" | custom-call | tf_op jit(solution)/shard_map/lookup/pallas_call | solution.py:132
  37.5 3.8 collective-permute-start.6
  41.3 8.6 %lookup.3.refs_0_ = bf16[512,512]{1,0:T(8,128)(2,1)} custom-call(s32[1,512]{1,0:T(1,128)} %bitcast.85, bf16[6400,512]{1,0:T(8,128)(2,1)} %refs_3_.6), custom_call_target="tpu_custom_call" | custom-call | tf_op jit(solution)/shard_map/lookup/pallas_call | solution.py:132
  49.9 4.4 collective-permute-done.5.refs_1_
  54.3 7.4 %collective-permute-done.6.refs_2_ = bf16[512,512]{1,0:T(8,128)(2,1)S(1)} collective-permute-done((bf16[512,512]{1,0:T(8,128)(2,1)}, bf16[512,512]{1,0:T(8,128)(2,1)S(1)}, u32[]{:S(2)}, u32[]{:S(2)}) %collective-permute-start.6) | collective-permute-done | bytes 524320 | tf_op jit(solution)/shard_map/ppermute | solution.py:52
  67.8 3.5 collective-permute-done.8.refs_2_
  80.8 12.3 %collective-permute-done.11.refs_1_ = bf16[128,2048]{1,0:T(8,128)(2,1)S(1)} collective-permute-done((bf16[128,2048]{1,0:T(8,128)(2,1)}, bf16[128,2048]{1,0:T(8,128)(2,1)S(1)}, u32[]{:S(2)}, u32[]{:S(2)}) %collective-permute-start.11) | collective-permute-done | bytes 524320 | tf_op jit(solution)/shard_map/ppermute | solution.py:52
  93.1 9.3 %collective-permute-start.12 = (bf16[64,2048]{1,0:T(8,128)(2,1)S(1)}, bf16[64,2048]{1,0:T(8,128)(2,1)S(1)}, u32[]{:S(2)}, u32[]{:S(2)}) collective-permute-start(bf16[64,2048]{1,0:T(8,128)(2,1)S(1)} %slice.170), channel_id=1, source_target_pairs={{0,1},{1,2},{2,3},{3,0},{4,5},{5,6},{6,7},{7,4},{8,9},{9,10},{10,1... | collective-permute-start | bytes 786440 | tf_op jit(solution)/shard_map/ppermute | solution.py:52
  106.6 5.0 %project.3 = (bf16[4,128,256]{2,1,0:T(8,128)(2,1)}, bf16[4,128,256]{2,1,0:T(8,128)(2,1)}, bf16[128,512]{1,0:T(8,128)(2,1)}, f32[4,176,128]{2,1,0:T(8,128)}) custom-call(s32[1]{0:T(128)} %copy.35.bound_ref, s32[1]{0:T(128)} %get-tuple-element.150.places_ref, bf16[128,2048]{1,0:T(8,128)(2,1)} %get-tuple-element.84.refs_0_, bf16[2048,640]{1,0:T(8,128)(2,1)} %refs_2_.8, ...), custom_call_target="tpu_custom_call" | custom-call | tf_op jit(solution)/shard_map/project/pallas_call | solution.py:289
  111.7 5.6 %project.4 = (bf16[4,256,256]{2,1,0:T(8,128)(2,1)}, bf16[4,256,256]{2,1,0:T(8,128)(2,1)}, bf16[256,512]{1,0:T(8,128)(2,1)}, f32[4,176,128]{2,1,0:T(8,128)}) custom-call(s32[1]{0:T(128)} %copy.35.bound_ref, s32[2]{0:T(128)} %slice.138.places_ref, bf16[128,2048]{1,0:T(8,128)(2,1)} %copy-done.8, bf16[128,2048]{1,0:T(8,128)(2,1)} %copy-done.6, ...), custom_call_target="tpu_custom_call" | custom-call | tf_op jit(solution)/shard_map/project/pallas_call | solution.py:289
  118.1 5.1 %project.5 = (bf16[4,128,256]{2,1,0:T(8,128)(2,1)}, bf16[4,128,256]{2,1,0:T(8,128)(2,1)}, bf16[128,512]{1,0:T(8,128)(2,1)}, bf16[4,176,128]{2,1,0:T(8,128)(2,1)}) custom-call(s32[1]{0:T(128)} %copy.35.bound_ref, s32[1]{0:T(128)} %get-tuple-element.149.places_ref, bf16[64,2048]{1,0:T(8,128)(2,1)} %copy-done.25, bf16[64,2048]{1,0:T(8,128)(2,1)} %copy-done.26, ...), custom_call_target="tpu_custom_call" | custom-call | tf_op jit(solution)/shard_map/project/pallas_call | solution.py:289
  124.6 3.2 collective-permute-start.15
  129.3 4.3 slice.153
  138.8 4.6 %within.1 = (f32[4,512,128]{2,1,0:T(8,128)}, f32[4,512,8]{2,1,0:T(8,128)}) custom-call(s32[1]{0:T(128)} %copy.35.bound_ref, s32[4]{0:T(128)} %copy-done.35, bf16[4,128,256]{2,1,0:T(8,128)(2,1)} %get-tuple-element.85.refs_0_, bf16[4,256,256]{2,1,0:T(8,128)(2,1)} %get-tuple-element.87.refs_1_, bf16[4,128,256]{2,1,0:T(8,128)(2,1)} %get-tuple-element.89.refs_2_, ...), custom_call_target="tpu_custom_call" | custom-call | tf_op jit(solution)/shard_map/within/pallas_call | solution.py:327
  143.5 4.6 %across.1 = (bf16[512,512]{1,0:T(8,128)(2,1)}, bf16[64,2048]{1,0:T(8,128)(2,1)}, bf16[64,2048]{1,0:T(8,128)(2,1)}) custom-call(s32[1]{0:T(128)} %copy.35.bound_ref, s32[4]{0:T(128)} %copy-done.35, s32[3]{0:T(128)} %add_convert_fusion.share_ref, bf16[4,128,256]{2,1,0:T(8,128)(2,1)} %get-tuple-element.85.refs_0_, ...), custom_call_target="tpu_custom_call" | custom-call | tf_op jit(solution)/shard_map/across/pallas_call | solution.py:375
  148.1 3.8 collective-permute-start.18
  151.9 3.9 near.2
  155.8 3.3 collective-permute-done.17.upper_ref
  159.1 3.7 collective-permute-done.18.lower_ref
  170.3 12.3 %collective-permute-done.19.refs_1_ = bf16[128,2048]{1,0:T(8,128)(2,1)S(1)} collective-permute-done((bf16[128,2048]{1,0:T(8,128)(2,1)}, bf16[128,2048]{1,0:T(8,128)(2,1)S(1)}, u32[]{:S(2)}, u32[]{:S(2)}) %collective-permute-start.19) | collective-permute-done | bytes 524320 | tf_op jit(solution)/shard_map/ppermute | solution.py:52
  182.7 10.5 %collective-permute-done.20.refs_2_ = bf16[128,2048]{1,0:T(8,128)(2,1)S(1)} collective-permute-done((bf16[128,2048]{1,0:T(8,128)(2,1)}, bf16[128,2048]{1,0:T(8,128)(2,1)S(1)}, u32[]{:S(2)}, u32[]{:S(2)}) %collective-permute-start.20) | collective-permute-done | bytes 524320 | tf_op jit(solution)/shard_map/ppermute | solution.py:52
  194.0 2.8 finish.2
  197.8 2.9 collective-permute-start.21
  200.6 13.0 %collective-permute-done.22.refs_1_ = bf16[128,2048]{1,0:T(8,128)(2,1)S(1)} collective-permute-done((bf16[128,2048]{1,0:T(8,128)(2,1)}, bf16[128,2048]{1,0:T(8,128)(2,1)S(1)}, u32[]{:S(2)}, u32[]{:S(2)}) %collective-permute-start.22) | collective-permute-done | bytes 524320 | tf_op jit(solution)/shard_map/ppermute | solution.py:52
  213.7 9.7 %collective-permute-done.21.refs_0_ = bf16[128,2048]{1,0:T(8,128)(2,1)S(1)} collective-permute-done((bf16[128,2048]{1,0:T(8,128)(2,1)}, bf16[128,2048]{1,0:T(8,128)(2,1)S(1)}, u32[]{:S(2)}, u32[]{:S(2)}) %collective-permute-start.21) | collective-permute-done | bytes 524320 | tf_op jit(solution)/shard_map/ppermute | solution.py:52
  229.0 5.3 %matmul.3.refs_0_ = bf16[128,1536]{1,0:T(8,128)(2,1)} custom-call(bf16[128,2048]{1,0:T(8,128)(2,1)} %get-tuple-element.108.refs_0_, bf16[2048,1536]{1,0:T(8,128)(2,1)} %refs_2_.10), custom_call_target="tpu_custom_call" | custom-call | tf_op jit(solution)/shard_map/matmul/pallas_call | solution.py:409
  234.3 6.2 %matmul.4.refs_1_ = bf16[256,1536]{1,0:T(8,128)(2,1)} custom-call(bf16[128,2048]{1,0:T(8,128)(2,1)} %copy-done.7, bf16[128,2048]{1,0:T(8,128)(2,1)} %copy-done.5, bf16[2048,1536]{1,0:T(8,128)(2,1)} %refs_2_.10), custom_call_target="tpu_custom_call" | custom-call | tf_op jit(solution)/shard_map/matmul/pallas_call | solution.py:409
  241.9 5.3 %matmul.5.refs_2_ = bf16[128,1536]{1,0:T(8,128)(2,1)} custom-call(bf16[64,2048]{1,0:T(8,128)(2,1)} %copy-done.17, bf16[64,2048]{1,0:T(8,128)(2,1)} %copy-done.18, bf16[2048,1536]{1,0:T(8,128)(2,1)} %refs_2_.10), custom_call_target="tpu_custom_call" | custom-call | tf_op jit(solution)/shard_map/matmul/pallas_call | solution.py:409
  251.4 3.8 collective-permute-start.32
  255.2 56.4 %collective-permute-done.32.refs_4_.refs_5_ = bf16[2560,512]{1,0:T(8,128)(2,1)S(1)} collective-permute-done((bf16[2560,512]{1,0:T(8,128)(2,1)S(1)}, bf16[2560,512]{1,0:T(8,128)(2,1)S(1)}, u32[]{:S(2)}, u32[]{:S(2)}) %collective-permute-start.32) | collective-permute-done | bytes 2621472 | tf_op jit(solution)/shard_map/ppermute | solution.py:721
  313.9 8.0 %local_window.1 = (bf16[512,512]{1,0:T(8,128)(2,1)}, bf16[64,1536]{1,0:T(8,128)(2,1)}) custom-call(s32[1]{0:T(128)} %copy.35.bound_ref, s32[4]{0:T(128)} %copy-done.35, bf16[128,1536]{1,0:T(8,128)(2,1)} %matmul.3.refs_0_, bf16[256,1536]{1,0:T(8,128)(2,1)} %matmul.4.refs_1_, bf16[128,1536]{1,0:T(8,128)(2,1)} %matmul.5.refs_2_), custom_call_target="tpu_custom_call" | custom-call | tf_op jit(solution)/shard_map/local_window/pallas_call | solution.py:473
  321.9 4.5 halo_window.1
  327.0 3.2 collective-permute-start.27
  330.3 3.8 near.3
  334.1 3.5 collective-permute-done.26.upper_ref
  337.6 3.7 collective-permute-done.27.lower_ref
  345.0 3.3 collective-permute-start.29
  348.8 12.5 %collective-permute-done.28.refs_1_ = bf16[128,2048]{1,0:T(8,128)(2,1)S(1)} collective-permute-done((bf16[128,2048]{1,0:T(8,128)(2,1)}, bf16[128,2048]{1,0:T(8,128)(2,1)S(1)}, u32[]{:S(2)}, u32[]{:S(2)}) %collective-permute-start.28) | collective-permute-done | bytes 524320 | tf_op jit(solution)/shard_map/ppermute | solution.py:52
  361.3 8.7 %collective-permute-done.29.refs_2_ = bf16[128,2048]{1,0:T(8,128)(2,1)S(1)} collective-permute-done((bf16[128,2048]{1,0:T(8,128)(2,1)}, bf16[128,2048]{1,0:T(8,128)(2,1)S(1)}, u32[]{:S(2)}, u32[]{:S(2)}) %collective-permute-start.29) | collective-permute-done | bytes 524320 | tf_op jit(solution)/shard_map/ppermute | solution.py:52
  378.1 12.5 %collective-permute-done.30.refs_1_ = bf16[128,2048]{1,0:T(8,128)(2,1)S(1)} collective-permute-done((bf16[128,2048]{1,0:T(8,128)(2,1)}, bf16[128,2048]{1,0:T(8,128)(2,1)S(1)}, u32[]{:S(2)}, u32[]{:S(2)}) %collective-permute-start.30) | collective-permute-done | bytes 524320 | tf_op jit(solution)/shard_map/ppermute | solution.py:52
  390.7 11.1 %collective-permute-done.36.refs_0_ = bf16[128,2048]{1,0:T(8,128)(2,1)S(1)} collective-permute-done((bf16[128,2048]{1,0:T(8,128)(2,1)}, bf16[128,2048]{1,0:T(8,128)(2,1)S(1)}, u32[]{:S(2)}, u32[]{:S(2)}) %collective-permute-start.36) | collective-permute-done | bytes 524320 | tf_op jit(solution)/shard_map/ppermute | solution.py:52
  403.8 10.8 %scores.4.refs_7_ = f32[3,8,256]{2,1,0:T(8,128)} custom-call(s32[4]{0:T(128)} %iota_xor_fusion.order_ref, bf16[128,2048]{1,0:T(8,128)(2,1)} %finish.3.refs_0_, bf16[128,2048]{1,0:T(8,128)(2,1)} %copy-done.3, bf16[6400,512]{1,0:T(8,128)(2,1)} %refs_3_.6, bf16[6400,512]{1,0:T(8,128)(2,1)} %collective-permute-done.31.refs_3_.refs_4_, ...), custom_call_target="tpu_custom_call" | custom-call | tf_op jit(solution)/shard_map/scores/pallas_call | solution.py:557
  414.6 8.0 %scores.5 = f32[3,8,256]{2,1,0:T(8,128)} custom-call(s32[4]{0:T(128)} %iota_xor_fusion.order_ref, bf16[128,2048]{1,0:T(8,128)(2,1)} %finish.3.refs_0_, bf16[128,2048]{1,0:T(8,128)(2,1)} %copy-done.3, bf16[6400,512]{1,0:T(8,128)(2,1)} %refs_3_.6, bf16[6400,512]{1,0:T(8,128)(2,1)} %collective-permute-done.31.refs_3_.refs_4_, bf16[2560,512]{1,0:T(8,128)(2,1)} %copy-done, ...), custom_call_target="tpu_custom_call" | custom-call | tf_op jit(solution)/shard_map/scores/pallas_call | solution.py:557
  424.9 10.8 %scores.6.refs_8_ = f32[3,8,256]{2,1,0:T(8,128)} custom-call(s32[4]{0:T(128)} %iota_xor_fusion.order_ref, bf16[128,2048]{1,0:T(8,128)(2,1)} %copy-done.2, bf16[64,2048]{1,0:T(8,128)(2,1)} %copy-done.9, bf16[64,2048]{1,0:T(8,128)(2,1)} %copy-done.10, bf16[6400,512]{1,0:T(8,128)(2,1)} %refs_3_.6, bf16[6400,512]{1,0:T(8,128)(2,1)} %collective-permute-done.31.refs_3_.refs_4_, ...), custom_call_target="tpu_custom_call" | custom-call | tf_op jit(solution)/shard_map/scores/pallas_call | solution.py:557
  435.6 8.0 %scores.7 = f32[3,8,256]{2,1,0:T(8,128)} custom-call(s32[4]{0:T(128)} %iota_xor_fusion.order_ref, bf16[128,2048]{1,0:T(8,128)(2,1)} %copy-done.2, bf16[64,2048]{1,0:T(8,128)(2,1)} %copy-done.9, bf16[64,2048]{1,0:T(8,128)(2,1)} %copy-done.10, bf16[6400,512]{1,0:T(8,128)(2,1)} %refs_3_.6, bf16[6400,512]{1,0:T(8,128)(2,1)} %collective-permute-done.31.refs_3_.refs_4_, ...), custom_call_target="tpu_custom_call" | custom-call | tf_op jit(solution)/shard_map/scores/pallas_call | solution.py:557
  445.9 3.1 collective-permute-start.41
  450.5 3.0 collective-permute-done.40
  (199 shorter events, 82.7 us)
Async XLA Ops:
  1.3 3.7 collective-permute-start.2
  3.7 3.6 collective-permute-start.1
  4.3 3.0 collective-permute-start
  16.6 17.7 %collective-permute-start.3 = (bf16[256,512]{1,0:T(8,128)(2,1)}, bf16[256,512]{1,0:T(8,128)(2,1)S(1)}, u32[]{:S(2)}, u32[]{:S(2)}) collective-permute-start(bf16[256,512]{1,0:T(8,128)(2,1)} %get-tuple-element.75), channel_id=1, source_target_pairs={{0,1},{1,2},{2,3},{3,0},{4,5},{5,6},{6,7},{7,4},{8,9},{9,10},{10,1... | collective-permute-start | bytes 786440 | tf_op jit(solution)/shard_map/ppermute | solution.py:52
  18.1 16.1 %collective-permute-start.4 = (bf16[256,512]{1,0:T(8,128)(2,1)}, bf16[256,512]{1,0:T(8,128)(2,1)S(1)}, u32[]{:S(2)}, u32[]{:S(2)}) collective-permute-start(bf16[256,512]{1,0:T(8,128)(2,1)} %get-tuple-element.76), channel_id=1, source_target_pairs={{0,3},{1,0},{2,1},{3,2},{4,7},{5,4},{6,5},{7,6},{8,11},{9,8},{10,9... | collective-permute-start | bytes 786440 | tf_op jit(solution)/shard_map/ppermute | solution.py:52
  37.5 16.9 %collective-permute-start.5 = (bf16[512,512]{1,0:T(8,128)(2,1)}, bf16[512,512]{1,0:T(8,128)(2,1)S(1)}, u32[]{:S(2)}, u32[]{:S(2)}) collective-permute-start(bf16[512,512]{1,0:T(8,128)(2,1)} %get-tuple-element.77), channel_id=1, source_target_pairs={{0,1},{1,2},{2,3},{3,0},{4,5},{5,6},{6,7},{7,4},{8,9},{9,10},{10,1... | collective-permute-start | bytes 1572872 | tf_op jit(solution)/shard_map/ppermute | solution.py:52
  37.5 24.3 %collective-permute-start.6 = (bf16[512,512]{1,0:T(8,128)(2,1)}, bf16[512,512]{1,0:T(8,128)(2,1)S(1)}, u32[]{:S(2)}, u32[]{:S(2)}) collective-permute-start(bf16[512,512]{1,0:T(8,128)(2,1)} %get-tuple-element.78), channel_id=1, source_target_pairs={{0,3},{1,0},{2,1},{3,2},{4,7},{5,4},{6,5},{7,6},{8,11},{9,8},{10,9... | collective-permute-start | bytes 1572872 | tf_op jit(solution)/shard_map/ppermute | solution.py:52
  41.3 38.8 %copy-start.41 = (s32[4]{0:T(128)S(1)}, s32[4]{0:T(128)}, u32[]{:S(2)}) copy-start(s32[4]{0:T(128)} %constant.148.clone) | copy-start | bytes 52
  64.8 3.0 collective-permute-start.7
  64.8 6.5 %collective-permute-start.8 = (bf16[128,512]{1,0:T(8,128)(2,1)}, bf16[128,512]{1,0:T(8,128)(2,1)S(1)}, u32[]{:S(2)}, u32[]{:S(2)}) collective-permute-start(bf16[128,512]{1,0:T(8,128)(2,1)} %get-tuple-element.81), channel_id=1, source_target_pairs={{0,8},{4,12},{8,0},{12,4},{1,9},{5,13},{9,1},{13,5},{2,10},{6,14},... | collective-permute-start | bytes 393224 | tf_op jit(solution)/shard_map/ppermute | solution.py:635
  65.4 8.0 %collective-permute-start.9 = (bf16[128,512]{1,0:T(8,128)(2,1)}, bf16[128,512]{1,0:T(8,128)(2,1)S(1)}, u32[]{:S(2)}, u32[]{:S(2)}) collective-permute-start(bf16[128,512]{1,0:T(8,128)(2,1)} %get-tuple-element.82), channel_id=1, source_target_pairs={{0,12},{4,8},{8,4},{12,0},{1,13},{5,9},{9,5},{13,1},{2,14},{6,10},... | collective-permute-start | bytes 393224 | tf_op jit(solution)/shard_map/ppermute | solution.py:635
  76.2 16.8 %collective-permute-start.11 = (bf16[128,2048]{1,0:T(8,128)(2,1)}, bf16[128,2048]{1,0:T(8,128)(2,1)S(1)}, u32[]{:S(2)}, u32[]{:S(2)}) collective-permute-start(bf16[128,2048]{1,0:T(8,128)(2,1)} %get-tuple-element.84.refs_0_), channel_id=1, source_target_pairs={{0,1},{1,2},{2,3},{3,0},{4,5},{5,6},{6,7},{7,4},{8,9},{9,10},{10,1... | collective-permute-start | bytes 1572872 | tf_op jit(solution)/shard_map/ppermute | solution.py:52
  77.2 25.5 %collective-permute-start.10 = (bf16[128,2048]{1,0:T(8,128)(2,1)}, bf16[128,2048]{1,0:T(8,128)(2,1)S(1)}, u32[]{:S(2)}, u32[]{:S(2)}) collective-permute-start(bf16[128,2048]{1,0:T(8,128)(2,1)} %get-tuple-element.84.refs_0_), channel_id=1, source_target_pairs={{0,3},{1,0},{2,1},{3,2},{4,7},{5,4},{6,5},{7,6},{8,11},{9,8},{10,9... | collective-permute-start | bytes 1572872 | tf_op jit(solution)/shard_map/ppermute | solution.py:52
  93.1 24.2 %collective-permute-start.12 = (bf16[64,2048]{1,0:T(8,128)(2,1)S(1)}, bf16[64,2048]{1,0:T(8,128)(2,1)S(1)}, u32[]{:S(2)}, u32[]{:S(2)}) collective-permute-start(bf16[64,2048]{1,0:T(8,128)(2,1)S(1)} %slice.170), channel_id=1, source_target_pairs={{0,1},{1,2},{2,3},{3,0},{4,5},{5,6},{6,7},{7,4},{8,9},{9,10},{10,1... | collective-permute-start | bytes 786440 | tf_op jit(solution)/shard_map/ppermute | solution.py:52
  102.7 14.6 %collective-permute-start.13 = (bf16[64,2048]{1,0:T(8,128)(2,1)S(1)}, bf16[64,2048]{1,0:T(8,128)(2,1)S(1)}, u32[]{:S(2)}, u32[]{:S(2)}) collective-permute-start(bf16[64,2048]{1,0:T(8,128)(2,1)S(1)} %slice.171), channel_id=1, source_target_pairs={{0,3},{1,0},{2,1},{3,2},{4,7},{5,4},{6,5},{7,6},{8,11},{9,8},{10,9... | collective-permute-start | bytes 786440 | tf_op jit(solution)/shard_map/ppermute | solution.py:52
  123.2 10.4 %collective-permute-start.14 = (bf16[4,176,128]{2,1,0:T(8,128)(2,1)}, bf16[4,176,128]{2,1,0:T(8,128)(2,1)S(1)}, u32[]{:S(2)}, u32[]{:S(2)}) collective-permute-start(bf16[4,176,128]{2,1,0:T(8,128)(2,1)} %get-tuple-element.98), channel_id=1, source_target_pairs={{0,4},{4,8},{8,12},{1,5},{5,9},{9,13},{2,6},{6,10},{10,14},{3,7},{... | collective-permute-start | bytes 540680 | tf_op jit(solution)/shard_map/ppermute | solution.py:664
  124.6 9.0 %collective-permute-start.15 = (bf16[4,176,128]{2,1,0:T(8,128)(2,1)}, bf16[4,176,128]{2,1,0:T(8,128)(2,1)S(1)}, u32[]{:S(2)}, u32[]{:S(2)}) collective-permute-start(bf16[4,176,128]{2,1,0:T(8,128)(2,1)} %get-tuple-element.98), channel_id=1, source_target_pairs={{0,8},{4,12},{1,9},{5,13},{2,10},{6,14},{3,11},{7,15},{16,24},{20,... | collective-permute-start | bytes 540680 | tf_op jit(solution)/shard_map/ppermute | solution.py:664
  127.8 6.6 %collective-permute-start.16 = (bf16[4,176,128]{2,1,0:T(8,128)(2,1)}, bf16[4,176,128]{2,1,0:T(8,128)(2,1)S(1)}, u32[]{:S(2)}, u32[]{:S(2)}) collective-permute-start(bf16[4,176,128]{2,1,0:T(8,128)(2,1)} %get-tuple-element.98), channel_id=1, source_target_pairs={{0,12},{1,13},{2,14},{3,15},{16,28},{17,29},{18,30},{19,31}} | collective-permute-start | bytes 540680 | tf_op jit(solution)/shard_map/ppermute | solution.py:664
  134.4 120.8 %collective-permute-start.34 = (bf16[3840,512]{1,0:T(8,128)(2,1)}, bf16[3840,512]{1,0:T(8,128)(2,1)}, u32[]{:S(2)}, u32[]{:S(2)}) collective-permute-start(bf16[3840,512]{1,0:T(8,128)(2,1)} %slice.153), channel_id=1, source_target_pairs={{0,8},{4,12},{8,0},{12,4},{1,9},{5,13},{9,1},{13,5},{2,10},{6,14},... | collective-permute-start | bytes 11796488 | tf_op jit(solution)/shard_map/ppermute | solution.py:693
  143.4 26.3 %copy-start.37 = (bf16[2048]{0:T(1024)(128)(2,1)S(1)}, bf16[2048]{0:T(1024)(128)(2,1)}, u32[]{:S(2)}) copy-start(bf16[2048]{0:T(1024)(128)(2,1)} %param.27) | copy-start | bytes 12292
  148.1 11.0 %collective-permute-start.17 = (bf16[64,2048]{1,0:T(8,128)(2,1)}, bf16[64,2048]{1,0:T(8,128)(2,1)S(1)}, u32[]{:S(2)}, u32[]{:S(2)}) collective-permute-start(bf16[64,2048]{1,0:T(8,128)(2,1)} %get-tuple-element.103), channel_id=1, source_target_pairs={{0,1},{1,2},{2,3},{3,0},{4,5},{5,6},{6,7},{7,4},{8,9},{9,10},{10,1... | collective-permute-start | bytes 786440 | tf_op jit(solution)/shard_map/ppermute | solution.py:52
  148.1 14.7 %collective-permute-start.18 = (bf16[64,2048]{1,0:T(8,128)(2,1)}, bf16[64,2048]{1,0:T(8,128)(2,1)S(1)}, u32[]{:S(2)}, u32[]{:S(2)}) collective-permute-start(bf16[64,2048]{1,0:T(8,128)(2,1)} %get-tuple-element.104), channel_id=1, source_target_pairs={{0,3},{1,0},{2,1},{3,2},{4,7},{5,4},{6,5},{7,6},{8,11},{9,8},{10,9... | collective-permute-start | bytes 786440 | tf_op jit(solution)/shard_map/ppermute | solution.py:52
  165.9 16.8 %collective-permute-start.19 = (bf16[128,2048]{1,0:T(8,128)(2,1)}, bf16[128,2048]{1,0:T(8,128)(2,1)S(1)}, u32[]{:S(2)}, u32[]{:S(2)}) collective-permute-start(bf16[128,2048]{1,0:T(8,128)(2,1)} %get-tuple-element.105), channel_id=1, source_target_pairs={{0,1},{1,2},{2,3},{3,0},{4,5},{5,6},{6,7},{7,4},{8,9},{9,10},{10,1... | collective-permute-start | bytes 1572872 | tf_op jit(solution)/shard_map/ppermute | solution.py:52
  167.8 25.4 %collective-permute-start.20 = (bf16[128,2048]{1,0:T(8,128)(2,1)}, bf16[128,2048]{1,0:T(8,128)(2,1)S(1)}, u32[]{:S(2)}, u32[]{:S(2)}) collective-permute-start(bf16[128,2048]{1,0:T(8,128)(2,1)} %get-tuple-element.106), channel_id=1, source_target_pairs={{0,3},{1,0},{2,1},{3,2},{4,7},{5,4},{6,5},{7,6},{8,11},{9,8},{10,9... | collective-permute-start | bytes 1572872 | tf_op jit(solution)/shard_map/ppermute | solution.py:52
  196.8 16.8 %collective-permute-start.22 = (bf16[128,2048]{1,0:T(8,128)(2,1)}, bf16[128,2048]{1,0:T(8,128)(2,1)S(1)}, u32[]{:S(2)}, u32[]{:S(2)}) collective-permute-start(bf16[128,2048]{1,0:T(8,128)(2,1)} %get-tuple-element.108.refs_0_), channel_id=1, source_target_pairs={{0,1},{1,2},{2,3},{3,0},{4,5},{5,6},{6,7},{7,4},{8,9},{9,10},{10,1... | collective-permute-start | bytes 1572872 | tf_op jit(solution)/shard_map/ppermute | solution.py:52
  197.8 25.6 %collective-permute-start.21 = (bf16[128,2048]{1,0:T(8,128)(2,1)}, bf16[128,2048]{1,0:T(8,128)(2,1)S(1)}, u32[]{:S(2)}, u32[]{:S(2)}) collective-permute-start(bf16[128,2048]{1,0:T(8,128)(2,1)} %get-tuple-element.108.refs_0_), channel_id=1, source_target_pairs={{0,3},{1,0},{2,1},{3,2},{4,7},{5,4},{6,5},{7,6},{8,11},{9,8},{10,9... | collective-permute-start | bytes 1572872 | tf_op jit(solution)/shard_map/ppermute | solution.py:52
  200.6 203.2 %collective-permute-start.31 = (bf16[6400,512]{1,0:T(8,128)(2,1)}, bf16[6400,512]{1,0:T(8,128)(2,1)}, u32[]{:S(2)}, u32[]{:S(2)}) collective-permute-start(bf16[6400,512]{1,0:T(8,128)(2,1)} %refs_3_.6), channel_id=1, source_target_pairs={{0,4},{4,0},{8,12},{12,8},{1,5},{5,1},{9,13},{13,9},{2,6},{6,2},{1... | collective-permute-start | bytes 19660808 | tf_op jit(solution)/shard_map/ppermute | solution.py:695
  213.7 26.8 %collective-permute-start.23 = (bf16[64,2048]{1,0:T(8,128)(2,1)S(1)}, bf16[64,2048]{1,0:T(8,128)(2,1)S(1)}, u32[]{:S(2)}, u32[]{:S(2)}) collective-permute-start(bf16[64,2048]{1,0:T(8,128)(2,1)S(1)} %slice.172), channel_id=1, source_target_pairs={{0,1},{1,2},{2,3},{3,0},{4,5},{5,6},{6,7},{7,4},{8,9},{9,10},{10,1... | collective-permute-start | bytes 786440 | tf_op jit(solution)/shard_map/ppermute | solution.py:52
  223.4 17.0 %collective-permute-start.24 = (bf16[64,2048]{1,0:T(8,128)(2,1)S(1)}, bf16[64,2048]{1,0:T(8,128)(2,1)S(1)}, u32[]{:S(2)}, u32[]{:S(2)}) collective-permute-start(bf16[64,2048]{1,0:T(8,128)(2,1)S(1)} %slice.173), channel_id=1, source_target_pairs={{0,3},{1,0},{2,1},{3,2},{4,7},{5,4},{6,5},{7,6},{8,11},{9,8},{10,9... | collective-permute-start | bytes 786440 | tf_op jit(solution)/shard_map/ppermute | solution.py:52
  248.1 3.2 collective-permute-start.25
  251.4 70.6 %copy-start.27 = (bf16[64,1536]{1,0:T(8,128)(2,1)}, bf16[64,1536]{1,0:T(8,128)(2,1)S(1)}, u32[]{:S(2)}) copy-start(bf16[64,1536]{1,0:T(8,128)(2,1)S(1)} %collective-permute-done.25.halo_ref) | copy-start | bytes 589828
  251.4 60.2 %collective-permute-start.32 = (bf16[2560,512]{1,0:T(8,128)(2,1)S(1)}, bf16[2560,512]{1,0:T(8,128)(2,1)S(1)}, u32[]{:S(2)}, u32[]{:S(2)}) collective-permute-start(bf16[2560,512]{1,0:T(8,128)(2,1)S(1)} %slice.152), channel_id=1, source_target_pairs={{0,8},{4,12},{8,0},{12,4},{1,9},{5,13},{9,1},{13,5},{2,10},{6,14},... | collective-permute-start | bytes 7864328 | tf_op jit(solution)/shard_map/ppermute | solution.py:721
  255.2 148.6 %collective-permute-start.35 = (bf16[3840,512]{1,0:T(8,128)(2,1)}, bf16[3840,512]{1,0:T(8,128)(2,1)}, u32[]{:S(2)}, u32[]{:S(2)}) collective-permute-start(bf16[3840,512]{1,0:T(8,128)(2,1)} %collective-permute-done.34.refs_4_.refs_5_), channel_id=1, source_target_pairs={{0,4},{4,0},{8,12},{12,8},{1,5},{5,1},{9,13},{13,9},{2,6},{6,2},{1... | collective-permute-start | bytes 11796488 | tf_op jit(solution)/shard_map/ppermute | solution.py:694
  311.6 32.8 %copy-start = (bf16[2560,512]{1,0:T(8,128)(2,1)}, bf16[2560,512]{1,0:T(8,128)(2,1)S(1)}, u32[]{:S(2)}) copy-start(bf16[2560,512]{1,0:T(8,128)(2,1)S(1)} %collective-permute-done.32.refs_4_.refs_5_) | copy-start | bytes 7864324
  311.6 103.0 %collective-permute-start.33 = (bf16[2560,512]{1,0:T(8,128)(2,1)S(1)}, bf16[2560,512]{1,0:T(8,128)(2,1)}, u32[]{:S(2)}, u32[]{:S(2)}) collective-permute-start(bf16[2560,512]{1,0:T(8,128)(2,1)S(1)} %collective-permute-done.32.refs_4_.refs_5_), channel_id=1, source_target_pairs={{0,4},{4,0},{8,12},{12,8},{1,5},{5,1},{9,13},{13,9},{2,6},{6,2},{1... | collective-permute-start | bytes 7864328 | tf_op jit(solution)/shard_map/ppermute | solution.py:722
  321.9 26.3 %copy-start.38 = (bf16[2048]{0:T(1024)(128)(2,1)S(1)}, bf16[2048]{0:T(1024)(128)(2,1)}, u32[]{:S(2)}) copy-start(bf16[2048]{0:T(1024)(128)(2,1)} %param.30) | copy-start | bytes 12292
  326.5 51.1 %copy-start.39 = (s32[512]{0:T(512)S(1)}, s32[512]{0:T(512)}, u32[]{:S(2)}) copy-start(s32[512]{0:T(512)} %param.20) | copy-start | bytes 6148
  326.5 11.2 %collective-permute-start.26 = (bf16[64,2048]{1,0:T(8,128)(2,1)}, bf16[64,2048]{1,0:T(8,128)(2,1)S(1)}, u32[]{:S(2)}, u32[]{:S(2)}) collective-permute-start(bf16[64,2048]{1,0:T(8,128)(2,1)} %get-tuple-element.115), channel_id=1, source_target_pairs={{0,1},{1,2},{2,3},{3,0},{4,5},{5,6},{6,7},{7,4},{8,9},{9,10},{10,1... | collective-permute-start | bytes 786440 | tf_op jit(solution)/shard_map/ppermute | solution.py:52
  327.0 14.2 %collective-permute-start.27 = (bf16[64,2048]{1,0:T(8,128)(2,1)}, bf16[64,2048]{1,0:T(8,128)(2,1)S(1)}, u32[]{:S(2)}, u32[]{:S(2)}) collective-permute-start(bf16[64,2048]{1,0:T(8,128)(2,1)} %get-tuple-element.116), channel_id=1, source_target_pairs={{0,3},{1,0},{2,1},{3,2},{4,7},{5,4},{6,5},{7,6},{8,11},{9,8},{10,9... | collective-permute-start | bytes 786440 | tf_op jit(solution)/shard_map/ppermute | solution.py:52
  344.4 16.9 %collective-permute-start.28 = (bf16[128,2048]{1,0:T(8,128)(2,1)}, bf16[128,2048]{1,0:T(8,128)(2,1)S(1)}, u32[]{:S(2)}, u32[]{:S(2)}) collective-permute-start(bf16[128,2048]{1,0:T(8,128)(2,1)} %get-tuple-element.117), channel_id=1, source_target_pairs={{0,1},{1,2},{2,3},{3,0},{4,5},{5,6},{6,7},{7,4},{8,9},{9,10},{10,1... | collective-permute-start | bytes 1572872 | tf_op jit(solution)/shard_map/ppermute | solution.py:52
  345.0 25.1 %collective-permute-start.29 = (bf16[128,2048]{1,0:T(8,128)(2,1)}, bf16[128,2048]{1,0:T(8,128)(2,1)S(1)}, u32[]{:S(2)}, u32[]{:S(2)}) collective-permute-start(bf16[128,2048]{1,0:T(8,128)(2,1)} %get-tuple-element.118), channel_id=1, source_target_pairs={{0,3},{1,0},{2,1},{3,2},{4,7},{5,4},{6,5},{7,6},{8,11},{9,8},{10,9... | collective-permute-start | bytes 1572872 | tf_op jit(solution)/shard_map/ppermute | solution.py:52
  373.7 16.9 %collective-permute-start.30 = (bf16[128,2048]{1,0:T(8,128)(2,1)}, bf16[128,2048]{1,0:T(8,128)(2,1)S(1)}, u32[]{:S(2)}, u32[]{:S(2)}) collective-permute-start(bf16[128,2048]{1,0:T(8,128)(2,1)} %finish.3.refs_0_), channel_id=1, source_target_pairs={{0,1},{1,2},{2,3},{3,0},{4,5},{5,6},{6,7},{7,4},{8,9},{9,10},{10,1... | collective-permute-start | bytes 1572872 | tf_op jit(solution)/shard_map/ppermute | solution.py:52
  375.0 26.8 %collective-permute-start.36 = (bf16[128,2048]{1,0:T(8,128)(2,1)}, bf16[128,2048]{1,0:T(8,128)(2,1)S(1)}, u32[]{:S(2)}, u32[]{:S(2)}) collective-permute-start(bf16[128,2048]{1,0:T(8,128)(2,1)} %finish.3.refs_0_), channel_id=1, source_target_pairs={{0,3},{1,0},{2,1},{3,2},{4,7},{5,4},{6,5},{7,6},{8,11},{9,8},{10,9... | collective-permute-start | bytes 1572872 | tf_op jit(solution)/shard_map/ppermute | solution.py:52
  390.6 33.4 %collective-permute-start.37 = (bf16[64,2048]{1,0:T(8,128)(2,1)S(1)}, bf16[64,2048]{1,0:T(8,128)(2,1)S(1)}, u32[]{:S(2)}, u32[]{:S(2)}) collective-permute-start(bf16[64,2048]{1,0:T(8,128)(2,1)S(1)} %slice.182), channel_id=1, source_target_pairs={{0,1},{1,2},{2,3},{3,0},{4,5},{5,6},{6,7},{7,4},{8,9},{9,10},{10,1... | collective-permute-start | bytes 786440 | tf_op jit(solution)/shard_map/ppermute | solution.py:52
  401.9 22.2 %collective-permute-start.38 = (bf16[64,2048]{1,0:T(8,128)(2,1)S(1)}, bf16[64,2048]{1,0:T(8,128)(2,1)S(1)}, u32[]{:S(2)}, u32[]{:S(2)}) collective-permute-start(bf16[64,2048]{1,0:T(8,128)(2,1)S(1)} %slice.183), channel_id=1, source_target_pairs={{0,3},{1,0},{2,1},{3,2},{4,7},{5,4},{6,5},{7,6},{8,11},{9,8},{10,9... | collective-permute-start | bytes 786440 | tf_op jit(solution)/shard_map/ppermute | solution.py:52
  445.1 5.4 %collective-permute-start.39 = (f32[3,128]{1,0:T(4,128)S(1)}, f32[3,128]{1,0:T(4,128)S(1)}, u32[]{:S(2)}, u32[]{:S(2)}) collective-permute-start(f32[3,128]{1,0:T(4,128)S(1)} %get-tuple-element.139), channel_id=1, source_target_pairs={{0,1},{1,2},{2,3},{3,0},{4,5},{5,6},{6,7},{7,4},{8,9},{9,10},{10,1... | collective-permute-start | bytes 4616 | tf_op jit(solution)/shard_map/ppermute | solution.py:52
  445.9 4.6 %collective-permute-start.41 = (f32[3,128]{1,0:T(4,128)S(1)}, f32[3,128]{1,0:T(4,128)S(1)}, u32[]{:S(2)}, u32[]{:S(2)}) collective-permute-start(f32[3,128]{1,0:T(4,128)S(1)} %get-tuple-element.138), channel_id=1, source_target_pairs={{0,3},{1,0},{2,1},{3,2},{4,7},{5,4},{6,5},{7,6},{8,11},{9,8},{10,9... | collective-permute-start | bytes 4616 | tf_op jit(solution)/shard_map/ppermute | solution.py:52
  449.0 4.5 collective-permute-start.40
  (36 other events, 240.5 us)

commit v3 on v2

--- a/solution.py
+++ b/solution.py
@@ -26,6 +26,10 @@
     return pltpu.CompilerParams(vmem_limit_bytes=VMEM_BYTES, **kw)
 
 
+def cost(us):
+    return pl.CostEstimate(flops=int(us * 6e8), transcendentals=0, bytes_accessed=int(us * 3e6))
+
+
 def whole():
     return pl.BlockSpec(memory_space=pltpu.VMEM)
 
@@ -65,14 +69,6 @@
     return [[own], [after], [turned(before[:half], 1), turned(after[half:], -1)], [before]]
 
 
-def add_kernel(next_ref, prev_ref, upper_ref, lower_ref, right_ref, left_ref):
-    half = upper_ref.shape[0]
-    right_ref[0:half] = (next_ref[0:half].astype(F32) + upper_ref[...].astype(F32)).astype(BF16)
-    right_ref[half:] = next_ref[half:]
-    left_ref[0:half] = prev_ref[0:half]
-    left_ref[half:] = (prev_ref[half:].astype(F32) + lower_ref[...].astype(F32)).astype(BF16)
-
-
 def scatter_rows(far, near):
     size = lax.axis_size("head")
     if size != 4:
@@ -81,18 +77,17 @@
         full = jnp.stack(
             [lax.dynamic_index_in_dim(full, (d - here) % size, 0, False) for d in range(size)]
         )
-        return [lax.psum_scatter(full, "head", scatter_dimension=0, tiled=True)[0]]
-    upper, lower = turned(far[0], 1), turned(far[1], -1)
-    own, after, before = near()
-    right, left = pl.pallas_call(
-        add_kernel,
-        in_specs=[whole()] * 4,
-        out_specs=[whole()] * 2,
-        out_shape=[jax.ShapeDtypeStruct(own.shape, BF16)] * 2,
-        compiler_params=params(),
-        name="pass_on",
-    )(after, before, upper, lower)
-    return [own, turned(right, 1), turned(left, -1)]
+        return [[lax.psum_scatter(full, "head", scatter_dimension=0, tiled=True)[0]]]
+    from_before, from_after = turned(far[0], 1), turned(far[1], -1)
+    own_upper, own_lower, next_upper, next_lower, prev_upper, prev_lower = near()
+    lower_right, upper_left = turned(next_lower, 1), turned(prev_upper, -1)
+    upper_right = turned(plus(next_upper, from_before), 1)
+    lower_left = turned(plus(prev_lower, from_after), -1)
+    return [[own_upper, upper_right, upper_left], [own_lower, lower_right, lower_left]]
+
+
+def plus(one, two):
+    return (one.astype(F32) + two.astype(F32)).astype(BF16)
 
 
 def chunk_order(size):
@@ -140,29 +135,41 @@
         out_shape=[jax.ShapeDtypeStruct((count // pieces, width), BF16)] * pieces,
         scratch_shapes=[pltpu.VMEM((count, width), F32)],
         compiler_params=params(),
+        cost_estimate=cost(8 * count / 512),
         name="lookup",
     )(ids.reshape(1, count), table)
 
 
-def collect_kernel(parts, *refs):
-    ins, outs = refs[:parts], refs[parts:]
+def gathered_sum(refs, sizes):
+    rows, at = [], 0
+    for size in sizes:
+        total = refs[at][...].astype(F32)
+        for ref in refs[at + 1 : at + size]:
+            total = total + ref[...].astype(F32)
+        rows.append(total)
+        at += size
+    return rows[0] if len(rows) == 1 else jnp.concatenate(rows, axis=0)
+
+
+def collect_kernel(sizes, *refs):
+    ins, outs = refs[: sum(sizes)], refs[sum(sizes) :]
     rows = outs[0].shape[0]
+    total = gathered_sum(ins, sizes)
     for n, out in enumerate(outs):
-        span = slice(n * rows, (n + 1) * rows)
-        total = ins[0][span].astype(F32)
-        for part in ins[1:]:
-            total = total + part[span].astype(F32)
-        out[...] = total.astype(BF16)
-
-
-def collect(parts, pieces):
-    rows, width = parts[0].shape
-    return pl.pallas_call(
-        functools.partial(collect_kernel, len(parts)),
+        out[...] = total[n * rows : (n + 1) * rows].astype(BF16)
+
+
+def collect(terms, pieces):
+    sizes = [len(part) for part in terms]
+    parts = [term for part in terms for term in part]
+    rows, width = sum(part[0].shape[0] for part in terms), parts[0].shape[1]
+    return pl.pallas_call(
+        functools.partial(collect_kernel, sizes),
         in_specs=[whole()] * len(parts),
         out_specs=[whole()] * pieces,
         out_shape=[jax.ShapeDtypeStruct((rows // pieces, width), BF16)] * pieces,
         compiler_params=params(),
+        cost_estimate=cost(2),
         name="collect",
     )(*parts)
 
@@ -187,29 +194,30 @@
         out_shape=[full, full],
         scratch_shapes=[pltpu.VMEM((len(pieces), rows, width), BF16)],
         compiler_params=params(),
+        cost_estimate=cost(2),
         name="begin",
     )(order, gain.reshape(1, -1), *pieces)
 
 
-def finish_kernel(parts, last, residual_ref, gain_ref, *refs):
-    total = refs[0][...].astype(F32)
-    for part in refs[1:parts]:
-        total = total + part[...].astype(F32)
-    total = total + residual_ref[...].astype(F32)
+def finish_kernel(sizes, last, residual_ref, gain_ref, *refs):
+    parts = sum(sizes)
+    total = gathered_sum(refs[:parts], sizes) + residual_ref[...].astype(F32)
     if not last:
         total = total.astype(BF16)
         refs[parts + 1][...] = total
     refs[parts][...] = rms(total.astype(F32), gain_ref[...])
 
 
-def finish(residual, gain, parts, last):
+def finish(residual, gain, terms, last):
     full = jax.ShapeDtypeStruct(residual.shape, BF16)
-    return pl.pallas_call(
-        functools.partial(finish_kernel, len(parts), last),
+    parts = [term for part in terms for term in part]
+    return pl.pallas_call(
+        functools.partial(finish_kernel, [len(part) for part in terms], last),
         in_specs=[whole()] * (2 + len(parts)),
         out_specs=[whole()] * (1 if last else 2),
         out_shape=[full] * (1 if last else 2),
         compiler_params=params(),
+        cost_estimate=cost(2.5),
         name="finish",
     )(residual, gain.reshape(1, -1), *parts)
 
@@ -297,6 +305,7 @@
             jax.ShapeDtypeStruct((heads, BUFFER_ROWS, HEAD_DIM), BF16 if last else F32),
         ],
         compiler_params=params(),
+        cost_estimate=cost(5),
         name="project",
     )(bound, places, *pieces, weight, *constants, *extra)
 
@@ -333,6 +342,7 @@
             jax.ShapeDtypeStruct((heads, count, 8), F32),
         ],
         compiler_params=params(),
+        cost_estimate=cost(4.5),
         name="within",
     )(bound, places, *fqs, *fks, *vs)
 
@@ -379,21 +389,25 @@
         out_shape=[jax.ShapeDtypeStruct((count, heads * HEAD_DIM), BF16)]
         + [jax.ShapeDtypeStruct((rows, weight.shape[1]), BF16)] * far,
         compiler_params=params(),
+        cost_estimate=cost(4.5),
         name="across",
     )(bound, places, share, *fqs, num, den, gain, weight, *states)
 
 
-def near_kernel(chunk, mixed_ref, weight_ref, *outs):
-    split_store(dot(mixed_ref[0 : chunk * len(outs)], weight_ref[...]), outs)
+def near_kernel(rows, mixed_ref, weight_ref, *outs):
+    split_store(dot(mixed_ref[0:rows], weight_ref[...]), outs)
 
 
 def near_chunks(mixed, weight, near, chunk):
-    return pl.pallas_call(
-        functools.partial(near_kernel, chunk),
+    pieces = 2 * near if near > 1 else 1
+    rows = near * chunk
+    return pl.pallas_call(
+        functools.partial(near_kernel, rows),
         in_specs=[whole()] * 2,
-        out_specs=[whole()] * near,
-        out_shape=[jax.ShapeDtypeStruct((chunk, weight.shape[1]), BF16)] * near,
-        compiler_params=params(),
+        out_specs=[whole()] * pieces,
+        out_shape=[jax.ShapeDtypeStruct((rows // pieces, weight.shape[1]), BF16)] * pieces,
+        compiler_params=params(),
+        cost_estimate=cost(4),
         name="near",
     )(mixed, weight)
 
@@ -416,6 +430,7 @@
         out_specs=pl.BlockSpec((rows, tile), lambda n: (0, n)),
         out_shape=jax.ShapeDtypeStruct((rows, b.shape[1]), BF16),
         compiler_params=params(),
+        cost_estimate=cost(5),
         name="matmul",
     )(*pieces, b)
 
@@ -479,6 +494,7 @@
             jax.ShapeDtypeStruct((WINDOW, qkvs[0].shape[1]), BF16),
         ],
         compiler_params=params(),
+        cost_estimate=cost(8),
         name="local_window",
     )(bound, places, *qkvs)
 
@@ -516,6 +532,7 @@
         out_shape=[jax.ShapeDtypeStruct(local.shape, BF16)]
         + [jax.ShapeDtypeStruct((rows, weight.shape[1]), BF16)] * far,
         compiler_params=params(),
+        cost_estimate=cost(4.5),
         name="halo_window",
     )(info, local, first, halo, weight)
 
@@ -568,6 +585,7 @@
         out_shape=jax.ShapeDtypeStruct((3, 8, count), F32),
         scratch_shapes=[pltpu.VMEM((units[0].shape[1], count), BF16)],
         compiler_params=params(),
+        cost_estimate=cost(9),
         name="scores",
     )(order, *units, *tables, goal, before)
 
@@ -616,6 +634,9 @@
     starts = jnp.sum(jnp.where(order[None, :] == block[:, None], starts[None, :], 0), axis=1)
     bound = doc_start.astype(jnp.int32)
 
+    lots = [vocab_rows * 3 // 5, vocab_rows * 2 // 5]
+    early, late = vocab_table[: lots[0]], vocab_table[lots[0] :]
+
     ids = (marks[:, :tok_count] - vocab_first).reshape(seq_count, head_count, chunk)
 
     def ids_of(k):
@@ -624,8 +645,8 @@
     if head_count == 4:
         outer = lookup(ids_of(2), vocab_table, 2)
         inner = lambda: (
-            lookup(ids_of(0), vocab_table, 1)
-            + lookup(jnp.concatenate([ids_of(1), ids_of(3)]), vocab_table, 2)
+            lookup(ids_of(0), vocab_table, 2)
+            + lookup(jnp.concatenate([ids_of(1), ids_of(3)]), vocab_table, 4)
         )
     else:
         outer = [lookup(ids_of(k), vocab_table, 1)[0] for k in range(1, head_count)]
@@ -688,8 +709,7 @@
     units, residual = finish(embedded, norm_gain_two, parts, False)
 
     if seq_count == 4:
-        lots = [vocab_rows * 3 // 5, vocab_rows * 2 // 5]
-        early, _ = lax.optimization_barrier((vocab_table[: lots[0]], states))
+        early, _ = lax.optimization_barrier((early, states))
         early = lax.ppermute(early, "seq", xor_pairs(seq_count, 2))
         early_corner = lax.ppermute(early, "seq", xor_pairs(seq_count, 1))
         beside = lax.ppermute(vocab_table, "seq", xor_pairs(seq_count, 1))
@@ -704,6 +724,7 @@
         tail = jnp.where(
             held_at[slot] == head_count - 1, qkvs[n][at + chunk - WINDOW : at + chunk], tail
         )
+    late, tail = lax.optimization_barrier((late, tail))
     halo = lax.ppermute(tail, "seq", [(i, i + 1) for i in range(seq_count - 1)])
     previous = jnp.sum(jnp.where(block == seq_index - 1, starts, 0))
     valid_from = jnp.where(
@@ -716,10 +737,11 @@
     parts = scatter_rows(outer, lambda: near_chunks(mixed, win_out, near, chunk))
     units = finish(residual, final_gain, parts, True)[0]
 
+    chunks = gather_rows(units)
     if seq_count == 4:
-        late, _ = lax.optimization_barrier((vocab_table[lots[0] :], halo))
         late = lax.ppermute(late, "seq", xor_pairs(seq_count, 2))
-        late_corner = lax.ppermute(late, "seq", xor_pairs(seq_count, 1))
+        corner, _ = lax.optimization_barrier((late, (chunks[1][0], chunks[-1][0])))
+        late_corner = lax.ppermute(corner, "seq", xor_pairs(seq_count, 1))
         lots = [
             (0, [vocab_table, beside, early, early_corner]),
             (lots[0], [vocab_table, beside, late, late_corner]),
@@ -727,7 +749,6 @@
     else:
         lots = [(0, [lax.all_gather(vocab_table, "seq", axis=1, tiled=True)])]
         order = jnp.zeros((1,), jnp.int32)
-    chunks = gather_rows(units)
     goals = (target_ids - vocab_first).reshape(head_count, chunk)
     found = {}
     for group in [[0, 3], [1, 2]] if head_count == 4 else [[k] for k in range(head_count)]:

time: 456 us -> 376 us (0.82)
  waiting for transfers between devices: 199 us -> 122 us
  other arithmetic: 10.2 us -> 17.3 us
  Pallas kernels: 147 us -> 140 us
    ppermute x1, waiting for transfers between devices: 56.4 us -> 0.01 us  [shards(): late = lax.ppermute(late, 'seq', xor_pairs(seq_count, 2))]
    ppermute x27 -> x33, waiting for transfers between devices: 134 us -> 117 us  [turned(): lax.ppermute(value, 'head', [(i, (i + step) % size) for i in range(size)])]
    pallas_call x8 -> x5, Pallas kernels: 22.9 us -> 15.5 us  [the longest x2 7.71 us: near_chunks(): pl.pallas_call(functools.partial(near_kernel, rows), in_specs=[whole()] *...]
    convert_element_type x0 -> x6, other arithmetic: none -> 6.09 us  [plus(): return (one.astype(F32) + two.astype(F32)).astype(BF16)]
    ppermute x27 -> x33, starting transfers between devices: 54.2 us -> 53 us  [turned(): lax.ppermute(value, 'head', [(i, (i + step) % size) for i in range(size)])]
  transfers between devices with their start and end apart: 42 -> 48, of which waited for: 24 -> 25; matrix products, arithmetic and copies ran while one was open for 4% -> 7% of each run, Pallas kernels for 24% -> 26%
where the time goes in v3:
time: 376 us; the launch traced here: 375 us
  Pallas kernels  140 us (37%)
  waiting for transfers between devices  122 us (32%)
  starting transfers between devices  67.1 us (18%)
  local copies, waits for them, and re-layouts  21.4 us (6%)
  other arithmetic  17.3 us (5%)
  between operations  6.66 us (2%)
    ppermute x33, waiting for transfers between devices, turned(): lax.ppermute(value, 'head', [(i, (i + step) % size) for i in range(size)])  117 us
    ppermute x33, starting transfers between devices, turned(): lax.ppermute(value, 'head', [(i, (i + step) % size) for i in range(size)])  53 us
    pallas_call x4, Pallas kernels, scores(): pl.pallas_call(functools.partial(score_kernel, len(units), len(tables), f...  37.5 us
    pallas_call x3, Pallas kernels, lookup(): pl.pallas_call(lookup_kernel, grid=(rows // tile,), in_specs=[pl.BlockSpe...  30.3 us
    pallas_call x3, Pallas kernels, matmul(): pl.pallas_call(matmul_kernel, grid=(b.shape[1] // tile,), in_specs=[pl.Bl...  16.6 us
    pallas_call x3, Pallas kernels, project(): pl.pallas_call(functools.partial(project_kernel, heads, slots, chunk, cou...  15.8 us
    unnamed x84, local copies, waits for them, and re-layouts  8.36 us
    pallas_call x1, Pallas kernels, local_window(): pl.pallas_call(functools.partial(local_kernel, heads, slots, spots, chunk...  7.99 us
  transfers between devices with their start and end apart: 48, of which 25 were waited for; matrix products, arithmetic and copies ran while one was open for 7% of the time, Pallas kernels for 26%

profile of v3, /device:TPU:0, one launch (start us, length us, event | category | flops | bytes accessed | tf_op | source)
XLA Modules:
  0.0 374.5 jit_solution(10845987212305036205)
XLA Ops:
  8.0 8.6 %lookup.5 = (bf16[256,512]{1,0:T(8,128)(2,1)}, bf16[256,512]{1,0:T(8,128)(2,1)}) custom-call(s32[1,512]{1,0:T(1,128)} %bitcast.89, bf16[6400,512]{1,0:T(8,128)(2,1)} %refs_3_.6), custom_call_target="tpu_custom_call" | custom-call | flops 4800000000 | bytes 24000000 | tf_op jit(solution)/shard_map/lookup/pallas_call | solution.py:127
  21.0 13.2 %lookup.4 = (bf16[256,512]{1,0:T(8,128)(2,1)}, bf16[256,512]{1,0:T(8,128)(2,1)}, bf16[256,512]{1,0:T(8,128)(2,1)}, bf16[256,512]{1,0:T(8,128)(2,1)}) custom-call(s32[1,1024]{1,0:T(1,128)} %bitcast.87, bf16[6400,512]{1,0:T(8,128)(2,1)} %refs_3_.6), custom_call_target="tpu_custom_call" | custom-call | flops 9600000000 | bytes 48000000 | tf_op jit(solution)/shard_map/lookup/pallas_call | solution.py:127
  38.3 3.9 %collective-permute-start.8 = (bf16[256,512]{1,0:T(8,128)(2,1)S(1)}, bf16[256,512]{1,0:T(8,128)(2,1)S(1)}, u32[]{:S(2)}, u32[]{:S(2)}) collective-permute-start(bf16[256,512]{1,0:T(8,128)(2,1)S(1)} %add_convert_fusion.4), channel_id=1, source_target_pairs={{0,3},{1,0},{2,1},{3,2},{4,7},{5,4},{6,5},{7,6},{8,11},{9,8},{10,9... | collective-permute-start | bytes 786440 | tf_op jit(solution)/shard_map/ppermute | solution.py:56
  42.2 8.5 %lookup.3 = (bf16[256,512]{1,0:T(8,128)(2,1)}, bf16[256,512]{1,0:T(8,128)(2,1)}) custom-call(s32[1,512]{1,0:T(1,128)} %bitcast.88, bf16[6400,512]{1,0:T(8,128)(2,1)} %refs_3_.6), custom_call_target="tpu_custom_call" | custom-call | flops 4800000000 | bytes 24000000 | tf_op jit(solution)/shard_map/lookup/pallas_call | solution.py:127
  50.7 3.8 %collective-permute-done.5.refs_2_ = bf16[256,512]{1,0:T(8,128)(2,1)S(1)} collective-permute-done((bf16[256,512]{1,0:T(8,128)(2,1)}, bf16[256,512]{1,0:T(8,128)(2,1)S(1)}, u32[]{:S(2)}, u32[]{:S(2)}) %collective-permute-start.5) | collective-permute-done | bytes 262176 | tf_op jit(solution)/shard_map/ppermute | solution.py:56
  55.2 3.3 collective-permute-done.8.refs_5_
  72.8 3.6 collective-permute-start.12
  79.9 5.0 %project.3 = (bf16[4,128,256]{2,1,0:T(8,128)(2,1)}, bf16[4,128,256]{2,1,0:T(8,128)(2,1)}, bf16[128,512]{1,0:T(8,128)(2,1)}, f32[4,176,128]{2,1,0:T(8,128)}) custom-call(s32[1]{0:T(128)} %copy.35.bound_ref, s32[1]{0:T(128)} %get-tuple-element.162.places_ref, bf16[128,2048]{1,0:T(8,128)(2,1)} %get-tuple-element.92.refs_0_, bf16[2048,640]{1,0:T(8,128)(2,1)} %refs_2_.8, ...), custom_call_target="tpu_custom_call" | custom-call | flops 3000000000 | bytes 15000000 | tf_op jit(solution)/shard_map/project/pallas_call | solution.py:297
  84.9 15.3 %collective-permute-done.13.refs_1_ = bf16[128,2048]{1,0:T(8,128)(2,1)S(1)} collective-permute-done((bf16[128,2048]{1,0:T(8,128)(2,1)}, bf16[128,2048]{1,0:T(8,128)(2,1)S(1)}, u32[]{:S(2)}, u32[]{:S(2)}) %collective-permute-start.13) | collective-permute-done | bytes 524320 | tf_op jit(solution)/shard_map/ppermute | solution.py:56
  104.2 5.7 %project.4 = (bf16[4,256,256]{2,1,0:T(8,128)(2,1)}, bf16[4,256,256]{2,1,0:T(8,128)(2,1)}, bf16[256,512]{1,0:T(8,128)(2,1)}, f32[4,176,128]{2,1,0:T(8,128)}) custom-call(s32[1]{0:T(128)} %copy.35.bound_ref, s32[2]{0:T(128)} %slice.138.places_ref, bf16[128,2048]{1,0:T(8,128)(2,1)} %copy-done.6, bf16[128,2048]{1,0:T(8,128)(2,1)} %copy-done.7, ...), custom_call_target="tpu_custom_call" | custom-call | flops 3000000000 | bytes 15000000 | tf_op jit(solution)/shard_map/project/pallas_call | solution.py:297
  111.3 3.8 %collective-permute-done.15.refs_1_ = bf16[64,2048]{1,0:T(8,128)(2,1)S(1)} collective-permute-done((bf16[64,2048]{1,0:T(8,128)(2,1)S(1)}, bf16[64,2048]{1,0:T(8,128)(2,1)S(1)}, u32[]{:S(2)}, u32[]{:S(2)}) %collective-permute-start.15) | collective-permute-done | bytes 262176 | tf_op jit(solution)/shard_map/ppermute | solution.py:56
  115.8 5.1 %project.5 = (bf16[4,128,256]{2,1,0:T(8,128)(2,1)}, bf16[4,128,256]{2,1,0:T(8,128)(2,1)}, bf16[128,512]{1,0:T(8,128)(2,1)}, bf16[4,176,128]{2,1,0:T(8,128)(2,1)}) custom-call(s32[1]{0:T(128)} %copy.35.bound_ref, s32[1]{0:T(128)} %get-tuple-element.161.places_ref, bf16[64,2048]{1,0:T(8,128)(2,1)} %copy-done.26, bf16[64,2048]{1,0:T(8,128)(2,1)} %copy-done.30, ...), custom_call_target="tpu_custom_call" | custom-call | flops 3000000000 | bytes 15000000 | tf_op jit(solution)/shard_map/project/pallas_call | solution.py:297
  122.2 3.4 collective-permute-start.17
  127.0 4.6 %within.1 = (f32[4,512,128]{2,1,0:T(8,128)}, f32[4,512,8]{2,1,0:T(8,128)}) custom-call(s32[1]{0:T(128)} %copy.35.bound_ref, s32[4]{0:T(128)} %copy-done.15, bf16[4,128,256]{2,1,0:T(8,128)(2,1)} %get-tuple-element.93.refs_0_, bf16[4,256,256]{2,1,0:T(8,128)(2,1)} %get-tuple-element.95.refs_1_, bf16[4,128,256]{2,1,0:T(8,128)(2,1)} %get-tuple-element.97.refs_2_, ...), custom_call_target="tpu_custom_call" | custom-call | flops 2700000000 | bytes 13500000 | tf_op jit(solution)/shard_map/within/pallas_call | solution.py:336
  132.8 4.7 %across.1 = (bf16[512,512]{1,0:T(8,128)(2,1)}, bf16[64,2048]{1,0:T(8,128)(2,1)}, bf16[64,2048]{1,0:T(8,128)(2,1)}) custom-call(s32[1]{0:T(128)} %copy.35.bound_ref, s32[4]{0:T(128)} %copy-done.15, s32[3]{0:T(128)} %add_convert_fusion.6.share_ref, bf16[4,128,256]{2,1,0:T(8,128)(2,1)} %get-tuple-element.93.refs_0_, ...), custom_call_target="tpu_custom_call" | custom-call | flops 2700000000 | bytes 13500000 | tf_op jit(solution)/shard_map/across/pallas_call | solution.py:385
  137.8 4.3 %slice.153 = bf16[3840,512]{1,0:T(8,128)(2,1)} slice(bf16[6400,512]{1,0:T(8,128)(2,1)} %refs_3_.6), slice={[0:3840], [0:512]} | slice | bytes 7864320 | tf_op jit(solution)/shard_map/slice | solution.py:638
  142.7 3.9 %near.2 = (bf16[64,2048]{1,0:T(8,128)(2,1)}, bf16[64,2048]{1,0:T(8,128)(2,1)}, bf16[64,2048]{1,0:T(8,128)(2,1)}, bf16[64,2048]{1,0:T(8,128)(2,1)}, bf16[64,2048]{1,0:T(8,128)(2,1)}, /*index=5*/bf16[64,2048]{1,0:T(8,128)(2,1)}) custom-call(bf16[512,512]{1,0:T(8,128)(2,1)} %get-tuple-element.107.mixed_ref, bf16[512,2048]{1,0:T(8,128)(2,1)} %weight_ref.3), custom_call_target="tpu_custom_call" | custom-call | flops 2400000000 | bytes 12000000 | tf_op jit(solution)/shard_map/near/pallas_call | solution.py:404
  146.5 3.5 collective-permute-start.21
  150.1 3.8 %collective-permute-start.23 = (bf16[64,2048]{1,0:T(8,128)(2,1)S(1)}, bf16[64,2048]{1,0:T(8,128)(2,1)S(1)}, u32[]{:S(2)}, u32[]{:S(2)}) collective-permute-start(bf16[64,2048]{1,0:T(8,128)(2,1)S(1)} %copy-done.22), channel_id=1, source_target_pairs={{0,3},{1,0},{2,1},{3,2},{4,7},{5,4},{6,5},{7,6},{8,11},{9,8},{10,9... | collective-permute-start | bytes 786440 | tf_op jit(solution)/shard_map/ppermute | solution.py:56
  155.0 13.2 %collective-permute-done.23 = bf16[64,2048]{1,0:T(8,128)(2,1)S(1)} collective-permute-done((bf16[64,2048]{1,0:T(8,128)(2,1)S(1)}, bf16[64,2048]{1,0:T(8,128)(2,1)S(1)}, u32[]{:S(2)}, u32[]{:S(2)}) %collective-permute-start.23) | collective-permute-done | bytes 262176 | tf_op jit(solution)/shard_map/ppermute | solution.py:56
  169.2 4.4 %collective-permute-start.24 = (bf16[64,2048]{1,0:T(8,128)(2,1)S(1)}, bf16[64,2048]{1,0:T(8,128)(2,1)S(1)}, u32[]{:S(2)}, u32[]{:S(2)}) collective-permute-start(bf16[64,2048]{1,0:T(8,128)(2,1)S(1)} %add_convert_fusion.2), channel_id=1, source_target_pairs={{0,3},{1,0},{2,1},{3,2},{4,7},{5,4},{6,5},{7,6},{8,11},{9,8},{10,9... | collective-permute-start | bytes 786440 | tf_op jit(solution)/shard_map/ppermute | solution.py:56
  174.5 5.7 %collective-permute-done.24.refs_5_ = bf16[64,2048]{1,0:T(8,128)(2,1)S(1)} collective-permute-done((bf16[64,2048]{1,0:T(8,128)(2,1)S(1)}, bf16[64,2048]{1,0:T(8,128)(2,1)S(1)}, u32[]{:S(2)}, u32[]{:S(2)}) %collective-permute-start.24) | collective-permute-done | bytes 262176 | tf_op jit(solution)/shard_map/ppermute | solution.py:56
  180.9 2.8 finish.2
  184.2 3.3 collective-permute-start.25
  195.1 5.2 %matmul.3.refs_0_ = bf16[128,1536]{1,0:T(8,128)(2,1)} custom-call(bf16[128,2048]{1,0:T(8,128)(2,1)} %get-tuple-element.117.refs_0_, bf16[2048,1536]{1,0:T(8,128)(2,1)} %refs_2_.10), custom_call_target="tpu_custom_call" | custom-call | flops 3000000000 | bytes 15000000 | tf_op jit(solution)/shard_map/matmul/pallas_call | solution.py:423
  200.6 8.9 %collective-permute-done.25.refs_0_ = bf16[128,2048]{1,0:T(8,128)(2,1)} collective-permute-done((bf16[128,2048]{1,0:T(8,128)(2,1)}, bf16[128,2048]{1,0:T(8,128)(2,1)}, u32[]{:S(2)}, u32[]{:S(2)}) %collective-permute-start.25) | collective-permute-done | bytes 524320 | tf_op jit(solution)/shard_map/ppermute | solution.py:56
  210.4 3.0 collective-permute-start.28
  213.4 6.1 %matmul.4.refs_1_ = bf16[256,1536]{1,0:T(8,128)(2,1)} custom-call(bf16[128,2048]{1,0:T(8,128)(2,1)} %collective-permute-done.25.refs_0_, bf16[128,2048]{1,0:T(8,128)(2,1)} %copy-done.8, bf16[2048,1536]{1,0:T(8,128)(2,1)} %refs_2_.10), custom_call_target="tpu_custom_call" | custom-call | flops 3000000000 | bytes 15000000 | tf_op jit(solution)/shard_map/matmul/pallas_call | solution.py:423
  222.9 5.2 %matmul.5.refs_2_ = bf16[128,1536]{1,0:T(8,128)(2,1)} custom-call(bf16[64,2048]{1,0:T(8,128)(2,1)} %copy-done.32, bf16[64,2048]{1,0:T(8,128)(2,1)} %copy-done.34, bf16[2048,1536]{1,0:T(8,128)(2,1)} %refs_2_.10), custom_call_target="tpu_custom_call" | custom-call | flops 3000000000 | bytes 15000000 | tf_op jit(solution)/shard_map/matmul/pallas_call | solution.py:423
  231.5 8.0 %local_window.1 = (bf16[512,512]{1,0:T(8,128)(2,1)}, bf16[64,1536]{1,0:T(8,128)(2,1)}) custom-call(s32[1]{0:T(128)} %copy.35.bound_ref, s32[4]{0:T(128)} %copy-done.15, bf16[128,1536]{1,0:T(8,128)(2,1)} %matmul.3.refs_0_, bf16[256,1536]{1,0:T(8,128)(2,1)} %matmul.4.refs_1_, bf16[128,1536]{1,0:T(8,128)(2,1)} %matmul.5.refs_2_), custom_call_target="tpu_custom_call" | custom-call | flops 4800000000 | bytes 24000000 | tf_op jit(solution)/shard_map/local_window/pallas_call | solution.py:488
  240.2 4.5 %halo_window.1 = (bf16[512,512]{1,0:T(8,128)(2,1)}, bf16[64,2048]{1,0:T(8,128)(2,1)}, bf16[64,2048]{1,0:T(8,128)(2,1)}) custom-call(s32[3]{0:T(128)} %pad_add_fusion.4.info_ref, bf16[512,512]{1,0:T(8,128)(2,1)} %get-tuple-element.118.local_ref, bf16[64,1536]{1,0:T(8,128)(2,1)} %get-tuple-element.119.first_ref, bf16[64,1536]{1,0:T(8,128)(2,1)} %copy-done.35, ...), custom_call_target="tpu_custom_call" | custom-call | flops 2700000000 | bytes 13500000 | tf_op jit(solution)/shard_map/halo_window/pallas_call | solution.py:528
  245.3 3.9 %near.3 = (bf16[64,2048]{1,0:T(8,128)(2,1)}, bf16[64,2048]{1,0:T(8,128)(2,1)}, bf16[64,2048]{1,0:T(8,128)(2,1)}, bf16[64,2048]{1,0:T(8,128)(2,1)}, bf16[64,2048]{1,0:T(8,128)(2,1)}, /*index=5*/bf16[64,2048]{1,0:T(8,128)(2,1)}) custom-call(bf16[512,512]{1,0:T(8,128)(2,1)} %get-tuple-element.121.mixed_ref, bf16[512,2048]{1,0:T(8,128)(2,1)} %weight_ref.5), custom_call_target="tpu_custom_call" | custom-call | flops 2400000000 | bytes 12000000 | tf_op jit(solution)/shard_map/near/pallas_call | solution.py:404
  249.2 3.2 collective-permute-start.32
  252.4 3.5 collective-permute-done.30
  257.0 9.2 %collective-permute-done.34 = bf16[64,2048]{1,0:T(8,128)(2,1)S(1)} collective-permute-done((bf16[64,2048]{1,0:T(8,128)(2,1)S(1)}, bf16[64,2048]{1,0:T(8,128)(2,1)S(1)}, u32[]{:S(2)}, u32[]{:S(2)}) %collective-permute-start.34) | collective-permute-done | bytes 262176 | tf_op jit(solution)/shard_map/ppermute | solution.py:56
  268.5 9.0 %collective-permute-done.33.refs_4_ = bf16[64,2048]{1,0:T(8,128)(2,1)S(1)} collective-permute-done((bf16[64,2048]{1,0:T(8,128)(2,1)}, bf16[64,2048]{1,0:T(8,128)(2,1)S(1)}, u32[]{:S(2)}, u32[]{:S(2)}) %collective-permute-start.33) | collective-permute-done | bytes 262176 | tf_op jit(solution)/shard_map/ppermute | solution.py:56
  278.1 5.0 %collective-permute-done.31.refs_1_ = bf16[64,2048]{1,0:T(8,128)(2,1)S(1)} collective-permute-done((bf16[64,2048]{1,0:T(8,128)(2,1)S(1)}, bf16[64,2048]{1,0:T(8,128)(2,1)S(1)}, u32[]{:S(2)}, u32[]{:S(2)}) %collective-permute-start.31) | collective-permute-done | bytes 262176 | tf_op jit(solution)/shard_map/ppermute | solution.py:56
  283.1 4.8 %collective-permute-done.35.refs_5_ = bf16[64,2048]{1,0:T(8,128)(2,1)S(1)} collective-permute-done((bf16[64,2048]{1,0:T(8,128)(2,1)S(1)}, bf16[64,2048]{1,0:T(8,128)(2,1)S(1)}, u32[]{:S(2)}, u32[]{:S(2)}) %collective-permute-start.35) | collective-permute-done | bytes 262176 | tf_op jit(solution)/shard_map/ppermute | solution.py:56
  291.9 3.4 collective-permute-start.39
  295.2 13.0 %collective-permute-done.36.refs_1_ = bf16[128,2048]{1,0:T(8,128)(2,1)S(1)} collective-permute-done((bf16[128,2048]{1,0:T(8,128)(2,1)}, bf16[128,2048]{1,0:T(8,128)(2,1)S(1)}, u32[]{:S(2)}, u32[]{:S(2)}) %collective-permute-start.36) | collective-permute-done | bytes 524320 | tf_op jit(solution)/shard_map/ppermute | solution.py:56
  308.2 8.7 %collective-permute-done.39.refs_0_ = bf16[128,2048]{1,0:T(8,128)(2,1)S(1)} collective-permute-done((bf16[128,2048]{1,0:T(8,128)(2,1)}, bf16[128,2048]{1,0:T(8,128)(2,1)S(1)}, u32[]{:S(2)}, u32[]{:S(2)}) %collective-permute-start.39) | collective-permute-done | bytes 524320 | tf_op jit(solution)/shard_map/ppermute | solution.py:56
  318.7 3.6 collective-permute-start.44
  324.2 10.8 %scores.4.refs_7_ = f32[3,8,256]{2,1,0:T(8,128)} custom-call(s32[4]{0:T(128)} %iota_xor_fusion.order_ref, bf16[128,2048]{1,0:T(8,128)(2,1)} %finish.3.refs_0_, bf16[128,2048]{1,0:T(8,128)(2,1)} %copy-done.2, bf16[6400,512]{1,0:T(8,128)(2,1)} %refs_3_.6, bf16[6400,512]{1,0:T(8,128)(2,1)} %collective-permute-done.37.refs_3_.refs_4_, ...), custom_call_target="tpu_custom_call" | custom-call | flops 5400000000 | bytes 27000000 | tf_op jit(solution)/shard_map/scores/pallas_call | solution.py:574
  335.0 8.0 %scores.5 = f32[3,8,256]{2,1,0:T(8,128)} custom-call(s32[4]{0:T(128)} %iota_xor_fusion.order_ref, bf16[128,2048]{1,0:T(8,128)(2,1)} %finish.3.refs_0_, bf16[128,2048]{1,0:T(8,128)(2,1)} %copy-done.2, bf16[6400,512]{1,0:T(8,128)(2,1)} %refs_3_.6, bf16[6400,512]{1,0:T(8,128)(2,1)} %collective-permute-done.37.refs_3_.refs_4_, ...), custom_call_target="tpu_custom_call" | custom-call | flops 5400000000 | bytes 27000000 | tf_op jit(solution)/shard_map/scores/pallas_call | solution.py:574
  345.3 10.8 %scores.6.refs_8_ = f32[3,8,256]{2,1,0:T(8,128)} custom-call(s32[4]{0:T(128)} %iota_xor_fusion.order_ref, bf16[128,2048]{1,0:T(8,128)(2,1)} %copy-done.1, bf16[64,2048]{1,0:T(8,128)(2,1)} %copy-done.3, bf16[64,2048]{1,0:T(8,128)(2,1)} %copy-done.4, bf16[6400,512]{1,0:T(8,128)(2,1)} %refs_3_.6, bf16[6400,512]{1,0:T(8,128)(2,1)} %collective-permute-done.37.refs_3_.refs_4_, ...), custom_call_target="tpu_custom_call" | custom-call | flops 5400000000 | bytes 27000000 | tf_op jit(solution)/shard_map/scores/pallas_call | solution.py:574
  356.0 8.0 %scores.7 = f32[3,8,256]{2,1,0:T(8,128)} custom-call(s32[4]{0:T(128)} %iota_xor_fusion.order_ref, bf16[128,2048]{1,0:T(8,128)(2,1)} %copy-done.1, bf16[64,2048]{1,0:T(8,128)(2,1)} %copy-done.3, bf16[64,2048]{1,0:T(8,128)(2,1)} %copy-done.4, bf16[6400,512]{1,0:T(8,128)(2,1)} %refs_3_.6, bf16[6400,512]{1,0:T(8,128)(2,1)} %collective-permute-done.37.refs_3_.refs_4_, ...), custom_call_target="tpu_custom_call" | custom-call | flops 5400000000 | bytes 27000000 | tf_op jit(solution)/shard_map/scores/pallas_call | solution.py:574
  365.6 3.9 %collective-permute-start.47 = (f32[3,128]{1,0:T(4,128)S(1)}, f32[3,128]{1,0:T(4,128)S(1)}, u32[]{:S(2)}, u32[]{:S(2)}) collective-permute-start(f32[3,128]{1,0:T(4,128)S(1)} %get-tuple-element.150), channel_id=1, source_target_pairs={{0,3},{1,0},{2,1},{3,2},{4,7},{5,4},{6,5},{7,6},{8,11},{9,8},{10,9... | collective-permute-start | bytes 4616 | tf_op jit(solution)/shard_map/ppermute | solution.py:56
  370.9 3.0 collective-permute-done.46
  (214 shorter events, 78.0 us)
Async XLA Ops:
  1.3 4.4 %collective-permute-start.2 = (s32[640]{0:T(1024)S(1)}, s32[640]{0:T(1024)S(1)}, u32[]{:S(2)}, u32[]{:S(2)}) collective-permute-start(s32[640]{0:T(1024)S(1)} %concatenate.15), channel_id=1, source_target_pairs={{0,12},{4,8},{8,4},{12,0},{1,13},{5,9},{9,5},{13,1},{2,14},{6,10},... | collective-permute-start | bytes 7688 | tf_op jit(solution)/shard_map/ppermute | solution.py:629
  3.7 3.6 collective-permute-start.1
  4.3 3.0 collective-permute-start
  16.5 19.7 %collective-permute-start.3 = (bf16[256,512]{1,0:T(8,128)(2,1)}, bf16[256,512]{1,0:T(8,128)(2,1)S(1)}, u32[]{:S(2)}, u32[]{:S(2)}) collective-permute-start(bf16[256,512]{1,0:T(8,128)(2,1)} %get-tuple-element.81), channel_id=1, source_target_pairs={{0,1},{1,2},{2,3},{3,0},{4,5},{5,6},{6,7},{7,4},{8,9},{9,10},{10,1... | collective-permute-start | bytes 786440 | tf_op jit(solution)/shard_map/ppermute | solution.py:56
  18.1 19.2 %collective-permute-start.7 = (bf16[256,512]{1,0:T(8,128)(2,1)}, bf16[256,512]{1,0:T(8,128)(2,1)S(1)}, u32[]{:S(2)}, u32[]{:S(2)}) collective-permute-start(bf16[256,512]{1,0:T(8,128)(2,1)} %get-tuple-element.86), channel_id=1, source_target_pairs={{0,3},{1,0},{2,1},{3,2},{4,7},{5,4},{6,5},{7,6},{8,11},{9,8},{10,9... | collective-permute-start | bytes 786440 | tf_op jit(solution)/shard_map/ppermute | solution.py:56
  34.2 20.4 %collective-permute-start.5 = (bf16[256,512]{1,0:T(8,128)(2,1)}, bf16[256,512]{1,0:T(8,128)(2,1)S(1)}, u32[]{:S(2)}, u32[]{:S(2)}) collective-permute-start(bf16[256,512]{1,0:T(8,128)(2,1)} %get-tuple-element.82), channel_id=1, source_target_pairs={{0,3},{1,0},{2,1},{3,2},{4,7},{5,4},{6,5},{7,6},{8,11},{9,8},{10,9... | collective-permute-start | bytes 786440 | tf_op jit(solution)/shard_map/ppermute | solution.py:56
  36.0 18.6 %collective-permute-start.6 = (bf16[256,512]{1,0:T(8,128)(2,1)}, bf16[256,512]{1,0:T(8,128)(2,1)S(1)}, u32[]{:S(2)}, u32[]{:S(2)}) collective-permute-start(bf16[256,512]{1,0:T(8,128)(2,1)} %get-tuple-element.84), channel_id=1, source_target_pairs={{0,1},{1,2},{2,3},{3,0},{4,5},{5,6},{6,7},{7,4},{8,9},{9,10},{10,1... | collective-permute-start | bytes 786440 | tf_op jit(solution)/shard_map/ppermute | solution.py:56
  37.2 17.9 %collective-permute-start.4 = (bf16[256,512]{1,0:T(8,128)(2,1)S(1)}, bf16[256,512]{1,0:T(8,128)(2,1)S(1)}, u32[]{:S(2)}, u32[]{:S(2)}) collective-permute-start(bf16[256,512]{1,0:T(8,128)(2,1)S(1)} %add_convert_fusion.5), channel_id=1, source_target_pairs={{0,1},{1,2},{2,3},{3,0},{4,5},{5,6},{6,7},{7,4},{8,9},{9,10},{10,1... | collective-permute-start | bytes 786440 | tf_op jit(solution)/shard_map/ppermute | solution.py:56
  38.3 20.2 %collective-permute-start.8 = (bf16[256,512]{1,0:T(8,128)(2,1)S(1)}, bf16[256,512]{1,0:T(8,128)(2,1)S(1)}, u32[]{:S(2)}, u32[]{:S(2)}) collective-permute-start(bf16[256,512]{1,0:T(8,128)(2,1)S(1)} %add_convert_fusion.4), channel_id=1, source_target_pairs={{0,3},{1,0},{2,1},{3,2},{4,7},{5,4},{6,5},{7,6},{8,11},{9,8},{10,9... | collective-permute-start | bytes 786440 | tf_op jit(solution)/shard_map/ppermute | solution.py:56
  61.4 5.0 %collective-permute-start.9 = (bf16[128,512]{1,0:T(8,128)(2,1)}, bf16[128,512]{1,0:T(8,128)(2,1)S(1)}, u32[]{:S(2)}, u32[]{:S(2)}) collective-permute-start(bf16[128,512]{1,0:T(8,128)(2,1)} %get-tuple-element.88), channel_id=1, source_target_pairs={{0,4},{4,0},{8,12},{12,8},{1,5},{5,1},{9,13},{13,9},{2,6},{6,2},{1... | collective-permute-start | bytes 393224 | tf_op jit(solution)/shard_map/ppermute | solution.py:656
  61.4 6.5 %collective-permute-start.10 = (bf16[128,512]{1,0:T(8,128)(2,1)}, bf16[128,512]{1,0:T(8,128)(2,1)S(1)}, u32[]{:S(2)}, u32[]{:S(2)}) collective-permute-start(bf16[128,512]{1,0:T(8,128)(2,1)} %get-tuple-element.89), channel_id=1, source_target_pairs={{0,8},{4,12},{8,0},{12,4},{1,9},{5,13},{9,1},{13,5},{2,10},{6,14},... | collective-permute-start | bytes 393224 | tf_op jit(solution)/shard_map/ppermute | solution.py:656
  62.2 7.7 %collective-permute-start.11 = (bf16[128,512]{1,0:T(8,128)(2,1)}, bf16[128,512]{1,0:T(8,128)(2,1)S(1)}, u32[]{:S(2)}, u32[]{:S(2)}) collective-permute-start(bf16[128,512]{1,0:T(8,128)(2,1)} %get-tuple-element.90), channel_id=1, source_target_pairs={{0,12},{4,8},{8,4},{12,0},{1,13},{5,9},{9,5},{13,1},{2,14},{6,10},... | collective-permute-start | bytes 393224 | tf_op jit(solution)/shard_map/ppermute | solution.py:656
  72.8 29.2 %collective-permute-start.12 = (bf16[128,2048]{1,0:T(8,128)(2,1)}, bf16[128,2048]{1,0:T(8,128)(2,1)S(1)}, u32[]{:S(2)}, u32[]{:S(2)}) collective-permute-start(bf16[128,2048]{1,0:T(8,128)(2,1)} %get-tuple-element.92.refs_0_), channel_id=1, source_target_pairs={{0,3},{1,0},{2,1},{3,2},{4,7},{5,4},{6,5},{7,6},{8,11},{9,8},{10,9... | collective-permute-start | bytes 1572872 | tf_op jit(solution)/shard_map/ppermute | solution.py:56
  76.4 23.7 %collective-permute-start.13 = (bf16[128,2048]{1,0:T(8,128)(2,1)}, bf16[128,2048]{1,0:T(8,128)(2,1)S(1)}, u32[]{:S(2)}, u32[]{:S(2)}) collective-permute-start(bf16[128,2048]{1,0:T(8,128)(2,1)} %get-tuple-element.92.refs_0_), channel_id=1, source_target_pairs={{0,1},{1,2},{2,3},{3,0},{4,5},{5,6},{6,7},{7,4},{8,9},{9,10},{10,1... | collective-permute-start | bytes 1572872 | tf_op jit(solution)/shard_map/ppermute | solution.py:56
  100.2 11.1 %collective-permute-start.14 = (bf16[64,2048]{1,0:T(8,128)(2,1)S(1)}, bf16[64,2048]{1,0:T(8,128)(2,1)S(1)}, u32[]{:S(2)}, u32[]{:S(2)}) collective-permute-start(bf16[64,2048]{1,0:T(8,128)(2,1)S(1)} %slice.170), channel_id=1, source_target_pairs={{0,1},{1,2},{2,3},{3,0},{4,5},{5,6},{6,7},{7,4},{8,9},{9,10},{10,1... | collective-permute-start | bytes 786440 | tf_op jit(solution)/shard_map/ppermute | solution.py:56
  102.1 13.0 %collective-permute-start.15 = (bf16[64,2048]{1,0:T(8,128)(2,1)S(1)}, bf16[64,2048]{1,0:T(8,128)(2,1)S(1)}, u32[]{:S(2)}, u32[]{:S(2)}) collective-permute-start(bf16[64,2048]{1,0:T(8,128)(2,1)S(1)} %slice.171), channel_id=1, source_target_pairs={{0,3},{1,0},{2,1},{3,2},{4,7},{5,4},{6,5},{7,6},{8,11},{9,8},{10,9... | collective-permute-start | bytes 786440 | tf_op jit(solution)/shard_map/ppermute | solution.py:56
  120.9 10.7 %collective-permute-start.16 = (bf16[4,176,128]{2,1,0:T(8,128)(2,1)}, bf16[4,176,128]{2,1,0:T(8,128)(2,1)S(1)}, u32[]{:S(2)}, u32[]{:S(2)}) collective-permute-start(bf16[4,176,128]{2,1,0:T(8,128)(2,1)} %get-tuple-element.106), channel_id=1, source_target_pairs={{0,4},{4,8},{8,12},{1,5},{5,9},{9,13},{2,6},{6,10},{10,14},{3,7},{... | collective-permute-start | bytes 540680 | tf_op jit(solution)/shard_map/ppermute | solution.py:685
  122.2 9.5 %collective-permute-start.17 = (bf16[4,176,128]{2,1,0:T(8,128)(2,1)}, bf16[4,176,128]{2,1,0:T(8,128)(2,1)S(1)}, u32[]{:S(2)}, u32[]{:S(2)}) collective-permute-start(bf16[4,176,128]{2,1,0:T(8,128)(2,1)} %get-tuple-element.106), channel_id=1, source_target_pairs={{0,8},{4,12},{1,9},{5,13},{2,10},{6,14},{3,11},{7,15},{16,24},{20,... | collective-permute-start | bytes 540680 | tf_op jit(solution)/shard_map/ppermute | solution.py:685
  125.6 6.6 %collective-permute-start.18 = (bf16[4,176,128]{2,1,0:T(8,128)(2,1)}, bf16[4,176,128]{2,1,0:T(8,128)(2,1)S(1)}, u32[]{:S(2)}, u32[]{:S(2)}) collective-permute-start(bf16[4,176,128]{2,1,0:T(8,128)(2,1)} %get-tuple-element.106), channel_id=1, source_target_pairs={{0,12},{1,13},{2,14},{3,15},{16,28},{17,29},{18,30},{19,31}} | collective-permute-start | bytes 540680 | tf_op jit(solution)/shard_map/ppermute | solution.py:685
  137.5 16.4 %collective-permute-start.19 = (bf16[64,2048]{1,0:T(8,128)(2,1)}, bf16[64,2048]{1,0:T(8,128)(2,1)S(1)}, u32[]{:S(2)}, u32[]{:S(2)}) collective-permute-start(bf16[64,2048]{1,0:T(8,128)(2,1)} %get-tuple-element.110), channel_id=1, source_target_pairs={{0,1},{1,2},{2,3},{3,0},{4,5},{5,6},{6,7},{7,4},{8,9},{9,10},{10,1... | collective-permute-start | bytes 786440 | tf_op jit(solution)/shard_map/ppermute | solution.py:56
  142.1 113.8 %collective-permute-start.41 = (bf16[3840,512]{1,0:T(8,128)(2,1)}, bf16[3840,512]{1,0:T(8,128)(2,1)}, u32[]{:S(2)}, u32[]{:S(2)}) collective-permute-start(bf16[3840,512]{1,0:T(8,128)(2,1)} %slice.153), channel_id=1, source_target_pairs={{0,8},{4,12},{8,0},{12,4},{1,9},{5,13},{9,1},{13,5},{2,10},{6,14},... | collective-permute-start | bytes 11796488 | tf_op jit(solution)/shard_map/ppermute | solution.py:713
  146.5 27.7 %collective-permute-start.21 = (bf16[64,2048]{1,0:T(8,128)(2,1)}, bf16[64,2048]{1,0:T(8,128)(2,1)S(1)}, u32[]{:S(2)}, u32[]{:S(2)}) collective-permute-start(bf16[64,2048]{1,0:T(8,128)(2,1)} %get-tuple-element.111), channel_id=1, source_target_pairs={{0,3},{1,0},{2,1},{3,2},{4,7},{5,4},{6,5},{7,6},{8,11},{9,8},{10,9... | collective-permute-start | bytes 786440 | tf_op jit(solution)/shard_map/ppermute | solution.py:56
  150.0 24.2 %collective-permute-start.22 = (bf16[64,2048]{1,0:T(8,128)(2,1)}, bf16[64,2048]{1,0:T(8,128)(2,1)S(1)}, u32[]{:S(2)}, u32[]{:S(2)}) collective-permute-start(bf16[64,2048]{1,0:T(8,128)(2,1)} %get-tuple-element.113), channel_id=1, source_target_pairs={{0,1},{1,2},{2,3},{3,0},{4,5},{5,6},{6,7},{7,4},{8,9},{9,10},{10,1... | collective-permute-start | bytes 786440 | tf_op jit(solution)/shard_map/ppermute | solution.py:56
  150.1 18.1 %collective-permute-start.23 = (bf16[64,2048]{1,0:T(8,128)(2,1)S(1)}, bf16[64,2048]{1,0:T(8,128)(2,1)S(1)}, u32[]{:S(2)}, u32[]{:S(2)}) collective-permute-start(bf16[64,2048]{1,0:T(8,128)(2,1)S(1)} %copy-done.22), channel_id=1, source_target_pairs={{0,3},{1,0},{2,1},{3,2},{4,7},{5,4},{6,5},{7,6},{8,11},{9,8},{10,9... | collective-permute-start | bytes 786440 | tf_op jit(solution)/shard_map/ppermute | solution.py:56
  154.9 19.6 %collective-permute-start.20 = (bf16[64,2048]{1,0:T(8,128)(2,1)S(1)}, bf16[64,2048]{1,0:T(8,128)(2,1)S(1)}, u32[]{:S(2)}, u32[]{:S(2)}) collective-permute-start(bf16[64,2048]{1,0:T(8,128)(2,1)S(1)} %add_convert_fusion.3), channel_id=1, source_target_pairs={{0,1},{1,2},{2,3},{3,0},{4,5},{5,6},{6,7},{7,4},{8,9},{9,10},{10,1... | collective-permute-start | bytes 786440 | tf_op jit(solution)/shard_map/ppermute | solution.py:56
  169.2 11.0 %collective-permute-start.24 = (bf16[64,2048]{1,0:T(8,128)(2,1)S(1)}, bf16[64,2048]{1,0:T(8,128)(2,1)S(1)}, u32[]{:S(2)}, u32[]{:S(2)}) collective-permute-start(bf16[64,2048]{1,0:T(8,128)(2,1)S(1)} %add_convert_fusion.2), channel_id=1, source_target_pairs={{0,3},{1,0},{2,1},{3,2},{4,7},{5,4},{6,5},{7,6},{8,11},{9,8},{10,9... | collective-permute-start | bytes 786440 | tf_op jit(solution)/shard_map/ppermute | solution.py:56
  174.2 148.0 %collective-permute-start.37 = (bf16[6400,512]{1,0:T(8,128)(2,1)}, bf16[6400,512]{1,0:T(8,128)(2,1)}, u32[]{:S(2)}, u32[]{:S(2)}) collective-permute-start(bf16[6400,512]{1,0:T(8,128)(2,1)} %refs_3_.6), channel_id=1, source_target_pairs={{0,4},{4,0},{8,12},{12,8},{1,5},{5,1},{9,13},{13,9},{2,6},{6,2},{1... | collective-permute-start | bytes 19660808 | tf_op jit(solution)/shard_map/ppermute | solution.py:715
  183.7 16.8 %collective-permute-start.26 = (bf16[128,2048]{1,0:T(8,128)(2,1)}, bf16[128,2048]{1,0:T(8,128)(2,1)S(1)}, u32[]{:S(2)}, u32[]{:S(2)}) collective-permute-start(bf16[128,2048]{1,0:T(8,128)(2,1)} %get-tuple-element.117.refs_0_), channel_id=1, source_target_pairs={{0,1},{1,2},{2,3},{3,0},{4,5},{5,6},{6,7},{7,4},{8,9},{9,10},{10,1... | collective-permute-start | bytes 1572872 | tf_op jit(solution)/shard_map/ppermute | solution.py:56
  184.2 25.3 %collective-permute-start.25 = (bf16[128,2048]{1,0:T(8,128)(2,1)}, bf16[128,2048]{1,0:T(8,128)(2,1)}, u32[]{:S(2)}, u32[]{:S(2)}) collective-permute-start(bf16[128,2048]{1,0:T(8,128)(2,1)} %get-tuple-element.117.refs_0_), channel_id=1, source_target_pairs={{0,3},{1,0},{2,1},{3,2},{4,7},{5,4},{6,5},{7,6},{8,11},{9,8},{10,9... | collective-permute-start | bytes 1572872 | tf_op jit(solution)/shard_map/ppermute | solution.py:56
  200.5 19.1 %collective-permute-start.27 = (bf16[64,2048]{1,0:T(8,128)(2,1)S(1)}, bf16[64,2048]{1,0:T(8,128)(2,1)S(1)}, u32[]{:S(2)}, u32[]{:S(2)}) collective-permute-start(bf16[64,2048]{1,0:T(8,128)(2,1)S(1)} %slice.172), channel_id=1, source_target_pairs={{0,1},{1,2},{2,3},{3,0},{4,5},{5,6},{6,7},{7,4},{8,9},{9,10},{10,1... | collective-permute-start | bytes 786440 | tf_op jit(solution)/shard_map/ppermute | solution.py:56
  210.4 11.7 %collective-permute-start.28 = (bf16[64,2048]{1,0:T(8,128)(2,1)S(1)}, bf16[64,2048]{1,0:T(8,128)(2,1)S(1)}, u32[]{:S(2)}, u32[]{:S(2)}) collective-permute-start(bf16[64,2048]{1,0:T(8,128)(2,1)S(1)} %slice.173), channel_id=1, source_target_pairs={{0,3},{1,0},{2,1},{3,2},{4,7},{5,4},{6,5},{7,6},{8,11},{9,8},{10,9... | collective-permute-start | bytes 786440 | tf_op jit(solution)/shard_map/ppermute | solution.py:56
  229.1 10.5 %collective-permute-start.29 = (bf16[64,1536]{1,0:T(8,128)(2,1)S(1)}, bf16[64,1536]{1,0:T(8,128)(2,1)S(1)}, u32[]{:S(2)}, u32[]{:S(2)}) collective-permute-start(bf16[64,1536]{1,0:T(8,128)(2,1)S(1)} %fusion.2), channel_id=1, source_target_pairs={{0,4},{4,8},{8,12},{1,5},{5,9},{9,13},{2,6},{6,10},{10,14},{3,7},{... | collective-permute-start | bytes 589832 | tf_op jit(solution)/shard_map/ppermute | solution.py:728
  231.1 85.9 %collective-permute-start.38 = (bf16[2560,512]{1,0:T(8,128)(2,1)S(1)}, bf16[2560,512]{1,0:T(8,128)(2,1)}, u32[]{:S(2)}, u32[]{:S(2)}) collective-permute-start(bf16[2560,512]{1,0:T(8,128)(2,1)S(1)} %slice.144), channel_id=1, source_target_pairs={{0,8},{4,12},{8,0},{12,4},{1,9},{5,13},{9,1},{13,5},{2,10},{6,14},... | collective-permute-start | bytes 7864328 | tf_op jit(solution)/shard_map/ppermute | solution.py:742
  244.7 11.2 %collective-permute-start.30 = (bf16[64,2048]{1,0:T(8,128)(2,1)}, bf16[64,2048]{1,0:T(8,128)(2,1)S(1)}, u32[]{:S(2)}, u32[]{:S(2)}) collective-permute-start(bf16[64,2048]{1,0:T(8,128)(2,1)} %get-tuple-element.124), channel_id=1, source_target_pairs={{0,1},{1,2},{2,3},{3,0},{4,5},{5,6},{6,7},{7,4},{8,9},{9,10},{10,1... | collective-permute-start | bytes 786440 | tf_op jit(solution)/shard_map/ppermute | solution.py:56
  249.2 18.6 %collective-permute-start.32 = (bf16[64,2048]{1,0:T(8,128)(2,1)}, bf16[64,2048]{1,0:T(8,128)(2,1)S(1)}, u32[]{:S(2)}, u32[]{:S(2)}) collective-permute-start(bf16[64,2048]{1,0:T(8,128)(2,1)} %get-tuple-element.125), channel_id=1, source_target_pairs={{0,3},{1,0},{2,1},{3,2},{4,7},{5,4},{6,5},{7,6},{8,11},{9,8},{10,9... | collective-permute-start | bytes 786440 | tf_op jit(solution)/shard_map/ppermute | solution.py:56
  255.9 10.3 %collective-permute-start.34 = (bf16[64,2048]{1,0:T(8,128)(2,1)S(1)}, bf16[64,2048]{1,0:T(8,128)(2,1)S(1)}, u32[]{:S(2)}, u32[]{:S(2)}) collective-permute-start(bf16[64,2048]{1,0:T(8,128)(2,1)S(1)} %copy-done.25), channel_id=1, source_target_pairs={{0,3},{1,0},{2,1},{3,2},{4,7},{5,4},{6,5},{7,6},{8,11},{9,8},{10,9... | collective-permute-start | bytes 786440 | tf_op jit(solution)/shard_map/ppermute | solution.py:56
  256.0 66.3 %collective-permute-start.42 = (bf16[3840,512]{1,0:T(8,128)(2,1)}, bf16[3840,512]{1,0:T(8,128)(2,1)S(1)}, u32[]{:S(2)}, u32[]{:S(2)}) collective-permute-start(bf16[3840,512]{1,0:T(8,128)(2,1)} %collective-permute-done.41.refs_4_.refs_5_), channel_id=1, source_target_pairs={{0,4},{4,0},{8,12},{12,8},{1,5},{5,1},{9,13},{13,9},{2,6},{6,2},{1... | collective-permute-start | bytes 11796488 | tf_op jit(solution)/shard_map/ppermute | solution.py:714
  266.2 11.2 %collective-permute-start.33 = (bf16[64,2048]{1,0:T(8,128)(2,1)}, bf16[64,2048]{1,0:T(8,128)(2,1)S(1)}, u32[]{:S(2)}, u32[]{:S(2)}) collective-permute-start(bf16[64,2048]{1,0:T(8,128)(2,1)} %get-tuple-element.127), channel_id=1, source_target_pairs={{0,1},{1,2},{2,3},{3,0},{4,5},{5,6},{6,7},{7,4},{8,9},{9,10},{10,1... | collective-permute-start | bytes 786440 | tf_op jit(solution)/shard_map/ppermute | solution.py:56
  267.8 15.3 %collective-permute-start.31 = (bf16[64,2048]{1,0:T(8,128)(2,1)S(1)}, bf16[64,2048]{1,0:T(8,128)(2,1)S(1)}, u32[]{:S(2)}, u32[]{:S(2)}) collective-permute-start(bf16[64,2048]{1,0:T(8,128)(2,1)S(1)} %add_convert_fusion.1), channel_id=1, source_target_pairs={{0,1},{1,2},{2,3},{3,0},{4,5},{5,6},{6,7},{7,4},{8,9},{9,10},{10,1... | collective-permute-start | bytes 786440 | tf_op jit(solution)/shard_map/ppermute | solution.py:56
  277.5 10.4 %collective-permute-start.35 = (bf16[64,2048]{1,0:T(8,128)(2,1)S(1)}, bf16[64,2048]{1,0:T(8,128)(2,1)S(1)}, u32[]{:S(2)}, u32[]{:S(2)}) collective-permute-start(bf16[64,2048]{1,0:T(8,128)(2,1)S(1)} %add_convert_fusion), channel_id=1, source_target_pairs={{0,3},{1,0},{2,1},{3,2},{4,7},{5,4},{6,5},{7,6},{8,11},{9,8},{10,9... | collective-permute-start | bytes 786440 | tf_op jit(solution)/shard_map/ppermute | solution.py:56
  291.4 16.8 %collective-permute-start.36 = (bf16[128,2048]{1,0:T(8,128)(2,1)}, bf16[128,2048]{1,0:T(8,128)(2,1)S(1)}, u32[]{:S(2)}, u32[]{:S(2)}) collective-permute-start(bf16[128,2048]{1,0:T(8,128)(2,1)} %finish.3.refs_0_), channel_id=1, source_target_pairs={{0,1},{1,2},{2,3},{3,0},{4,5},{5,6},{6,7},{7,4},{8,9},{9,10},{10,1... | collective-permute-start | bytes 1572872 | tf_op jit(solution)/shard_map/ppermute | solution.py:56
  291.9 25.1 %collective-permute-start.39 = (bf16[128,2048]{1,0:T(8,128)(2,1)}, bf16[128,2048]{1,0:T(8,128)(2,1)S(1)}, u32[]{:S(2)}, u32[]{:S(2)}) collective-permute-start(bf16[128,2048]{1,0:T(8,128)(2,1)} %finish.3.refs_0_), channel_id=1, source_target_pairs={{0,3},{1,0},{2,1},{3,2},{4,7},{5,4},{6,5},{7,6},{8,11},{9,8},{10,9... | collective-permute-start | bytes 1572872 | tf_op jit(solution)/shard_map/ppermute | solution.py:56
  317.0 18.0 %collective-permute-start.40 = (bf16[2560,512]{1,0:T(8,128)(2,1)}, bf16[2560,512]{1,0:T(8,128)(2,1)}, u32[]{:S(2)}, u32[]{:S(2)}) collective-permute-start(bf16[2560,512]{1,0:T(8,128)(2,1)} %collective-permute-done.38.refs_4_.refs_5_), channel_id=1, source_target_pairs={{0,4},{4,0},{8,12},{12,8},{1,5},{5,1},{9,13},{13,9},{2,6},{6,2},{1... | collective-permute-start | bytes 7864328 | tf_op jit(solution)/shard_map/ppermute | solution.py:744
  318.3 26.2 %collective-permute-start.43 = (bf16[64,2048]{1,0:T(8,128)(2,1)S(1)}, bf16[64,2048]{1,0:T(8,128)(2,1)S(1)}, u32[]{:S(2)}, u32[]{:S(2)}) collective-permute-start(bf16[64,2048]{1,0:T(8,128)(2,1)S(1)} %slice.182), channel_id=1, source_target_pairs={{0,1},{1,2},{2,3},{3,0},{4,5},{5,6},{6,7},{7,4},{8,9},{9,10},{10,1... | collective-permute-start | bytes 786440 | tf_op jit(solution)/shard_map/ppermute | solution.py:56
  318.7 25.8 %collective-permute-start.44 = (bf16[64,2048]{1,0:T(8,128)(2,1)S(1)}, bf16[64,2048]{1,0:T(8,128)(2,1)S(1)}, u32[]{:S(2)}, u32[]{:S(2)}) collective-permute-start(bf16[64,2048]{1,0:T(8,128)(2,1)S(1)} %slice.183), channel_id=1, source_target_pairs={{0,3},{1,0},{2,1},{3,2},{4,7},{5,4},{6,5},{7,6},{8,11},{9,8},{10,9... | collective-permute-start | bytes 786440 | tf_op jit(solution)/shard_map/ppermute | solution.py:56
  365.5 5.4 %collective-permute-start.45 = (f32[3,128]{1,0:T(4,128)S(1)}, f32[3,128]{1,0:T(4,128)S(1)}, u32[]{:S(2)}, u32[]{:S(2)}) collective-permute-start(f32[3,128]{1,0:T(4,128)S(1)} %get-tuple-element.151), channel_id=1, source_target_pairs={{0,1},{1,2},{2,3},{3,0},{4,5},{5,6},{6,7},{7,4},{8,9},{9,10},{10,1... | collective-permute-start | bytes 4616 | tf_op jit(solution)/shard_map/ppermute | solution.py:56
  365.6 5.3 %collective-permute-start.47 = (f32[3,128]{1,0:T(4,128)S(1)}, f32[3,128]{1,0:T(4,128)S(1)}, u32[]{:S(2)}, u32[]{:S(2)}) collective-permute-start(f32[3,128]{1,0:T(4,128)S(1)} %get-tuple-element.150), channel_id=1, source_target_pairs={{0,3},{1,0},{2,1},{3,2},{4,7},{5,4},{6,5},{7,6},{8,11},{9,8},{10,9... | collective-permute-start | bytes 4616 | tf_op jit(solution)/shard_map/ppermute | solution.py:56
  369.4 4.5 %collective-permute-start.46 = (f32[3,128]{1,0:T(4,128)S(1)}, f32[3,128]{1,0:T(4,128)S(1)}, u32[]{:S(2)}, u32[]{:S(2)}) collective-permute-start(f32[3,128]{1,0:T(4,128)S(1)} %get-tuple-element.152), channel_id=1, source_target_pairs={{0,2},{1,3},{2,0},{3,1},{4,6},{5,7},{6,4},{7,5},{8,10},{9,11},{10,... | collective-permute-start | bytes 4616 | tf_op jit(solution)/shard_map/ppermute | solution.py:56
  (42 other events, 403.2 us)

commit v4 on v3

--- a/solution.py
+++ b/solution.py
@@ -81,13 +81,26 @@
     from_before, from_after = turned(far[0], 1), turned(far[1], -1)
     own_upper, own_lower, next_upper, next_lower, prev_upper, prev_lower = near()
     lower_right, upper_left = turned(next_lower, 1), turned(prev_upper, -1)
-    upper_right = turned(plus(next_upper, from_before), 1)
-    lower_left = turned(plus(prev_lower, from_after), -1)
+    upper_right, lower_left = pass_on(next_upper, from_before, prev_lower, from_after)
+    upper_right, lower_left = turned(upper_right, 1), turned(lower_left, -1)
     return [[own_upper, upper_right, upper_left], [own_lower, lower_right, lower_left]]
 
 
-def plus(one, two):
-    return (one.astype(F32) + two.astype(F32)).astype(BF16)
+def pass_on_kernel(next_ref, before_ref, prev_ref, after_ref, right_ref, left_ref):
+    right_ref[...] = (next_ref[...].astype(F32) + before_ref[...].astype(F32)).astype(BF16)
+    left_ref[...] = (prev_ref[...].astype(F32) + after_ref[...].astype(F32)).astype(BF16)
+
+
+def pass_on(next_upper, from_before, prev_lower, from_after):
+    return pl.pallas_call(
+        pass_on_kernel,
+        in_specs=[whole()] * 4,
+        out_specs=[whole()] * 2,
+        out_shape=[jax.ShapeDtypeStruct(next_upper.shape, BF16)] * 2,
+        compiler_params=params(),
+        cost_estimate=cost(1.5),
+        name="pass_on",
+    )(next_upper, from_before, prev_lower, from_after)
 
 
 def chunk_order(size):
@@ -537,57 +550,86 @@
     )(info, local, first, halo, weight)
 
 
-def score_kernel(units_count, pieces, first, order_ref, *refs):
+def score_kernel(units_count, pieces, lots, tile, order_ref, *refs):
     units, refs = refs[:units_count], refs[units_count:]
-    tables, (goal_ref, before_ref, out_ref, turned_ref) = refs[:pieces], refs[pieces:]
+    tables, (goal_ref, out_ref, turned_ref, held) = refs[: len(lots) * pieces], refs[len(lots) * pieces :]
     step = pl.program_id(0)
-    tile, width = tables[0].shape
+    width = tables[0].shape[1]
+    count = goal_ref.shape[1]
+    part = 128
 
     @pl.when(step == 0)
     def _():
         rows = jnp.concatenate([ref[...] for ref in units], axis=0)
         turned_ref[...] = jnp.transpose(rows)
-        out_ref[...] = before_ref[...]
-
-    logits = None
-    for n in range(pieces):
-        part = turned_ref[pl.ds(pl.multiple_of(order_ref[n] * width, width), width), :]
-        more = dot(tables[n][...], part)
-        logits = more if logits is None else logits + more
-    count = logits.shape[1]
-    logits = logits.reshape(tile // 8, 8, count)
-    row = lax.broadcasted_iota(jnp.int32, (tile // 8, 8, count), 0) * 8
-    row = row + lax.broadcasted_iota(jnp.int32, (tile // 8, 8, count), 1)
-    goal = (goal_ref[...] - (step * tile + first)).reshape(1, 1, count)
-    old = out_ref[0]
-    peak = jnp.maximum(old, jnp.max(logits, axis=0))
-    out_ref[0] = peak
-    out_ref[1] = out_ref[1] * jnp.exp(old - peak) + jnp.sum(jnp.exp(logits - peak[None]), axis=0)
-    out_ref[2] = out_ref[2] + jnp.sum(jnp.where(row == goal, logits, 0.0), axis=0)
-
-
-def scores(order, units, tables, goal, before, first):
+        held[0] = jnp.full((8, count), NEGATIVE, F32)
+        held[1] = jnp.zeros((8, count), F32)
+        held[2] = jnp.zeros((8, count), F32)
+
+    def run(mine):
+        inner = lax.broadcasted_iota(jnp.int32, (part // 8, 8, count), 0) * 8
+        inner = inner + lax.broadcasted_iota(jnp.int32, (part // 8, 8, count), 1)
+        peak, total, picked = held[0], held[1], held[2]
+        sides = [
+            turned_ref[pl.ds(pl.multiple_of(order_ref[n] * width, width), width), :] for n in range(pieces)
+        ]
+        for at in range(0, tile, part):
+            logits = None
+            for n in range(pieces):
+                more = dot(mine[n][at : at + part], sides[n])
+                logits = more if logits is None else logits + more
+            logits = logits.reshape(part // 8, 8, count)
+            goal = (goal_ref[...] - (step * tile + at)).reshape(1, 1, count)
+            old = peak
+            peak = jnp.maximum(old, jnp.max(logits, axis=0))
+            total = total * jnp.exp(old - peak) + jnp.sum(jnp.exp(logits - peak[None]), axis=0)
+            picked = picked + jnp.sum(jnp.where(inner == goal, logits, 0.0), axis=0)
+        held[0], held[1], held[2] = peak, total, picked
+
+    for lot, (start, stop) in enumerate(lots):
+        pl.when((step >= start) & (step < stop))(
+            lambda lot=lot: run(tables[lot * pieces : (lot + 1) * pieces])
+        )
+
+    @pl.when(step == pl.num_programs(0) - 1)
+    def _():
+        peak = jnp.max(held[0], axis=0, keepdims=True)
+        total = jnp.sum(held[1] * jnp.exp(held[0] - peak), axis=0, keepdims=True)
+        picked = jnp.sum(held[2], axis=0, keepdims=True)
+        out_ref[...] = jnp.concatenate([peak, total, picked, jnp.zeros((5, count), F32)], axis=0)
+
+
+def scores(order, units, lots, goal):
     count = goal.shape[1]
-    tile = 640
-    rows, width = tables[-1].shape
-    skips = [first // tile if table.shape[0] != rows else 0 for table in tables]
-    return pl.pallas_call(
-        functools.partial(score_kernel, len(units), len(tables), first),
+    rows = lots[-1][1]
+    tile = 1280 if rows % 1280 == 0 else 640
+    pieces = len(lots[0][2])
+    specs, steps = [], []
+    for first, last, tables in lots:
+        start, stop = first // tile, last // tile
+        steps.append((start, stop))
+        for table in tables:
+            shift = 0 if table.shape[0] == rows else start
+            specs.append(
+                pl.BlockSpec(
+                    (tile, table.shape[1]),
+                    lambda i, start=start, stop=stop, shift=shift: (jnp.clip(i, start, stop - 1) - shift, 0),
+                )
+            )
+    return pl.pallas_call(
+        functools.partial(score_kernel, len(units), pieces, steps, tile),
         in_specs=[smem()]
         + [pl.BlockSpec(piece.shape, lambda i: (0, 0), pipeline_mode=pl.Buffered(1)) for piece in units]
-        + [pl.BlockSpec((tile, width), lambda i, skip=skip: (i + skip, 0)) for skip in skips]
-        + [
-            pl.BlockSpec((1, count), lambda i: (0, 0)),
-            pl.BlockSpec((3, 8, count), lambda i: (0, 0, 0)),
-        ],
-        out_specs=pl.BlockSpec((3, 8, count), lambda i: (0, 0, 0)),
+        + specs
+        + [pl.BlockSpec((1, count), lambda i: (0, 0))],
+        out_specs=pl.BlockSpec((8, count), lambda i: (0, 0)),
         grid=(rows // tile,),
-        out_shape=jax.ShapeDtypeStruct((3, 8, count), F32),
-        scratch_shapes=[pltpu.VMEM((units[0].shape[1], count), BF16)],
-        compiler_params=params(),
-        cost_estimate=cost(9),
+        out_shape=jax.ShapeDtypeStruct((8, count), F32),
+        scratch_shapes=[pltpu.VMEM((units[0].shape[1], count), BF16), pltpu.VMEM((3, 8, count), F32)],
+        compiler_params=params(),
+        cost_estimate=cost(14),
         name="scores",
-    )(order, *units, *tables, goal, before)
+    )(order, *units, *[table for lot in lots for table in lot[2]], goal)
 
 
 def shards(
@@ -743,11 +785,11 @@
         corner, _ = lax.optimization_barrier((late, (chunks[1][0], chunks[-1][0])))
         late_corner = lax.ppermute(corner, "seq", xor_pairs(seq_count, 1))
         lots = [
-            (0, [vocab_table, beside, early, early_corner]),
-            (lots[0], [vocab_table, beside, late, late_corner]),
+            (0, lots[0], [vocab_table, beside, early, early_corner]),
+            (lots[0], vocab_rows, [vocab_table, beside, late, late_corner]),
         ]
     else:
-        lots = [(0, [lax.all_gather(vocab_table, "seq", axis=1, tiled=True)])]
+        lots = [(0, vocab_rows, [lax.all_gather(vocab_table, "seq", axis=1, tiled=True)])]
         order = jnp.zeros((1,), jnp.int32)
     goals = (target_ids - vocab_first).reshape(head_count, chunk)
     found = {}
@@ -758,16 +800,9 @@
                 for k in group
             ]
         ).reshape(1, -1)
-        state = jnp.zeros((3, 8, goal.shape[1]), F32).at[0].set(NEGATIVE)
-        for first, tables in lots:
-            state = scores(
-                order, [piece for k in group for piece in chunks[k]], tables, goal, state, first
-            )
-        peak = jnp.max(state[0], axis=0)
-        total = jnp.sum(state[1] * jnp.exp(state[0] - peak), axis=0)
-        triple = jnp.stack([peak, total, jnp.sum(state[2], axis=0)])
+        triple = scores(order, [piece for k in group for piece in chunks[k]], lots, goal)
         for at, k in enumerate(group):
-            found[k] = triple[:, at * chunk : (at + 1) * chunk]
+            found[k] = triple[:3, at * chunk : (at + 1) * chunk]
 
     shares = jnp.stack([found[0]] + [turned(found[k], k) for k in range(1, head_count)])
     peak = jnp.max(shares[:, 0], axis=0)

time: 376 us -> 408 us (1.085)
  starting transfers between devices: 67.1 us -> 110 us
  other arithmetic: 17.3 us -> 7.7 us
  waiting for transfers between devices: 122 us -> 115 us
  local copies, waits for them, and re-layouts: 21.4 us -> 26.8 us
    ppermute x1, starting transfers between devices: 0.07 us -> 46.1 us  [shards(): early_corner = lax.ppermute(early, 'seq', xor_pairs(seq_count, 1))]
    ppermute x33, waiting for transfers between devices: 117 us -> 105 us  [turned(): lax.ppermute(value, 'head', [(i, (i + step) % size) for i in range(size)])]
    convert_element_type x6 -> x0, other arithmetic: 6.09 us -> none  [plus(): return (one.astype(F32) + two.astype(F32)).astype(BF16)]
    unnamed x84 -> x100, local copies, waits for them, and re-layouts: 8.36 us -> 10.6 us
    pallas_call x4 -> x5, Pallas kernels: 37.5 us -> 38.2 us  [the longest x2 32 us: scores(): pl.pallas_call(functools.partial(score_kernel, len(units), pieces, steps,...]
  transfers between devices with their start and end apart: 48 -> 48, of which waited for: 25 -> 27; matrix products, arithmetic and copies ran while one was open for 7% -> 5% of each run, Pallas kernels for 26% -> 30%
where the time goes in v4:
time: 408 us; the launch traced here: 406 us
  Pallas kernels  140 us (34%)
  waiting for transfers between devices  115 us (28%)
  starting transfers between devices  110 us (27%)
  local copies, waits for them, and re-layouts  26.8 us (7%)
  other arithmetic  7.7 us (2%)
  between operations  6.4 us (2%)
    ppermute x33, waiting for transfers between devices, turned(): lax.ppermute(value, 'head', [(i, (i + step) % size) for i in range(size)])  105 us
    ppermute x33, starting transfers between devices, turned(): lax.ppermute(value, 'head', [(i, (i + step) % size) for i in range(size)])  50.9 us
    ppermute x1, starting transfers between devices, shards(): early_corner = lax.ppermute(early, 'seq', xor_pairs(seq_count, 1))  46.1 us
    pallas_call x2, Pallas kernels, scores(): pl.pallas_call(functools.partial(score_kernel, len(units), pieces, steps,...  32 us
    pallas_call x3, Pallas kernels, lookup(): pl.pallas_call(lookup_kernel, grid=(rows // tile,), in_specs=[pl.BlockSpe...  30.3 us
    pallas_call x3, Pallas kernels, matmul(): pl.pallas_call(matmul_kernel, grid=(b.shape[1] // tile,), in_specs=[pl.Bl...  16.6 us
    pallas_call x3, Pallas kernels, project(): pl.pallas_call(functools.partial(project_kernel, heads, slots, chunk, cou...  15.8 us
    unnamed x100, local copies, waits for them, and re-layouts  10.6 us
  transfers between devices with their start and end apart: 48, of which 27 were waited for; matrix products, arithmetic and copies ran while one was open for 5% of the time, Pallas kernels for 30%

profile of v4, /device:TPU:0, one launch (start us, length us, event | category | flops | bytes accessed | tf_op | source)
XLA Modules:
  0.0 406.2 jit_solution(14749314185922217332)
XLA Ops:
  8.0 8.6 %lookup.5 = (bf16[256,512]{1,0:T(8,128)(2,1)}, bf16[256,512]{1,0:T(8,128)(2,1)}) custom-call(s32[1,512]{1,0:T(1,128)} %bitcast.51, bf16[6400,512]{1,0:T(8,128)(2,1)} %refs_7_.1), custom_call_target="tpu_custom_call" | custom-call | flops 4800000000 | bytes 24000000 | tf_op jit(solution)/shard_map/lookup/pallas_call | solution.py:140
  21.0 13.2 %lookup.4 = (bf16[256,512]{1,0:T(8,128)(2,1)}, bf16[256,512]{1,0:T(8,128)(2,1)}, bf16[256,512]{1,0:T(8,128)(2,1)}, bf16[256,512]{1,0:T(8,128)(2,1)}) custom-call(s32[1,1024]{1,0:T(1,128)} %bitcast.46, bf16[6400,512]{1,0:T(8,128)(2,1)} %refs_7_.1), custom_call_target="tpu_custom_call" | custom-call | flops 9600000000 | bytes 48000000 | tf_op jit(solution)/shard_map/lookup/pallas_call | solution.py:140
  39.0 3.8 collective-permute-start.8
  42.9 8.5 %lookup.3 = (bf16[256,512]{1,0:T(8,128)(2,1)}, bf16[256,512]{1,0:T(8,128)(2,1)}) custom-call(s32[1,512]{1,0:T(1,128)} %bitcast.47, bf16[6400,512]{1,0:T(8,128)(2,1)} %refs_7_.1), custom_call_target="tpu_custom_call" | custom-call | flops 4800000000 | bytes 24000000 | tf_op jit(solution)/shard_map/lookup/pallas_call | solution.py:140
  55.1 3.3 collective-permute-done.8.refs_5_
  65.0 2.8 collective-permute-done.10.refs_2_
  72.8 3.6 collective-permute-start.12
  76.4 4.3 %slice.103 = bf16[3840,512]{1,0:T(8,128)(2,1)} slice(bf16[6400,512]{1,0:T(8,128)(2,1)} %refs_7_.1), slice={[0:3840], [0:512]} | slice | bytes 7864320 | tf_op jit(solution)/shard_map/slice | solution.py:680
  82.8 5.1 %project.3 = (bf16[4,128,256]{2,1,0:T(8,128)(2,1)}, bf16[4,128,256]{2,1,0:T(8,128)(2,1)}, bf16[128,512]{1,0:T(8,128)(2,1)}, f32[4,176,128]{2,1,0:T(8,128)}) custom-call(s32[1]{0:T(128)} %copy.35.bound_ref, s32[1]{0:T(128)} %get-tuple-element.151.places_ref, bf16[128,2048]{1,0:T(8,128)(2,1)} %get-tuple-element.80.refs_0_, bf16[2048,640]{1,0:T(8,128)(2,1)} %refs_2_.7, ...), custom_call_target="tpu_custom_call" | custom-call | flops 3000000000 | bytes 15000000 | tf_op jit(solution)/shard_map/project/pallas_call | solution.py:310
  87.9 12.2 %collective-permute-done.13.refs_1_ = bf16[128,2048]{1,0:T(8,128)(2,1)S(1)} collective-permute-done((bf16[128,2048]{1,0:T(8,128)(2,1)}, bf16[128,2048]{1,0:T(8,128)(2,1)S(1)}, u32[]{:S(2)}, u32[]{:S(2)}) %collective-permute-start.13) | collective-permute-done | bytes 524320 | tf_op jit(solution)/shard_map/ppermute | solution.py:56
  104.1 5.6 %project.4 = (bf16[4,256,256]{2,1,0:T(8,128)(2,1)}, bf16[4,256,256]{2,1,0:T(8,128)(2,1)}, bf16[256,512]{1,0:T(8,128)(2,1)}, f32[4,176,128]{2,1,0:T(8,128)}) custom-call(s32[1]{0:T(128)} %copy.35.bound_ref, s32[2]{0:T(128)} %slice.88.places_ref, bf16[128,2048]{1,0:T(8,128)(2,1)} %copy-done.8, bf16[128,2048]{1,0:T(8,128)(2,1)} %copy-done.9, ...), custom_call_target="tpu_custom_call" | custom-call | flops 3000000000 | bytes 15000000 | tf_op jit(solution)/shard_map/project/pallas_call | solution.py:310
  111.2 3.8 collective-permute-done.15.refs_1_
  115.7 5.1 %project.5 = (bf16[4,128,256]{2,1,0:T(8,128)(2,1)}, bf16[4,128,256]{2,1,0:T(8,128)(2,1)}, bf16[128,512]{1,0:T(8,128)(2,1)}, bf16[4,176,128]{2,1,0:T(8,128)(2,1)}) custom-call(s32[1]{0:T(128)} %copy.35.bound_ref, s32[1]{0:T(128)} %get-tuple-element.150.places_ref, bf16[64,2048]{1,0:T(8,128)(2,1)} %copy-done.29, bf16[64,2048]{1,0:T(8,128)(2,1)} %copy-done.38, ...), custom_call_target="tpu_custom_call" | custom-call | flops 3000000000 | bytes 15000000 | tf_op jit(solution)/shard_map/project/pallas_call | solution.py:310
  122.1 3.2 collective-permute-start.17
  132.4 4.5 %within.1 = (f32[4,512,128]{2,1,0:T(8,128)}, f32[4,512,8]{2,1,0:T(8,128)}) custom-call(s32[1]{0:T(128)} %copy.35.bound_ref, s32[4]{0:T(128)} %copy-done.17, bf16[4,128,256]{2,1,0:T(8,128)(2,1)} %get-tuple-element.81.refs_0_, bf16[4,256,256]{2,1,0:T(8,128)(2,1)} %get-tuple-element.83.refs_1_, bf16[4,128,256]{2,1,0:T(8,128)(2,1)} %get-tuple-element.85.refs_2_, ...), custom_call_target="tpu_custom_call" | custom-call | flops 2700000000 | bytes 13500000 | tf_op jit(solution)/shard_map/within/pallas_call | solution.py:349
  137.0 4.7 %across.1 = (bf16[512,512]{1,0:T(8,128)(2,1)}, bf16[64,2048]{1,0:T(8,128)(2,1)}, bf16[64,2048]{1,0:T(8,128)(2,1)}) custom-call(s32[1]{0:T(128)} %copy.35.bound_ref, s32[4]{0:T(128)} %copy-done.17, s32[3]{0:T(128)} %add_convert_fusion.share_ref, bf16[4,128,256]{2,1,0:T(8,128)(2,1)} %get-tuple-element.81.refs_0_, ...), custom_call_target="tpu_custom_call" | custom-call | flops 2700000000 | bytes 13500000 | tf_op jit(solution)/shard_map/across/pallas_call | solution.py:398
  142.0 3.5 collective-permute-start.20
  145.5 3.9 near.2
  152.6 4.2 %collective-permute-done.20.after_ref = bf16[64,2048]{1,0:T(8,128)(2,1)S(1)} collective-permute-done((bf16[64,2048]{1,0:T(8,128)(2,1)}, bf16[64,2048]{1,0:T(8,128)(2,1)S(1)}, u32[]{:S(2)}, u32[]{:S(2)}) %collective-permute-start.20) | collective-permute-done | bytes 262176 | tf_op jit(solution)/shard_map/ppermute | solution.py:56
  161.0 2.4 collective-permute-start.24
  164.0 5.5 %collective-permute-done.23.refs_4_ = bf16[64,2048]{1,0:T(8,128)(2,1)S(1)} collective-permute-done((bf16[64,2048]{1,0:T(8,128)(2,1)}, bf16[64,2048]{1,0:T(8,128)(2,1)S(1)}, u32[]{:S(2)}, u32[]{:S(2)}) %collective-permute-start.23) | collective-permute-done | bytes 262176 | tf_op jit(solution)/shard_map/ppermute | solution.py:56
  169.5 5.6 %collective-permute-done.21.refs_1_ = bf16[64,2048]{1,0:T(8,128)(2,1)S(1)} collective-permute-done((bf16[64,2048]{1,0:T(8,128)(2,1)}, bf16[64,2048]{1,0:T(8,128)(2,1)S(1)}, u32[]{:S(2)}, u32[]{:S(2)}) %collective-permute-start.21) | collective-permute-done | bytes 262176 | tf_op jit(solution)/shard_map/ppermute | solution.py:56
  175.1 5.6 %collective-permute-done.24.refs_5_ = bf16[64,2048]{1,0:T(8,128)(2,1)S(1)} collective-permute-done((bf16[64,2048]{1,0:T(8,128)(2,1)}, bf16[64,2048]{1,0:T(8,128)(2,1)S(1)}, u32[]{:S(2)}, u32[]{:S(2)}) %collective-permute-start.24) | collective-permute-done | bytes 262176 | tf_op jit(solution)/shard_map/ppermute | solution.py:56
  181.5 2.8 finish.2
  185.1 3.0 collective-permute-start.25
  188.1 3.4 slice.94
  194.6 5.2 %matmul.3.refs_0_ = bf16[128,1536]{1,0:T(8,128)(2,1)} custom-call(bf16[128,2048]{1,0:T(8,128)(2,1)} %get-tuple-element.107.refs_0_, bf16[2048,1536]{1,0:T(8,128)(2,1)} %refs_2_.9), custom_call_target="tpu_custom_call" | custom-call | flops 3000000000 | bytes 15000000 | tf_op jit(solution)/shard_map/matmul/pallas_call | solution.py:436
  201.2 9.1 %collective-permute-done.25.refs_0_ = bf16[128,2048]{1,0:T(8,128)(2,1)S(1)} collective-permute-done((bf16[128,2048]{1,0:T(8,128)(2,1)}, bf16[128,2048]{1,0:T(8,128)(2,1)S(1)}, u32[]{:S(2)}, u32[]{:S(2)}) %collective-permute-start.25) | collective-permute-done | bytes 524320 | tf_op jit(solution)/shard_map/ppermute | solution.py:56
  210.3 2.9 collective-permute-start.28
  213.2 6.2 %matmul.4.refs_1_ = bf16[256,1536]{1,0:T(8,128)(2,1)} custom-call(bf16[128,2048]{1,0:T(8,128)(2,1)} %copy-done.11, bf16[128,2048]{1,0:T(8,128)(2,1)} %copy-done.10, bf16[2048,1536]{1,0:T(8,128)(2,1)} %refs_2_.9), custom_call_target="tpu_custom_call" | custom-call | flops 3000000000 | bytes 15000000 | tf_op jit(solution)/shard_map/matmul/pallas_call | solution.py:436
  219.4 3.0 collective-permute-done.28.refs_1_
  223.1 5.2 %matmul.5.refs_2_ = bf16[128,1536]{1,0:T(8,128)(2,1)} custom-call(bf16[64,2048]{1,0:T(8,128)(2,1)} %copy-done.40, bf16[64,2048]{1,0:T(8,128)(2,1)} %copy-done.42, bf16[2048,1536]{1,0:T(8,128)(2,1)} %refs_2_.9), custom_call_target="tpu_custom_call" | custom-call | flops 3000000000 | bytes 15000000 | tf_op jit(solution)/shard_map/matmul/pallas_call | solution.py:436
  233.6 8.0 %local_window.1 = (bf16[512,512]{1,0:T(8,128)(2,1)}, bf16[64,1536]{1,0:T(8,128)(2,1)}) custom-call(s32[1]{0:T(128)} %copy.35.bound_ref, s32[4]{0:T(128)} %copy-done.17, bf16[128,1536]{1,0:T(8,128)(2,1)} %matmul.3.refs_0_, bf16[256,1536]{1,0:T(8,128)(2,1)} %matmul.4.refs_1_, bf16[128,1536]{1,0:T(8,128)(2,1)} %matmul.5.refs_2_), custom_call_target="tpu_custom_call" | custom-call | flops 4800000000 | bytes 24000000 | tf_op jit(solution)/shard_map/local_window/pallas_call | solution.py:501
  242.2 4.6 %halo_window.1 = (bf16[512,512]{1,0:T(8,128)(2,1)}, bf16[64,2048]{1,0:T(8,128)(2,1)}, bf16[64,2048]{1,0:T(8,128)(2,1)}) custom-call(s32[3]{0:T(128)} %pad_add_fusion.4.info_ref, bf16[512,512]{1,0:T(8,128)(2,1)} %get-tuple-element.108.local_ref, bf16[64,1536]{1,0:T(8,128)(2,1)} %get-tuple-element.109.first_ref, bf16[64,1536]{1,0:T(8,128)(2,1)} %copy-done.43, ...), custom_call_target="tpu_custom_call" | custom-call | flops 2700000000 | bytes 13500000 | tf_op jit(solution)/shard_map/halo_window/pallas_call | solution.py:541
  247.6 3.0 collective-permute-start.31
  250.6 46.1 %collective-permute-start.39 = (bf16[3840,512]{1,0:T(8,128)(2,1)}, bf16[3840,512]{1,0:T(8,128)(2,1)S(1)}, u32[]{:S(2)}, u32[]{:S(2)}) collective-permute-start(bf16[3840,512]{1,0:T(8,128)(2,1)} %collective-permute-done.38.refs_4_.refs_5_), channel_id=1, source_target_pairs={{0,4},{4,0},{8,12},{12,8},{1,5},{5,1},{9,13},{13,9},{2,6},{6,2},{1... | collective-permute-start | bytes 11796488 | tf_op jit(solution)/shard_map/ppermute | solution.py:756
  296.7 3.8 near.3
  304.9 5.1 %collective-permute-done.33.refs_2_ = bf16[64,2048]{1,0:T(8,128)(2,1)S(1)} collective-permute-done((bf16[64,2048]{1,0:T(8,128)(2,1)}, bf16[64,2048]{1,0:T(8,128)(2,1)S(1)}, u32[]{:S(2)}, u32[]{:S(2)}) %collective-permute-start.33) | collective-permute-done | bytes 262176 | tf_op jit(solution)/shard_map/ppermute | solution.py:56
  310.0 4.2 %collective-permute-done.34.refs_4_ = bf16[64,2048]{1,0:T(8,128)(2,1)S(1)} collective-permute-done((bf16[64,2048]{1,0:T(8,128)(2,1)}, bf16[64,2048]{1,0:T(8,128)(2,1)S(1)}, u32[]{:S(2)}, u32[]{:S(2)}) %collective-permute-start.34) | collective-permute-done | bytes 262176 | tf_op jit(solution)/shard_map/ppermute | solution.py:56
  315.8 5.5 %collective-permute-done.32.refs_1_ = bf16[64,2048]{1,0:T(8,128)(2,1)S(1)} collective-permute-done((bf16[64,2048]{1,0:T(8,128)(2,1)}, bf16[64,2048]{1,0:T(8,128)(2,1)S(1)}, u32[]{:S(2)}, u32[]{:S(2)}) %collective-permute-start.32) | collective-permute-done | bytes 262176 | tf_op jit(solution)/shard_map/ppermute | solution.py:56
  321.3 4.9 %collective-permute-done.35.refs_5_ = bf16[64,2048]{1,0:T(8,128)(2,1)S(1)} collective-permute-done((bf16[64,2048]{1,0:T(8,128)(2,1)}, bf16[64,2048]{1,0:T(8,128)(2,1)S(1)}, u32[]{:S(2)}, u32[]{:S(2)}) %collective-permute-start.35) | collective-permute-done | bytes 262176 | tf_op jit(solution)/shard_map/ppermute | solution.py:56
  326.9 2.8 finish.3.refs_0_
  330.3 3.3 collective-permute-start.41
  333.5 13.0 %collective-permute-done.36.refs_1_ = bf16[128,2048]{1,0:T(8,128)(2,1)S(1)} collective-permute-done((bf16[128,2048]{1,0:T(8,128)(2,1)}, bf16[128,2048]{1,0:T(8,128)(2,1)S(1)}, u32[]{:S(2)}, u32[]{:S(2)}) %collective-permute-start.36) | collective-permute-done | bytes 524320 | tf_op jit(solution)/shard_map/ppermute | solution.py:56
  346.6 8.7 %collective-permute-done.41.refs_0_ = bf16[128,2048]{1,0:T(8,128)(2,1)S(1)} collective-permute-done((bf16[128,2048]{1,0:T(8,128)(2,1)}, bf16[128,2048]{1,0:T(8,128)(2,1)S(1)}, u32[]{:S(2)}, u32[]{:S(2)}) %collective-permute-start.41) | collective-permute-done | bytes 524320 | tf_op jit(solution)/shard_map/ppermute | solution.py:56
  358.5 3.5 collective-permute-start.44
  365.5 16.0 %scores.2 = f32[8,256]{1,0:T(8,128)} custom-call(s32[4]{0:T(128)} %iota_xor_fusion.order_ref, bf16[128,2048]{1,0:T(8,128)(2,1)} %finish.3.refs_0_, bf16[128,2048]{1,0:T(8,128)(2,1)} %copy-done.4, bf16[6400,512]{1,0:T(8,128)(2,1)} %refs_7_.1, bf16[6400,512]{1,0:T(8,128)(2,1)} %collective-permute-done.37.refs_3_.refs_7_.refs_4_.refs_8_, ...), custom_call_target="tpu_custom_call" | custom-call | flops 8400000000 | bytes 42000000 | tf_op jit(solution)/shard_map/scores/pallas_call | solution.py:619
  383.3 16.0 %scores.3 = f32[8,256]{1,0:T(8,128)} custom-call(s32[4]{0:T(128)} %iota_xor_fusion.order_ref, bf16[128,2048]{1,0:T(8,128)(2,1)} %copy-done.3, bf16[64,2048]{1,0:T(8,128)(2,1)} %copy-done.5, bf16[64,2048]{1,0:T(8,128)(2,1)} %copy-done.6, bf16[6400,512]{1,0:T(8,128)(2,1)} %refs_7_.1, bf16[6400,512]{1,0:T(8,128)(2,1)} %collective-permute-done.37.refs_3_.refs_7_.refs_4_.refs_8_, ...), custom_call_target="tpu_custom_call" | custom-call | flops 8400000000 | bytes 42000000 | tf_op jit(solution)/shard_map/scores/pallas_call | solution.py:619
  (215 shorter events, 87.4 us)
Async XLA Ops:
  1.3 3.7 collective-permute-start.2
  3.7 3.6 collective-permute-start.1
  4.3 3.0 collective-permute-start
  16.5 19.6 %collective-permute-start.3 = (bf16[256,512]{1,0:T(8,128)(2,1)}, bf16[256,512]{1,0:T(8,128)(2,1)S(1)}, u32[]{:S(2)}, u32[]{:S(2)}) collective-permute-start(bf16[256,512]{1,0:T(8,128)(2,1)} %get-tuple-element.67), channel_id=1, source_target_pairs={{0,1},{1,2},{2,3},{3,0},{4,5},{5,6},{6,7},{7,4},{8,9},{9,10},{10,1... | collective-permute-start | bytes 786440 | tf_op jit(solution)/shard_map/ppermute | solution.py:56
  18.1 18.1 %collective-permute-start.4 = (bf16[256,512]{1,0:T(8,128)(2,1)}, bf16[256,512]{1,0:T(8,128)(2,1)S(1)}, u32[]{:S(2)}, u32[]{:S(2)}) collective-permute-start(bf16[256,512]{1,0:T(8,128)(2,1)} %get-tuple-element.69), channel_id=1, source_target_pairs={{0,3},{1,0},{2,1},{3,2},{4,7},{5,4},{6,5},{7,6},{8,11},{9,8},{10,9... | collective-permute-start | bytes 786440 | tf_op jit(solution)/shard_map/ppermute | solution.py:56
  34.1 19.4 %collective-permute-start.6 = (bf16[256,512]{1,0:T(8,128)(2,1)}, bf16[256,512]{1,0:T(8,128)(2,1)S(1)}, u32[]{:S(2)}, u32[]{:S(2)}) collective-permute-start(bf16[256,512]{1,0:T(8,128)(2,1)} %get-tuple-element.71), channel_id=1, source_target_pairs={{0,3},{1,0},{2,1},{3,2},{4,7},{5,4},{6,5},{7,6},{8,11},{9,8},{10,9... | collective-permute-start | bytes 786440 | tf_op jit(solution)/shard_map/ppermute | solution.py:56
  36.0 17.6 %collective-permute-start.7 = (bf16[256,512]{1,0:T(8,128)(2,1)}, bf16[256,512]{1,0:T(8,128)(2,1)S(1)}, u32[]{:S(2)}, u32[]{:S(2)}) collective-permute-start(bf16[256,512]{1,0:T(8,128)(2,1)} %get-tuple-element.73), channel_id=1, source_target_pairs={{0,1},{1,2},{2,3},{3,0},{4,5},{5,6},{6,7},{7,4},{8,9},{9,10},{10,1... | collective-permute-start | bytes 786440 | tf_op jit(solution)/shard_map/ppermute | solution.py:56
  39.0 16.1 %collective-permute-start.5 = (bf16[256,512]{1,0:T(8,128)(2,1)}, bf16[256,512]{1,0:T(8,128)(2,1)S(1)}, u32[]{:S(2)}, u32[]{:S(2)}) collective-permute-start(bf16[256,512]{1,0:T(8,128)(2,1)} %get-tuple-element.70), channel_id=1, source_target_pairs={{0,1},{1,2},{2,3},{3,0},{4,5},{5,6},{6,7},{7,4},{8,9},{9,10},{10,1... | collective-permute-start | bytes 786440 | tf_op jit(solution)/shard_map/ppermute | solution.py:56
  39.0 19.4 %collective-permute-start.8 = (bf16[256,512]{1,0:T(8,128)(2,1)}, bf16[256,512]{1,0:T(8,128)(2,1)S(1)}, u32[]{:S(2)}, u32[]{:S(2)}) collective-permute-start(bf16[256,512]{1,0:T(8,128)(2,1)} %get-tuple-element.74), channel_id=1, source_target_pairs={{0,3},{1,0},{2,1},{3,2},{4,7},{5,4},{6,5},{7,6},{8,11},{9,8},{10,9... | collective-permute-start | bytes 786440 | tf_op jit(solution)/shard_map/ppermute | solution.py:56
  61.4 3.7 collective-permute-start.9
  61.4 6.5 %collective-permute-start.10 = (bf16[128,512]{1,0:T(8,128)(2,1)}, bf16[128,512]{1,0:T(8,128)(2,1)S(1)}, u32[]{:S(2)}, u32[]{:S(2)}) collective-permute-start(bf16[128,512]{1,0:T(8,128)(2,1)} %get-tuple-element.77), channel_id=1, source_target_pairs={{0,8},{4,12},{8,0},{12,4},{1,9},{5,13},{9,1},{13,5},{2,10},{6,14},... | collective-permute-start | bytes 393224 | tf_op jit(solution)/shard_map/ppermute | solution.py:698
  62.0 7.9 %collective-permute-start.11 = (bf16[128,512]{1,0:T(8,128)(2,1)}, bf16[128,512]{1,0:T(8,128)(2,1)S(1)}, u32[]{:S(2)}, u32[]{:S(2)}) collective-permute-start(bf16[128,512]{1,0:T(8,128)(2,1)} %get-tuple-element.78), channel_id=1, source_target_pairs={{0,12},{4,8},{8,4},{12,0},{1,13},{5,9},{9,5},{13,1},{2,14},{6,10},... | collective-permute-start | bytes 393224 | tf_op jit(solution)/shard_map/ppermute | solution.py:698
  72.8 29.2 %collective-permute-start.12 = (bf16[128,2048]{1,0:T(8,128)(2,1)}, bf16[128,2048]{1,0:T(8,128)(2,1)S(1)}, u32[]{:S(2)}, u32[]{:S(2)}) collective-permute-start(bf16[128,2048]{1,0:T(8,128)(2,1)} %get-tuple-element.80.refs_0_), channel_id=1, source_target_pairs={{0,3},{1,0},{2,1},{3,2},{4,7},{5,4},{6,5},{7,6},{8,11},{9,8},{10,9... | collective-permute-start | bytes 1572872 | tf_op jit(solution)/shard_map/ppermute | solution.py:56
  76.4 23.8 %collective-permute-start.13 = (bf16[128,2048]{1,0:T(8,128)(2,1)}, bf16[128,2048]{1,0:T(8,128)(2,1)S(1)}, u32[]{:S(2)}, u32[]{:S(2)}) collective-permute-start(bf16[128,2048]{1,0:T(8,128)(2,1)} %get-tuple-element.80.refs_0_), channel_id=1, source_target_pairs={{0,1},{1,2},{2,3},{3,0},{4,5},{5,6},{6,7},{7,4},{8,9},{9,10},{10,1... | collective-permute-start | bytes 1572872 | tf_op jit(solution)/shard_map/ppermute | solution.py:56
  100.1 11.1 %collective-permute-start.14 = (bf16[64,2048]{1,0:T(8,128)(2,1)S(1)}, bf16[64,2048]{1,0:T(8,128)(2,1)S(1)}, u32[]{:S(2)}, u32[]{:S(2)}) collective-permute-start(bf16[64,2048]{1,0:T(8,128)(2,1)S(1)} %slice.114), channel_id=1, source_target_pairs={{0,1},{1,2},{2,3},{3,0},{4,5},{5,6},{6,7},{7,4},{8,9},{9,10},{10,1... | collective-permute-start | bytes 786440 | tf_op jit(solution)/shard_map/ppermute | solution.py:56
  102.0 13.0 %collective-permute-start.15 = (bf16[64,2048]{1,0:T(8,128)(2,1)S(1)}, bf16[64,2048]{1,0:T(8,128)(2,1)S(1)}, u32[]{:S(2)}, u32[]{:S(2)}) collective-permute-start(bf16[64,2048]{1,0:T(8,128)(2,1)S(1)} %slice.115), channel_id=1, source_target_pairs={{0,3},{1,0},{2,1},{3,2},{4,7},{5,4},{6,5},{7,6},{8,11},{9,8},{10,9... | collective-permute-start | bytes 786440 | tf_op jit(solution)/shard_map/ppermute | solution.py:56
  120.8 9.2 %collective-permute-start.16 = (bf16[4,176,128]{2,1,0:T(8,128)(2,1)}, bf16[4,176,128]{2,1,0:T(8,128)(2,1)S(1)}, u32[]{:S(2)}, u32[]{:S(2)}) collective-permute-start(bf16[4,176,128]{2,1,0:T(8,128)(2,1)} %get-tuple-element.94), channel_id=1, source_target_pairs={{0,4},{4,8},{8,12},{1,5},{5,9},{9,13},{2,6},{6,10},{10,14},{3,7},{... | collective-permute-start | bytes 540680 | tf_op jit(solution)/shard_map/ppermute | solution.py:727
  122.1 7.9 %collective-permute-start.17 = (bf16[4,176,128]{2,1,0:T(8,128)(2,1)}, bf16[4,176,128]{2,1,0:T(8,128)(2,1)S(1)}, u32[]{:S(2)}, u32[]{:S(2)}) collective-permute-start(bf16[4,176,128]{2,1,0:T(8,128)(2,1)} %get-tuple-element.94), channel_id=1, source_target_pairs={{0,8},{4,12},{1,9},{5,13},{2,10},{6,14},{3,11},{7,15},{16,24},{20,... | collective-permute-start | bytes 540680 | tf_op jit(solution)/shard_map/ppermute | solution.py:727
  125.3 6.6 %collective-permute-start.18 = (bf16[4,176,128]{2,1,0:T(8,128)(2,1)}, bf16[4,176,128]{2,1,0:T(8,128)(2,1)S(1)}, u32[]{:S(2)}, u32[]{:S(2)}) collective-permute-start(bf16[4,176,128]{2,1,0:T(8,128)(2,1)} %get-tuple-element.94), channel_id=1, source_target_pairs={{0,12},{1,13},{2,14},{3,15},{16,28},{17,29},{18,30},{19,31}} | collective-permute-start | bytes 540680 | tf_op jit(solution)/shard_map/ppermute | solution.py:727
  131.9 118.7 %collective-permute-start.38 = (bf16[3840,512]{1,0:T(8,128)(2,1)}, bf16[3840,512]{1,0:T(8,128)(2,1)}, u32[]{:S(2)}, u32[]{:S(2)}) collective-permute-start(bf16[3840,512]{1,0:T(8,128)(2,1)} %slice.103), channel_id=1, source_target_pairs={{0,8},{4,12},{8,0},{12,4},{1,9},{5,13},{9,1},{13,5},{2,10},{6,14},... | collective-permute-start | bytes 11796488 | tf_op jit(solution)/shard_map/ppermute | solution.py:755
  141.6 11.0 %collective-permute-start.19 = (bf16[64,2048]{1,0:T(8,128)(2,1)}, bf16[64,2048]{1,0:T(8,128)(2,1)S(1)}, u32[]{:S(2)}, u32[]{:S(2)}) collective-permute-start(bf16[64,2048]{1,0:T(8,128)(2,1)} %get-tuple-element.98), channel_id=1, source_target_pairs={{0,1},{1,2},{2,3},{3,0},{4,5},{5,6},{6,7},{7,4},{8,9},{9,10},{10,1... | collective-permute-start | bytes 786440 | tf_op jit(solution)/shard_map/ppermute | solution.py:56
  142.0 14.8 %collective-permute-start.20 = (bf16[64,2048]{1,0:T(8,128)(2,1)}, bf16[64,2048]{1,0:T(8,128)(2,1)S(1)}, u32[]{:S(2)}, u32[]{:S(2)}) collective-permute-start(bf16[64,2048]{1,0:T(8,128)(2,1)} %get-tuple-element.100), channel_id=1, source_target_pairs={{0,3},{1,0},{2,1},{3,2},{4,7},{5,4},{6,5},{7,6},{8,11},{9,8},{10,9... | collective-permute-start | bytes 786440 | tf_op jit(solution)/shard_map/ppermute | solution.py:56
  149.3 14.7 %collective-permute-start.22 = (bf16[64,2048]{1,0:T(8,128)(2,1)}, bf16[64,2048]{1,0:T(8,128)(2,1)S(1)}, u32[]{:S(2)}, u32[]{:S(2)}) collective-permute-start(bf16[64,2048]{1,0:T(8,128)(2,1)} %get-tuple-element.102), channel_id=1, source_target_pairs={{0,3},{1,0},{2,1},{3,2},{4,7},{5,4},{6,5},{7,6},{8,11},{9,8},{10,9... | collective-permute-start | bytes 786440 | tf_op jit(solution)/shard_map/ppermute | solution.py:56
  149.5 20.0 %collective-permute-start.23 = (bf16[64,2048]{1,0:T(8,128)(2,1)}, bf16[64,2048]{1,0:T(8,128)(2,1)S(1)}, u32[]{:S(2)}, u32[]{:S(2)}) collective-permute-start(bf16[64,2048]{1,0:T(8,128)(2,1)} %get-tuple-element.104), channel_id=1, source_target_pairs={{0,1},{1,2},{2,3},{3,0},{4,5},{5,6},{6,7},{7,4},{8,9},{9,10},{10,1... | collective-permute-start | bytes 786440 | tf_op jit(solution)/shard_map/ppermute | solution.py:56
  159.6 15.6 %collective-permute-start.21 = (bf16[64,2048]{1,0:T(8,128)(2,1)}, bf16[64,2048]{1,0:T(8,128)(2,1)S(1)}, u32[]{:S(2)}, u32[]{:S(2)}) collective-permute-start(bf16[64,2048]{1,0:T(8,128)(2,1)} %get-tuple-element.101), channel_id=1, source_target_pairs={{0,1},{1,2},{2,3},{3,0},{4,5},{5,6},{6,7},{7,4},{8,9},{9,10},{10,1... | collective-permute-start | bytes 786440 | tf_op jit(solution)/shard_map/ppermute | solution.py:56
  161.0 19.8 %collective-permute-start.24 = (bf16[64,2048]{1,0:T(8,128)(2,1)}, bf16[64,2048]{1,0:T(8,128)(2,1)S(1)}, u32[]{:S(2)}, u32[]{:S(2)}) collective-permute-start(bf16[64,2048]{1,0:T(8,128)(2,1)} %get-tuple-element.105), channel_id=1, source_target_pairs={{0,3},{1,0},{2,1},{3,2},{4,7},{5,4},{6,5},{7,6},{8,11},{9,8},{10,9... | collective-permute-start | bytes 786440 | tf_op jit(solution)/shard_map/ppermute | solution.py:56
  184.3 16.8 %collective-permute-start.26 = (bf16[128,2048]{1,0:T(8,128)(2,1)}, bf16[128,2048]{1,0:T(8,128)(2,1)S(1)}, u32[]{:S(2)}, u32[]{:S(2)}) collective-permute-start(bf16[128,2048]{1,0:T(8,128)(2,1)} %get-tuple-element.107.refs_0_), channel_id=1, source_target_pairs={{0,1},{1,2},{2,3},{3,0},{4,5},{5,6},{6,7},{7,4},{8,9},{9,10},{10,1... | collective-permute-start | bytes 1572872 | tf_op jit(solution)/shard_map/ppermute | solution.py:56
  185.1 25.2 %collective-permute-start.25 = (bf16[128,2048]{1,0:T(8,128)(2,1)}, bf16[128,2048]{1,0:T(8,128)(2,1)S(1)}, u32[]{:S(2)}, u32[]{:S(2)}) collective-permute-start(bf16[128,2048]{1,0:T(8,128)(2,1)} %get-tuple-element.107.refs_0_), channel_id=1, source_target_pairs={{0,3},{1,0},{2,1},{3,2},{4,7},{5,4},{6,5},{7,6},{8,11},{9,8},{10,9... | collective-permute-start | bytes 1572872 | tf_op jit(solution)/shard_map/ppermute | solution.py:56
  188.1 174.0 %collective-permute-start.37 = (bf16[6400,512]{1,0:T(8,128)(2,1)}, bf16[6400,512]{1,0:T(8,128)(2,1)}, u32[]{:S(2)}, u32[]{:S(2)}) collective-permute-start(bf16[6400,512]{1,0:T(8,128)(2,1)} %refs_7_.1), channel_id=1, source_target_pairs={{0,4},{4,0},{8,12},{12,8},{1,5},{5,1},{9,13},{13,9},{2,6},{6,2},{1... | collective-permute-start | bytes 19660808 | tf_op jit(solution)/shard_map/ppermute | solution.py:757
  201.1 18.3 %collective-permute-start.27 = (bf16[64,2048]{1,0:T(8,128)(2,1)S(1)}, bf16[64,2048]{1,0:T(8,128)(2,1)S(1)}, u32[]{:S(2)}, u32[]{:S(2)}) collective-permute-start(bf16[64,2048]{1,0:T(8,128)(2,1)S(1)} %slice.116), channel_id=1, source_target_pairs={{0,1},{1,2},{2,3},{3,0},{4,5},{5,6},{6,7},{7,4},{8,9},{9,10},{10,1... | collective-permute-start | bytes 786440 | tf_op jit(solution)/shard_map/ppermute | solution.py:56
  210.3 12.1 %collective-permute-start.28 = (bf16[64,2048]{1,0:T(8,128)(2,1)S(1)}, bf16[64,2048]{1,0:T(8,128)(2,1)S(1)}, u32[]{:S(2)}, u32[]{:S(2)}) collective-permute-start(bf16[64,2048]{1,0:T(8,128)(2,1)S(1)} %slice.117), channel_id=1, source_target_pairs={{0,3},{1,0},{2,1},{3,2},{4,7},{5,4},{6,5},{7,6},{8,11},{9,8},{10,9... | collective-permute-start | bytes 786440 | tf_op jit(solution)/shard_map/ppermute | solution.py:56
  229.3 126.0 %collective-permute-start.40 = (bf16[2560,512]{1,0:T(8,128)(2,1)}, bf16[2560,512]{1,0:T(8,128)(2,1)S(1)}, u32[]{:S(2)}, u32[]{:S(2)}) collective-permute-start(bf16[2560,512]{1,0:T(8,128)(2,1)} %slice.94), channel_id=1, source_target_pairs={{0,8},{4,12},{8,0},{12,4},{1,9},{5,13},{9,1},{13,5},{2,10},{6,14},... | collective-permute-start | bytes 7864328 | tf_op jit(solution)/shard_map/ppermute | solution.py:784
  231.8 9.7 %collective-permute-start.29 = (bf16[64,1536]{1,0:T(8,128)(2,1)S(1)}, bf16[64,1536]{1,0:T(8,128)(2,1)S(1)}, u32[]{:S(2)}, u32[]{:S(2)}) collective-permute-start(bf16[64,1536]{1,0:T(8,128)(2,1)S(1)} %fusion.2), channel_id=1, source_target_pairs={{0,4},{4,8},{8,12},{1,5},{5,9},{9,13},{2,6},{6,10},{10,14},{3,7},{... | collective-permute-start | bytes 589832 | tf_op jit(solution)/shard_map/ppermute | solution.py:770
  246.8 53.8 %collective-permute-start.30 = (bf16[64,2048]{1,0:T(8,128)(2,1)}, bf16[64,2048]{1,0:T(8,128)(2,1)S(1)}, u32[]{:S(2)}, u32[]{:S(2)}) collective-permute-start(bf16[64,2048]{1,0:T(8,128)(2,1)} %get-tuple-element.114), channel_id=1, source_target_pairs={{0,1},{1,2},{2,3},{3,0},{4,5},{5,6},{6,7},{7,4},{8,9},{9,10},{10,1... | collective-permute-start | bytes 786440 | tf_op jit(solution)/shard_map/ppermute | solution.py:56
  247.6 53.5 %collective-permute-start.31 = (bf16[64,2048]{1,0:T(8,128)(2,1)}, bf16[64,2048]{1,0:T(8,128)(2,1)S(1)}, u32[]{:S(2)}, u32[]{:S(2)}) collective-permute-start(bf16[64,2048]{1,0:T(8,128)(2,1)} %get-tuple-element.116), channel_id=1, source_target_pairs={{0,3},{1,0},{2,1},{3,2},{4,7},{5,4},{6,5},{7,6},{8,11},{9,8},{10,9... | collective-permute-start | bytes 786440 | tf_op jit(solution)/shard_map/ppermute | solution.py:56
  250.6 111.5 %collective-permute-start.39 = (bf16[3840,512]{1,0:T(8,128)(2,1)}, bf16[3840,512]{1,0:T(8,128)(2,1)S(1)}, u32[]{:S(2)}, u32[]{:S(2)}) collective-permute-start(bf16[3840,512]{1,0:T(8,128)(2,1)} %collective-permute-done.38.refs_4_.refs_5_), channel_id=1, source_target_pairs={{0,4},{4,0},{8,12},{12,8},{1,5},{5,1},{9,13},{13,9},{2,6},{6,2},{1... | collective-permute-start | bytes 11796488 | tf_op jit(solution)/shard_map/ppermute | solution.py:756
  300.6 9.4 %collective-permute-start.33 = (bf16[64,2048]{1,0:T(8,128)(2,1)}, bf16[64,2048]{1,0:T(8,128)(2,1)S(1)}, u32[]{:S(2)}, u32[]{:S(2)}) collective-permute-start(bf16[64,2048]{1,0:T(8,128)(2,1)} %get-tuple-element.118), channel_id=1, source_target_pairs={{0,3},{1,0},{2,1},{3,2},{4,7},{5,4},{6,5},{7,6},{8,11},{9,8},{10,9... | collective-permute-start | bytes 786440 | tf_op jit(solution)/shard_map/ppermute | solution.py:56
  301.1 13.0 %collective-permute-start.34 = (bf16[64,2048]{1,0:T(8,128)(2,1)}, bf16[64,2048]{1,0:T(8,128)(2,1)S(1)}, u32[]{:S(2)}, u32[]{:S(2)}) collective-permute-start(bf16[64,2048]{1,0:T(8,128)(2,1)} %get-tuple-element.120), channel_id=1, source_target_pairs={{0,1},{1,2},{2,3},{3,0},{4,5},{5,6},{6,7},{7,4},{8,9},{9,10},{10,1... | collective-permute-start | bytes 786440 | tf_op jit(solution)/shard_map/ppermute | solution.py:56
  310.0 11.3 %collective-permute-start.32 = (bf16[64,2048]{1,0:T(8,128)(2,1)}, bf16[64,2048]{1,0:T(8,128)(2,1)S(1)}, u32[]{:S(2)}, u32[]{:S(2)}) collective-permute-start(bf16[64,2048]{1,0:T(8,128)(2,1)} %get-tuple-element.117), channel_id=1, source_target_pairs={{0,1},{1,2},{2,3},{3,0},{4,5},{5,6},{6,7},{7,4},{8,9},{9,10},{10,1... | collective-permute-start | bytes 786440 | tf_op jit(solution)/shard_map/ppermute | solution.py:56
  314.2 12.1 %collective-permute-start.35 = (bf16[64,2048]{1,0:T(8,128)(2,1)}, bf16[64,2048]{1,0:T(8,128)(2,1)S(1)}, u32[]{:S(2)}, u32[]{:S(2)}) collective-permute-start(bf16[64,2048]{1,0:T(8,128)(2,1)} %get-tuple-element.121), channel_id=1, source_target_pairs={{0,3},{1,0},{2,1},{3,2},{4,7},{5,4},{6,5},{7,6},{8,11},{9,8},{10,9... | collective-permute-start | bytes 786440 | tf_op jit(solution)/shard_map/ppermute | solution.py:56
  329.7 16.8 %collective-permute-start.36 = (bf16[128,2048]{1,0:T(8,128)(2,1)}, bf16[128,2048]{1,0:T(8,128)(2,1)S(1)}, u32[]{:S(2)}, u32[]{:S(2)}) collective-permute-start(bf16[128,2048]{1,0:T(8,128)(2,1)} %finish.3.refs_0_), channel_id=1, source_target_pairs={{0,1},{1,2},{2,3},{3,0},{4,5},{5,6},{6,7},{7,4},{8,9},{9,10},{10,1... | collective-permute-start | bytes 1572872 | tf_op jit(solution)/shard_map/ppermute | solution.py:56
  330.3 25.0 %collective-permute-start.41 = (bf16[128,2048]{1,0:T(8,128)(2,1)}, bf16[128,2048]{1,0:T(8,128)(2,1)S(1)}, u32[]{:S(2)}, u32[]{:S(2)}) collective-permute-start(bf16[128,2048]{1,0:T(8,128)(2,1)} %finish.3.refs_0_), channel_id=1, source_target_pairs={{0,3},{1,0},{2,1},{3,2},{4,7},{5,4},{6,5},{7,6},{8,11},{9,8},{10,9... | collective-permute-start | bytes 1572872 | tf_op jit(solution)/shard_map/ppermute | solution.py:56
  355.3 6.8 %collective-permute-start.42 = (bf16[2560,512]{1,0:T(8,128)(2,1)S(1)}, bf16[2560,512]{1,0:T(8,128)(2,1)S(1)}, u32[]{:S(2)}, u32[]{:S(2)}) collective-permute-start(bf16[2560,512]{1,0:T(8,128)(2,1)S(1)} %collective-permute-done.40.refs_8_.refs_9_), channel_id=1, source_target_pairs={{0,4},{4,0},{8,12},{12,8},{1,5},{5,1},{9,13},{13,9},{2,6},{6,2},{1... | collective-permute-start | bytes 7864328 | tf_op jit(solution)/shard_map/ppermute | solution.py:786
  357.5 24.9 %collective-permute-start.43 = (bf16[64,2048]{1,0:T(8,128)(2,1)}, bf16[64,2048]{1,0:T(8,128)(2,1)S(1)}, u32[]{:S(2)}, u32[]{:S(2)}) collective-permute-start(bf16[64,2048]{1,0:T(8,128)(2,1)} %slice.123), channel_id=1, source_target_pairs={{0,1},{1,2},{2,3},{3,0},{4,5},{5,6},{6,7},{7,4},{8,9},{9,10},{10,1... | collective-permute-start | bytes 786440 | tf_op jit(solution)/shard_map/ppermute | solution.py:56
  358.5 23.9 %collective-permute-start.44 = (bf16[64,2048]{1,0:T(8,128)(2,1)}, bf16[64,2048]{1,0:T(8,128)(2,1)S(1)}, u32[]{:S(2)}, u32[]{:S(2)}) collective-permute-start(bf16[64,2048]{1,0:T(8,128)(2,1)} %slice.124), channel_id=1, source_target_pairs={{0,3},{1,0},{2,1},{3,2},{4,7},{5,4},{6,5},{7,6},{8,11},{9,8},{10,9... | collective-permute-start | bytes 786440 | tf_op jit(solution)/shard_map/ppermute | solution.py:56
  382.2 19.9 %collective-permute-start.47 = (f32[3,128]{1,0:T(4,128)S(1)}, f32[3,128]{1,0:T(4,128)S(1)}, u32[]{:S(2)}, u32[]{:S(2)}) collective-permute-start(f32[3,128]{1,0:T(4,128)S(1)} %get-tuple-element.135), channel_id=1, source_target_pairs={{0,3},{1,0},{2,1},{3,2},{4,7},{5,4},{6,5},{7,6},{8,11},{9,8},{10,9... | collective-permute-start | bytes 4616 | tf_op jit(solution)/shard_map/ppermute | solution.py:56
  399.9 4.5 %collective-permute-start.46 = (f32[3,128]{1,0:T(4,128)S(1)}, f32[3,128]{1,0:T(4,128)S(1)}, u32[]{:S(2)}, u32[]{:S(2)}) collective-permute-start(f32[3,128]{1,0:T(4,128)S(1)} %get-tuple-element.137), channel_id=1, source_target_pairs={{0,2},{1,3},{2,0},{3,1},{4,6},{5,7},{6,4},{7,5},{8,10},{9,11},{10,... | collective-permute-start | bytes 4616 | tf_op jit(solution)/shard_map/ppermute | solution.py:56
  400.1 5.5 %collective-permute-start.45 = (f32[3,128]{1,0:T(4,128)S(1)}, f32[3,128]{1,0:T(4,128)S(1)}, u32[]{:S(2)}, u32[]{:S(2)}) collective-permute-start(f32[3,128]{1,0:T(4,128)S(1)} %get-tuple-element.136), channel_id=1, source_target_pairs={{0,1},{1,2},{2,3},{3,0},{4,5},{5,6},{6,7},{7,4},{8,9},{9,10},{10,1... | collective-permute-start | bytes 4616 | tf_op jit(solution)/shard_map/ppermute | solution.py:56
  (50 other events, 353.5 us)

commit v5 on v4

--- a/solution.py
+++ b/solution.py
@@ -56,17 +56,21 @@
     return lax.ppermute(value, "head", [(i, (i + step) % size) for i in range(size)])
 
 
-def gather_rows(own):
+def gather_rows(own, work=None):
     size = lax.axis_size("head")
+    made = None if work is None else work(own)
     if size != 4:
         full = lax.all_gather(own, "head")
         here = lax.axis_index("head")
         return [[own]] + [
             [lax.dynamic_index_in_dim(full, (here + k) % size, 0, False)] for k in range(1, size)
-        ]
+        ], made
     half = own.shape[0] // 2
-    before, after = turned(own, 1), turned(own, -1)
-    return [[own], [after], [turned(before[:half], 1), turned(after[half:], -1)], [before]]
+    before = turned(own, 1)
+    if work is not None:
+        own, made = lax.optimization_barrier((own, made))
+    after = turned(own, -1)
+    return [[own], [after], [turned(before[:half], 1), turned(after[half:], -1)], [before]], made
 
 
 def scatter_rows(far, near):
@@ -698,17 +702,16 @@
         lax.ppermute(found[k], "seq", xor_pairs(seq_count, k)) for k in range(1, seq_count)
     ]
     embedded, units = begin(order, norm_gain_one, gathered)
-    chunks = gather_rows(units)
 
     constants = selectors()
     sets, state = [], None
-    for n, call in enumerate(calls):
-        pieces = [piece for k in call for piece in chunks[k]]
+
+    def project_call(n, pieces, state):
         first = sum(len(c) for c in calls[:n])
-        made = project(
+        return project(
             bound,
-            places[first : first + len(call)],
-            list(range(len(call))),
+            places[first : first + len(calls[n])],
+            list(range(len(calls[n]))),
             chunk,
             tok_count,
             pieces,
@@ -718,6 +721,11 @@
             n == len(calls) - 1,
             heads,
         )
+
+    chunks, made = gather_rows(units, lambda own: project_call(0, [own], None))
+    for n, call in enumerate(calls):
+        if n:
+            made = project_call(n, [piece for k in call for piece in chunks[k]], state)
         sets.append(made[:3])
         state = made[3]
     fqs, fks, vs = zip(*sets)
@@ -756,9 +764,9 @@
         early_corner = lax.ppermute(early, "seq", xor_pairs(seq_count, 1))
         beside = lax.ppermute(vocab_table, "seq", xor_pairs(seq_count, 1))
 
-    chunks = gather_rows(units)
-    qkvs = []
-    for call in calls:
+    chunks, made = gather_rows(units, lambda own: matmul([own], win_qkv, 3 * HEAD_DIM))
+    qkvs = [made]
+    for call in calls[1:]:
         qkvs.append(matmul([piece for k in call for piece in chunks[k]], win_qkv, 3 * HEAD_DIM))
     tail = jnp.zeros((WINDOW, win_qkv.shape[1]), BF16)
     for slot, k in enumerate(slots):
@@ -766,7 +774,6 @@
         tail = jnp.where(
             held_at[slot] == head_count - 1, qkvs[n][at + chunk - WINDOW : at + chunk], tail
         )
-    late, tail = lax.optimization_barrier((late, tail))
     halo = lax.ppermute(tail, "seq", [(i, i + 1) for i in range(seq_count - 1)])
     previous = jnp.sum(jnp.where(block == seq_index - 1, starts, 0))
     valid_from = jnp.where(
@@ -774,12 +781,13 @@
     ).astype(jnp.int32)
     first_spot = jnp.sum(jnp.where(held_at == 0, jnp.arange(head_count) * chunk, 0)).astype(jnp.int32)
     local, first = local_window(bound, places, slots, spots, chunk, qkvs, heads)
+    late, local, halo = lax.optimization_barrier((late, local, halo))
     info = jnp.stack([bound[0], valid_from, first_spot])
     mixed, *outer = halo_window(info, near, chunk, far, local, first, halo, win_out, heads)
     parts = scatter_rows(outer, lambda: near_chunks(mixed, win_out, near, chunk))
     units = finish(residual, final_gain, parts, True)[0]
 
-    chunks = gather_rows(units)
+    chunks, _ = gather_rows(units)
     if seq_count == 4:
         late = lax.ppermute(late, "seq", xor_pairs(seq_count, 2))
         corner, _ = lax.optimization_barrier((late, (chunks[1][0], chunks[-1][0])))

time: 408 us -> 363 us (0.89)
  starting transfers between devices: 110 us -> 71.9 us
  waiting for transfers between devices: 115 us -> 105 us
    ppermute x1, starting transfers between devices: 46.1 us -> 0.01 us  [shards(): early_corner = lax.ppermute(early, 'seq', xor_pairs(seq_count, 1))]
    ppermute x1, starting transfers between devices: 0.07 us -> 10.4 us  [shards(): late = lax.ppermute(late, 'seq', xor_pairs(seq_count, 2))]
    ppermute x33, waiting for transfers between devices: 105 us -> 98.4 us  [turned(): lax.ppermute(value, 'head', [(i, (i + step) % size) for i in range(size)])]
    unnamed x100 -> x102, local copies, waits for them, and re-layouts: 10.6 us -> 11.4 us
  transfers between devices with their start and end apart: 48 -> 48, of which waited for: 27 -> 26; matrix products, arithmetic and copies ran while one was open for 5% -> 6% of each run, Pallas kernels for 30% -> 33%
where the time goes in v5:
time: 363 us; the launch traced here: 361 us
  Pallas kernels  141 us (39%)
  waiting for transfers between devices  105 us (29%)
  starting transfers between devices  71.9 us (20%)
  local copies, waits for them, and re-layouts  27.5 us (8%)
  other arithmetic  8.35 us (2%)
  between operations  6.84 us (2%)
    ppermute x33, waiting for transfers between devices, turned(): lax.ppermute(value, 'head', [(i, (i + step) % size) for i in range(size)])  98.4 us
    ppermute x33, starting transfers between devices, turned(): lax.ppermute(value, 'head', [(i, (i + step) % size) for i in range(size)])  48.2 us
    pallas_call x2, Pallas kernels, scores(): pl.pallas_call(functools.partial(score_kernel, len(units), pieces, steps,...  32 us
    pallas_call x3, Pallas kernels, lookup(): pl.pallas_call(lookup_kernel, grid=(rows // tile,), in_specs=[pl.BlockSpe...  30.3 us
    pallas_call x3, Pallas kernels, matmul(): pl.pallas_call(matmul_kernel, grid=(b.shape[1] // tile,), in_specs=[pl.Bl...  17 us
    pallas_call x3, Pallas kernels, project(): pl.pallas_call(functools.partial(project_kernel, heads, slots, chunk, cou...  15.8 us
    unnamed x102, local copies, waits for them, and re-layouts  11.4 us
    ppermute x1, starting transfers between devices, shards(): late = lax.ppermute(late, 'seq', xor_pairs(seq_count, 2))  10.4 us
  transfers between devices with their start and end apart: 48, of which 26 were waited for; matrix products, arithmetic and copies ran while one was open for 6% of the time, Pallas kernels for 33%

profile of v5, /device:TPU:0, one launch (start us, length us, event | category | flops | bytes accessed | tf_op | source)
XLA Modules:
  0.0 360.9 jit_solution(13223970113950654558)
XLA Ops:
  1.3 2.4 collective-permute-start.2
  8.0 8.6 %lookup.5 = (bf16[256,512]{1,0:T(8,128)(2,1)}, bf16[256,512]{1,0:T(8,128)(2,1)}) custom-call(s32[1,512]{1,0:T(1,128)} %bitcast.51, bf16[6400,512]{1,0:T(8,128)(2,1)} %refs_7_.1), custom_call_target="tpu_custom_call" | custom-call | flops 4800000000 | bytes 24000000 | tf_op jit(solution)/shard_map/lookup/pallas_call | solution.py:144
  21.0 13.2 %lookup.4 = (bf16[256,512]{1,0:T(8,128)(2,1)}, bf16[256,512]{1,0:T(8,128)(2,1)}, bf16[256,512]{1,0:T(8,128)(2,1)}, bf16[256,512]{1,0:T(8,128)(2,1)}) custom-call(s32[1,1024]{1,0:T(1,128)} %bitcast.46, bf16[6400,512]{1,0:T(8,128)(2,1)} %refs_7_.1), custom_call_target="tpu_custom_call" | custom-call | flops 9600000000 | bytes 48000000 | tf_op jit(solution)/shard_map/lookup/pallas_call | solution.py:144
  39.1 3.8 %collective-permute-start.8 = (bf16[256,512]{1,0:T(8,128)(2,1)}, bf16[256,512]{1,0:T(8,128)(2,1)S(1)}, u32[]{:S(2)}, u32[]{:S(2)}) collective-permute-start(bf16[256,512]{1,0:T(8,128)(2,1)} %get-tuple-element.82), channel_id=1, source_target_pairs={{0,3},{1,0},{2,1},{3,2},{4,7},{5,4},{6,5},{7,6},{8,11},{9,8},{10,9... | collective-permute-start | bytes 786440 | tf_op jit(solution)/shard_map/ppermute | solution.py:56
  42.9 8.6 %lookup.3 = (bf16[256,512]{1,0:T(8,128)(2,1)}, bf16[256,512]{1,0:T(8,128)(2,1)}) custom-call(s32[1,512]{1,0:T(1,128)} %bitcast.47, bf16[6400,512]{1,0:T(8,128)(2,1)} %refs_7_.1), custom_call_target="tpu_custom_call" | custom-call | flops 4800000000 | bytes 24000000 | tf_op jit(solution)/shard_map/lookup/pallas_call | solution.py:144
  55.2 3.3 collective-permute-done.8.refs_5_
  65.0 2.9 collective-permute-done.10.refs_2_
  72.9 5.0 %project.3 = (bf16[4,128,256]{2,1,0:T(8,128)(2,1)}, bf16[4,128,256]{2,1,0:T(8,128)(2,1)}, bf16[128,512]{1,0:T(8,128)(2,1)}, f32[4,176,128]{2,1,0:T(8,128)}) custom-call(s32[1]{0:T(128)} %copy.35.bound_ref, s32[1]{0:T(128)} %get-tuple-element.167.places_ref, bf16[128,2048]{1,0:T(8,128)(2,1)} %get-tuple-element.94.refs_0_, bf16[2048,640]{1,0:T(8,128)(2,1)} %refs_2_.7, ...), custom_call_target="tpu_custom_call" | custom-call | flops 3000000000 | bytes 15000000 | tf_op jit(solution)/shard_map/project/pallas_call | solution.py:314
  77.9 3.8 %collective-permute-start.12 = (bf16[128,2048]{1,0:T(8,128)(2,1)S(1)}, bf16[128,2048]{1,0:T(8,128)(2,1)S(1)}, u32[]{:S(2)}, u32[]{:S(2)}) collective-permute-start(bf16[128,2048]{1,0:T(8,128)(2,1)S(1)} %copy-done.20), channel_id=1, source_target_pairs={{0,3},{1,0},{2,1},{3,2},{4,7},{5,4},{6,5},{7,6},{8,11},{9,8},{10,9... | collective-permute-start | bytes 1572872 | tf_op jit(solution)/shard_map/ppermute | solution.py:56
  86.4 3.2 collective-permute-done.13.refs_1_
  89.8 10.4 %collective-permute-done.12.refs_0_ = bf16[128,2048]{1,0:T(8,128)(2,1)S(1)} collective-permute-done((bf16[128,2048]{1,0:T(8,128)(2,1)S(1)}, bf16[128,2048]{1,0:T(8,128)(2,1)S(1)}, u32[]{:S(2)}, u32[]{:S(2)}) %collective-permute-start.12) | collective-permute-done | bytes 524320 | tf_op jit(solution)/shard_map/ppermute | solution.py:56
  102.1 5.7 %project.4 = (bf16[4,256,256]{2,1,0:T(8,128)(2,1)}, bf16[4,256,256]{2,1,0:T(8,128)(2,1)}, bf16[256,512]{1,0:T(8,128)(2,1)}, f32[4,176,128]{2,1,0:T(8,128)}) custom-call(s32[1]{0:T(128)} %copy.35.bound_ref, s32[2]{0:T(128)} %slice.88.places_ref, bf16[128,2048]{1,0:T(8,128)(2,1)} %copy-done.9, bf16[128,2048]{1,0:T(8,128)(2,1)} %copy-done.8, ...), custom_call_target="tpu_custom_call" | custom-call | flops 3000000000 | bytes 15000000 | tf_op jit(solution)/shard_map/project/pallas_call | solution.py:314
  109.2 4.2 %collective-permute-done.15.refs_1_ = bf16[64,2048]{1,0:T(8,128)(2,1)S(1)} collective-permute-done((bf16[64,2048]{1,0:T(8,128)(2,1)S(1)}, bf16[64,2048]{1,0:T(8,128)(2,1)S(1)}, u32[]{:S(2)}, u32[]{:S(2)}) %collective-permute-start.15) | collective-permute-done | bytes 262176 | tf_op jit(solution)/shard_map/ppermute | solution.py:56
  114.2 5.1 %project.5 = (bf16[4,128,256]{2,1,0:T(8,128)(2,1)}, bf16[4,128,256]{2,1,0:T(8,128)(2,1)}, bf16[128,512]{1,0:T(8,128)(2,1)}, bf16[4,176,128]{2,1,0:T(8,128)(2,1)}) custom-call(s32[1]{0:T(128)} %copy.35.bound_ref, s32[1]{0:T(128)} %get-tuple-element.166.places_ref, bf16[64,2048]{1,0:T(8,128)(2,1)} %copy-done.31, bf16[64,2048]{1,0:T(8,128)(2,1)} %copy-done.39, ...), custom_call_target="tpu_custom_call" | custom-call | flops 3000000000 | bytes 15000000 | tf_op jit(solution)/shard_map/project/pallas_call | solution.py:314
  121.2 2.7 collective-permute-start.17
  125.4 4.6 %within.1 = (f32[4,512,128]{2,1,0:T(8,128)}, f32[4,512,8]{2,1,0:T(8,128)}) custom-call(s32[1]{0:T(128)} %copy.35.bound_ref, s32[4]{0:T(128)} %copy-done.17, bf16[4,128,256]{2,1,0:T(8,128)(2,1)} %get-tuple-element.93.refs_0_, bf16[4,256,256]{2,1,0:T(8,128)(2,1)} %get-tuple-element.96.refs_1_, bf16[4,128,256]{2,1,0:T(8,128)(2,1)} %get-tuple-element.98.refs_2_, ...), custom_call_target="tpu_custom_call" | custom-call | flops 2700000000 | bytes 13500000 | tf_op jit(solution)/shard_map/within/pallas_call | solution.py:353
  131.2 4.6 %across.1 = (bf16[512,512]{1,0:T(8,128)(2,1)}, bf16[64,2048]{1,0:T(8,128)(2,1)}, bf16[64,2048]{1,0:T(8,128)(2,1)}) custom-call(s32[1]{0:T(128)} %copy.35.bound_ref, s32[4]{0:T(128)} %copy-done.17, s32[3]{0:T(128)} %add_convert_fusion.share_ref, bf16[4,128,256]{2,1,0:T(8,128)(2,1)} %get-tuple-element.93.refs_0_, ...), custom_call_target="tpu_custom_call" | custom-call | flops 2700000000 | bytes 13500000 | tf_op jit(solution)/shard_map/across/pallas_call | solution.py:402
  136.4 3.3 collective-permute-start.20
  139.6 4.3 %slice.103 = bf16[3840,512]{1,0:T(8,128)(2,1)} slice(bf16[6400,512]{1,0:T(8,128)(2,1)} %refs_7_.1), slice={[0:3840], [0:512]} | slice | bytes 7864320 | tf_op jit(solution)/shard_map/slice | solution.py:684
  143.9 3.9 %near.2 = (bf16[64,2048]{1,0:T(8,128)(2,1)}, bf16[64,2048]{1,0:T(8,128)(2,1)}, bf16[64,2048]{1,0:T(8,128)(2,1)}, bf16[64,2048]{1,0:T(8,128)(2,1)}, bf16[64,2048]{1,0:T(8,128)(2,1)}, /*index=5*/bf16[64,2048]{1,0:T(8,128)(2,1)}) custom-call(bf16[512,512]{1,0:T(8,128)(2,1)} %get-tuple-element.108.mixed_ref, bf16[512,2048]{1,0:T(8,128)(2,1)} %weight_ref.3), custom_call_target="tpu_custom_call" | custom-call | flops 2400000000 | bytes 12000000 | tf_op jit(solution)/shard_map/near/pallas_call | solution.py:421
  153.7 3.4 collective-permute-start.24
  157.7 6.4 %collective-permute-done.23.refs_4_ = bf16[64,2048]{1,0:T(8,128)(2,1)S(1)} collective-permute-done((bf16[64,2048]{1,0:T(8,128)(2,1)}, bf16[64,2048]{1,0:T(8,128)(2,1)S(1)}, u32[]{:S(2)}, u32[]{:S(2)}) %collective-permute-start.23) | collective-permute-done | bytes 262176 | tf_op jit(solution)/shard_map/ppermute | solution.py:56
  164.1 5.5 %collective-permute-done.21.refs_1_ = bf16[64,2048]{1,0:T(8,128)(2,1)S(1)} collective-permute-done((bf16[64,2048]{1,0:T(8,128)(2,1)}, bf16[64,2048]{1,0:T(8,128)(2,1)S(1)}, u32[]{:S(2)}, u32[]{:S(2)}) %collective-permute-start.21) | collective-permute-done | bytes 262176 | tf_op jit(solution)/shard_map/ppermute | solution.py:56
  172.4 2.8 finish.2
  176.1 5.6 %matmul.3.refs_0_ = bf16[128,1536]{1,0:T(8,128)(2,1)} custom-call(bf16[128,2048]{1,0:T(8,128)(2,1)} %get-tuple-element.122.refs_0_, bf16[2048,1536]{1,0:T(8,128)(2,1)} %refs_2_.9), custom_call_target="tpu_custom_call" | custom-call | flops 3000000000 | bytes 15000000 | tf_op jit(solution)/shard_map/matmul/pallas_call | solution.py:440
  181.6 2.6 collective-permute-start.25
  184.3 3.4 slice.92
  192.2 11.2 %collective-permute-done.25.refs_0_ = bf16[128,2048]{1,0:T(8,128)(2,1)S(1)} collective-permute-done((bf16[128,2048]{1,0:T(8,128)(2,1)S(1)}, bf16[128,2048]{1,0:T(8,128)(2,1)S(1)}, u32[]{:S(2)}, u32[]{:S(2)}) %collective-permute-start.25) | collective-permute-done | bytes 524320 | tf_op jit(solution)/shard_map/ppermute | solution.py:56
  204.3 6.2 %matmul.4.refs_1_ = bf16[256,1536]{1,0:T(8,128)(2,1)} custom-call(bf16[128,2048]{1,0:T(8,128)(2,1)} %copy-done.11, bf16[128,2048]{1,0:T(8,128)(2,1)} %copy-done.10, bf16[2048,1536]{1,0:T(8,128)(2,1)} %refs_2_.9), custom_call_target="tpu_custom_call" | custom-call | flops 3000000000 | bytes 15000000 | tf_op jit(solution)/shard_map/matmul/pallas_call | solution.py:440
  210.5 2.6 collective-permute-done.28.refs_1_
  213.8 5.2 %matmul.5.refs_2_ = bf16[128,1536]{1,0:T(8,128)(2,1)} custom-call(bf16[64,2048]{1,0:T(8,128)(2,1)} %copy-done.41, bf16[64,2048]{1,0:T(8,128)(2,1)} %copy-done.43, bf16[2048,1536]{1,0:T(8,128)(2,1)} %refs_2_.9), custom_call_target="tpu_custom_call" | custom-call | flops 3000000000 | bytes 15000000 | tf_op jit(solution)/shard_map/matmul/pallas_call | solution.py:440
  221.7 8.0 %local_window.1 = (bf16[512,512]{1,0:T(8,128)(2,1)}, bf16[64,1536]{1,0:T(8,128)(2,1)}) custom-call(s32[1]{0:T(128)} %copy.35.bound_ref, s32[4]{0:T(128)} %copy-done.17, bf16[128,1536]{1,0:T(8,128)(2,1)} %matmul.3.refs_0_, bf16[256,1536]{1,0:T(8,128)(2,1)} %matmul.4.refs_1_, bf16[128,1536]{1,0:T(8,128)(2,1)} %matmul.5.refs_2_), custom_call_target="tpu_custom_call" | custom-call | flops 4800000000 | bytes 24000000 | tf_op jit(solution)/shard_map/local_window/pallas_call | solution.py:505
  229.7 10.4 %collective-permute-start.40 = (bf16[2560,512]{1,0:T(8,128)(2,1)}, bf16[2560,512]{1,0:T(8,128)(2,1)S(1)}, u32[]{:S(2)}, u32[]{:S(2)}) collective-permute-start(bf16[2560,512]{1,0:T(8,128)(2,1)} %slice.92), channel_id=1, source_target_pairs={{0,8},{4,12},{8,0},{12,4},{1,9},{5,13},{9,1},{13,5},{2,10},{6,14},... | collective-permute-start | bytes 7864328 | tf_op jit(solution)/shard_map/ppermute | solution.py:792
  242.7 4.5 %halo_window.1 = (bf16[512,512]{1,0:T(8,128)(2,1)}, bf16[64,2048]{1,0:T(8,128)(2,1)}, bf16[64,2048]{1,0:T(8,128)(2,1)}) custom-call(s32[3]{0:T(128)} %pad_add_fusion.4.info_ref, bf16[512,512]{1,0:T(8,128)(2,1)} %get-tuple-element.124.local_ref, bf16[64,1536]{1,0:T(8,128)(2,1)} %get-tuple-element.125.first_ref, bf16[64,1536]{1,0:T(8,128)(2,1)} %copy-done.44, ...), custom_call_target="tpu_custom_call" | custom-call | flops 2700000000 | bytes 13500000 | tf_op jit(solution)/shard_map/halo_window/pallas_call | solution.py:545
  247.5 3.5 collective-permute-start.31
  251.1 3.8 %near.3 = (bf16[64,2048]{1,0:T(8,128)(2,1)}, bf16[64,2048]{1,0:T(8,128)(2,1)}, bf16[64,2048]{1,0:T(8,128)(2,1)}, bf16[64,2048]{1,0:T(8,128)(2,1)}, bf16[64,2048]{1,0:T(8,128)(2,1)}, /*index=5*/bf16[64,2048]{1,0:T(8,128)(2,1)}) custom-call(bf16[512,512]{1,0:T(8,128)(2,1)} %get-tuple-element.127.mixed_ref, bf16[512,2048]{1,0:T(8,128)(2,1)} %weight_ref.5), custom_call_target="tpu_custom_call" | custom-call | flops 2400000000 | bytes 12000000 | tf_op jit(solution)/shard_map/near/pallas_call | solution.py:421
  254.9 3.6 collective-permute-done.30.before_ref
  258.5 3.6 collective-permute-start.33
  267.8 7.6 %collective-permute-done.34.refs_4_ = bf16[64,2048]{1,0:T(8,128)(2,1)S(1)} collective-permute-done((bf16[64,2048]{1,0:T(8,128)(2,1)}, bf16[64,2048]{1,0:T(8,128)(2,1)S(1)}, u32[]{:S(2)}, u32[]{:S(2)}) %collective-permute-start.34) | collective-permute-done | bytes 262176 | tf_op jit(solution)/shard_map/ppermute | solution.py:56
  276.2 4.4 %collective-permute-done.32.refs_1_ = bf16[64,2048]{1,0:T(8,128)(2,1)S(1)} collective-permute-done((bf16[64,2048]{1,0:T(8,128)(2,1)}, bf16[64,2048]{1,0:T(8,128)(2,1)S(1)}, u32[]{:S(2)}, u32[]{:S(2)}) %collective-permute-start.32) | collective-permute-done | bytes 262176 | tf_op jit(solution)/shard_map/ppermute | solution.py:56
  280.6 2.8 collective-permute-done.35.refs_5_
  284.0 2.8 finish.3.refs_0_
  286.8 3.8 %collective-permute-start.41 = (bf16[128,2048]{1,0:T(8,128)(2,1)}, bf16[128,2048]{1,0:T(8,128)(2,1)S(1)}, u32[]{:S(2)}, u32[]{:S(2)}) collective-permute-start(bf16[128,2048]{1,0:T(8,128)(2,1)} %finish.3.refs_0_), channel_id=1, source_target_pairs={{0,3},{1,0},{2,1},{3,2},{4,7},{5,4},{6,5},{7,6},{8,11},{9,8},{10,9... | collective-permute-start | bytes 1572872 | tf_op jit(solution)/shard_map/ppermute | solution.py:56
  290.7 13.0 %collective-permute-done.36.refs_1_ = bf16[128,2048]{1,0:T(8,128)(2,1)S(1)} collective-permute-done((bf16[128,2048]{1,0:T(8,128)(2,1)}, bf16[128,2048]{1,0:T(8,128)(2,1)S(1)}, u32[]{:S(2)}, u32[]{:S(2)}) %collective-permute-start.36) | collective-permute-done | bytes 524320 | tf_op jit(solution)/shard_map/ppermute | solution.py:56
  303.7 6.0 %collective-permute-done.41.refs_0_ = bf16[128,2048]{1,0:T(8,128)(2,1)S(1)} collective-permute-done((bf16[128,2048]{1,0:T(8,128)(2,1)}, bf16[128,2048]{1,0:T(8,128)(2,1)S(1)}, u32[]{:S(2)}, u32[]{:S(2)}) %collective-permute-start.41) | collective-permute-done | bytes 524320 | tf_op jit(solution)/shard_map/ppermute | solution.py:56
  312.8 3.8 %collective-permute-start.44 = (bf16[64,2048]{1,0:T(8,128)(2,1)}, bf16[64,2048]{1,0:T(8,128)(2,1)S(1)}, u32[]{:S(2)}, u32[]{:S(2)}) collective-permute-start(bf16[64,2048]{1,0:T(8,128)(2,1)} %slice.123), channel_id=1, source_target_pairs={{0,3},{1,0},{2,1},{3,2},{4,7},{5,4},{6,5},{7,6},{8,11},{9,8},{10,9... | collective-permute-start | bytes 786440 | tf_op jit(solution)/shard_map/ppermute | solution.py:56
  320.0 16.0 %scores.2 = f32[8,256]{1,0:T(8,128)} custom-call(s32[4]{0:T(128)} %iota_xor_fusion.order_ref, bf16[128,2048]{1,0:T(8,128)(2,1)} %finish.3.refs_0_, bf16[128,2048]{1,0:T(8,128)(2,1)} %copy-done.4, bf16[6400,512]{1,0:T(8,128)(2,1)} %refs_7_.1, bf16[6400,512]{1,0:T(8,128)(2,1)} %collective-permute-done.37.refs_3_.refs_7_.refs_4_.refs_8_, ...), custom_call_target="tpu_custom_call" | custom-call | flops 8400000000 | bytes 42000000 | tf_op jit(solution)/shard_map/scores/pallas_call | solution.py:623
  337.9 16.0 %scores.3 = f32[8,256]{1,0:T(8,128)} custom-call(s32[4]{0:T(128)} %iota_xor_fusion.order_ref, bf16[128,2048]{1,0:T(8,128)(2,1)} %copy-done.3, bf16[64,2048]{1,0:T(8,128)(2,1)} %copy-done.5, bf16[64,2048]{1,0:T(8,128)(2,1)} %copy-done.6, bf16[6400,512]{1,0:T(8,128)(2,1)} %refs_7_.1, bf16[6400,512]{1,0:T(8,128)(2,1)} %collective-permute-done.37.refs_3_.refs_7_.refs_4_.refs_8_, ...), custom_call_target="tpu_custom_call" | custom-call | flops 8400000000 | bytes 42000000 | tf_op jit(solution)/shard_map/scores/pallas_call | solution.py:623
  (217 shorter events, 81.7 us)
Async XLA Ops:
  1.3 4.4 %collective-permute-start.2 = (s32[640]{0:T(1024)S(1)}, s32[640]{0:T(1024)S(1)}, u32[]{:S(2)}, u32[]{:S(2)}) collective-permute-start(s32[640]{0:T(1024)S(1)} %concatenate.12), channel_id=1, source_target_pairs={{0,12},{4,8},{8,4},{12,0},{1,13},{5,9},{9,5},{13,1},{2,14},{6,10},... | collective-permute-start | bytes 7688 | tf_op jit(solution)/shard_map/ppermute | solution.py:675
  3.7 3.6 collective-permute-start.1
  4.3 3.0 collective-permute-start
  16.6 19.6 %collective-permute-start.3 = (bf16[256,512]{1,0:T(8,128)(2,1)}, bf16[256,512]{1,0:T(8,128)(2,1)S(1)}, u32[]{:S(2)}, u32[]{:S(2)}) collective-permute-start(bf16[256,512]{1,0:T(8,128)(2,1)} %get-tuple-element.75), channel_id=1, source_target_pairs={{0,1},{1,2},{2,3},{3,0},{4,5},{5,6},{6,7},{7,4},{8,9},{9,10},{10,1... | collective-permute-start | bytes 786440 | tf_op jit(solution)/shard_map/ppermute | solution.py:56
  18.1 18.1 %collective-permute-start.4 = (bf16[256,512]{1,0:T(8,128)(2,1)}, bf16[256,512]{1,0:T(8,128)(2,1)S(1)}, u32[]{:S(2)}, u32[]{:S(2)}) collective-permute-start(bf16[256,512]{1,0:T(8,128)(2,1)} %get-tuple-element.77), channel_id=1, source_target_pairs={{0,3},{1,0},{2,1},{3,2},{4,7},{5,4},{6,5},{7,6},{8,11},{9,8},{10,9... | collective-permute-start | bytes 786440 | tf_op jit(solution)/shard_map/ppermute | solution.py:56
  34.2 19.4 %collective-permute-start.6 = (bf16[256,512]{1,0:T(8,128)(2,1)}, bf16[256,512]{1,0:T(8,128)(2,1)S(1)}, u32[]{:S(2)}, u32[]{:S(2)}) collective-permute-start(bf16[256,512]{1,0:T(8,128)(2,1)} %get-tuple-element.79), channel_id=1, source_target_pairs={{0,3},{1,0},{2,1},{3,2},{4,7},{5,4},{6,5},{7,6},{8,11},{9,8},{10,9... | collective-permute-start | bytes 786440 | tf_op jit(solution)/shard_map/ppermute | solution.py:56
  36.0 17.6 %collective-permute-start.7 = (bf16[256,512]{1,0:T(8,128)(2,1)}, bf16[256,512]{1,0:T(8,128)(2,1)S(1)}, u32[]{:S(2)}, u32[]{:S(2)}) collective-permute-start(bf16[256,512]{1,0:T(8,128)(2,1)} %get-tuple-element.81), channel_id=1, source_target_pairs={{0,1},{1,2},{2,3},{3,0},{4,5},{5,6},{6,7},{7,4},{8,9},{9,10},{10,1... | collective-permute-start | bytes 786440 | tf_op jit(solution)/shard_map/ppermute | solution.py:56
  39.1 16.1 %collective-permute-start.5 = (bf16[256,512]{1,0:T(8,128)(2,1)}, bf16[256,512]{1,0:T(8,128)(2,1)S(1)}, u32[]{:S(2)}, u32[]{:S(2)}) collective-permute-start(bf16[256,512]{1,0:T(8,128)(2,1)} %get-tuple-element.78), channel_id=1, source_target_pairs={{0,1},{1,2},{2,3},{3,0},{4,5},{5,6},{6,7},{7,4},{8,9},{9,10},{10,1... | collective-permute-start | bytes 786440 | tf_op jit(solution)/shard_map/ppermute | solution.py:56
  39.1 19.4 %collective-permute-start.8 = (bf16[256,512]{1,0:T(8,128)(2,1)}, bf16[256,512]{1,0:T(8,128)(2,1)S(1)}, u32[]{:S(2)}, u32[]{:S(2)}) collective-permute-start(bf16[256,512]{1,0:T(8,128)(2,1)} %get-tuple-element.82), channel_id=1, source_target_pairs={{0,3},{1,0},{2,1},{3,2},{4,7},{5,4},{6,5},{7,6},{8,11},{9,8},{10,9... | collective-permute-start | bytes 786440 | tf_op jit(solution)/shard_map/ppermute | solution.py:56
  61.4 3.6 collective-permute-start.9
  61.4 6.5 %collective-permute-start.10 = (bf16[128,512]{1,0:T(8,128)(2,1)}, bf16[128,512]{1,0:T(8,128)(2,1)S(1)}, u32[]{:S(2)}, u32[]{:S(2)}) collective-permute-start(bf16[128,512]{1,0:T(8,128)(2,1)} %get-tuple-element.85), channel_id=1, source_target_pairs={{0,8},{4,12},{8,0},{12,4},{1,9},{5,13},{9,1},{13,5},{2,10},{6,14},... | collective-permute-start | bytes 393224 | tf_op jit(solution)/shard_map/ppermute | solution.py:702
  62.2 7.7 %collective-permute-start.11 = (bf16[128,512]{1,0:T(8,128)(2,1)}, bf16[128,512]{1,0:T(8,128)(2,1)S(1)}, u32[]{:S(2)}, u32[]{:S(2)}) collective-permute-start(bf16[128,512]{1,0:T(8,128)(2,1)} %get-tuple-element.86), channel_id=1, source_target_pairs={{0,12},{4,8},{8,4},{12,0},{1,13},{5,9},{9,5},{13,1},{2,14},{6,10},... | collective-permute-start | bytes 393224 | tf_op jit(solution)/shard_map/ppermute | solution.py:702
  72.8 16.9 %collective-permute-start.13 = (bf16[128,2048]{1,0:T(8,128)(2,1)}, bf16[128,2048]{1,0:T(8,128)(2,1)S(1)}, u32[]{:S(2)}, u32[]{:S(2)}) collective-permute-start(bf16[128,2048]{1,0:T(8,128)(2,1)} %get-tuple-element.94.refs_0_), channel_id=1, source_target_pairs={{0,1},{1,2},{2,3},{3,0},{4,5},{5,6},{6,7},{7,4},{8,9},{9,10},{10,1... | collective-permute-start | bytes 1572872 | tf_op jit(solution)/shard_map/ppermute | solution.py:56
  77.9 22.3 %collective-permute-start.12 = (bf16[128,2048]{1,0:T(8,128)(2,1)S(1)}, bf16[128,2048]{1,0:T(8,128)(2,1)S(1)}, u32[]{:S(2)}, u32[]{:S(2)}) collective-permute-start(bf16[128,2048]{1,0:T(8,128)(2,1)S(1)} %copy-done.20), channel_id=1, source_target_pairs={{0,3},{1,0},{2,1},{3,2},{4,7},{5,4},{6,5},{7,6},{8,11},{9,8},{10,9... | collective-permute-start | bytes 1572872 | tf_op jit(solution)/shard_map/ppermute | solution.py:56
  89.7 19.5 %collective-permute-start.14 = (bf16[64,2048]{1,0:T(8,128)(2,1)S(1)}, bf16[64,2048]{1,0:T(8,128)(2,1)S(1)}, u32[]{:S(2)}, u32[]{:S(2)}) collective-permute-start(bf16[64,2048]{1,0:T(8,128)(2,1)S(1)} %slice.114), channel_id=1, source_target_pairs={{0,1},{1,2},{2,3},{3,0},{4,5},{5,6},{6,7},{7,4},{8,9},{9,10},{10,1... | collective-permute-start | bytes 786440 | tf_op jit(solution)/shard_map/ppermute | solution.py:56
  100.2 13.3 %collective-permute-start.15 = (bf16[64,2048]{1,0:T(8,128)(2,1)S(1)}, bf16[64,2048]{1,0:T(8,128)(2,1)S(1)}, u32[]{:S(2)}, u32[]{:S(2)}) collective-permute-start(bf16[64,2048]{1,0:T(8,128)(2,1)S(1)} %slice.115), channel_id=1, source_target_pairs={{0,3},{1,0},{2,1},{3,2},{4,7},{5,4},{6,5},{7,6},{8,11},{9,8},{10,9... | collective-permute-start | bytes 786440 | tf_op jit(solution)/shard_map/ppermute | solution.py:56
  119.3 10.7 %collective-permute-start.16 = (bf16[4,176,128]{2,1,0:T(8,128)(2,1)}, bf16[4,176,128]{2,1,0:T(8,128)(2,1)S(1)}, u32[]{:S(2)}, u32[]{:S(2)}) collective-permute-start(bf16[4,176,128]{2,1,0:T(8,128)(2,1)} %get-tuple-element.107), channel_id=1, source_target_pairs={{0,4},{4,8},{8,12},{1,5},{5,9},{9,13},{2,6},{6,10},{10,14},{3,7},{... | collective-permute-start | bytes 540680 | tf_op jit(solution)/shard_map/ppermute | solution.py:735
  121.2 8.8 %collective-permute-start.17 = (bf16[4,176,128]{2,1,0:T(8,128)(2,1)}, bf16[4,176,128]{2,1,0:T(8,128)(2,1)S(1)}, u32[]{:S(2)}, u32[]{:S(2)}) collective-permute-start(bf16[4,176,128]{2,1,0:T(8,128)(2,1)} %get-tuple-element.107), channel_id=1, source_target_pairs={{0,8},{4,12},{1,9},{5,13},{2,10},{6,14},{3,11},{7,15},{16,24},{20,... | collective-permute-start | bytes 540680 | tf_op jit(solution)/shard_map/ppermute | solution.py:735
  123.9 6.6 %collective-permute-start.18 = (bf16[4,176,128]{2,1,0:T(8,128)(2,1)}, bf16[4,176,128]{2,1,0:T(8,128)(2,1)S(1)}, u32[]{:S(2)}, u32[]{:S(2)}) collective-permute-start(bf16[4,176,128]{2,1,0:T(8,128)(2,1)} %get-tuple-element.107), channel_id=1, source_target_pairs={{0,12},{1,13},{2,14},{3,15},{16,28},{17,29},{18,30},{19,31}} | collective-permute-start | bytes 540680 | tf_op jit(solution)/shard_map/ppermute | solution.py:735
  135.8 14.5 %collective-permute-start.19 = (bf16[64,2048]{1,0:T(8,128)(2,1)}, bf16[64,2048]{1,0:T(8,128)(2,1)S(1)}, u32[]{:S(2)}, u32[]{:S(2)}) collective-permute-start(bf16[64,2048]{1,0:T(8,128)(2,1)} %get-tuple-element.111), channel_id=1, source_target_pairs={{0,1},{1,2},{2,3},{3,0},{4,5},{5,6},{6,7},{7,4},{8,9},{9,10},{10,1... | collective-permute-start | bytes 786440 | tf_op jit(solution)/shard_map/ppermute | solution.py:56
  136.4 14.0 %collective-permute-start.20 = (bf16[64,2048]{1,0:T(8,128)(2,1)}, bf16[64,2048]{1,0:T(8,128)(2,1)S(1)}, u32[]{:S(2)}, u32[]{:S(2)}) collective-permute-start(bf16[64,2048]{1,0:T(8,128)(2,1)} %get-tuple-element.113), channel_id=1, source_target_pairs={{0,3},{1,0},{2,1},{3,2},{4,7},{5,4},{6,5},{7,6},{8,11},{9,8},{10,9... | collective-permute-start | bytes 786440 | tf_op jit(solution)/shard_map/ppermute | solution.py:56
  147.8 9.9 %collective-permute-start.22 = (bf16[64,2048]{1,0:T(8,128)(2,1)}, bf16[64,2048]{1,0:T(8,128)(2,1)S(1)}, u32[]{:S(2)}, u32[]{:S(2)}) collective-permute-start(bf16[64,2048]{1,0:T(8,128)(2,1)} %get-tuple-element.115), channel_id=1, source_target_pairs={{0,3},{1,0},{2,1},{3,2},{4,7},{5,4},{6,5},{7,6},{8,11},{9,8},{10,9... | collective-permute-start | bytes 786440 | tf_op jit(solution)/shard_map/ppermute | solution.py:56
  147.8 16.3 %collective-permute-start.23 = (bf16[64,2048]{1,0:T(8,128)(2,1)}, bf16[64,2048]{1,0:T(8,128)(2,1)S(1)}, u32[]{:S(2)}, u32[]{:S(2)}) collective-permute-start(bf16[64,2048]{1,0:T(8,128)(2,1)} %get-tuple-element.117), channel_id=1, source_target_pairs={{0,1},{1,2},{2,3},{3,0},{4,5},{5,6},{6,7},{7,4},{8,9},{9,10},{10,1... | collective-permute-start | bytes 786440 | tf_op jit(solution)/shard_map/ppermute | solution.py:56
  149.8 101.2 %collective-permute-start.38 = (bf16[3840,512]{1,0:T(8,128)(2,1)}, bf16[3840,512]{1,0:T(8,128)(2,1)}, u32[]{:S(2)}, u32[]{:S(2)}) collective-permute-start(bf16[3840,512]{1,0:T(8,128)(2,1)} %slice.103), channel_id=1, source_target_pairs={{0,8},{4,12},{8,0},{12,4},{1,9},{5,13},{9,1},{13,5},{2,10},{6,14},... | collective-permute-start | bytes 11796488 | tf_op jit(solution)/shard_map/ppermute | solution.py:763
  153.2 16.3 %collective-permute-start.21 = (bf16[64,2048]{1,0:T(8,128)(2,1)}, bf16[64,2048]{1,0:T(8,128)(2,1)S(1)}, u32[]{:S(2)}, u32[]{:S(2)}) collective-permute-start(bf16[64,2048]{1,0:T(8,128)(2,1)} %get-tuple-element.114), channel_id=1, source_target_pairs={{0,1},{1,2},{2,3},{3,0},{4,5},{5,6},{6,7},{7,4},{8,9},{9,10},{10,1... | collective-permute-start | bytes 786440 | tf_op jit(solution)/shard_map/ppermute | solution.py:56
  153.7 18.0 %collective-permute-start.24 = (bf16[64,2048]{1,0:T(8,128)(2,1)}, bf16[64,2048]{1,0:T(8,128)(2,1)S(1)}, u32[]{:S(2)}, u32[]{:S(2)}) collective-permute-start(bf16[64,2048]{1,0:T(8,128)(2,1)} %get-tuple-element.118), channel_id=1, source_target_pairs={{0,3},{1,0},{2,1},{3,2},{4,7},{5,4},{6,5},{7,6},{8,11},{9,8},{10,9... | collective-permute-start | bytes 786440 | tf_op jit(solution)/shard_map/ppermute | solution.py:56
  175.2 16.9 %collective-permute-start.26 = (bf16[128,2048]{1,0:T(8,128)(2,1)}, bf16[128,2048]{1,0:T(8,128)(2,1)S(1)}, u32[]{:S(2)}, u32[]{:S(2)}) collective-permute-start(bf16[128,2048]{1,0:T(8,128)(2,1)} %get-tuple-element.122.refs_0_), channel_id=1, source_target_pairs={{0,1},{1,2},{2,3},{3,0},{4,5},{5,6},{6,7},{7,4},{8,9},{9,10},{10,1... | collective-permute-start | bytes 1572872 | tf_op jit(solution)/shard_map/ppermute | solution.py:56
  181.6 21.7 %collective-permute-start.25 = (bf16[128,2048]{1,0:T(8,128)(2,1)S(1)}, bf16[128,2048]{1,0:T(8,128)(2,1)S(1)}, u32[]{:S(2)}, u32[]{:S(2)}) collective-permute-start(bf16[128,2048]{1,0:T(8,128)(2,1)S(1)} %copy-done.21), channel_id=1, source_target_pairs={{0,3},{1,0},{2,1},{3,2},{4,7},{5,4},{6,5},{7,6},{8,11},{9,8},{10,9... | collective-permute-start | bytes 1572872 | tf_op jit(solution)/shard_map/ppermute | solution.py:56
  184.2 132.4 %collective-permute-start.37 = (bf16[6400,512]{1,0:T(8,128)(2,1)}, bf16[6400,512]{1,0:T(8,128)(2,1)}, u32[]{:S(2)}, u32[]{:S(2)}) collective-permute-start(bf16[6400,512]{1,0:T(8,128)(2,1)} %refs_7_.1), channel_id=1, source_target_pairs={{0,4},{4,0},{8,12},{12,8},{1,5},{5,1},{9,13},{13,9},{2,6},{6,2},{1... | collective-permute-start | bytes 19660808 | tf_op jit(solution)/shard_map/ppermute | solution.py:765
  192.1 18.3 %collective-permute-start.27 = (bf16[64,2048]{1,0:T(8,128)(2,1)S(1)}, bf16[64,2048]{1,0:T(8,128)(2,1)S(1)}, u32[]{:S(2)}, u32[]{:S(2)}) collective-permute-start(bf16[64,2048]{1,0:T(8,128)(2,1)S(1)} %slice.116), channel_id=1, source_target_pairs={{0,1},{1,2},{2,3},{3,0},{4,5},{5,6},{6,7},{7,4},{8,9},{9,10},{10,1... | collective-permute-start | bytes 786440 | tf_op jit(solution)/shard_map/ppermute | solution.py:56
  203.4 9.7 %collective-permute-start.28 = (bf16[64,2048]{1,0:T(8,128)(2,1)S(1)}, bf16[64,2048]{1,0:T(8,128)(2,1)S(1)}, u32[]{:S(2)}, u32[]{:S(2)}) collective-permute-start(bf16[64,2048]{1,0:T(8,128)(2,1)S(1)} %slice.117), channel_id=1, source_target_pairs={{0,3},{1,0},{2,1},{3,2},{4,7},{5,4},{6,5},{7,6},{8,11},{9,8},{10,9... | collective-permute-start | bytes 786440 | tf_op jit(solution)/shard_map/ppermute | solution.py:56
  220.0 9.6 %collective-permute-start.29 = (bf16[64,1536]{1,0:T(8,128)(2,1)S(1)}, bf16[64,1536]{1,0:T(8,128)(2,1)S(1)}, u32[]{:S(2)}, u32[]{:S(2)}) collective-permute-start(bf16[64,1536]{1,0:T(8,128)(2,1)S(1)} %fusion.1), channel_id=1, source_target_pairs={{0,4},{4,8},{8,12},{1,5},{5,9},{9,13},{2,6},{6,10},{10,14},{3,7},{... | collective-permute-start | bytes 589832 | tf_op jit(solution)/shard_map/ppermute | solution.py:777
  229.7 80.1 %collective-permute-start.40 = (bf16[2560,512]{1,0:T(8,128)(2,1)}, bf16[2560,512]{1,0:T(8,128)(2,1)S(1)}, u32[]{:S(2)}, u32[]{:S(2)}) collective-permute-start(bf16[2560,512]{1,0:T(8,128)(2,1)} %slice.92), channel_id=1, source_target_pairs={{0,8},{4,12},{8,0},{12,4},{1,9},{5,13},{9,1},{13,5},{2,10},{6,14},... | collective-permute-start | bytes 7864328 | tf_op jit(solution)/shard_map/ppermute | solution.py:792
  247.2 11.3 %collective-permute-start.30 = (bf16[64,2048]{1,0:T(8,128)(2,1)}, bf16[64,2048]{1,0:T(8,128)(2,1)S(1)}, u32[]{:S(2)}, u32[]{:S(2)}) collective-permute-start(bf16[64,2048]{1,0:T(8,128)(2,1)} %get-tuple-element.130), channel_id=1, source_target_pairs={{0,1},{1,2},{2,3},{3,0},{4,5},{5,6},{6,7},{7,4},{8,9},{9,10},{10,1... | collective-permute-start | bytes 786440 | tf_op jit(solution)/shard_map/ppermute | solution.py:56
  247.5 14.6 %collective-permute-start.31 = (bf16[64,2048]{1,0:T(8,128)(2,1)}, bf16[64,2048]{1,0:T(8,128)(2,1)S(1)}, u32[]{:S(2)}, u32[]{:S(2)}) collective-permute-start(bf16[64,2048]{1,0:T(8,128)(2,1)} %get-tuple-element.132), channel_id=1, source_target_pairs={{0,3},{1,0},{2,1},{3,2},{4,7},{5,4},{6,5},{7,6},{8,11},{9,8},{10,9... | collective-permute-start | bytes 786440 | tf_op jit(solution)/shard_map/ppermute | solution.py:56
  251.1 65.6 %collective-permute-start.39 = (bf16[3840,512]{1,0:T(8,128)(2,1)}, bf16[3840,512]{1,0:T(8,128)(2,1)S(1)}, u32[]{:S(2)}, u32[]{:S(2)}) collective-permute-start(bf16[3840,512]{1,0:T(8,128)(2,1)} %collective-permute-done.38.refs_4_.refs_5_), channel_id=1, source_target_pairs={{0,4},{4,0},{8,12},{12,8},{1,5},{5,1},{9,13},{13,9},{2,6},{6,2},{1... | collective-permute-start | bytes 11796488 | tf_op jit(solution)/shard_map/ppermute | solution.py:764
  258.5 8.6 %collective-permute-start.33 = (bf16[64,2048]{1,0:T(8,128)(2,1)}, bf16[64,2048]{1,0:T(8,128)(2,1)S(1)}, u32[]{:S(2)}, u32[]{:S(2)}) collective-permute-start(bf16[64,2048]{1,0:T(8,128)(2,1)} %get-tuple-element.134), channel_id=1, source_target_pairs={{0,3},{1,0},{2,1},{3,2},{4,7},{5,4},{6,5},{7,6},{8,11},{9,8},{10,9... | collective-permute-start | bytes 786440 | tf_op jit(solution)/shard_map/ppermute | solution.py:56
  262.1 13.3 %collective-permute-start.34 = (bf16[64,2048]{1,0:T(8,128)(2,1)}, bf16[64,2048]{1,0:T(8,128)(2,1)S(1)}, u32[]{:S(2)}, u32[]{:S(2)}) collective-permute-start(bf16[64,2048]{1,0:T(8,128)(2,1)} %get-tuple-element.136), channel_id=1, source_target_pairs={{0,1},{1,2},{2,3},{3,0},{4,5},{5,6},{6,7},{7,4},{8,9},{9,10},{10,1... | collective-permute-start | bytes 786440 | tf_op jit(solution)/shard_map/ppermute | solution.py:56
  267.1 13.5 %collective-permute-start.32 = (bf16[64,2048]{1,0:T(8,128)(2,1)}, bf16[64,2048]{1,0:T(8,128)(2,1)S(1)}, u32[]{:S(2)}, u32[]{:S(2)}) collective-permute-start(bf16[64,2048]{1,0:T(8,128)(2,1)} %get-tuple-element.133), channel_id=1, source_target_pairs={{0,1},{1,2},{2,3},{3,0},{4,5},{5,6},{6,7},{7,4},{8,9},{9,10},{10,1... | collective-permute-start | bytes 786440 | tf_op jit(solution)/shard_map/ppermute | solution.py:56
  275.4 7.9 %collective-permute-start.35 = (bf16[64,2048]{1,0:T(8,128)(2,1)}, bf16[64,2048]{1,0:T(8,128)(2,1)S(1)}, u32[]{:S(2)}, u32[]{:S(2)}) collective-permute-start(bf16[64,2048]{1,0:T(8,128)(2,1)} %get-tuple-element.137), channel_id=1, source_target_pairs={{0,3},{1,0},{2,1},{3,2},{4,7},{5,4},{6,5},{7,6},{8,11},{9,8},{10,9... | collective-permute-start | bytes 786440 | tf_op jit(solution)/shard_map/ppermute | solution.py:56
  286.8 16.9 %collective-permute-start.36 = (bf16[128,2048]{1,0:T(8,128)(2,1)}, bf16[128,2048]{1,0:T(8,128)(2,1)S(1)}, u32[]{:S(2)}, u32[]{:S(2)}) collective-permute-start(bf16[128,2048]{1,0:T(8,128)(2,1)} %finish.3.refs_0_), channel_id=1, source_target_pairs={{0,1},{1,2},{2,3},{3,0},{4,5},{5,6},{6,7},{7,4},{8,9},{9,10},{10,1... | collective-permute-start | bytes 1572872 | tf_op jit(solution)/shard_map/ppermute | solution.py:56
  286.8 22.9 %collective-permute-start.41 = (bf16[128,2048]{1,0:T(8,128)(2,1)}, bf16[128,2048]{1,0:T(8,128)(2,1)S(1)}, u32[]{:S(2)}, u32[]{:S(2)}) collective-permute-start(bf16[128,2048]{1,0:T(8,128)(2,1)} %finish.3.refs_0_), channel_id=1, source_target_pairs={{0,3},{1,0},{2,1},{3,2},{4,7},{5,4},{6,5},{7,6},{8,11},{9,8},{10,9... | collective-permute-start | bytes 1572872 | tf_op jit(solution)/shard_map/ppermute | solution.py:56
  309.8 6.9 %collective-permute-start.42 = (bf16[2560,512]{1,0:T(8,128)(2,1)S(1)}, bf16[2560,512]{1,0:T(8,128)(2,1)S(1)}, u32[]{:S(2)}, u32[]{:S(2)}) collective-permute-start(bf16[2560,512]{1,0:T(8,128)(2,1)S(1)} %collective-permute-done.40.refs_8_.refs_9_), channel_id=1, source_target_pairs={{0,4},{4,0},{8,12},{12,8},{1,5},{5,1},{9,13},{13,9},{2,6},{6,2},{1... | collective-permute-start | bytes 7864328 | tf_op jit(solution)/shard_map/ppermute | solution.py:794
  312.0 25.0 %collective-permute-start.43 = (bf16[64,2048]{1,0:T(8,128)(2,1)}, bf16[64,2048]{1,0:T(8,128)(2,1)S(1)}, u32[]{:S(2)}, u32[]{:S(2)}) collective-permute-start(bf16[64,2048]{1,0:T(8,128)(2,1)} %slice.122), channel_id=1, source_target_pairs={{0,1},{1,2},{2,3},{3,0},{4,5},{5,6},{6,7},{7,4},{8,9},{9,10},{10,1... | collective-permute-start | bytes 786440 | tf_op jit(solution)/shard_map/ppermute | solution.py:56
  312.8 24.3 %collective-permute-start.44 = (bf16[64,2048]{1,0:T(8,128)(2,1)}, bf16[64,2048]{1,0:T(8,128)(2,1)S(1)}, u32[]{:S(2)}, u32[]{:S(2)}) collective-permute-start(bf16[64,2048]{1,0:T(8,128)(2,1)} %slice.123), channel_id=1, source_target_pairs={{0,3},{1,0},{2,1},{3,2},{4,7},{5,4},{6,5},{7,6},{8,11},{9,8},{10,9... | collective-permute-start | bytes 786440 | tf_op jit(solution)/shard_map/ppermute | solution.py:56
  336.8 20.1 %collective-permute-start.47 = (f32[3,128]{1,0:T(4,128)S(1)}, f32[3,128]{1,0:T(4,128)S(1)}, u32[]{:S(2)}, u32[]{:S(2)}) collective-permute-start(f32[3,128]{1,0:T(4,128)S(1)} %get-tuple-element.151), channel_id=1, source_target_pairs={{0,3},{1,0},{2,1},{3,2},{4,7},{5,4},{6,5},{7,6},{8,11},{9,8},{10,9... | collective-permute-start | bytes 4616 | tf_op jit(solution)/shard_map/ppermute | solution.py:56
  354.5 4.5 %collective-permute-start.46 = (f32[3,128]{1,0:T(4,128)S(1)}, f32[3,128]{1,0:T(4,128)S(1)}, u32[]{:S(2)}, u32[]{:S(2)}) collective-permute-start(f32[3,128]{1,0:T(4,128)S(1)} %get-tuple-element.153), channel_id=1, source_target_pairs={{0,2},{1,3},{2,0},{3,1},{4,6},{5,7},{6,4},{7,5},{8,10},{9,11},{10,... | collective-permute-start | bytes 4616 | tf_op jit(solution)/shard_map/ppermute | solution.py:56
  354.9 5.4 %collective-permute-start.45 = (f32[3,128]{1,0:T(4,128)S(1)}, f32[3,128]{1,0:T(4,128)S(1)}, u32[]{:S(2)}, u32[]{:S(2)}) collective-permute-start(f32[3,128]{1,0:T(4,128)S(1)} %get-tuple-element.152), channel_id=1, source_target_pairs={{0,1},{1,2},{2,3},{3,0},{4,5},{5,6},{6,7},{7,4},{8,9},{9,10},{10,1... | collective-permute-start | bytes 4616 | tf_op jit(solution)/shard_map/ppermute | solution.py:56
  (51 other events, 406.8 us)

commit v6 on v4

--- a/solution.py
+++ b/solution.py
@@ -105,7 +105,7 @@
 
 def chunk_order(size):
     if size == 4:
-        return [[0], [1, 3], [2]]
+        return [[0, 1, 3], [2]]
     return [[k] for k in range(size)]
 
 
@@ -448,13 +448,23 @@
     )(*pieces, b)
 
 
-def attend(query, keys, values, allowed):
-    scores = dot(query, keys, ((1,), (1,))) * HEAD_DIM ** (-0.5)
+def attend(queries, keys, values, allowed):
+    rows = queries[0].shape[0]
+    scores = jnp.concatenate(
+        [dot(q, k, ((1,), (1,))) for q, k in zip(queries, keys)], axis=0
+    ) * HEAD_DIM ** (-0.5)
+    allowed = jnp.concatenate([allowed.astype(F32)] * len(queries), axis=0) > 0
     scores = jnp.where(allowed, scores, NEGATIVE)
     peak = jnp.max(scores, axis=-1, keepdims=True)
     weights = jnp.where(allowed, jnp.exp(scores - peak), 0.0)
-    probabilities = (weights / jnp.sum(weights, axis=-1, keepdims=True)).astype(BF16)
-    return dot(probabilities, values).astype(BF16)
+    probabilities = (weights * (1.0 / jnp.sum(weights, axis=-1, keepdims=True))).astype(BF16)
+    return jnp.concatenate(
+        [
+            dot(probabilities[n * rows : (n + 1) * rows], value).astype(BF16)
+            for n, value in enumerate(values)
+        ],
+        axis=1,
+    )
 
 
 def local_kernel(heads, slots, spots, chunk, sets, bound_ref, places_ref, *refs):
@@ -480,21 +490,14 @@
         def _():
             first_ref[...] = qkvs[mine][at : at + WINDOW]
 
+        queries, keys, values = [], [], []
         for head in range(heads):
             lane = head * 3 * HEAD_DIM
-            keys, values = [
-                jnp.concatenate(
-                    [
-                        qkvs[theirs][tail, lane + n * HEAD_DIM : lane + (n + 1) * HEAD_DIM],
-                        qkvs[mine][rows, lane + n * HEAD_DIM : lane + (n + 1) * HEAD_DIM],
-                    ],
-                    axis=0,
-                )
-                for n in (1, 2)
-            ]
-            result_ref[slot * chunk : (slot + 1) * chunk, head * HEAD_DIM : (head + 1) * HEAD_DIM] = attend(
-                qkvs[mine][rows, lane : lane + HEAD_DIM], keys, values, allowed
-            )
+            queries.append(qkvs[mine][rows, lane : lane + HEAD_DIM])
+            for n, held in ((1, keys), (2, values)):
+                lanes = slice(lane + n * HEAD_DIM, lane + (n + 1) * HEAD_DIM)
+                held.append(jnp.concatenate([qkvs[theirs][tail, lanes], qkvs[mine][rows, lanes]], axis=0))
+        result_ref[slot * chunk : (slot + 1) * chunk] = attend(queries, keys, values, allowed)
 
 
 def local_window(bound, places, slots, spots, chunk, qkvs, heads):
@@ -521,17 +524,14 @@
     allowed = (col > row) & (col <= row + WINDOW) & ((row >= bound) == (key_place >= bound))
     allowed = allowed & ((key_place >= 0) | (key_place + count >= valid_from))
     spot = pl.multiple_of(spot, WINDOW)
+    queries, keys, values = [], [], []
     for head in range(heads):
         lane = head * 3 * HEAD_DIM
-        keys, values = [
-            jnp.concatenate(
-                [ref[:, lane + n * HEAD_DIM : lane + (n + 1) * HEAD_DIM] for ref in (halo_ref, first_ref)], axis=0
-            )
-            for n in (1, 2)
-        ]
-        result_ref[pl.ds(spot, WINDOW), head * HEAD_DIM : (head + 1) * HEAD_DIM] = attend(
-            first_ref[:, lane : lane + HEAD_DIM], keys, values, allowed
-        )
+        queries.append(first_ref[:, lane : lane + HEAD_DIM])
+        for n, held in ((1, keys), (2, values)):
+            lanes = slice(lane + n * HEAD_DIM, lane + (n + 1) * HEAD_DIM)
+            held.append(jnp.concatenate([halo_ref[:, lanes], first_ref[:, lanes]], axis=0))
+    result_ref[pl.ds(spot, WINDOW), :] = attend(queries, keys, values, allowed)
     split_store(dot(result_ref[start:], weight_ref[...]), fars)
 
 
@@ -602,7 +602,7 @@
 def scores(order, units, lots, goal):
     count = goal.shape[1]
     rows = lots[-1][1]
-    tile = 1280 if rows % 1280 == 0 else 640
+    tile = 640
     pieces = len(lots[0][2])
     specs, steps = [], []
     for first, last, tables in lots:
@@ -627,7 +627,7 @@
         out_shape=jax.ShapeDtypeStruct((8, count), F32),
         scratch_shapes=[pltpu.VMEM((units[0].shape[1], count), BF16), pltpu.VMEM((3, 8, count), F32)],
         compiler_params=params(),
-        cost_estimate=cost(14),
+        cost_estimate=cost(20),
         name="scores",
     )(order, *units, *[table for lot in lots for table in lot[2]], goal)
 
@@ -676,8 +676,8 @@
     starts = jnp.sum(jnp.where(order[None, :] == block[:, None], starts[None, :], 0), axis=1)
     bound = doc_start.astype(jnp.int32)
 
-    lots = [vocab_rows * 3 // 5, vocab_rows * 2 // 5]
-    early, late = vocab_table[: lots[0]], vocab_table[lots[0] :]
+    marks_at = [0, vocab_rows // 5, vocab_rows * 3 // 5, vocab_rows]
+    lots = [vocab_table[i:j] for i, j in zip(marks_at[:-1], marks_at[1:])]
 
     ids = (marks[:, :tok_count] - vocab_first).reshape(seq_count, head_count, chunk)
 
@@ -693,22 +693,24 @@
     else:
         outer = [lookup(ids_of(k), vocab_table, 1)[0] for k in range(1, head_count)]
         inner = lambda: lookup(ids_of(0), vocab_table, 1)
-    found = collect(scatter_rows(outer, inner), seq_count)
+    found, lots[:2] = lax.optimization_barrier((scatter_rows(outer, inner), lots[:2]))
+    found = collect(found, seq_count)
     gathered = [found[0]] + [
         lax.ppermute(found[k], "seq", xor_pairs(seq_count, k)) for k in range(1, seq_count)
     ]
+    lots[0], gathered = lax.optimization_barrier((lots[0], gathered))
     embedded, units = begin(order, norm_gain_one, gathered)
-    chunks = gather_rows(units)
+    across_x, corners = [None] * 3, [None] * 3
 
     constants = selectors()
     sets, state = [], None
-    for n, call in enumerate(calls):
-        pieces = [piece for k in call for piece in chunks[k]]
+
+    def project_call(n, pieces, state):
         first = sum(len(c) for c in calls[:n])
-        made = project(
+        return project(
             bound,
-            places[first : first + len(call)],
-            list(range(len(call))),
+            places[first : first + len(calls[n])],
+            list(range(len(calls[n]))),
             chunk,
             tok_count,
             pieces,
@@ -718,9 +720,18 @@
             n == len(calls) - 1,
             heads,
         )
+
+    chunks = gather_rows(units)
+    if seq_count == 4:
+        across_x[0] = lax.ppermute(lots[0], "seq", xor_pairs(seq_count, 2))
+        corners[0] = lax.ppermute(across_x[0], "seq", xor_pairs(seq_count, 1))
+    for n, call in enumerate(calls):
+        made = project_call(n, [piece for k in call for piece in chunks[k]], state)
         sets.append(made[:3])
         state = made[3]
     fqs, fks, vs = zip(*sets)
+    if seq_count == 4:
+        state, across_x[0] = lax.optimization_barrier((state, across_x[0]))
     states, shares = [], []
     for back in range(1, seq_count):
         states.append(
@@ -748,12 +759,13 @@
         heads,
     )
     parts = scatter_rows(outer, lambda: near_chunks(mixed, lin_out, near, chunk))
+    parts, lots[2] = lax.optimization_barrier((parts, lots[2]))
     units, residual = finish(embedded, norm_gain_two, parts, False)
 
     if seq_count == 4:
-        early, _ = lax.optimization_barrier((early, states))
-        early = lax.ppermute(early, "seq", xor_pairs(seq_count, 2))
-        early_corner = lax.ppermute(early, "seq", xor_pairs(seq_count, 1))
+        lots[1], _ = lax.optimization_barrier((lots[1], states))
+        across_x[1] = lax.ppermute(lots[1], "seq", xor_pairs(seq_count, 2))
+        corners[1] = lax.ppermute(across_x[1], "seq", xor_pairs(seq_count, 1))
         beside = lax.ppermute(vocab_table, "seq", xor_pairs(seq_count, 1))
 
     chunks = gather_rows(units)
@@ -766,7 +778,8 @@
         tail = jnp.where(
             held_at[slot] == head_count - 1, qkvs[n][at + chunk - WINDOW : at + chunk], tail
         )
-    late, tail = lax.optimization_barrier((late, tail))
+    if seq_count == 4:
+        tail, across_x[1] = lax.optimization_barrier((tail, across_x[1]))
     halo = lax.ppermute(tail, "seq", [(i, i + 1) for i in range(seq_count - 1)])
     previous = jnp.sum(jnp.where(block == seq_index - 1, starts, 0))
     valid_from = jnp.where(
@@ -774,6 +787,7 @@
     ).astype(jnp.int32)
     first_spot = jnp.sum(jnp.where(held_at == 0, jnp.arange(head_count) * chunk, 0)).astype(jnp.int32)
     local, first = local_window(bound, places, slots, spots, chunk, qkvs, heads)
+    lots[2], local, halo = lax.optimization_barrier((lots[2], local, halo))
     info = jnp.stack([bound[0], valid_from, first_spot])
     mixed, *outer = halo_window(info, near, chunk, far, local, first, halo, win_out, heads)
     parts = scatter_rows(outer, lambda: near_chunks(mixed, win_out, near, chunk))
@@ -781,28 +795,22 @@
 
     chunks = gather_rows(units)
     if seq_count == 4:
-        late = lax.ppermute(late, "seq", xor_pairs(seq_count, 2))
-        corner, _ = lax.optimization_barrier((late, (chunks[1][0], chunks[-1][0])))
-        late_corner = lax.ppermute(corner, "seq", xor_pairs(seq_count, 1))
+        across_x[2] = lax.ppermute(lots[2], "seq", xor_pairs(seq_count, 2))
+        corner, _ = lax.optimization_barrier((across_x[2], (chunks[1][0], chunks[-1][0])))
+        corners[2] = lax.ppermute(corner, "seq", xor_pairs(seq_count, 1))
         lots = [
-            (0, lots[0], [vocab_table, beside, early, early_corner]),
-            (lots[0], vocab_rows, [vocab_table, beside, late, late_corner]),
+            (marks_at[n], marks_at[n + 1], [vocab_table, beside, across_x[n], corners[n]])
+            for n in range(3)
         ]
     else:
         lots = [(0, vocab_rows, [lax.all_gather(vocab_table, "seq", axis=1, tiled=True)])]
         order = jnp.zeros((1,), jnp.int32)
     goals = (target_ids - vocab_first).reshape(head_count, chunk)
-    found = {}
-    for group in [[0, 3], [1, 2]] if head_count == 4 else [[k] for k in range(head_count)]:
-        goal = jnp.concatenate(
-            [
-                lax.dynamic_index_in_dim(goals, (head_index + k) % head_count, 0, False)
-                for k in group
-            ]
-        ).reshape(1, -1)
-        triple = scores(order, [piece for k in group for piece in chunks[k]], lots, goal)
-        for at, k in enumerate(group):
-            found[k] = triple[:3, at * chunk : (at + 1) * chunk]
+    goal = jnp.concatenate(
+        [lax.dynamic_index_in_dim(goals, (head_index + k) % head_count, 0, False) for k in slots]
+    ).reshape(1, -1)
+    triple = scores(order, [piece for k in slots for piece in chunks[k]], lots, goal)
+    found = {k: triple[:3, at * chunk : (at + 1) * chunk] for at, k in enumerate(slots)}
 
     shares = jnp.stack([found[0]] + [turned(found[k], k) for k in range(1, head_count)])
     peak = jnp.max(shares[:, 0], axis=0)

time: 408 us -> 364 us (0.89)
  starting transfers between devices: 110 us -> 79.4 us
  Pallas kernels: 140 us -> 119 us
  waiting for transfers between devices: 115 us -> 129 us
  local copies, waits for them, and re-layouts: 26.8 us -> 21.6 us
    ppermute x4 -> x6, starting transfers between devices: 46.8 us -> 8.2 us  [the longest x1 3.22 us: shards(): across_x[2] = lax.ppermute(lots[2], 'seq', xor_pairs(seq_count, 2))]
    ppermute x33, waiting for transfers between devices: 105 us -> 116 us  [turned(): lax.ppermute(value, 'head', [(i, (i + step) % size) for i in range(size)])]
    pallas_call x2 -> x1, Pallas kernels: 32 us -> 23.2 us  [scores(): pl.pallas_call(functools.partial(score_kernel, len(units), pieces, steps,...]
    ppermute x33, starting transfers between devices: 50.9 us -> 59.2 us  [turned(): lax.ppermute(value, 'head', [(i, (i + step) % size) for i in range(size)])]
    ppermute x4 -> x6, waiting for transfers between devices: 0.01 us -> 6.12 us  [the longest x1 6.11 us: shards(): corners[0] = lax.ppermute(across_x[0], 'seq', xor_pairs(seq_count, 1))]
    pallas_call x3 -> x2, Pallas kernels: 16.6 us -> 12.4 us  [matmul(): pl.pallas_call(matmul_kernel, grid=(b.shape[1] // tile,), in_specs=[pl.Bl...]
    pallas_call x3 -> x2, Pallas kernels: 15.8 us -> 11.7 us  [project(): pl.pallas_call(functools.partial(project_kernel, heads, slots, chunk, cou...]
    slice x5 -> x3, local copies, waits for them, and re-layouts: 9.68 us -> 7.54 us  [the longest x2 6.9 us: shards(): lots = [vocab_table[i:j] for i, j in zip(marks_at[:-1], marks_at[1:])]]
  transfers between devices with their start and end apart: 48 -> 50, of which waited for: 27 -> 32; matrix products, arithmetic and copies ran while one was open for 5% -> 5% of each run, Pallas kernels for 30% -> 23%
where the time goes in v6:
time: 364 us; the launch traced here: 363 us
  waiting for transfers between devices  129 us (35%)
  Pallas kernels  119 us (33%)
  starting transfers between devices  79.4 us (22%)
  local copies, waits for them, and re-layouts  21.6 us (6%)
  other arithmetic  6.8 us (2%)
  between operations  6.75 us (2%)
    ppermute x33, waiting for transfers between devices, turned(): lax.ppermute(value, 'head', [(i, (i + step) % size) for i in range(size)])  116 us
    ppermute x33, starting transfers between devices, turned(): lax.ppermute(value, 'head', [(i, (i + step) % size) for i in range(size)])  59.2 us
    pallas_call x3, Pallas kernels, lookup(): pl.pallas_call(lookup_kernel, grid=(rows // tile,), in_specs=[pl.BlockSpe...  30.3 us
    pallas_call x1, Pallas kernels, scores(): pl.pallas_call(functools.partial(score_kernel, len(units), pieces, steps,...  23.2 us
    pallas_call x2, Pallas kernels, matmul(): pl.pallas_call(matmul_kernel, grid=(b.shape[1] // tile,), in_specs=[pl.Bl...  12.4 us
    pallas_call x2, Pallas kernels, project(): pl.pallas_call(functools.partial(project_kernel, heads, slots, chunk, cou...  11.7 us
    unnamed x102, local copies, waits for them, and re-layouts  8.88 us
    pallas_call x2, Pallas kernels, near_chunks(): pl.pallas_call(functools.partial(near_kernel, rows), in_specs=[whole()] *...  7.69 us
  transfers between devices with their start and end apart: 50, of which 32 were waited for; matrix products, arithmetic and copies ran while one was open for 5% of the time, Pallas kernels for 23%

profile of v6, /device:TPU:0, one launch (start us, length us, event | category | flops | bytes accessed | tf_op | source)
XLA Modules:
  0.0 363.1 jit_solution(15299725615720415305)
XLA Ops:
  4.4 4.4 %fusion.14 = (bf16[2560,512]{1,0:T(8,128)(2,1)S(1)}, bf16[2560,512]{1,0:T(8,128)(2,1)}) fusion(bf16[6400,512]{1,0:T(8,128)(2,1)} %refs_13_.1), kind=kLoop, calls=%fused_computation.53 | loop fusion | bytes 10485760 | tf_op jit(solution)/shard_map/slice | solution.py:680
  12.0 8.5 %lookup.5 = (bf16[256,512]{1,0:T(8,128)(2,1)}, bf16[256,512]{1,0:T(8,128)(2,1)}) custom-call(s32[1,512]{1,0:T(1,128)} %bitcast.50, bf16[6400,512]{1,0:T(8,128)(2,1)} %refs_13_.1), custom_call_target="tpu_custom_call" | custom-call | flops 4800000000 | bytes 24000000 | tf_op jit(solution)/shard_map/lookup/pallas_call | solution.py:140
  25.0 13.2 %lookup.4 = (bf16[256,512]{1,0:T(8,128)(2,1)}, bf16[256,512]{1,0:T(8,128)(2,1)}, bf16[256,512]{1,0:T(8,128)(2,1)}, bf16[256,512]{1,0:T(8,128)(2,1)}) custom-call(s32[1,1024]{1,0:T(1,128)} %bitcast.45, bf16[6400,512]{1,0:T(8,128)(2,1)} %refs_13_.1), custom_call_target="tpu_custom_call" | custom-call | flops 9600000000 | bytes 48000000 | tf_op jit(solution)/shard_map/lookup/pallas_call | solution.py:140
  43.1 3.8 %collective-permute-start.8 = (bf16[256,512]{1,0:T(8,128)(2,1)}, bf16[256,512]{1,0:T(8,128)(2,1)S(1)}, u32[]{:S(2)}, u32[]{:S(2)}) collective-permute-start(bf16[256,512]{1,0:T(8,128)(2,1)} %get-tuple-element.95), channel_id=1, source_target_pairs={{0,3},{1,0},{2,1},{3,2},{4,7},{5,4},{6,5},{7,6},{8,11},{9,8},{10,9... | collective-permute-start | bytes 786440 | tf_op jit(solution)/shard_map/ppermute | solution.py:56
  46.9 8.6 %lookup.3 = (bf16[256,512]{1,0:T(8,128)(2,1)}, bf16[256,512]{1,0:T(8,128)(2,1)}) custom-call(s32[1,512]{1,0:T(1,128)} %bitcast.46, bf16[6400,512]{1,0:T(8,128)(2,1)} %refs_13_.1), custom_call_target="tpu_custom_call" | custom-call | flops 4800000000 | bytes 24000000 | tf_op jit(solution)/shard_map/lookup/pallas_call | solution.py:140
  55.5 2.8 collective-permute-done.6.refs_2_
  59.4 4.0 %collective-permute-done.8.refs_5_ = bf16[256,512]{1,0:T(8,128)(2,1)S(1)} collective-permute-done((bf16[256,512]{1,0:T(8,128)(2,1)}, bf16[256,512]{1,0:T(8,128)(2,1)S(1)}, u32[]{:S(2)}, u32[]{:S(2)}) %collective-permute-start.8) | collective-permute-done | bytes 262176 | tf_op jit(solution)/shard_map/ppermute | solution.py:56
  68.9 4.1 %collective-permute-done.10.refs_2_ = bf16[128,512]{1,0:T(8,128)(2,1)S(1)} collective-permute-done((bf16[128,512]{1,0:T(8,128)(2,1)}, bf16[128,512]{1,0:T(8,128)(2,1)S(1)}, u32[]{:S(2)}, u32[]{:S(2)}) %collective-permute-start.10) | collective-permute-done | bytes 131104 | tf_op jit(solution)/shard_map/ppermute | solution.py:699
  79.4 3.5 collective-permute-start.12
  85.0 10.9 %collective-permute-done.13.refs_2_ = bf16[128,2048]{1,0:T(8,128)(2,1)S(1)} collective-permute-done((bf16[128,2048]{1,0:T(8,128)(2,1)}, bf16[128,2048]{1,0:T(8,128)(2,1)S(1)}, u32[]{:S(2)}, u32[]{:S(2)}) %collective-permute-start.13) | collective-permute-done | bytes 524320 | tf_op jit(solution)/shard_map/ppermute | solution.py:56
  96.0 8.4 %collective-permute-done.12.refs_1_ = bf16[128,2048]{1,0:T(8,128)(2,1)S(1)} collective-permute-done((bf16[128,2048]{1,0:T(8,128)(2,1)}, bf16[128,2048]{1,0:T(8,128)(2,1)S(1)}, u32[]{:S(2)}, u32[]{:S(2)}) %collective-permute-start.12) | collective-permute-done | bytes 524320 | tf_op jit(solution)/shard_map/ppermute | solution.py:56
  104.4 3.7 %collective-permute-start.15 = (bf16[64,2048]{1,0:T(8,128)(2,1)S(1)}, bf16[64,2048]{1,0:T(8,128)(2,1)S(1)}, u32[]{:S(2)}, u32[]{:S(2)}) collective-permute-start(bf16[64,2048]{1,0:T(8,128)(2,1)S(1)} %slice.115), channel_id=1, source_target_pairs={{0,3},{1,0},{2,1},{3,2},{4,7},{5,4},{6,5},{7,6},{8,11},{9,8},{10,9... | collective-permute-start | bytes 786440 | tf_op jit(solution)/shard_map/ppermute | solution.py:56
  108.1 6.6 %project.2 = (bf16[4,384,256]{2,1,0:T(8,128)(2,1)}, bf16[4,384,256]{2,1,0:T(8,128)(2,1)}, bf16[384,512]{1,0:T(8,128)(2,1)}, f32[4,176,128]{2,1,0:T(8,128)}) custom-call(s32[1]{0:T(128)} %copy.35.bound_ref, s32[3]{0:T(128)} %bitcast.51, bf16[128,2048]{1,0:T(8,128)(2,1)} %get-tuple-element.112.refs_0_, bf16[128,2048]{1,0:T(8,128)(2,1)} %copy-done.13, ...), custom_call_target="tpu_custom_call" | custom-call | flops 3000000000 | bytes 15000000 | tf_op jit(solution)/shard_map/project/pallas_call | solution.py:310
  115.3 3.6 collective-permute-done.15.refs_1_
  119.6 5.1 %project.3 = (bf16[4,128,256]{2,1,0:T(8,128)(2,1)}, bf16[4,128,256]{2,1,0:T(8,128)(2,1)}, bf16[128,512]{1,0:T(8,128)(2,1)}, bf16[4,176,128]{2,1,0:T(8,128)(2,1)}) custom-call(s32[1]{0:T(128)} %copy.35.bound_ref, s32[1]{0:T(128)} %slice.90.places_ref, bf16[64,2048]{1,0:T(8,128)(2,1)} %copy-done.30, bf16[64,2048]{1,0:T(8,128)(2,1)} %copy-done.39, ...), custom_call_target="tpu_custom_call" | custom-call | flops 3000000000 | bytes 15000000 | tf_op jit(solution)/shard_map/project/pallas_call | solution.py:310
  135.3 3.1 collective-permute-start.30
  138.4 4.5 %within.1 = (f32[4,512,128]{2,1,0:T(8,128)}, f32[4,512,8]{2,1,0:T(8,128)}) custom-call(s32[1]{0:T(128)} %copy.35.bound_ref, s32[4]{0:T(128)} %copy-done.50, bf16[4,384,256]{2,1,0:T(8,128)(2,1)} %get-tuple-element.113.refs_0_, bf16[4,128,256]{2,1,0:T(8,128)(2,1)} %get-tuple-element.115.refs_1_, bf16[4,384,256]{2,1,0:T(8,128)(2,1)} %get-tuple-element.116.refs_2_, ...), custom_call_target="tpu_custom_call" | custom-call | flops 2700000000 | bytes 13500000 | tf_op jit(solution)/shard_map/within/pallas_call | solution.py:349
  142.9 4.7 %across.1 = (bf16[512,512]{1,0:T(8,128)(2,1)}, bf16[64,2048]{1,0:T(8,128)(2,1)}, bf16[64,2048]{1,0:T(8,128)(2,1)}) custom-call(s32[1]{0:T(128)} %copy.35.bound_ref, s32[4]{0:T(128)} %copy-done.50, s32[3]{0:T(128)} %add_convert_fusion.share_ref, bf16[4,384,256]{2,1,0:T(8,128)(2,1)} %get-tuple-element.113.refs_0_, ...), custom_call_target="tpu_custom_call" | custom-call | flops 2700000000 | bytes 13500000 | tf_op jit(solution)/shard_map/across/pallas_call | solution.py:398
  148.1 3.3 collective-permute-start.21
  151.4 3.9 %near.2 = (bf16[64,2048]{1,0:T(8,128)(2,1)}, bf16[64,2048]{1,0:T(8,128)(2,1)}, bf16[64,2048]{1,0:T(8,128)(2,1)}, bf16[64,2048]{1,0:T(8,128)(2,1)}, bf16[64,2048]{1,0:T(8,128)(2,1)}, /*index=5*/bf16[64,2048]{1,0:T(8,128)(2,1)}) custom-call(bf16[512,512]{1,0:T(8,128)(2,1)} %get-tuple-element.125.mixed_ref, bf16[512,2048]{1,0:T(8,128)(2,1)} %weight_ref.3), custom_call_target="tpu_custom_call" | custom-call | flops 2400000000 | bytes 12000000 | tf_op jit(solution)/shard_map/near/pallas_call | solution.py:417
  164.8 3.3 collective-permute-start.25
  168.7 6.6 %collective-permute-done.23.refs_2_ = bf16[64,2048]{1,0:T(8,128)(2,1)S(1)} collective-permute-done((bf16[64,2048]{1,0:T(8,128)(2,1)}, bf16[64,2048]{1,0:T(8,128)(2,1)S(1)}, u32[]{:S(2)}, u32[]{:S(2)}) %collective-permute-start.23) | collective-permute-done | bytes 262176 | tf_op jit(solution)/shard_map/ppermute | solution.py:56
  175.7 5.3 %collective-permute-done.22.refs_1_ = bf16[64,2048]{1,0:T(8,128)(2,1)S(1)} collective-permute-done((bf16[64,2048]{1,0:T(8,128)(2,1)}, bf16[64,2048]{1,0:T(8,128)(2,1)S(1)}, u32[]{:S(2)}, u32[]{:S(2)}) %collective-permute-start.22) | collective-permute-done | bytes 262176 | tf_op jit(solution)/shard_map/ppermute | solution.py:56
  186.0 3.5 collective-permute-start.26
  192.7 9.8 %collective-permute-done.27.refs_2_ = bf16[128,2048]{1,0:T(8,128)(2,1)S(1)} collective-permute-done((bf16[128,2048]{1,0:T(8,128)(2,1)}, bf16[128,2048]{1,0:T(8,128)(2,1)S(1)}, u32[]{:S(2)}, u32[]{:S(2)}) %collective-permute-start.27) | collective-permute-done | bytes 524320 | tf_op jit(solution)/shard_map/ppermute | solution.py:56
  202.6 7.7 %collective-permute-start.28 = (bf16[64,2048]{1,0:T(8,128)(2,1)S(1)}, bf16[64,2048]{1,0:T(8,128)(2,1)S(1)}, u32[]{:S(2)}, u32[]{:S(2)}) collective-permute-start(bf16[64,2048]{1,0:T(8,128)(2,1)S(1)} %slice.116), channel_id=1, source_target_pairs={{0,1},{1,2},{2,3},{3,0},{4,5},{5,6},{6,7},{7,4},{8,9},{9,10},{10,1... | collective-permute-start | bytes 786440 | tf_op jit(solution)/shard_map/ppermute | solution.py:56
  210.8 3.4 collective-permute-start.29
  214.3 7.2 %matmul.2.refs_0_ = bf16[384,1536]{1,0:T(8,128)(2,1)} custom-call(bf16[128,2048]{1,0:T(8,128)(2,1)} %get-tuple-element.144.refs_0_, bf16[128,2048]{1,0:T(8,128)(2,1)} %copy-done.12, bf16[128,2048]{1,0:T(8,128)(2,1)} %copy-done.10, bf16[2048,1536]{1,0:T(8,128)(2,1)} %refs_2_.3), custom_call_target="tpu_custom_call" | custom-call | flops 3000000000 | bytes 15000000 | tf_op jit(solution)/shard_map/matmul/pallas_call | solution.py:436
  222.9 5.2 %matmul.3.refs_1_ = bf16[128,1536]{1,0:T(8,128)(2,1)} custom-call(bf16[64,2048]{1,0:T(8,128)(2,1)} %copy-done.41, bf16[64,2048]{1,0:T(8,128)(2,1)} %copy-done.42, bf16[2048,1536]{1,0:T(8,128)(2,1)} %refs_2_.3), custom_call_target="tpu_custom_call" | custom-call | flops 3000000000 | bytes 15000000 | tf_op jit(solution)/shard_map/matmul/pallas_call | solution.py:436
  230.4 4.6 %local_window.1 = (bf16[512,512]{1,0:T(8,128)(2,1)}, bf16[64,1536]{1,0:T(8,128)(2,1)}) custom-call(s32[1]{0:T(128)} %copy.35.bound_ref, s32[4]{0:T(128)} %copy-done.50, bf16[384,1536]{1,0:T(8,128)(2,1)} %matmul.2.refs_0_, bf16[128,1536]{1,0:T(8,128)(2,1)} %matmul.3.refs_1_), custom_call_target="tpu_custom_call" | custom-call | flops 4800000000 | bytes 24000000 | tf_op jit(solution)/shard_map/local_window/pallas_call | solution.py:504
  235.0 3.2 collective-permute-start.45
  240.8 3.6 %halo_window.1 = (bf16[512,512]{1,0:T(8,128)(2,1)}, bf16[64,2048]{1,0:T(8,128)(2,1)}, bf16[64,2048]{1,0:T(8,128)(2,1)}) custom-call(s32[3]{0:T(128)} %pad_add_fusion.3.info_ref, bf16[512,512]{1,0:T(8,128)(2,1)} %get-tuple-element.149.local_ref, bf16[64,1536]{1,0:T(8,128)(2,1)} %get-tuple-element.150.first_ref, bf16[64,1536]{1,0:T(8,128)(2,1)} %copy-done.43, ...), custom_call_target="tpu_custom_call" | custom-call | flops 2700000000 | bytes 13500000 | tf_op jit(solution)/shard_map/halo_window/pallas_call | solution.py:541
  248.2 3.8 %near.3 = (bf16[64,2048]{1,0:T(8,128)(2,1)}, bf16[64,2048]{1,0:T(8,128)(2,1)}, bf16[64,2048]{1,0:T(8,128)(2,1)}, bf16[64,2048]{1,0:T(8,128)(2,1)}, bf16[64,2048]{1,0:T(8,128)(2,1)}, /*index=5*/bf16[64,2048]{1,0:T(8,128)(2,1)}) custom-call(bf16[512,512]{1,0:T(8,128)(2,1)} %get-tuple-element.152.mixed_ref, bf16[512,2048]{1,0:T(8,128)(2,1)} %weight_ref.5), custom_call_target="tpu_custom_call" | custom-call | flops 2400000000 | bytes 12000000 | tf_op jit(solution)/shard_map/near/pallas_call | solution.py:417
  252.1 3.6 collective-permute-done.32.before_ref
  255.6 4.5 %collective-permute-done.33.after_ref = bf16[64,2048]{1,0:T(8,128)(2,1)S(1)} collective-permute-done((bf16[64,2048]{1,0:T(8,128)(2,1)}, bf16[64,2048]{1,0:T(8,128)(2,1)S(1)}, u32[]{:S(2)}, u32[]{:S(2)}) %collective-permute-start.33) | collective-permute-done | bytes 262176 | tf_op jit(solution)/shard_map/ppermute | solution.py:56
  264.7 3.2 collective-permute-start.37
  268.5 4.1 %collective-permute-done.36.refs_4_ = bf16[64,2048]{1,0:T(8,128)(2,1)S(1)} collective-permute-done((bf16[64,2048]{1,0:T(8,128)(2,1)}, bf16[64,2048]{1,0:T(8,128)(2,1)S(1)}, u32[]{:S(2)}, u32[]{:S(2)}) %collective-permute-start.36) | collective-permute-done | bytes 262176 | tf_op jit(solution)/shard_map/ppermute | solution.py:56
  272.6 5.5 %collective-permute-done.34.refs_1_ = bf16[64,2048]{1,0:T(8,128)(2,1)S(1)} collective-permute-done((bf16[64,2048]{1,0:T(8,128)(2,1)}, bf16[64,2048]{1,0:T(8,128)(2,1)S(1)}, u32[]{:S(2)}, u32[]{:S(2)}) %collective-permute-start.34) | collective-permute-done | bytes 262176 | tf_op jit(solution)/shard_map/ppermute | solution.py:56
  278.1 4.0 %collective-permute-done.37.refs_5_ = bf16[64,2048]{1,0:T(8,128)(2,1)S(1)} collective-permute-done((bf16[64,2048]{1,0:T(8,128)(2,1)}, bf16[64,2048]{1,0:T(8,128)(2,1)S(1)}, u32[]{:S(2)}, u32[]{:S(2)}) %collective-permute-start.37) | collective-permute-done | bytes 262176 | tf_op jit(solution)/shard_map/ppermute | solution.py:56
  282.9 2.9 finish.3.refs_0_
  286.6 3.0 collective-permute-start.38
  289.6 13.0 %collective-permute-done.39.refs_2_ = bf16[128,2048]{1,0:T(8,128)(2,1)S(1)} collective-permute-done((bf16[128,2048]{1,0:T(8,128)(2,1)}, bf16[128,2048]{1,0:T(8,128)(2,1)S(1)}, u32[]{:S(2)}, u32[]{:S(2)}) %collective-permute-start.39) | collective-permute-done | bytes 524320 | tf_op jit(solution)/shard_map/ppermute | solution.py:56
  302.7 9.0 %collective-permute-done.38.refs_1_ = bf16[128,2048]{1,0:T(8,128)(2,1)S(1)} collective-permute-done((bf16[128,2048]{1,0:T(8,128)(2,1)}, bf16[128,2048]{1,0:T(8,128)(2,1)S(1)}, u32[]{:S(2)}, u32[]{:S(2)}) %collective-permute-start.38) | collective-permute-done | bytes 524320 | tf_op jit(solution)/shard_map/ppermute | solution.py:56
  312.5 6.1 %collective-permute-done.43.refs_8_ = bf16[1280,512]{1,0:T(8,128)(2,1)S(1)} collective-permute-done((bf16[1280,512]{1,0:T(8,128)(2,1)}, bf16[1280,512]{1,0:T(8,128)(2,1)S(1)}, u32[]{:S(2)}, u32[]{:S(2)}) %collective-permute-start.43) | collective-permute-done | bytes 1310752 | tf_op jit(solution)/shard_map/ppermute | solution.py:727
  322.4 5.5 %collective-permute-done.41.refs_4_ = bf16[64,2048]{1,0:T(8,128)(2,1)S(1)} collective-permute-done((bf16[64,2048]{1,0:T(8,128)(2,1)S(1)}, bf16[64,2048]{1,0:T(8,128)(2,1)S(1)}, u32[]{:S(2)}, u32[]{:S(2)}) %collective-permute-start.41) | collective-permute-done | bytes 262176 | tf_op jit(solution)/shard_map/ppermute | solution.py:56
  330.3 23.2 %scores.1 = f32[8,512]{1,0:T(8,128)} custom-call(s32[4]{0:T(128)} %iota_xor_fusion.order_ref, bf16[128,2048]{1,0:T(8,128)(2,1)} %finish.3.refs_0_, bf16[128,2048]{1,0:T(8,128)(2,1)} %copy-done.6, bf16[128,2048]{1,0:T(8,128)(2,1)} %copy-done.5, bf16[64,2048]{1,0:T(8,128)(2,1)} %copy-done.8, bf16[64,2048]{1,0:T(8,128)(2,1)} %copy-done.9, ...), custom_call_target="tpu_custom_call" | custom-call | flops 12000000000 | bytes 60000000 | tf_op jit(solution)/shard_map/scores/pallas_call | solution.py:619
  354.2 2.9 collective-permute-start.49
  358.5 3.2 collective-permute-done.48
  (215 shorter events, 84.5 us)
Async XLA Ops:
  1.3 10.0 %collective-permute-start.2 = (s32[640]{0:T(1024)S(1)}, s32[640]{0:T(1024)S(1)}, u32[]{:S(2)}, u32[]{:S(2)}) collective-permute-start(s32[640]{0:T(1024)S(1)} %concatenate.9), channel_id=1, source_target_pairs={{0,12},{4,8},{8,4},{12,0},{1,13},{5,9},{9,5},{13,1},{2,14},{6,10},... | collective-permute-start | bytes 7688 | tf_op jit(solution)/shard_map/ppermute | solution.py:671
  3.7 7.6 %collective-permute-start.1 = (s32[640]{0:T(1024)S(1)}, s32[640]{0:T(1024)S(1)}, u32[]{:S(2)}, u32[]{:S(2)}) collective-permute-start(s32[640]{0:T(1024)S(1)} %concatenate.9), channel_id=1, source_target_pairs={{0,8},{4,12},{8,0},{12,4},{1,9},{5,13},{9,1},{13,5},{2,10},{6,14},... | collective-permute-start | bytes 7688 | tf_op jit(solution)/shard_map/ppermute | solution.py:671
  4.3 7.0 %collective-permute-start = (s32[640]{0:T(1024)S(1)}, s32[640]{0:T(1024)S(1)}, u32[]{:S(2)}, u32[]{:S(2)}) collective-permute-start(s32[640]{0:T(1024)S(1)} %concatenate.9), channel_id=1, source_target_pairs={{0,4},{4,0},{8,12},{12,8},{1,5},{5,1},{9,13},{13,9},{2,6},{6,2},{1... | collective-permute-start | bytes 7688 | tf_op jit(solution)/shard_map/ppermute | solution.py:671
  20.5 19.7 %collective-permute-start.3 = (bf16[256,512]{1,0:T(8,128)(2,1)}, bf16[256,512]{1,0:T(8,128)(2,1)S(1)}, u32[]{:S(2)}, u32[]{:S(2)}) collective-permute-start(bf16[256,512]{1,0:T(8,128)(2,1)} %get-tuple-element.88), channel_id=1, source_target_pairs={{0,1},{1,2},{2,3},{3,0},{4,5},{5,6},{6,7},{7,4},{8,9},{9,10},{10,1... | collective-permute-start | bytes 786440 | tf_op jit(solution)/shard_map/ppermute | solution.py:56
  22.4 17.9 %collective-permute-start.4 = (bf16[256,512]{1,0:T(8,128)(2,1)}, bf16[256,512]{1,0:T(8,128)(2,1)S(1)}, u32[]{:S(2)}, u32[]{:S(2)}) collective-permute-start(bf16[256,512]{1,0:T(8,128)(2,1)} %get-tuple-element.90), channel_id=1, source_target_pairs={{0,3},{1,0},{2,1},{3,2},{4,7},{5,4},{6,5},{7,6},{8,11},{9,8},{10,9... | collective-permute-start | bytes 786440 | tf_op jit(solution)/shard_map/ppermute | solution.py:56
  38.2 20.1 %collective-permute-start.6 = (bf16[256,512]{1,0:T(8,128)(2,1)}, bf16[256,512]{1,0:T(8,128)(2,1)S(1)}, u32[]{:S(2)}, u32[]{:S(2)}) collective-permute-start(bf16[256,512]{1,0:T(8,128)(2,1)} %get-tuple-element.92), channel_id=1, source_target_pairs={{0,3},{1,0},{2,1},{3,2},{4,7},{5,4},{6,5},{7,6},{8,11},{9,8},{10,9... | collective-permute-start | bytes 786440 | tf_op jit(solution)/shard_map/ppermute | solution.py:56
  40.3 18.1 %collective-permute-start.7 = (bf16[256,512]{1,0:T(8,128)(2,1)}, bf16[256,512]{1,0:T(8,128)(2,1)S(1)}, u32[]{:S(2)}, u32[]{:S(2)}) collective-permute-start(bf16[256,512]{1,0:T(8,128)(2,1)} %get-tuple-element.94), channel_id=1, source_target_pairs={{0,1},{1,2},{2,3},{3,0},{4,5},{5,6},{6,7},{7,4},{8,9},{9,10},{10,1... | collective-permute-start | bytes 786440 | tf_op jit(solution)/shard_map/ppermute | solution.py:56
  43.1 16.3 %collective-permute-start.5 = (bf16[256,512]{1,0:T(8,128)(2,1)}, bf16[256,512]{1,0:T(8,128)(2,1)S(1)}, u32[]{:S(2)}, u32[]{:S(2)}) collective-permute-start(bf16[256,512]{1,0:T(8,128)(2,1)} %get-tuple-element.91), channel_id=1, source_target_pairs={{0,1},{1,2},{2,3},{3,0},{4,5},{5,6},{6,7},{7,4},{8,9},{9,10},{10,1... | collective-permute-start | bytes 786440 | tf_op jit(solution)/shard_map/ppermute | solution.py:56
  43.1 20.3 %collective-permute-start.8 = (bf16[256,512]{1,0:T(8,128)(2,1)}, bf16[256,512]{1,0:T(8,128)(2,1)S(1)}, u32[]{:S(2)}, u32[]{:S(2)}) collective-permute-start(bf16[256,512]{1,0:T(8,128)(2,1)} %get-tuple-element.95), channel_id=1, source_target_pairs={{0,3},{1,0},{2,1},{3,2},{4,7},{5,4},{6,5},{7,6},{8,11},{9,8},{10,9... | collective-permute-start | bytes 786440 | tf_op jit(solution)/shard_map/ppermute | solution.py:56
  66.4 6.6 %collective-permute-start.10 = (bf16[128,512]{1,0:T(8,128)(2,1)}, bf16[128,512]{1,0:T(8,128)(2,1)S(1)}, u32[]{:S(2)}, u32[]{:S(2)}) collective-permute-start(bf16[128,512]{1,0:T(8,128)(2,1)} %get-tuple-element.105), channel_id=1, source_target_pairs={{0,8},{4,12},{8,0},{12,4},{1,9},{5,13},{9,1},{13,5},{2,10},{6,14},... | collective-permute-start | bytes 393224 | tf_op jit(solution)/shard_map/ppermute | solution.py:699
  67.9 7.0 %collective-permute-start.11 = (bf16[128,512]{1,0:T(8,128)(2,1)}, bf16[128,512]{1,0:T(8,128)(2,1)S(1)}, u32[]{:S(2)}, u32[]{:S(2)}) collective-permute-start(bf16[128,512]{1,0:T(8,128)(2,1)} %get-tuple-element.106), channel_id=1, source_target_pairs={{0,12},{4,8},{8,4},{12,0},{1,13},{5,9},{9,5},{13,1},{2,14},{6,10},... | collective-permute-start | bytes 393224 | tf_op jit(solution)/shard_map/ppermute | solution.py:699
  74.9 49.9 %collective-permute-start.16 = (bf16[1280,512]{1,0:T(8,128)(2,1)}, bf16[1280,512]{1,0:T(8,128)(2,1)}, u32[]{:S(2)}, u32[]{:S(2)}) collective-permute-start(bf16[1280,512]{1,0:T(8,128)(2,1)} %slice.86), channel_id=1, source_target_pairs={{0,8},{4,12},{8,0},{12,4},{1,9},{5,13},{9,1},{13,5},{2,10},{6,14},... | collective-permute-start | bytes 3932168 | tf_op jit(solution)/shard_map/ppermute | solution.py:726
  79.1 16.8 %collective-permute-start.13 = (bf16[128,2048]{1,0:T(8,128)(2,1)}, bf16[128,2048]{1,0:T(8,128)(2,1)S(1)}, u32[]{:S(2)}, u32[]{:S(2)}) collective-permute-start(bf16[128,2048]{1,0:T(8,128)(2,1)} %get-tuple-element.112.refs_0_), channel_id=1, source_target_pairs={{0,1},{1,2},{2,3},{3,0},{4,5},{5,6},{6,7},{7,4},{8,9},{9,10},{10,1... | collective-permute-start | bytes 1572872 | tf_op jit(solution)/shard_map/ppermute | solution.py:56
  79.4 25.0 %collective-permute-start.12 = (bf16[128,2048]{1,0:T(8,128)(2,1)}, bf16[128,2048]{1,0:T(8,128)(2,1)S(1)}, u32[]{:S(2)}, u32[]{:S(2)}) collective-permute-start(bf16[128,2048]{1,0:T(8,128)(2,1)} %get-tuple-element.112.refs_0_), channel_id=1, source_target_pairs={{0,3},{1,0},{2,1},{3,2},{4,7},{5,4},{6,5},{7,6},{8,11},{9,8},{10,9... | collective-permute-start | bytes 1572872 | tf_op jit(solution)/shard_map/ppermute | solution.py:56
  95.9 19.3 %collective-permute-start.14 = (bf16[64,2048]{1,0:T(8,128)(2,1)S(1)}, bf16[64,2048]{1,0:T(8,128)(2,1)S(1)}, u32[]{:S(2)}, u32[]{:S(2)}) collective-permute-start(bf16[64,2048]{1,0:T(8,128)(2,1)S(1)} %slice.114), channel_id=1, source_target_pairs={{0,1},{1,2},{2,3},{3,0},{4,5},{5,6},{6,7},{7,4},{8,9},{9,10},{10,1... | collective-permute-start | bytes 786440 | tf_op jit(solution)/shard_map/ppermute | solution.py:56
  104.4 14.5 %collective-permute-start.15 = (bf16[64,2048]{1,0:T(8,128)(2,1)S(1)}, bf16[64,2048]{1,0:T(8,128)(2,1)S(1)}, u32[]{:S(2)}, u32[]{:S(2)}) collective-permute-start(bf16[64,2048]{1,0:T(8,128)(2,1)S(1)} %slice.115), channel_id=1, source_target_pairs={{0,3},{1,0},{2,1},{3,2},{4,7},{5,4},{6,5},{7,6},{8,11},{9,8},{10,9... | collective-permute-start | bytes 786440 | tf_op jit(solution)/shard_map/ppermute | solution.py:56
  124.7 9.0 %collective-permute-start.19 = (bf16[4,176,128]{2,1,0:T(8,128)(2,1)}, bf16[4,176,128]{2,1,0:T(8,128)(2,1)S(1)}, u32[]{:S(2)}, u32[]{:S(2)}) collective-permute-start(bf16[4,176,128]{2,1,0:T(8,128)(2,1)} %get-tuple-element.124), channel_id=1, source_target_pairs={{0,12},{1,13},{2,14},{3,15},{16,28},{17,29},{18,30},{19,31}} | collective-permute-start | bytes 540680 | tf_op jit(solution)/shard_map/ppermute | solution.py:738
  126.9 8.4 %collective-permute-start.18 = (bf16[4,176,128]{2,1,0:T(8,128)(2,1)}, bf16[4,176,128]{2,1,0:T(8,128)(2,1)S(1)}, u32[]{:S(2)}, u32[]{:S(2)}) collective-permute-start(bf16[4,176,128]{2,1,0:T(8,128)(2,1)} %get-tuple-element.124), channel_id=1, source_target_pairs={{0,8},{4,12},{1,9},{5,13},{2,10},{6,14},{3,11},{7,15},{16,24},{20,... | collective-permute-start | bytes 540680 | tf_op jit(solution)/shard_map/ppermute | solution.py:738
  128.2 7.1 %collective-permute-start.17 = (bf16[4,176,128]{2,1,0:T(8,128)(2,1)}, bf16[4,176,128]{2,1,0:T(8,128)(2,1)S(1)}, u32[]{:S(2)}, u32[]{:S(2)}) collective-permute-start(bf16[4,176,128]{2,1,0:T(8,128)(2,1)} %get-tuple-element.124), channel_id=1, source_target_pairs={{0,4},{4,8},{8,12},{1,5},{5,9},{9,13},{2,6},{6,10},{10,14},{3,7},{... | collective-permute-start | bytes 540680 | tf_op jit(solution)/shard_map/ppermute | solution.py:738
  135.3 93.8 %collective-permute-start.30 = (bf16[2560,512]{1,0:T(8,128)(2,1)}, bf16[2560,512]{1,0:T(8,128)(2,1)S(1)}, u32[]{:S(2)}, u32[]{:S(2)}) collective-permute-start(bf16[2560,512]{1,0:T(8,128)(2,1)} %get-tuple-element.147), channel_id=1, source_target_pairs={{0,8},{4,12},{8,0},{12,4},{1,9},{5,13},{9,1},{13,5},{2,10},{6,14},... | collective-permute-start | bytes 7864328 | tf_op jit(solution)/shard_map/ppermute | solution.py:767
  147.6 11.3 %collective-permute-start.20 = (bf16[64,2048]{1,0:T(8,128)(2,1)}, bf16[64,2048]{1,0:T(8,128)(2,1)S(1)}, u32[]{:S(2)}, u32[]{:S(2)}) collective-permute-start(bf16[64,2048]{1,0:T(8,128)(2,1)} %get-tuple-element.128), channel_id=1, source_target_pairs={{0,1},{1,2},{2,3},{3,0},{4,5},{5,6},{6,7},{7,4},{8,9},{9,10},{10,1... | collective-permute-start | bytes 786440 | tf_op jit(solution)/shard_map/ppermute | solution.py:56
  148.1 13.3 %collective-permute-start.21 = (bf16[64,2048]{1,0:T(8,128)(2,1)}, bf16[64,2048]{1,0:T(8,128)(2,1)S(1)}, u32[]{:S(2)}, u32[]{:S(2)}) collective-permute-start(bf16[64,2048]{1,0:T(8,128)(2,1)} %get-tuple-element.130), channel_id=1, source_target_pairs={{0,3},{1,0},{2,1},{3,2},{4,7},{5,4},{6,5},{7,6},{8,11},{9,8},{10,9... | collective-permute-start | bytes 786440 | tf_op jit(solution)/shard_map/ppermute | solution.py:56
  155.3 20.0 %collective-permute-start.23 = (bf16[64,2048]{1,0:T(8,128)(2,1)}, bf16[64,2048]{1,0:T(8,128)(2,1)S(1)}, u32[]{:S(2)}, u32[]{:S(2)}) collective-permute-start(bf16[64,2048]{1,0:T(8,128)(2,1)} %get-tuple-element.132), channel_id=1, source_target_pairs={{0,3},{1,0},{2,1},{3,2},{4,7},{5,4},{6,5},{7,6},{8,11},{9,8},{10,9... | collective-permute-start | bytes 786440 | tf_op jit(solution)/shard_map/ppermute | solution.py:56
  155.3 20.5 %collective-permute-start.24 = (bf16[64,2048]{1,0:T(8,128)(2,1)}, bf16[64,2048]{1,0:T(8,128)(2,1)S(1)}, u32[]{:S(2)}, u32[]{:S(2)}) collective-permute-start(bf16[64,2048]{1,0:T(8,128)(2,1)} %get-tuple-element.134), channel_id=1, source_target_pairs={{0,1},{1,2},{2,3},{3,0},{4,5},{5,6},{6,7},{7,4},{8,9},{9,10},{10,1... | collective-permute-start | bytes 786440 | tf_op jit(solution)/shard_map/ppermute | solution.py:56
  164.2 16.8 %collective-permute-start.22 = (bf16[64,2048]{1,0:T(8,128)(2,1)}, bf16[64,2048]{1,0:T(8,128)(2,1)S(1)}, u32[]{:S(2)}, u32[]{:S(2)}) collective-permute-start(bf16[64,2048]{1,0:T(8,128)(2,1)} %get-tuple-element.131), channel_id=1, source_target_pairs={{0,1},{1,2},{2,3},{3,0},{4,5},{5,6},{6,7},{7,4},{8,9},{9,10},{10,1... | collective-permute-start | bytes 786440 | tf_op jit(solution)/shard_map/ppermute | solution.py:56
  164.8 17.4 %collective-permute-start.25 = (bf16[64,2048]{1,0:T(8,128)(2,1)}, bf16[64,2048]{1,0:T(8,128)(2,1)S(1)}, u32[]{:S(2)}, u32[]{:S(2)}) collective-permute-start(bf16[64,2048]{1,0:T(8,128)(2,1)} %get-tuple-element.135), channel_id=1, source_target_pairs={{0,3},{1,0},{2,1},{3,2},{4,7},{5,4},{6,5},{7,6},{8,11},{9,8},{10,9... | collective-permute-start | bytes 786440 | tf_op jit(solution)/shard_map/ppermute | solution.py:56
  185.7 16.9 %collective-permute-start.27 = (bf16[128,2048]{1,0:T(8,128)(2,1)}, bf16[128,2048]{1,0:T(8,128)(2,1)S(1)}, u32[]{:S(2)}, u32[]{:S(2)}) collective-permute-start(bf16[128,2048]{1,0:T(8,128)(2,1)} %get-tuple-element.144.refs_0_), channel_id=1, source_target_pairs={{0,1},{1,2},{2,3},{3,0},{4,5},{5,6},{6,7},{7,4},{8,9},{9,10},{10,1... | collective-permute-start | bytes 1572872 | tf_op jit(solution)/shard_map/ppermute | solution.py:56
  186.0 24.8 %collective-permute-start.26 = (bf16[128,2048]{1,0:T(8,128)(2,1)}, bf16[128,2048]{1,0:T(8,128)(2,1)S(1)}, u32[]{:S(2)}, u32[]{:S(2)}) collective-permute-start(bf16[128,2048]{1,0:T(8,128)(2,1)} %get-tuple-element.144.refs_0_), channel_id=1, source_target_pairs={{0,3},{1,0},{2,1},{3,2},{4,7},{5,4},{6,5},{7,6},{8,11},{9,8},{10,9... | collective-permute-start | bytes 1572872 | tf_op jit(solution)/shard_map/ppermute | solution.py:56
  189.5 138.4 %collective-permute-start.42 = (bf16[6400,512]{1,0:T(8,128)(2,1)}, bf16[6400,512]{1,0:T(8,128)(2,1)}, u32[]{:S(2)}, u32[]{:S(2)}) collective-permute-start(bf16[6400,512]{1,0:T(8,128)(2,1)} %refs_13_.1), channel_id=1, source_target_pairs={{0,4},{4,0},{8,12},{12,8},{1,5},{5,1},{9,13},{13,9},{2,6},{6,2},{1... | collective-permute-start | bytes 19660808 | tf_op jit(solution)/shard_map/ppermute | solution.py:769
  202.6 18.9 %collective-permute-start.28 = (bf16[64,2048]{1,0:T(8,128)(2,1)S(1)}, bf16[64,2048]{1,0:T(8,128)(2,1)S(1)}, u32[]{:S(2)}, u32[]{:S(2)}) collective-permute-start(bf16[64,2048]{1,0:T(8,128)(2,1)S(1)} %slice.116), channel_id=1, source_target_pairs={{0,1},{1,2},{2,3},{3,0},{4,5},{5,6},{6,7},{7,4},{8,9},{9,10},{10,1... | collective-permute-start | bytes 786440 | tf_op jit(solution)/shard_map/ppermute | solution.py:56
  210.8 10.7 %collective-permute-start.29 = (bf16[64,2048]{1,0:T(8,128)(2,1)S(1)}, bf16[64,2048]{1,0:T(8,128)(2,1)S(1)}, u32[]{:S(2)}, u32[]{:S(2)}) collective-permute-start(bf16[64,2048]{1,0:T(8,128)(2,1)S(1)} %slice.117), channel_id=1, source_target_pairs={{0,3},{1,0},{2,1},{3,2},{4,7},{5,4},{6,5},{7,6},{8,11},{9,8},{10,9... | collective-permute-start | bytes 786440 | tf_op jit(solution)/shard_map/ppermute | solution.py:56
  229.1 5.9 %collective-permute-start.31 = (bf16[64,1536]{1,0:T(8,128)(2,1)S(1)}, bf16[64,1536]{1,0:T(8,128)(2,1)S(1)}, u32[]{:S(2)}, u32[]{:S(2)}) collective-permute-start(bf16[64,1536]{1,0:T(8,128)(2,1)S(1)} %fusion.2), channel_id=1, source_target_pairs={{0,4},{4,8},{8,12},{1,5},{5,9},{9,13},{2,6},{6,10},{10,14},{3,7},{... | collective-permute-start | bytes 589832 | tf_op jit(solution)/shard_map/ppermute | solution.py:783
  235.0 76.6 %collective-permute-start.45 = (bf16[2560,512]{1,0:T(8,128)(2,1)S(1)}, bf16[2560,512]{1,0:T(8,128)(2,1)}, u32[]{:S(2)}, u32[]{:S(2)}) collective-permute-start(bf16[2560,512]{1,0:T(8,128)(2,1)S(1)} %get-tuple-element.165), channel_id=1, source_target_pairs={{0,8},{4,12},{8,0},{12,4},{1,9},{5,13},{9,1},{13,5},{2,10},{6,14},... | collective-permute-start | bytes 7864328 | tf_op jit(solution)/shard_map/ppermute | solution.py:798
  244.4 11.2 %collective-permute-start.32 = (bf16[64,2048]{1,0:T(8,128)(2,1)}, bf16[64,2048]{1,0:T(8,128)(2,1)S(1)}, u32[]{:S(2)}, u32[]{:S(2)}) collective-permute-start(bf16[64,2048]{1,0:T(8,128)(2,1)} %get-tuple-element.155), channel_id=1, source_target_pairs={{0,1},{1,2},{2,3},{3,0},{4,5},{5,6},{6,7},{7,4},{8,9},{9,10},{10,1... | collective-permute-start | bytes 786440 | tf_op jit(solution)/shard_map/ppermute | solution.py:56
  245.4 14.7 %collective-permute-start.33 = (bf16[64,2048]{1,0:T(8,128)(2,1)}, bf16[64,2048]{1,0:T(8,128)(2,1)S(1)}, u32[]{:S(2)}, u32[]{:S(2)}) collective-permute-start(bf16[64,2048]{1,0:T(8,128)(2,1)} %get-tuple-element.157), channel_id=1, source_target_pairs={{0,3},{1,0},{2,1},{3,2},{4,7},{5,4},{6,5},{7,6},{8,11},{9,8},{10,9... | collective-permute-start | bytes 786440 | tf_op jit(solution)/shard_map/ppermute | solution.py:56
  252.1 12.6 %collective-permute-start.35 = (bf16[64,2048]{1,0:T(8,128)(2,1)}, bf16[64,2048]{1,0:T(8,128)(2,1)S(1)}, u32[]{:S(2)}, u32[]{:S(2)}) collective-permute-start(bf16[64,2048]{1,0:T(8,128)(2,1)} %get-tuple-element.159), channel_id=1, source_target_pairs={{0,3},{1,0},{2,1},{3,2},{4,7},{5,4},{6,5},{7,6},{8,11},{9,8},{10,9... | collective-permute-start | bytes 786440 | tf_op jit(solution)/shard_map/ppermute | solution.py:56
  255.6 17.0 %collective-permute-start.36 = (bf16[64,2048]{1,0:T(8,128)(2,1)}, bf16[64,2048]{1,0:T(8,128)(2,1)S(1)}, u32[]{:S(2)}, u32[]{:S(2)}) collective-permute-start(bf16[64,2048]{1,0:T(8,128)(2,1)} %get-tuple-element.161), channel_id=1, source_target_pairs={{0,1},{1,2},{2,3},{3,0},{4,5},{5,6},{6,7},{7,4},{8,9},{9,10},{10,1... | collective-permute-start | bytes 786440 | tf_op jit(solution)/shard_map/ppermute | solution.py:56
  262.9 15.3 %collective-permute-start.34 = (bf16[64,2048]{1,0:T(8,128)(2,1)}, bf16[64,2048]{1,0:T(8,128)(2,1)S(1)}, u32[]{:S(2)}, u32[]{:S(2)}) collective-permute-start(bf16[64,2048]{1,0:T(8,128)(2,1)} %get-tuple-element.158), channel_id=1, source_target_pairs={{0,1},{1,2},{2,3},{3,0},{4,5},{5,6},{6,7},{7,4},{8,9},{9,10},{10,1... | collective-permute-start | bytes 786440 | tf_op jit(solution)/shard_map/ppermute | solution.py:56
  264.7 17.5 %collective-permute-start.37 = (bf16[64,2048]{1,0:T(8,128)(2,1)}, bf16[64,2048]{1,0:T(8,128)(2,1)S(1)}, u32[]{:S(2)}, u32[]{:S(2)}) collective-permute-start(bf16[64,2048]{1,0:T(8,128)(2,1)} %get-tuple-element.162), channel_id=1, source_target_pairs={{0,3},{1,0},{2,1},{3,2},{4,7},{5,4},{6,5},{7,6},{8,11},{9,8},{10,9... | collective-permute-start | bytes 786440 | tf_op jit(solution)/shard_map/ppermute | solution.py:56
  285.8 16.8 %collective-permute-start.39 = (bf16[128,2048]{1,0:T(8,128)(2,1)}, bf16[128,2048]{1,0:T(8,128)(2,1)S(1)}, u32[]{:S(2)}, u32[]{:S(2)}) collective-permute-start(bf16[128,2048]{1,0:T(8,128)(2,1)} %finish.3.refs_0_), channel_id=1, source_target_pairs={{0,1},{1,2},{2,3},{3,0},{4,5},{5,6},{6,7},{7,4},{8,9},{9,10},{10,1... | collective-permute-start | bytes 1572872 | tf_op jit(solution)/shard_map/ppermute | solution.py:56
  286.6 25.0 %collective-permute-start.38 = (bf16[128,2048]{1,0:T(8,128)(2,1)}, bf16[128,2048]{1,0:T(8,128)(2,1)S(1)}, u32[]{:S(2)}, u32[]{:S(2)}) collective-permute-start(bf16[128,2048]{1,0:T(8,128)(2,1)} %finish.3.refs_0_), channel_id=1, source_target_pairs={{0,3},{1,0},{2,1},{3,2},{4,7},{5,4},{6,5},{7,6},{8,11},{9,8},{10,9... | collective-permute-start | bytes 1572872 | tf_op jit(solution)/shard_map/ppermute | solution.py:56
  289.6 38.3 %collective-permute-start.44 = (bf16[2560,512]{1,0:T(8,128)(2,1)S(1)}, bf16[2560,512]{1,0:T(8,128)(2,1)S(1)}, u32[]{:S(2)}, u32[]{:S(2)}) collective-permute-start(bf16[2560,512]{1,0:T(8,128)(2,1)S(1)} %copy-done.1), channel_id=1, source_target_pairs={{0,4},{4,0},{8,12},{12,8},{1,5},{5,1},{9,13},{13,9},{2,6},{6,2},{1... | collective-permute-start | bytes 7864328 | tf_op jit(solution)/shard_map/ppermute | solution.py:768
  311.6 16.3 %collective-permute-start.46 = (bf16[2560,512]{1,0:T(8,128)(2,1)}, bf16[2560,512]{1,0:T(8,128)(2,1)S(1)}, u32[]{:S(2)}, u32[]{:S(2)}) collective-permute-start(bf16[2560,512]{1,0:T(8,128)(2,1)} %collective-permute-done.45.refs_15_), channel_id=1, source_target_pairs={{0,4},{4,0},{8,12},{12,8},{1,5},{5,1},{9,13},{13,9},{2,6},{6,2},{1... | collective-permute-start | bytes 7864328 | tf_op jit(solution)/shard_map/ppermute | solution.py:800
  311.7 7.0 %collective-permute-start.43 = (bf16[1280,512]{1,0:T(8,128)(2,1)}, bf16[1280,512]{1,0:T(8,128)(2,1)S(1)}, u32[]{:S(2)}, u32[]{:S(2)}) collective-permute-start(bf16[1280,512]{1,0:T(8,128)(2,1)} %collective-permute-done.16.refs_7_), channel_id=1, source_target_pairs={{0,4},{4,0},{8,12},{12,8},{1,5},{5,1},{9,13},{13,9},{2,6},{6,2},{1... | collective-permute-start | bytes 3932168 | tf_op jit(solution)/shard_map/ppermute | solution.py:727
  312.2 10.3 %collective-permute-start.40 = (bf16[64,2048]{1,0:T(8,128)(2,1)S(1)}, bf16[64,2048]{1,0:T(8,128)(2,1)S(1)}, u32[]{:S(2)}, u32[]{:S(2)}) collective-permute-start(bf16[64,2048]{1,0:T(8,128)(2,1)S(1)} %slice.122), channel_id=1, source_target_pairs={{0,1},{1,2},{2,3},{3,0},{4,5},{5,6},{6,7},{7,4},{8,9},{9,10},{10,1... | collective-permute-start | bytes 786440 | tf_op jit(solution)/shard_map/ppermute | solution.py:56
  318.6 9.3 %collective-permute-start.41 = (bf16[64,2048]{1,0:T(8,128)(2,1)S(1)}, bf16[64,2048]{1,0:T(8,128)(2,1)S(1)}, u32[]{:S(2)}, u32[]{:S(2)}) collective-permute-start(bf16[64,2048]{1,0:T(8,128)(2,1)S(1)} %slice.123), channel_id=1, source_target_pairs={{0,3},{1,0},{2,1},{3,2},{4,7},{5,4},{6,5},{7,6},{8,11},{9,8},{10,9... | collective-permute-start | bytes 786440 | tf_op jit(solution)/shard_map/ppermute | solution.py:56
  357.2 4.5 %collective-permute-start.48 = (f32[3,128]{1,0:T(4,128)S(1)}, f32[3,128]{1,0:T(4,128)S(1)}, u32[]{:S(2)}, u32[]{:S(2)}) collective-permute-start(f32[3,128]{1,0:T(4,128)S(1)} %get-tuple-element.177), channel_id=1, source_target_pairs={{0,2},{1,3},{2,0},{3,1},{4,6},{5,7},{6,4},{7,5},{8,10},{9,11},{10,... | collective-permute-start | bytes 4616 | tf_op jit(solution)/shard_map/ppermute | solution.py:56
  357.2 5.4 %collective-permute-start.47 = (f32[3,128]{1,0:T(4,128)S(1)}, f32[3,128]{1,0:T(4,128)S(1)}, u32[]{:S(2)}, u32[]{:S(2)}) collective-permute-start(f32[3,128]{1,0:T(4,128)S(1)} %get-tuple-element.178), channel_id=1, source_target_pairs={{0,1},{1,2},{2,3},{3,0},{4,5},{5,6},{6,7},{7,4},{8,9},{9,10},{10,1... | collective-permute-start | bytes 4616 | tf_op jit(solution)/shard_map/ppermute | solution.py:56
  (53 other events, 386.3 us)

commit v7 on v6

--- a/solution.py
+++ b/solution.py
@@ -109,9 +109,15 @@
     return [[k] for k in range(size)]
 
 
-def lookup_kernel(ids_ref, table_ref, *refs):
-    outs, total = refs[:-1], refs[-1]
+def lookup_kernel(lots, ids_ref, table_ref, *refs):
+    outs, copies, total = refs[: -1 - len(lots)], refs[-1 - len(lots) : -1], refs[-1]
     step = pl.program_id(0)
+    for (start, stop), copy in zip(lots, copies):
+
+        @pl.when((step >= start) & (step < stop))
+        def _():
+            copy[...] = table_ref[...]
+
     tile = table_ref.shape[0]
     count = ids_ref.shape[1]
     ids = jnp.transpose(jnp.broadcast_to(ids_ref[...], (8, count)))[:, 0:1] - step * tile
@@ -133,19 +139,27 @@
             out[...] = total[n * rows : (n + 1) * rows].astype(BF16)
 
 
-def lookup(ids, table, pieces):
+TABLE_STEPS = 5
+
+
+def lookup(ids, table, pieces, lots=()):
     count = ids.shape[0]
     rows, width = table.shape
-    tile = rows // 5
-    return pl.pallas_call(
-        lookup_kernel,
-        grid=(rows // tile,),
+    tile = rows // TABLE_STEPS
+    return pl.pallas_call(
+        functools.partial(lookup_kernel, lots),
+        grid=(TABLE_STEPS,),
         in_specs=[
             pl.BlockSpec((1, count), lambda i: (0, 0)),
             pl.BlockSpec((tile, width), lambda i: (i, 0)),
         ],
-        out_specs=[pl.BlockSpec((count // pieces, width), lambda i: (0, 0))] * pieces,
-        out_shape=[jax.ShapeDtypeStruct((count // pieces, width), BF16)] * pieces,
+        out_specs=[pl.BlockSpec((count // pieces, width), lambda i: (0, 0))] * pieces
+        + [
+            pl.BlockSpec((tile, width), lambda i, start=start, stop=stop: (jnp.clip(i, start, stop - 1) - start, 0))
+            for start, stop in lots
+        ],
+        out_shape=[jax.ShapeDtypeStruct((count // pieces, width), BF16)] * pieces
+        + [jax.ShapeDtypeStruct(((stop - start) * tile, width), BF16) for start, stop in lots],
         scratch_shapes=[pltpu.VMEM((count, width), F32)],
         compiler_params=params(),
         cost_estimate=cost(8 * count / 512),
@@ -676,8 +690,9 @@
     starts = jnp.sum(jnp.where(order[None, :] == block[:, None], starts[None, :], 0), axis=1)
     bound = doc_start.astype(jnp.int32)
 
-    marks_at = [0, vocab_rows // 5, vocab_rows * 3 // 5, vocab_rows]
-    lots = [vocab_table[i:j] for i, j in zip(marks_at[:-1], marks_at[1:])]
+    steps = [(0, 1), (1, 3), (3, TABLE_STEPS)]
+    marks_at = [start * (vocab_rows // TABLE_STEPS) for start, _ in steps] + [vocab_rows]
+    lots = []
 
     ids = (marks[:, :tok_count] - vocab_first).reshape(seq_count, head_count, chunk)
 
@@ -686,15 +701,22 @@
 
     if head_count == 4:
         outer = lookup(ids_of(2), vocab_table, 2)
-        inner = lambda: (
-            lookup(ids_of(0), vocab_table, 2)
-            + lookup(jnp.concatenate([ids_of(1), ids_of(3)]), vocab_table, 4)
-        )
+
+        def inner():
+            beside = lookup(jnp.concatenate([ids_of(1), ids_of(3)]), vocab_table, 4)
+            own = lookup(ids_of(0), vocab_table, 2, steps)
+            lots.extend(own[2:])
+            return own[:2] + beside
+
     else:
         outer = [lookup(ids_of(k), vocab_table, 1)[0] for k in range(1, head_count)]
-        inner = lambda: lookup(ids_of(0), vocab_table, 1)
-    found, lots[:2] = lax.optimization_barrier((scatter_rows(outer, inner), lots[:2]))
-    found = collect(found, seq_count)
+
+        def inner():
+            own = lookup(ids_of(0), vocab_table, 1, steps)
+            lots.extend(own[1:])
+            return own[:1]
+
+    found = collect(scatter_rows(outer, inner), seq_count)
     gathered = [found[0]] + [
         lax.ppermute(found[k], "seq", xor_pairs(seq_count, k)) for k in range(1, seq_count)
     ]
@@ -759,11 +781,10 @@
         heads,
     )
     parts = scatter_rows(outer, lambda: near_chunks(mixed, lin_out, near, chunk))
-    parts, lots[2] = lax.optimization_barrier((parts, lots[2]))
     units, residual = finish(embedded, norm_gain_two, parts, False)
 
     if seq_count == 4:
-        lots[1], _ = lax.optimization_barrier((lots[1], states))
+        lots[1], _ = lax.optimization_barrier((lots[1], (states, num)))
         across_x[1] = lax.ppermute(lots[1], "seq", xor_pairs(seq_count, 2))
         corners[1] = lax.ppermute(across_x[1], "seq", xor_pairs(seq_count, 1))
         beside = lax.ppermute(vocab_table, "seq", xor_pairs(seq_count, 1))
@@ -779,7 +800,9 @@
             held_at[slot] == head_count - 1, qkvs[n][at + chunk - WINDOW : at + chunk], tail
         )
     if seq_count == 4:
-        tail, across_x[1] = lax.optimization_barrier((tail, across_x[1]))
+        tail, across_x[1], corners[0], beside = lax.optimization_barrier(
+            (tail, across_x[1], corners[0], beside)
+        )
     halo = lax.ppermute(tail, "seq", [(i, i + 1) for i in range(seq_count - 1)])
     previous = jnp.sum(jnp.where(block == seq_index - 1, starts, 0))
     valid_from = jnp.where(
@@ -791,6 +814,8 @@
     info = jnp.stack([bound[0], valid_from, first_spot])
     mixed, *outer = halo_window(info, near, chunk, far, local, first, halo, win_out, heads)
     parts = scatter_rows(outer, lambda: near_chunks(mixed, win_out, near, chunk))
+    if seq_count == 4:
+        parts, corners[1] = lax.optimization_barrier((parts, corners[1]))
     units = finish(residual, final_gain, parts, True)[0]
 
     chunks = gather_rows(units)

time: 364 us -> 358 us (0.984)
  local copies, waits for them, and re-layouts: 21.6 us -> 13.9 us
  starting transfers between devices: 79.4 us -> 72.7 us
  waiting for transfers between devices: 129 us -> 135 us
    ppermute x33, waiting for transfers between devices: 116 us -> 127 us  [turned(): lax.ppermute(value, 'head', [(i, (i + step) % size) for i in range(size)])]
    slice x2 -> x0, local copies, waits for them, and re-layouts: 6.9 us -> none  [shards(): lots = [vocab_table[i:j] for i, j in zip(marks_at[:-1], marks_at[1:])]]
    ppermute x33, starting transfers between devices: 59.2 us -> 52.5 us  [turned(): lax.ppermute(value, 'head', [(i, (i + step) % size) for i in range(size)])]
    ppermute x1, waiting for transfers between devices: 6.11 us -> 0.01 us  [shards(): corners[0] = lax.ppermute(across_x[0], 'seq', xor_pairs(seq_count, 1))]
  transfers between devices with their start and end apart: 50 -> 50, of which waited for: 32 -> 31; matrix products, arithmetic and copies ran while one was open for 5% -> 3% of each run, Pallas kernels for 23% -> 27%
where the time goes in v7:
time: 358 us; the launch traced here: 357 us
  waiting for transfers between devices  135 us (38%)
  Pallas kernels  121 us (34%)
  starting transfers between devices  72.7 us (20%)
  local copies, waits for them, and re-layouts  13.9 us (4%)
  other arithmetic  6.88 us (2%)
  between operations  6.52 us (2%)
    ppermute x33, waiting for transfers between devices, turned(): lax.ppermute(value, 'head', [(i, (i + step) % size) for i in range(size)])  127 us
    ppermute x33, starting transfers between devices, turned(): lax.ppermute(value, 'head', [(i, (i + step) % size) for i in range(size)])  52.5 us
    pallas_call x3, Pallas kernels, lookup(): pl.pallas_call(functools.partial(lookup_kernel, lots), grid=(TABLE_STEPS,...  32.6 us
    pallas_call x1, Pallas kernels, scores(): pl.pallas_call(functools.partial(score_kernel, len(units), pieces, steps,...  23.2 us
    pallas_call x2, Pallas kernels, matmul(): pl.pallas_call(matmul_kernel, grid=(b.shape[1] // tile,), in_specs=[pl.Bl...  12.4 us
    pallas_call x2, Pallas kernels, project(): pl.pallas_call(functools.partial(project_kernel, heads, slots, chunk, cou...  11.6 us
    unnamed x102, local copies, waits for them, and re-layouts  8.19 us
    pallas_call x2, Pallas kernels, near_chunks(): pl.pallas_call(functools.partial(near_kernel, rows), in_specs=[whole()] *...  7.69 us
  transfers between devices with their start and end apart: 50, of which 31 were waited for; matrix products, arithmetic and copies ran while one was open for 3% of the time, Pallas kernels for 27%

profile of v7, /device:TPU:0, one launch (start us, length us, event | category | flops | bytes accessed | tf_op | source)
XLA Modules:
  0.0 356.7 jit_solution(9269806097110871698)
XLA Ops:
  8.0 8.6 %lookup.5 = (bf16[256,512]{1,0:T(8,128)(2,1)}, bf16[256,512]{1,0:T(8,128)(2,1)}) custom-call(s32[1,512]{1,0:T(1,128)} %bitcast.50, bf16[6400,512]{1,0:T(8,128)(2,1)} %refs_13_.1), custom_call_target="tpu_custom_call" | custom-call | flops 4800000000 | bytes 24000000 | tf_op jit(solution)/shard_map/lookup/pallas_call | solution.py:149
  21.0 13.2 %lookup.4 = (bf16[256,512]{1,0:T(8,128)(2,1)}, bf16[256,512]{1,0:T(8,128)(2,1)}, bf16[256,512]{1,0:T(8,128)(2,1)}, bf16[256,512]{1,0:T(8,128)(2,1)}) custom-call(s32[1,1024]{1,0:T(1,128)} %bitcast.45, bf16[6400,512]{1,0:T(8,128)(2,1)} %refs_13_.1), custom_call_target="tpu_custom_call" | custom-call | flops 9600000000 | bytes 48000000 | tf_op jit(solution)/shard_map/lookup/pallas_call | solution.py:149
  39.1 3.8 %collective-permute-start.8 = (bf16[256,512]{1,0:T(8,128)(2,1)}, bf16[256,512]{1,0:T(8,128)(2,1)S(1)}, u32[]{:S(2)}, u32[]{:S(2)}) collective-permute-start(bf16[256,512]{1,0:T(8,128)(2,1)} %get-tuple-element.93), channel_id=1, source_target_pairs={{0,3},{1,0},{2,1},{3,2},{4,7},{5,4},{6,5},{7,6},{8,11},{9,8},{10,9... | collective-permute-start | bytes 786440 | tf_op jit(solution)/shard_map/ppermute | solution.py:56
  42.9 10.8 %lookup.3 = (bf16[256,512]{1,0:T(8,128)(2,1)}, bf16[256,512]{1,0:T(8,128)(2,1)}, bf16[1280,512]{1,0:T(8,128)(2,1)}, bf16[2560,512]{1,0:T(8,128)(2,1)}, bf16[2560,512]{1,0:T(8,128)(2,1)}) custom-call(s32[1,512]{1,0:T(1,128)} %bitcast.46, bf16[6400,512]{1,0:T(8,128)(2,1)} %refs_13_.1), custom_call_target="tpu_custom_call" | custom-call | flops 4800000000 | bytes 24000000 | tf_op jit(solution)/shard_map/lookup/pallas_call | solution.py:149
  55.1 3.3 collective-permute-done.8.refs_5_
  63.8 4.1 %collective-permute-done.10.refs_2_ = bf16[128,512]{1,0:T(8,128)(2,1)S(1)} collective-permute-done((bf16[128,512]{1,0:T(8,128)(2,1)}, bf16[128,512]{1,0:T(8,128)(2,1)S(1)}, u32[]{:S(2)}, u32[]{:S(2)}) %collective-permute-start.10) | collective-permute-done | bytes 131104 | tf_op jit(solution)/shard_map/ppermute | solution.py:721
  73.3 3.8 %collective-permute-start.12 = (bf16[128,2048]{1,0:T(8,128)(2,1)}, bf16[128,2048]{1,0:T(8,128)(2,1)S(1)}, u32[]{:S(2)}, u32[]{:S(2)}) collective-permute-start(bf16[128,2048]{1,0:T(8,128)(2,1)} %get-tuple-element.103.refs_0_), channel_id=1, source_target_pairs={{0,3},{1,0},{2,1},{3,2},{4,7},{5,4},{6,5},{7,6},{8,11},{9,8},{10,9... | collective-permute-start | bytes 1572872 | tf_op jit(solution)/shard_map/ppermute | solution.py:56
  78.3 11.7 %collective-permute-done.13.refs_2_ = bf16[128,2048]{1,0:T(8,128)(2,1)S(1)} collective-permute-done((bf16[128,2048]{1,0:T(8,128)(2,1)}, bf16[128,2048]{1,0:T(8,128)(2,1)S(1)}, u32[]{:S(2)}, u32[]{:S(2)}) %collective-permute-start.13) | collective-permute-done | bytes 524320 | tf_op jit(solution)/shard_map/ppermute | solution.py:56
  90.2 8.4 %collective-permute-done.12.refs_1_ = bf16[128,2048]{1,0:T(8,128)(2,1)S(1)} collective-permute-done((bf16[128,2048]{1,0:T(8,128)(2,1)}, bf16[128,2048]{1,0:T(8,128)(2,1)S(1)}, u32[]{:S(2)}, u32[]{:S(2)}) %collective-permute-start.12) | collective-permute-done | bytes 524320 | tf_op jit(solution)/shard_map/ppermute | solution.py:56
  98.6 3.8 %collective-permute-start.15 = (bf16[64,2048]{1,0:T(8,128)(2,1)S(1)}, bf16[64,2048]{1,0:T(8,128)(2,1)S(1)}, u32[]{:S(2)}, u32[]{:S(2)}) collective-permute-start(bf16[64,2048]{1,0:T(8,128)(2,1)S(1)} %slice.103), channel_id=1, source_target_pairs={{0,3},{1,0},{2,1},{3,2},{4,7},{5,4},{6,5},{7,6},{8,11},{9,8},{10,9... | collective-permute-start | bytes 786440 | tf_op jit(solution)/shard_map/ppermute | solution.py:56
  102.3 6.5 %project.2 = (bf16[4,384,256]{2,1,0:T(8,128)(2,1)}, bf16[4,384,256]{2,1,0:T(8,128)(2,1)}, bf16[384,512]{1,0:T(8,128)(2,1)}, f32[4,176,128]{2,1,0:T(8,128)}) custom-call(s32[1]{0:T(128)} %copy.35.bound_ref, s32[3]{0:T(128)} %bitcast.51, bf16[128,2048]{1,0:T(8,128)(2,1)} %get-tuple-element.103.refs_0_, bf16[128,2048]{1,0:T(8,128)(2,1)} %copy-done.13, ...), custom_call_target="tpu_custom_call" | custom-call | flops 3000000000 | bytes 15000000 | tf_op jit(solution)/shard_map/project/pallas_call | solution.py:324
  109.5 3.6 %collective-permute-done.15.refs_1_ = bf16[64,2048]{1,0:T(8,128)(2,1)S(1)} collective-permute-done((bf16[64,2048]{1,0:T(8,128)(2,1)S(1)}, bf16[64,2048]{1,0:T(8,128)(2,1)S(1)}, u32[]{:S(2)}, u32[]{:S(2)}) %collective-permute-start.15) | collective-permute-done | bytes 262176 | tf_op jit(solution)/shard_map/ppermute | solution.py:56
  113.8 5.1 %project.3 = (bf16[4,128,256]{2,1,0:T(8,128)(2,1)}, bf16[4,128,256]{2,1,0:T(8,128)(2,1)}, bf16[128,512]{1,0:T(8,128)(2,1)}, bf16[4,176,128]{2,1,0:T(8,128)(2,1)}) custom-call(s32[1]{0:T(128)} %copy.35.bound_ref, s32[1]{0:T(128)} %slice.79.places_ref, bf16[64,2048]{1,0:T(8,128)(2,1)} %copy-done.31, bf16[64,2048]{1,0:T(8,128)(2,1)} %copy-done.38, ...), custom_call_target="tpu_custom_call" | custom-call | flops 3000000000 | bytes 15000000 | tf_op jit(solution)/shard_map/project/pallas_call | solution.py:324
  125.3 4.5 %within.1 = (f32[4,512,128]{2,1,0:T(8,128)}, f32[4,512,8]{2,1,0:T(8,128)}) custom-call(s32[1]{0:T(128)} %copy.35.bound_ref, s32[4]{0:T(128)} %copy-done.50, bf16[4,384,256]{2,1,0:T(8,128)(2,1)} %get-tuple-element.104.refs_0_, bf16[4,128,256]{2,1,0:T(8,128)(2,1)} %get-tuple-element.106.refs_1_, bf16[4,384,256]{2,1,0:T(8,128)(2,1)} %get-tuple-element.107.refs_2_, ...), custom_call_target="tpu_custom_call" | custom-call | flops 2700000000 | bytes 13500000 | tf_op jit(solution)/shard_map/within/pallas_call | solution.py:363
  130.1 3.1 collective-permute-start.30
  137.3 4.6 %across.1 = (bf16[512,512]{1,0:T(8,128)(2,1)}, bf16[64,2048]{1,0:T(8,128)(2,1)}, bf16[64,2048]{1,0:T(8,128)(2,1)}) custom-call(s32[1]{0:T(128)} %copy.35.bound_ref, s32[4]{0:T(128)} %copy-done.50, s32[3]{0:T(128)} %add_convert_fusion.share_ref, bf16[4,384,256]{2,1,0:T(8,128)(2,1)} %get-tuple-element.104.refs_0_, ...), custom_call_target="tpu_custom_call" | custom-call | flops 2700000000 | bytes 13500000 | tf_op jit(solution)/shard_map/across/pallas_call | solution.py:412
  142.8 2.9 collective-permute-start.21
  145.7 3.9 %near.2 = (bf16[64,2048]{1,0:T(8,128)(2,1)}, bf16[64,2048]{1,0:T(8,128)(2,1)}, bf16[64,2048]{1,0:T(8,128)(2,1)}, bf16[64,2048]{1,0:T(8,128)(2,1)}, bf16[64,2048]{1,0:T(8,128)(2,1)}, /*index=5*/bf16[64,2048]{1,0:T(8,128)(2,1)}) custom-call(bf16[512,512]{1,0:T(8,128)(2,1)} %get-tuple-element.116.mixed_ref, bf16[512,2048]{1,0:T(8,128)(2,1)} %weight_ref.3), custom_call_target="tpu_custom_call" | custom-call | flops 2400000000 | bytes 12000000 | tf_op jit(solution)/shard_map/near/pallas_call | solution.py:431
  149.6 3.6 collective-permute-done.20.before_ref
  159.0 3.0 collective-permute-done.23.refs_2_
  162.0 3.3 collective-permute-start.25
  165.9 4.1 %collective-permute-done.24.refs_4_ = bf16[64,2048]{1,0:T(8,128)(2,1)S(1)} collective-permute-done((bf16[64,2048]{1,0:T(8,128)(2,1)}, bf16[64,2048]{1,0:T(8,128)(2,1)S(1)}, u32[]{:S(2)}, u32[]{:S(2)}) %collective-permute-start.24) | collective-permute-done | bytes 262176 | tf_op jit(solution)/shard_map/ppermute | solution.py:56
  170.0 5.3 %collective-permute-done.22.refs_1_ = bf16[64,2048]{1,0:T(8,128)(2,1)S(1)} collective-permute-done((bf16[64,2048]{1,0:T(8,128)(2,1)}, bf16[64,2048]{1,0:T(8,128)(2,1)S(1)}, u32[]{:S(2)}, u32[]{:S(2)}) %collective-permute-start.22) | collective-permute-done | bytes 262176 | tf_op jit(solution)/shard_map/ppermute | solution.py:56
  177.6 2.9 finish.2
  180.7 3.6 %collective-permute-start.26 = (bf16[128,2048]{1,0:T(8,128)(2,1)}, bf16[128,2048]{1,0:T(8,128)(2,1)S(1)}, u32[]{:S(2)}, u32[]{:S(2)}) collective-permute-start(bf16[128,2048]{1,0:T(8,128)(2,1)} %get-tuple-element.129.refs_0_), channel_id=1, source_target_pairs={{0,3},{1,0},{2,1},{3,2},{4,7},{5,4},{6,5},{7,6},{8,11},{9,8},{10,9... | collective-permute-start | bytes 1572872 | tf_op jit(solution)/shard_map/ppermute | solution.py:56
  187.2 10.2 %collective-permute-done.27.refs_2_ = bf16[128,2048]{1,0:T(8,128)(2,1)S(1)} collective-permute-done((bf16[128,2048]{1,0:T(8,128)(2,1)}, bf16[128,2048]{1,0:T(8,128)(2,1)S(1)}, u32[]{:S(2)}, u32[]{:S(2)}) %collective-permute-start.27) | collective-permute-done | bytes 524320 | tf_op jit(solution)/shard_map/ppermute | solution.py:56
  197.4 7.5 %collective-permute-done.26.refs_1_ = bf16[128,2048]{1,0:T(8,128)(2,1)S(1)} collective-permute-done((bf16[128,2048]{1,0:T(8,128)(2,1)}, bf16[128,2048]{1,0:T(8,128)(2,1)S(1)}, u32[]{:S(2)}, u32[]{:S(2)}) %collective-permute-start.26) | collective-permute-done | bytes 524320 | tf_op jit(solution)/shard_map/ppermute | solution.py:56
  204.9 4.0 %collective-permute-start.29 = (bf16[64,2048]{1,0:T(8,128)(2,1)S(1)}, bf16[64,2048]{1,0:T(8,128)(2,1)S(1)}, u32[]{:S(2)}, u32[]{:S(2)}) collective-permute-start(bf16[64,2048]{1,0:T(8,128)(2,1)S(1)} %slice.105), channel_id=1, source_target_pairs={{0,3},{1,0},{2,1},{3,2},{4,7},{5,4},{6,5},{7,6},{8,11},{9,8},{10,9... | collective-permute-start | bytes 786440 | tf_op jit(solution)/shard_map/ppermute | solution.py:56
  208.9 7.2 %matmul.2.refs_0_ = bf16[384,1536]{1,0:T(8,128)(2,1)} custom-call(bf16[128,2048]{1,0:T(8,128)(2,1)} %get-tuple-element.129.refs_0_, bf16[128,2048]{1,0:T(8,128)(2,1)} %copy-done.11, bf16[128,2048]{1,0:T(8,128)(2,1)} %copy-done.10, bf16[2048,1536]{1,0:T(8,128)(2,1)} %refs_2_.3), custom_call_target="tpu_custom_call" | custom-call | flops 3000000000 | bytes 15000000 | tf_op jit(solution)/shard_map/matmul/pallas_call | solution.py:450
  217.6 5.2 %matmul.3.refs_1_ = bf16[128,1536]{1,0:T(8,128)(2,1)} custom-call(bf16[64,2048]{1,0:T(8,128)(2,1)} %copy-done.41, bf16[64,2048]{1,0:T(8,128)(2,1)} %copy-done.42, bf16[2048,1536]{1,0:T(8,128)(2,1)} %refs_2_.3), custom_call_target="tpu_custom_call" | custom-call | flops 3000000000 | bytes 15000000 | tf_op jit(solution)/shard_map/matmul/pallas_call | solution.py:450
  226.3 4.6 %local_window.1 = (bf16[512,512]{1,0:T(8,128)(2,1)}, bf16[64,1536]{1,0:T(8,128)(2,1)}) custom-call(s32[1]{0:T(128)} %copy.35.bound_ref, s32[4]{0:T(128)} %copy-done.50, bf16[384,1536]{1,0:T(8,128)(2,1)} %matmul.2.refs_0_, bf16[128,1536]{1,0:T(8,128)(2,1)} %matmul.3.refs_1_), custom_call_target="tpu_custom_call" | custom-call | flops 4800000000 | bytes 24000000 | tf_op jit(solution)/shard_map/local_window/pallas_call | solution.py:518
  236.0 3.6 %halo_window.1 = (bf16[512,512]{1,0:T(8,128)(2,1)}, bf16[64,2048]{1,0:T(8,128)(2,1)}, bf16[64,2048]{1,0:T(8,128)(2,1)}) custom-call(s32[3]{0:T(128)} %pad_add_fusion.3.info_ref, bf16[512,512]{1,0:T(8,128)(2,1)} %get-tuple-element.134.local_ref, bf16[64,1536]{1,0:T(8,128)(2,1)} %get-tuple-element.135.first_ref, bf16[64,1536]{1,0:T(8,128)(2,1)} %copy-done.43, ...), custom_call_target="tpu_custom_call" | custom-call | flops 2700000000 | bytes 13500000 | tf_op jit(solution)/shard_map/halo_window/pallas_call | solution.py:555
  240.4 3.1 collective-permute-start.35
  243.5 3.8 %near.3 = (bf16[64,2048]{1,0:T(8,128)(2,1)}, bf16[64,2048]{1,0:T(8,128)(2,1)}, bf16[64,2048]{1,0:T(8,128)(2,1)}, bf16[64,2048]{1,0:T(8,128)(2,1)}, bf16[64,2048]{1,0:T(8,128)(2,1)}, /*index=5*/bf16[64,2048]{1,0:T(8,128)(2,1)}) custom-call(bf16[512,512]{1,0:T(8,128)(2,1)} %get-tuple-element.137.mixed_ref, bf16[512,2048]{1,0:T(8,128)(2,1)} %weight_ref.5), custom_call_target="tpu_custom_call" | custom-call | flops 2400000000 | bytes 12000000 | tf_op jit(solution)/shard_map/near/pallas_call | solution.py:431
  247.3 3.6 collective-permute-done.34.before_ref
  250.9 4.5 %collective-permute-done.35.after_ref = bf16[64,2048]{1,0:T(8,128)(2,1)S(1)} collective-permute-done((bf16[64,2048]{1,0:T(8,128)(2,1)}, bf16[64,2048]{1,0:T(8,128)(2,1)S(1)}, u32[]{:S(2)}, u32[]{:S(2)}) %collective-permute-start.35) | collective-permute-done | bytes 262176 | tf_op jit(solution)/shard_map/ppermute | solution.py:56
  259.5 3.4 collective-permute-start.39
  263.5 4.4 %collective-permute-done.38.refs_4_ = bf16[64,2048]{1,0:T(8,128)(2,1)S(1)} collective-permute-done((bf16[64,2048]{1,0:T(8,128)(2,1)}, bf16[64,2048]{1,0:T(8,128)(2,1)S(1)}, u32[]{:S(2)}, u32[]{:S(2)}) %collective-permute-start.38) | collective-permute-done | bytes 262176 | tf_op jit(solution)/shard_map/ppermute | solution.py:56
  267.9 5.5 %collective-permute-done.36.refs_1_ = bf16[64,2048]{1,0:T(8,128)(2,1)S(1)} collective-permute-done((bf16[64,2048]{1,0:T(8,128)(2,1)}, bf16[64,2048]{1,0:T(8,128)(2,1)S(1)}, u32[]{:S(2)}, u32[]{:S(2)}) %collective-permute-start.36) | collective-permute-done | bytes 262176 | tf_op jit(solution)/shard_map/ppermute | solution.py:56
  273.4 4.1 %collective-permute-done.39.refs_5_ = bf16[64,2048]{1,0:T(8,128)(2,1)S(1)} collective-permute-done((bf16[64,2048]{1,0:T(8,128)(2,1)}, bf16[64,2048]{1,0:T(8,128)(2,1)S(1)}, u32[]{:S(2)}, u32[]{:S(2)}) %collective-permute-start.39) | collective-permute-done | bytes 262176 | tf_op jit(solution)/shard_map/ppermute | solution.py:56
  278.3 2.8 finish.3.refs_0_
  281.8 3.1 collective-permute-start.41
  284.9 13.0 %collective-permute-done.42.refs_2_ = bf16[128,2048]{1,0:T(8,128)(2,1)S(1)} collective-permute-done((bf16[128,2048]{1,0:T(8,128)(2,1)}, bf16[128,2048]{1,0:T(8,128)(2,1)S(1)}, u32[]{:S(2)}, u32[]{:S(2)}) %collective-permute-start.42) | collective-permute-done | bytes 524320 | tf_op jit(solution)/shard_map/ppermute | solution.py:56
  297.9 9.0 %collective-permute-done.41.refs_1_ = bf16[128,2048]{1,0:T(8,128)(2,1)S(1)} collective-permute-done((bf16[128,2048]{1,0:T(8,128)(2,1)}, bf16[128,2048]{1,0:T(8,128)(2,1)S(1)}, u32[]{:S(2)}, u32[]{:S(2)}) %collective-permute-start.41) | collective-permute-done | bytes 524320 | tf_op jit(solution)/shard_map/ppermute | solution.py:56
  307.3 3.8 %collective-permute-start.44 = (bf16[64,2048]{1,0:T(8,128)(2,1)S(1)}, bf16[64,2048]{1,0:T(8,128)(2,1)S(1)}, u32[]{:S(2)}, u32[]{:S(2)}) collective-permute-start(bf16[64,2048]{1,0:T(8,128)(2,1)S(1)} %slice.111), channel_id=1, source_target_pairs={{0,3},{1,0},{2,1},{3,2},{4,7},{5,4},{6,5},{7,6},{8,11},{9,8},{10,9... | collective-permute-start | bytes 786440 | tf_op jit(solution)/shard_map/ppermute | solution.py:56
  311.8 6.2 %collective-permute-done.43.refs_3_ = bf16[64,2048]{1,0:T(8,128)(2,1)S(1)} collective-permute-done((bf16[64,2048]{1,0:T(8,128)(2,1)S(1)}, bf16[64,2048]{1,0:T(8,128)(2,1)S(1)}, u32[]{:S(2)}, u32[]{:S(2)}) %collective-permute-start.43) | collective-permute-done | bytes 262176 | tf_op jit(solution)/shard_map/ppermute | solution.py:56
  318.0 4.0 %collective-permute-done.44.refs_4_ = bf16[64,2048]{1,0:T(8,128)(2,1)S(1)} collective-permute-done((bf16[64,2048]{1,0:T(8,128)(2,1)S(1)}, bf16[64,2048]{1,0:T(8,128)(2,1)S(1)}, u32[]{:S(2)}, u32[]{:S(2)}) %collective-permute-start.44) | collective-permute-done | bytes 262176 | tf_op jit(solution)/shard_map/ppermute | solution.py:56
  323.6 23.2 %scores.1 = f32[8,512]{1,0:T(8,128)} custom-call(s32[4]{0:T(128)} %iota_xor_fusion.order_ref, bf16[128,2048]{1,0:T(8,128)(2,1)} %finish.3.refs_0_, bf16[128,2048]{1,0:T(8,128)(2,1)} %copy-done.6, bf16[128,2048]{1,0:T(8,128)(2,1)} %copy-done.5, bf16[64,2048]{1,0:T(8,128)(2,1)} %copy-done.8, bf16[64,2048]{1,0:T(8,128)(2,1)} %copy-done.9, ...), custom_call_target="tpu_custom_call" | custom-call | flops 12000000000 | bytes 60000000 | tf_op jit(solution)/shard_map/scores/pallas_call | solution.py:633
  (213 shorter events, 78.9 us)
Async XLA Ops:
  1.3 3.7 %collective-permute-start.2 = (s32[640]{0:T(1024)S(1)}, s32[640]{0:T(1024)S(1)}, u32[]{:S(2)}, u32[]{:S(2)}) collective-permute-start(s32[640]{0:T(1024)S(1)} %concatenate.9), channel_id=1, source_target_pairs={{0,12},{4,8},{8,4},{12,0},{1,13},{5,9},{9,5},{13,1},{2,14},{6,10},... | collective-permute-start | bytes 7688 | tf_op jit(solution)/shard_map/ppermute | solution.py:685
  3.7 3.6 %collective-permute-start.1 = (s32[640]{0:T(1024)S(1)}, s32[640]{0:T(1024)S(1)}, u32[]{:S(2)}, u32[]{:S(2)}) collective-permute-start(s32[640]{0:T(1024)S(1)} %concatenate.9), channel_id=1, source_target_pairs={{0,8},{4,12},{8,0},{12,4},{1,9},{5,13},{9,1},{13,5},{2,10},{6,14},... | collective-permute-start | bytes 7688 | tf_op jit(solution)/shard_map/ppermute | solution.py:685
  4.4 219.7 %collective-permute-start.32 = (bf16[6400,512]{1,0:T(8,128)(2,1)}, bf16[6400,512]{1,0:T(8,128)(2,1)}, u32[]{:S(2)}, u32[]{:S(2)}) collective-permute-start(bf16[6400,512]{1,0:T(8,128)(2,1)} %refs_13_.1), channel_id=1, source_target_pairs={{0,4},{4,0},{8,12},{12,8},{1,5},{5,1},{9,13},{13,9},{2,6},{6,2},{1... | collective-permute-start | bytes 19660808 | tf_op jit(solution)/shard_map/ppermute | solution.py:790
  16.6 19.6 %collective-permute-start.3 = (bf16[256,512]{1,0:T(8,128)(2,1)}, bf16[256,512]{1,0:T(8,128)(2,1)S(1)}, u32[]{:S(2)}, u32[]{:S(2)}) collective-permute-start(bf16[256,512]{1,0:T(8,128)(2,1)} %get-tuple-element.86), channel_id=1, source_target_pairs={{0,1},{1,2},{2,3},{3,0},{4,5},{5,6},{6,7},{7,4},{8,9},{9,10},{10,1... | collective-permute-start | bytes 786440 | tf_op jit(solution)/shard_map/ppermute | solution.py:56
  18.2 18.1 %collective-permute-start.4 = (bf16[256,512]{1,0:T(8,128)(2,1)}, bf16[256,512]{1,0:T(8,128)(2,1)S(1)}, u32[]{:S(2)}, u32[]{:S(2)}) collective-permute-start(bf16[256,512]{1,0:T(8,128)(2,1)} %get-tuple-element.88), channel_id=1, source_target_pairs={{0,3},{1,0},{2,1},{3,2},{4,7},{5,4},{6,5},{7,6},{8,11},{9,8},{10,9... | collective-permute-start | bytes 786440 | tf_op jit(solution)/shard_map/ppermute | solution.py:56
  34.2 19.6 %collective-permute-start.6 = (bf16[256,512]{1,0:T(8,128)(2,1)}, bf16[256,512]{1,0:T(8,128)(2,1)S(1)}, u32[]{:S(2)}, u32[]{:S(2)}) collective-permute-start(bf16[256,512]{1,0:T(8,128)(2,1)} %get-tuple-element.90), channel_id=1, source_target_pairs={{0,3},{1,0},{2,1},{3,2},{4,7},{5,4},{6,5},{7,6},{8,11},{9,8},{10,9... | collective-permute-start | bytes 786440 | tf_op jit(solution)/shard_map/ppermute | solution.py:56
  36.0 17.8 %collective-permute-start.7 = (bf16[256,512]{1,0:T(8,128)(2,1)}, bf16[256,512]{1,0:T(8,128)(2,1)S(1)}, u32[]{:S(2)}, u32[]{:S(2)}) collective-permute-start(bf16[256,512]{1,0:T(8,128)(2,1)} %get-tuple-element.92), channel_id=1, source_target_pairs={{0,1},{1,2},{2,3},{3,0},{4,5},{5,6},{6,7},{7,4},{8,9},{9,10},{10,1... | collective-permute-start | bytes 786440 | tf_op jit(solution)/shard_map/ppermute | solution.py:56
  39.1 16.0 %collective-permute-start.5 = (bf16[256,512]{1,0:T(8,128)(2,1)}, bf16[256,512]{1,0:T(8,128)(2,1)S(1)}, u32[]{:S(2)}, u32[]{:S(2)}) collective-permute-start(bf16[256,512]{1,0:T(8,128)(2,1)} %get-tuple-element.89), channel_id=1, source_target_pairs={{0,1},{1,2},{2,3},{3,0},{4,5},{5,6},{6,7},{7,4},{8,9},{9,10},{10,1... | collective-permute-start | bytes 786440 | tf_op jit(solution)/shard_map/ppermute | solution.py:56
  39.1 19.4 %collective-permute-start.8 = (bf16[256,512]{1,0:T(8,128)(2,1)}, bf16[256,512]{1,0:T(8,128)(2,1)S(1)}, u32[]{:S(2)}, u32[]{:S(2)}) collective-permute-start(bf16[256,512]{1,0:T(8,128)(2,1)} %get-tuple-element.93), channel_id=1, source_target_pairs={{0,3},{1,0},{2,1},{3,2},{4,7},{5,4},{6,5},{7,6},{8,11},{9,8},{10,9... | collective-permute-start | bytes 786440 | tf_op jit(solution)/shard_map/ppermute | solution.py:56
  61.4 6.6 %collective-permute-start.10 = (bf16[128,512]{1,0:T(8,128)(2,1)}, bf16[128,512]{1,0:T(8,128)(2,1)S(1)}, u32[]{:S(2)}, u32[]{:S(2)}) collective-permute-start(bf16[128,512]{1,0:T(8,128)(2,1)} %get-tuple-element.96), channel_id=1, source_target_pairs={{0,8},{4,12},{8,0},{12,4},{1,9},{5,13},{9,1},{13,5},{2,10},{6,14},... | collective-permute-start | bytes 393224 | tf_op jit(solution)/shard_map/ppermute | solution.py:721
  62.1 7.8 %collective-permute-start.11 = (bf16[128,512]{1,0:T(8,128)(2,1)}, bf16[128,512]{1,0:T(8,128)(2,1)S(1)}, u32[]{:S(2)}, u32[]{:S(2)}) collective-permute-start(bf16[128,512]{1,0:T(8,128)(2,1)} %get-tuple-element.97), channel_id=1, source_target_pairs={{0,12},{4,8},{8,4},{12,0},{1,13},{5,9},{9,5},{13,1},{2,14},{6,10},... | collective-permute-start | bytes 393224 | tf_op jit(solution)/shard_map/ppermute | solution.py:721
  69.8 49.1 %collective-permute-start.16 = (bf16[1280,512]{1,0:T(8,128)(2,1)}, bf16[1280,512]{1,0:T(8,128)(2,1)S(1)}, u32[]{:S(2)}, u32[]{:S(2)}) collective-permute-start(bf16[1280,512]{1,0:T(8,128)(2,1)} %get-tuple-element.114), channel_id=1, source_target_pairs={{0,8},{4,12},{8,0},{12,4},{1,9},{5,13},{9,1},{13,5},{2,10},{6,14},... | collective-permute-start | bytes 3932168 | tf_op jit(solution)/shard_map/ppermute | solution.py:748
  73.3 16.8 %collective-permute-start.13 = (bf16[128,2048]{1,0:T(8,128)(2,1)}, bf16[128,2048]{1,0:T(8,128)(2,1)S(1)}, u32[]{:S(2)}, u32[]{:S(2)}) collective-permute-start(bf16[128,2048]{1,0:T(8,128)(2,1)} %get-tuple-element.103.refs_0_), channel_id=1, source_target_pairs={{0,1},{1,2},{2,3},{3,0},{4,5},{5,6},{6,7},{7,4},{8,9},{9,10},{10,1... | collective-permute-start | bytes 1572872 | tf_op jit(solution)/shard_map/ppermute | solution.py:56
  73.3 25.2 %collective-permute-start.12 = (bf16[128,2048]{1,0:T(8,128)(2,1)}, bf16[128,2048]{1,0:T(8,128)(2,1)S(1)}, u32[]{:S(2)}, u32[]{:S(2)}) collective-permute-start(bf16[128,2048]{1,0:T(8,128)(2,1)} %get-tuple-element.103.refs_0_), channel_id=1, source_target_pairs={{0,3},{1,0},{2,1},{3,2},{4,7},{5,4},{6,5},{7,6},{8,11},{9,8},{10,9... | collective-permute-start | bytes 1572872 | tf_op jit(solution)/shard_map/ppermute | solution.py:56
  90.1 19.4 %collective-permute-start.14 = (bf16[64,2048]{1,0:T(8,128)(2,1)S(1)}, bf16[64,2048]{1,0:T(8,128)(2,1)S(1)}, u32[]{:S(2)}, u32[]{:S(2)}) collective-permute-start(bf16[64,2048]{1,0:T(8,128)(2,1)S(1)} %slice.102), channel_id=1, source_target_pairs={{0,1},{1,2},{2,3},{3,0},{4,5},{5,6},{6,7},{7,4},{8,9},{9,10},{10,1... | collective-permute-start | bytes 786440 | tf_op jit(solution)/shard_map/ppermute | solution.py:56
  98.6 14.6 %collective-permute-start.15 = (bf16[64,2048]{1,0:T(8,128)(2,1)S(1)}, bf16[64,2048]{1,0:T(8,128)(2,1)S(1)}, u32[]{:S(2)}, u32[]{:S(2)}) collective-permute-start(bf16[64,2048]{1,0:T(8,128)(2,1)S(1)} %slice.103), channel_id=1, source_target_pairs={{0,3},{1,0},{2,1},{3,2},{4,7},{5,4},{6,5},{7,6},{8,11},{9,8},{10,9... | collective-permute-start | bytes 786440 | tf_op jit(solution)/shard_map/ppermute | solution.py:56
  118.9 10.9 %collective-permute-start.19 = (bf16[4,176,128]{2,1,0:T(8,128)(2,1)}, bf16[4,176,128]{2,1,0:T(8,128)(2,1)S(1)}, u32[]{:S(2)}, u32[]{:S(2)}) collective-permute-start(bf16[4,176,128]{2,1,0:T(8,128)(2,1)} %get-tuple-element.115), channel_id=1, source_target_pairs={{0,12},{1,13},{2,14},{3,15},{16,28},{17,29},{18,30},{19,31}} | collective-permute-start | bytes 540680 | tf_op jit(solution)/shard_map/ppermute | solution.py:760
  121.7 8.4 %collective-permute-start.18 = (bf16[4,176,128]{2,1,0:T(8,128)(2,1)}, bf16[4,176,128]{2,1,0:T(8,128)(2,1)S(1)}, u32[]{:S(2)}, u32[]{:S(2)}) collective-permute-start(bf16[4,176,128]{2,1,0:T(8,128)(2,1)} %get-tuple-element.115), channel_id=1, source_target_pairs={{0,8},{4,12},{1,9},{5,13},{2,10},{6,14},{3,11},{7,15},{16,24},{20,... | collective-permute-start | bytes 540680 | tf_op jit(solution)/shard_map/ppermute | solution.py:760
  123.0 7.1 %collective-permute-start.17 = (bf16[4,176,128]{2,1,0:T(8,128)(2,1)}, bf16[4,176,128]{2,1,0:T(8,128)(2,1)S(1)}, u32[]{:S(2)}, u32[]{:S(2)}) collective-permute-start(bf16[4,176,128]{2,1,0:T(8,128)(2,1)} %get-tuple-element.115), channel_id=1, source_target_pairs={{0,4},{4,8},{8,12},{1,5},{5,9},{9,13},{2,6},{6,10},{10,14},{3,7},{... | collective-permute-start | bytes 540680 | tf_op jit(solution)/shard_map/ppermute | solution.py:760
  130.1 92.7 %collective-permute-start.30 = (bf16[2560,512]{1,0:T(8,128)(2,1)}, bf16[2560,512]{1,0:T(8,128)(2,1)S(1)}, u32[]{:S(2)}, u32[]{:S(2)}) collective-permute-start(bf16[2560,512]{1,0:T(8,128)(2,1)} %get-tuple-element.132), channel_id=1, source_target_pairs={{0,8},{4,12},{8,0},{12,4},{1,9},{5,13},{9,1},{13,5},{2,10},{6,14},... | collective-permute-start | bytes 7864328 | tf_op jit(solution)/shard_map/ppermute | solution.py:788
  141.9 11.3 %collective-permute-start.20 = (bf16[64,2048]{1,0:T(8,128)(2,1)}, bf16[64,2048]{1,0:T(8,128)(2,1)S(1)}, u32[]{:S(2)}, u32[]{:S(2)}) collective-permute-start(bf16[64,2048]{1,0:T(8,128)(2,1)} %get-tuple-element.119), channel_id=1, source_target_pairs={{0,1},{1,2},{2,3},{3,0},{4,5},{5,6},{6,7},{7,4},{8,9},{9,10},{10,1... | collective-permute-start | bytes 786440 | tf_op jit(solution)/shard_map/ppermute | solution.py:56
  142.8 12.9 %collective-permute-start.21 = (bf16[64,2048]{1,0:T(8,128)(2,1)}, bf16[64,2048]{1,0:T(8,128)(2,1)S(1)}, u32[]{:S(2)}, u32[]{:S(2)}) collective-permute-start(bf16[64,2048]{1,0:T(8,128)(2,1)} %get-tuple-element.121), channel_id=1, source_target_pairs={{0,3},{1,0},{2,1},{3,2},{4,7},{5,4},{6,5},{7,6},{8,11},{9,8},{10,9... | collective-permute-start | bytes 786440 | tf_op jit(solution)/shard_map/ppermute | solution.py:56
  149.6 12.4 %collective-permute-start.23 = (bf16[64,2048]{1,0:T(8,128)(2,1)}, bf16[64,2048]{1,0:T(8,128)(2,1)S(1)}, u32[]{:S(2)}, u32[]{:S(2)}) collective-permute-start(bf16[64,2048]{1,0:T(8,128)(2,1)} %get-tuple-element.123), channel_id=1, source_target_pairs={{0,3},{1,0},{2,1},{3,2},{4,7},{5,4},{6,5},{7,6},{8,11},{9,8},{10,9... | collective-permute-start | bytes 786440 | tf_op jit(solution)/shard_map/ppermute | solution.py:56
  153.1 16.9 %collective-permute-start.24 = (bf16[64,2048]{1,0:T(8,128)(2,1)}, bf16[64,2048]{1,0:T(8,128)(2,1)S(1)}, u32[]{:S(2)}, u32[]{:S(2)}) collective-permute-start(bf16[64,2048]{1,0:T(8,128)(2,1)} %get-tuple-element.125), channel_id=1, source_target_pairs={{0,1},{1,2},{2,3},{3,0},{4,5},{5,6},{6,7},{7,4},{8,9},{9,10},{10,1... | collective-permute-start | bytes 786440 | tf_op jit(solution)/shard_map/ppermute | solution.py:56
  158.5 16.8 %collective-permute-start.22 = (bf16[64,2048]{1,0:T(8,128)(2,1)}, bf16[64,2048]{1,0:T(8,128)(2,1)S(1)}, u32[]{:S(2)}, u32[]{:S(2)}) collective-permute-start(bf16[64,2048]{1,0:T(8,128)(2,1)} %get-tuple-element.122), channel_id=1, source_target_pairs={{0,1},{1,2},{2,3},{3,0},{4,5},{5,6},{6,7},{7,4},{8,9},{9,10},{10,1... | collective-permute-start | bytes 786440 | tf_op jit(solution)/shard_map/ppermute | solution.py:56
  162.0 14.9 %collective-permute-start.25 = (bf16[64,2048]{1,0:T(8,128)(2,1)}, bf16[64,2048]{1,0:T(8,128)(2,1)S(1)}, u32[]{:S(2)}, u32[]{:S(2)}) collective-permute-start(bf16[64,2048]{1,0:T(8,128)(2,1)} %get-tuple-element.126), channel_id=1, source_target_pairs={{0,3},{1,0},{2,1},{3,2},{4,7},{5,4},{6,5},{7,6},{8,11},{9,8},{10,9... | collective-permute-start | bytes 786440 | tf_op jit(solution)/shard_map/ppermute | solution.py:56
  180.5 16.9 %collective-permute-start.27 = (bf16[128,2048]{1,0:T(8,128)(2,1)}, bf16[128,2048]{1,0:T(8,128)(2,1)S(1)}, u32[]{:S(2)}, u32[]{:S(2)}) collective-permute-start(bf16[128,2048]{1,0:T(8,128)(2,1)} %get-tuple-element.129.refs_0_), channel_id=1, source_target_pairs={{0,1},{1,2},{2,3},{3,0},{4,5},{5,6},{6,7},{7,4},{8,9},{9,10},{10,1... | collective-permute-start | bytes 1572872 | tf_op jit(solution)/shard_map/ppermute | solution.py:56
  180.7 24.2 %collective-permute-start.26 = (bf16[128,2048]{1,0:T(8,128)(2,1)}, bf16[128,2048]{1,0:T(8,128)(2,1)S(1)}, u32[]{:S(2)}, u32[]{:S(2)}) collective-permute-start(bf16[128,2048]{1,0:T(8,128)(2,1)} %get-tuple-element.129.refs_0_), channel_id=1, source_target_pairs={{0,3},{1,0},{2,1},{3,2},{4,7},{5,4},{6,5},{7,6},{8,11},{9,8},{10,9... | collective-permute-start | bytes 1572872 | tf_op jit(solution)/shard_map/ppermute | solution.py:56
  184.3 39.8 %collective-permute-start.31 = (bf16[1280,512]{1,0:T(8,128)(2,1)S(1)}, bf16[1280,512]{1,0:T(8,128)(2,1)S(1)}, u32[]{:S(2)}, u32[]{:S(2)}) collective-permute-start(bf16[1280,512]{1,0:T(8,128)(2,1)S(1)} %copy-done.3), channel_id=1, source_target_pairs={{0,4},{4,0},{8,12},{12,8},{1,5},{5,1},{9,13},{13,9},{2,6},{6,2},{1... | collective-permute-start | bytes 3932168 | tf_op jit(solution)/shard_map/ppermute | solution.py:749
  197.4 18.8 %collective-permute-start.28 = (bf16[64,2048]{1,0:T(8,128)(2,1)S(1)}, bf16[64,2048]{1,0:T(8,128)(2,1)S(1)}, u32[]{:S(2)}, u32[]{:S(2)}) collective-permute-start(bf16[64,2048]{1,0:T(8,128)(2,1)S(1)} %slice.104), channel_id=1, source_target_pairs={{0,1},{1,2},{2,3},{3,0},{4,5},{5,6},{6,7},{7,4},{8,9},{9,10},{10,1... | collective-permute-start | bytes 786440 | tf_op jit(solution)/shard_map/ppermute | solution.py:56
  204.9 11.2 %collective-permute-start.29 = (bf16[64,2048]{1,0:T(8,128)(2,1)S(1)}, bf16[64,2048]{1,0:T(8,128)(2,1)S(1)}, u32[]{:S(2)}, u32[]{:S(2)}) collective-permute-start(bf16[64,2048]{1,0:T(8,128)(2,1)S(1)} %slice.105), channel_id=1, source_target_pairs={{0,3},{1,0},{2,1},{3,2},{4,7},{5,4},{6,5},{7,6},{8,11},{9,8},{10,9... | collective-permute-start | bytes 786440 | tf_op jit(solution)/shard_map/ppermute | solution.py:56
  222.8 54.8 %collective-permute-start.40 = (bf16[2560,512]{1,0:T(8,128)(2,1)S(1)}, bf16[2560,512]{1,0:T(8,128)(2,1)}, u32[]{:S(2)}, u32[]{:S(2)}) collective-permute-start(bf16[2560,512]{1,0:T(8,128)(2,1)S(1)} %collective-permute-done.30.refs_11_), channel_id=1, source_target_pairs={{0,4},{4,0},{8,12},{12,8},{1,5},{5,1},{9,13},{13,9},{2,6},{6,2},{1... | collective-permute-start | bytes 7864328 | tf_op jit(solution)/shard_map/ppermute | solution.py:789
  224.1 6.8 %collective-permute-start.33 = (bf16[64,1536]{1,0:T(8,128)(2,1)S(1)}, bf16[64,1536]{1,0:T(8,128)(2,1)S(1)}, u32[]{:S(2)}, u32[]{:S(2)}) collective-permute-start(bf16[64,1536]{1,0:T(8,128)(2,1)S(1)} %fusion.2), channel_id=1, source_target_pairs={{0,4},{4,8},{8,12},{1,5},{5,9},{9,13},{2,6},{6,10},{10,14},{3,7},{... | collective-permute-start | bytes 589832 | tf_op jit(solution)/shard_map/ppermute | solution.py:806
  230.9 76.0 %collective-permute-start.45 = (bf16[2560,512]{1,0:T(8,128)(2,1)}, bf16[2560,512]{1,0:T(8,128)(2,1)}, u32[]{:S(2)}, u32[]{:S(2)}) collective-permute-start(bf16[2560,512]{1,0:T(8,128)(2,1)} %get-tuple-element.159), channel_id=1, source_target_pairs={{0,8},{4,12},{8,0},{12,4},{1,9},{5,13},{9,1},{13,5},{2,10},{6,14},... | collective-permute-start | bytes 7864328 | tf_op jit(solution)/shard_map/ppermute | solution.py:823
  239.7 11.2 %collective-permute-start.34 = (bf16[64,2048]{1,0:T(8,128)(2,1)}, bf16[64,2048]{1,0:T(8,128)(2,1)S(1)}, u32[]{:S(2)}, u32[]{:S(2)}) collective-permute-start(bf16[64,2048]{1,0:T(8,128)(2,1)} %get-tuple-element.140), channel_id=1, source_target_pairs={{0,1},{1,2},{2,3},{3,0},{4,5},{5,6},{6,7},{7,4},{8,9},{9,10},{10,1... | collective-permute-start | bytes 786440 | tf_op jit(solution)/shard_map/ppermute | solution.py:56
  240.4 15.0 %collective-permute-start.35 = (bf16[64,2048]{1,0:T(8,128)(2,1)}, bf16[64,2048]{1,0:T(8,128)(2,1)S(1)}, u32[]{:S(2)}, u32[]{:S(2)}) collective-permute-start(bf16[64,2048]{1,0:T(8,128)(2,1)} %get-tuple-element.142), channel_id=1, source_target_pairs={{0,3},{1,0},{2,1},{3,2},{4,7},{5,4},{6,5},{7,6},{8,11},{9,8},{10,9... | collective-permute-start | bytes 786440 | tf_op jit(solution)/shard_map/ppermute | solution.py:56
  247.3 12.2 %collective-permute-start.37 = (bf16[64,2048]{1,0:T(8,128)(2,1)}, bf16[64,2048]{1,0:T(8,128)(2,1)S(1)}, u32[]{:S(2)}, u32[]{:S(2)}) collective-permute-start(bf16[64,2048]{1,0:T(8,128)(2,1)} %get-tuple-element.144), channel_id=1, source_target_pairs={{0,3},{1,0},{2,1},{3,2},{4,7},{5,4},{6,5},{7,6},{8,11},{9,8},{10,9... | collective-permute-start | bytes 786440 | tf_op jit(solution)/shard_map/ppermute | solution.py:56
  250.9 17.0 %collective-permute-start.38 = (bf16[64,2048]{1,0:T(8,128)(2,1)}, bf16[64,2048]{1,0:T(8,128)(2,1)S(1)}, u32[]{:S(2)}, u32[]{:S(2)}) collective-permute-start(bf16[64,2048]{1,0:T(8,128)(2,1)} %get-tuple-element.146), channel_id=1, source_target_pairs={{0,1},{1,2},{2,3},{3,0},{4,5},{5,6},{6,7},{7,4},{8,9},{9,10},{10,1... | collective-permute-start | bytes 786440 | tf_op jit(solution)/shard_map/ppermute | solution.py:56
  258.2 15.2 %collective-permute-start.36 = (bf16[64,2048]{1,0:T(8,128)(2,1)}, bf16[64,2048]{1,0:T(8,128)(2,1)S(1)}, u32[]{:S(2)}, u32[]{:S(2)}) collective-permute-start(bf16[64,2048]{1,0:T(8,128)(2,1)} %get-tuple-element.143), channel_id=1, source_target_pairs={{0,1},{1,2},{2,3},{3,0},{4,5},{5,6},{6,7},{7,4},{8,9},{9,10},{10,1... | collective-permute-start | bytes 786440 | tf_op jit(solution)/shard_map/ppermute | solution.py:56
  259.5 18.1 %collective-permute-start.39 = (bf16[64,2048]{1,0:T(8,128)(2,1)}, bf16[64,2048]{1,0:T(8,128)(2,1)S(1)}, u32[]{:S(2)}, u32[]{:S(2)}) collective-permute-start(bf16[64,2048]{1,0:T(8,128)(2,1)} %get-tuple-element.147), channel_id=1, source_target_pairs={{0,3},{1,0},{2,1},{3,2},{4,7},{5,4},{6,5},{7,6},{8,11},{9,8},{10,9... | collective-permute-start | bytes 786440 | tf_op jit(solution)/shard_map/ppermute | solution.py:56
  281.1 16.8 %collective-permute-start.42 = (bf16[128,2048]{1,0:T(8,128)(2,1)}, bf16[128,2048]{1,0:T(8,128)(2,1)S(1)}, u32[]{:S(2)}, u32[]{:S(2)}) collective-permute-start(bf16[128,2048]{1,0:T(8,128)(2,1)} %finish.3.refs_0_), channel_id=1, source_target_pairs={{0,1},{1,2},{2,3},{3,0},{4,5},{5,6},{6,7},{7,4},{8,9},{9,10},{10,1... | collective-permute-start | bytes 1572872 | tf_op jit(solution)/shard_map/ppermute | solution.py:56
  281.8 25.1 %collective-permute-start.41 = (bf16[128,2048]{1,0:T(8,128)(2,1)}, bf16[128,2048]{1,0:T(8,128)(2,1)S(1)}, u32[]{:S(2)}, u32[]{:S(2)}) collective-permute-start(bf16[128,2048]{1,0:T(8,128)(2,1)} %finish.3.refs_0_), channel_id=1, source_target_pairs={{0,3},{1,0},{2,1},{3,2},{4,7},{5,4},{6,5},{7,6},{8,11},{9,8},{10,9... | collective-permute-start | bytes 1572872 | tf_op jit(solution)/shard_map/ppermute | solution.py:56
  306.9 15.0 %collective-permute-start.46 = (bf16[2560,512]{1,0:T(8,128)(2,1)}, bf16[2560,512]{1,0:T(8,128)(2,1)S(1)}, u32[]{:S(2)}, u32[]{:S(2)}) collective-permute-start(bf16[2560,512]{1,0:T(8,128)(2,1)} %collective-permute-done.45.refs_15_), channel_id=1, source_target_pairs={{0,4},{4,0},{8,12},{12,8},{1,5},{5,1},{9,13},{13,9},{2,6},{6,2},{1... | collective-permute-start | bytes 7864328 | tf_op jit(solution)/shard_map/ppermute | solution.py:825
  307.0 11.0 %collective-permute-start.43 = (bf16[64,2048]{1,0:T(8,128)(2,1)S(1)}, bf16[64,2048]{1,0:T(8,128)(2,1)S(1)}, u32[]{:S(2)}, u32[]{:S(2)}) collective-permute-start(bf16[64,2048]{1,0:T(8,128)(2,1)S(1)} %slice.110), channel_id=1, source_target_pairs={{0,1},{1,2},{2,3},{3,0},{4,5},{5,6},{6,7},{7,4},{8,9},{9,10},{10,1... | collective-permute-start | bytes 786440 | tf_op jit(solution)/shard_map/ppermute | solution.py:56
  307.3 14.6 %collective-permute-start.44 = (bf16[64,2048]{1,0:T(8,128)(2,1)S(1)}, bf16[64,2048]{1,0:T(8,128)(2,1)S(1)}, u32[]{:S(2)}, u32[]{:S(2)}) collective-permute-start(bf16[64,2048]{1,0:T(8,128)(2,1)S(1)} %slice.111), channel_id=1, source_target_pairs={{0,3},{1,0},{2,1},{3,2},{4,7},{5,4},{6,5},{7,6},{8,11},{9,8},{10,9... | collective-permute-start | bytes 786440 | tf_op jit(solution)/shard_map/ppermute | solution.py:56
  347.5 3.8 %collective-permute-start.49 = (f32[3,128]{1,0:T(4,128)S(1)}, f32[3,128]{1,0:T(4,128)S(1)}, u32[]{:S(2)}, u32[]{:S(2)}) collective-permute-start(f32[3,128]{1,0:T(4,128)S(1)} %get-tuple-element.168), channel_id=1, source_target_pairs={{0,3},{1,0},{2,1},{3,2},{4,7},{5,4},{6,5},{7,6},{8,11},{9,8},{10,9... | collective-permute-start | bytes 4616 | tf_op jit(solution)/shard_map/ppermute | solution.py:56
  349.1 4.5 %collective-permute-start.48 = (f32[3,128]{1,0:T(4,128)S(1)}, f32[3,128]{1,0:T(4,128)S(1)}, u32[]{:S(2)}, u32[]{:S(2)}) collective-permute-start(f32[3,128]{1,0:T(4,128)S(1)} %get-tuple-element.169), channel_id=1, source_target_pairs={{0,2},{1,3},{2,0},{3,1},{4,6},{5,7},{6,4},{7,5},{8,10},{9,11},{10,... | collective-permute-start | bytes 4616 | tf_op jit(solution)/shard_map/ppermute | solution.py:56
  350.7 5.4 %collective-permute-start.47 = (f32[3,128]{1,0:T(4,128)S(1)}, f32[3,128]{1,0:T(4,128)S(1)}, u32[]{:S(2)}, u32[]{:S(2)}) collective-permute-start(f32[3,128]{1,0:T(4,128)S(1)} %get-tuple-element.170), channel_id=1, source_target_pairs={{0,1},{1,2},{2,3},{3,0},{4,5},{5,6},{6,7},{7,4},{8,9},{9,10},{10,1... | collective-permute-start | bytes 4616 | tf_op jit(solution)/shard_map/ppermute | solution.py:56
  (53 other events, 376.6 us)

commit v8 on v7

--- a/solution.py
+++ b/solution.py
@@ -112,13 +112,16 @@
 def lookup_kernel(lots, ids_ref, table_ref, *refs):
     outs, copies, total = refs[: -1 - len(lots)], refs[-1 - len(lots) : -1], refs[-1]
     step = pl.program_id(0)
-    for (start, stop), copy in zip(lots, copies):
-
-        @pl.when((step >= start) & (step < stop))
+    tile = table_ref.shape[0]
+    for at in range(0, TABLE_STEPS * tile if lots else 0, tile):
+
+        @pl.when(step == at // tile)
         def _():
-            copy[...] = table_ref[...]
-
-    tile = table_ref.shape[0]
+            for (start, stop), copy in zip(lots, copies):
+                low, high = max(start, at), min(stop, at + tile)
+                if low < high:
+                    copy[low - start : high - start] = table_ref[low - at : high - at]
+
     count = ids_ref.shape[1]
     ids = jnp.transpose(jnp.broadcast_to(ids_ref[...], (8, count)))[:, 0:1] - step * tile
     hot = (lax.broadcasted_iota(jnp.int32, (count, tile), 1) == ids).astype(F32).astype(BF16)
@@ -155,11 +158,11 @@
         ],
         out_specs=[pl.BlockSpec((count // pieces, width), lambda i: (0, 0))] * pieces
         + [
-            pl.BlockSpec((tile, width), lambda i, start=start, stop=stop: (jnp.clip(i, start, stop - 1) - start, 0))
+            pl.BlockSpec((stop - start, width), lambda i: (0, 0), pipeline_mode=pl.Buffered(1))
             for start, stop in lots
         ],
         out_shape=[jax.ShapeDtypeStruct((count // pieces, width), BF16)] * pieces
-        + [jax.ShapeDtypeStruct(((stop - start) * tile, width), BF16) for start, stop in lots],
+        + [jax.ShapeDtypeStruct((stop - start, width), BF16) for start, stop in lots],
         scratch_shapes=[pltpu.VMEM((count, width), F32)],
         compiler_params=params(),
         cost_estimate=cost(8 * count / 512),
@@ -564,18 +567,40 @@
     )(info, local, first, halo, weight)
 
 
-def score_kernel(units_count, pieces, lots, tile, order_ref, *refs):
-    units, refs = refs[:units_count], refs[units_count:]
+def turn_kernel(*refs):
+    refs[-1][...] = jnp.transpose(jnp.concatenate([ref[...] for ref in refs[:-1]], axis=0))
+
+
+def turn(pieces):
+    rows, width = sum(piece.shape[0] for piece in pieces), pieces[0].shape[1]
+    return pl.pallas_call(
+        turn_kernel,
+        in_specs=[whole()] * len(pieces),
+        out_specs=whole(),
+        out_shape=jax.ShapeDtypeStruct((width, rows), BF16),
+        compiler_params=params(),
+        cost_estimate=cost(3),
+        name="turn",
+    )(*pieces)
+
+
+def score_kernel(ready, rest, common, pieces, lots, tile, order_ref, *refs):
+    early, refs = refs[:ready], refs[ready:]
+    units, refs = refs[:rest], refs[rest:]
+    shared, refs = refs[:common], refs[common:]
     tables, (goal_ref, out_ref, turned_ref, held) = refs[: len(lots) * pieces], refs[len(lots) * pieces :]
     step = pl.program_id(0)
-    width = tables[0].shape[1]
+    width = (shared or tables)[0].shape[1]
     count = goal_ref.shape[1]
     part = 128
 
     @pl.when(step == 0)
     def _():
-        rows = jnp.concatenate([ref[...] for ref in units], axis=0)
-        turned_ref[...] = jnp.transpose(rows)
+        at = 0
+        for ref in early:
+            at = ref.shape[1]
+            turned_ref[:, 0:at] = ref[...]
+        turned_ref[:, at:] = jnp.transpose(jnp.concatenate([ref[...] for ref in units], axis=0))
         held[0] = jnp.full((8, count), NEGATIVE, F32)
         held[1] = jnp.zeros((8, count), F32)
         held[2] = jnp.zeros((8, count), F32)
@@ -585,12 +610,12 @@
         inner = inner + lax.broadcasted_iota(jnp.int32, (part // 8, 8, count), 1)
         peak, total, picked = held[0], held[1], held[2]
         sides = [
-            turned_ref[pl.ds(pl.multiple_of(order_ref[n] * width, width), width), :] for n in range(pieces)
+            turned_ref[pl.ds(pl.multiple_of(order_ref[n] * width, width), width), :] for n in range(len(mine))
         ]
         for at in range(0, tile, part):
             logits = None
-            for n in range(pieces):
-                more = dot(mine[n][at : at + part], sides[n])
+            for table, side in zip(mine, sides):
+                more = dot(table[at : at + part], side)
                 logits = more if logits is None else logits + more
             logits = logits.reshape(part // 8, 8, count)
             goal = (goal_ref[...] - (step * tile + at)).reshape(1, 1, count)
@@ -602,7 +627,7 @@
 
     for lot, (start, stop) in enumerate(lots):
         pl.when((step >= start) & (step < stop))(
-            lambda lot=lot: run(tables[lot * pieces : (lot + 1) * pieces])
+            lambda lot=lot: run(list(shared) + list(tables[lot * pieces : (lot + 1) * pieces]))
         )
 
     @pl.when(step == pl.num_programs(0) - 1)
@@ -613,29 +638,30 @@
         out_ref[...] = jnp.concatenate([peak, total, picked, jnp.zeros((5, count), F32)], axis=0)
 
 
-def scores(order, units, lots, goal):
+def scores(order, early, units, shared, lots, goal):
     count = goal.shape[1]
     rows = lots[-1][1]
     tile = 640
-    pieces = len(lots[0][2])
-    specs, steps = [], []
+    specs = [pl.BlockSpec((tile, table.shape[1]), lambda i: (i, 0)) for table in shared]
+    steps = []
     for first, last, tables in lots:
         start, stop = first // tile, last // tile
         steps.append((start, stop))
         for table in tables:
-            shift = 0 if table.shape[0] == rows else start
             specs.append(
                 pl.BlockSpec(
                     (tile, table.shape[1]),
-                    lambda i, start=start, stop=stop, shift=shift: (jnp.clip(i, start, stop - 1) - shift, 0),
+                    lambda i, start=start, stop=stop: (jnp.clip(i, start, stop - 1) - start, 0),
                 )
             )
-    return pl.pallas_call(
-        functools.partial(score_kernel, len(units), pieces, steps, tile),
-        in_specs=[smem()]
-        + [pl.BlockSpec(piece.shape, lambda i: (0, 0), pipeline_mode=pl.Buffered(1)) for piece in units]
-        + specs
-        + [pl.BlockSpec((1, count), lambda i: (0, 0))],
+    still = [
+        pl.BlockSpec(piece.shape, lambda i: (0, 0), pipeline_mode=pl.Buffered(1)) for piece in early + units
+    ]
+    return pl.pallas_call(
+        functools.partial(
+            score_kernel, len(early), len(units), len(shared), len(lots[0][2]), steps, tile
+        ),
+        in_specs=[smem()] + still + specs + [pl.BlockSpec((1, count), lambda i: (0, 0))],
         out_specs=pl.BlockSpec((8, count), lambda i: (0, 0)),
         grid=(rows // tile,),
         out_shape=jax.ShapeDtypeStruct((8, count), F32),
@@ -643,7 +669,7 @@
         compiler_params=params(),
         cost_estimate=cost(20),
         name="scores",
-    )(order, *units, *[table for lot in lots for table in lot[2]], goal)
+    )(order, *early, *units, *shared, *[table for lot in lots for table in lot[2]], goal)
 
 
 def shards(
@@ -690,8 +716,8 @@
     starts = jnp.sum(jnp.where(order[None, :] == block[:, None], starts[None, :], 0), axis=1)
     bound = doc_start.astype(jnp.int32)
 
-    steps = [(0, 1), (1, 3), (3, TABLE_STEPS)]
-    marks_at = [start * (vocab_rows // TABLE_STEPS) for start, _ in steps] + [vocab_rows]
+    marks_at = [part * (vocab_rows // 10) for part in (0, 3, 8, 10)]
+    bounds = list(zip(marks_at[:-1], marks_at[1:])) if seq_count == 4 else []
     lots = []
 
     ids = (marks[:, :tok_count] - vocab_first).reshape(seq_count, head_count, chunk)
@@ -703,16 +729,19 @@
         outer = lookup(ids_of(2), vocab_table, 2)
 
         def inner():
-            beside = lookup(jnp.concatenate([ids_of(1), ids_of(3)]), vocab_table, 4)
-            own = lookup(ids_of(0), vocab_table, 2, steps)
+            after, before, _ = lax.optimization_barrier((ids_of(1), ids_of(3), outer))
+            half = after.shape[0] // 2
+            next_lower, prev_upper = lookup(jnp.concatenate([after[half:], before[:half]]), vocab_table, 2)
+            next_upper, prev_lower = lookup(jnp.concatenate([after[:half], before[half:]]), vocab_table, 2)
+            own = lookup(ids_of(0), vocab_table, 2, bounds)
             lots.extend(own[2:])
-            return own[:2] + beside
+            return [own[0], own[1], next_upper, next_lower, prev_upper, prev_lower]
 
     else:
         outer = [lookup(ids_of(k), vocab_table, 1)[0] for k in range(1, head_count)]
 
         def inner():
-            own = lookup(ids_of(0), vocab_table, 1, steps)
+            own = lookup(ids_of(0), vocab_table, 1, bounds)
             lots.extend(own[1:])
             return own[:1]
 
@@ -720,7 +749,8 @@
     gathered = [found[0]] + [
         lax.ppermute(found[k], "seq", xor_pairs(seq_count, k)) for k in range(1, seq_count)
     ]
-    lots[0], gathered = lax.optimization_barrier((lots[0], gathered))
+    if lots:
+        lots[0], gathered = lax.optimization_barrier((lots[0], gathered))
     embedded, units = begin(order, norm_gain_one, gathered)
     across_x, corners = [None] * 3, [None] * 3
 
@@ -744,6 +774,24 @@
         )
 
     chunks = gather_rows(units)
+
+    shares = []
+    for back in range(1, seq_count):
+        between = (block > seq_index - back) & (block < seq_index)
+        broken = jnp.sum(jnp.where(between & (starts != tok_count), 1, 0))
+        shares.append(((broken == 0) & (seq_index >= back)).astype(jnp.int32))
+    shares = jnp.stack(shares)
+    previous = jnp.sum(jnp.where(block == seq_index - 1, starts, 0))
+    valid_from = jnp.where(
+        seq_index == 0, tok_count, jnp.where(previous == tok_count, 0, previous)
+    ).astype(jnp.int32)
+    first_spot = jnp.sum(jnp.where(held_at == 0, jnp.arange(head_count) * chunk, 0)).astype(jnp.int32)
+    info = jnp.stack([bound[0], valid_from, first_spot])
+    goals = (target_ids - vocab_first).reshape(head_count, chunk)
+    goal = jnp.concatenate(
+        [lax.dynamic_index_in_dim(goals, (head_index + k) % head_count, 0, False) for k in slots]
+    ).reshape(1, -1)
+    chunks[slots[-1]], shares, info, goal = lax.optimization_barrier((chunks[slots[-1]], shares, info, goal))
     if seq_count == 4:
         across_x[0] = lax.ppermute(lots[0], "seq", xor_pairs(seq_count, 2))
         corners[0] = lax.ppermute(across_x[0], "seq", xor_pairs(seq_count, 1))
@@ -754,20 +802,16 @@
     fqs, fks, vs = zip(*sets)
     if seq_count == 4:
         state, across_x[0] = lax.optimization_barrier((state, across_x[0]))
-    states, shares = [], []
-    for back in range(1, seq_count):
-        states.append(
-            lax.ppermute(state, "seq", [(i, i + back) for i in range(seq_count - back)])
-        )
-        between = (block > seq_index - back) & (block < seq_index)
-        broken = jnp.sum(jnp.where(between & (starts != tok_count), 1, 0))
-        shares.append(((broken == 0) & (seq_index >= back)).astype(jnp.int32))
+    states = [
+        lax.ppermute(state, "seq", [(i, i + back) for i in range(seq_count - back)])
+        for back in range(1, seq_count)
+    ]
     position = list(range(head_count))
     num, den = within(bound, places, position, chunk, fqs, fks, vs, heads)
     mixed, *outer = across(
         bound,
         places,
-        jnp.stack(shares),
+        shares,
         position,
         chunk,
         near,
@@ -780,13 +824,13 @@
         states,
         heads,
     )
+    far_rows = outer
     parts = scatter_rows(outer, lambda: near_chunks(mixed, lin_out, near, chunk))
     units, residual = finish(embedded, norm_gain_two, parts, False)
 
     if seq_count == 4:
-        lots[1], _ = lax.optimization_barrier((lots[1], (states, num)))
+        lots[1], _ = lax.optimization_barrier((lots[1], (states, far_rows)))
         across_x[1] = lax.ppermute(lots[1], "seq", xor_pairs(seq_count, 2))
-        corners[1] = lax.ppermute(across_x[1], "seq", xor_pairs(seq_count, 1))
         beside = lax.ppermute(vocab_table, "seq", xor_pairs(seq_count, 1))
 
     chunks = gather_rows(units)
@@ -804,14 +848,10 @@
             (tail, across_x[1], corners[0], beside)
         )
     halo = lax.ppermute(tail, "seq", [(i, i + 1) for i in range(seq_count - 1)])
-    previous = jnp.sum(jnp.where(block == seq_index - 1, starts, 0))
-    valid_from = jnp.where(
-        seq_index == 0, tok_count, jnp.where(previous == tok_count, 0, previous)
-    ).astype(jnp.int32)
-    first_spot = jnp.sum(jnp.where(held_at == 0, jnp.arange(head_count) * chunk, 0)).astype(jnp.int32)
     local, first = local_window(bound, places, slots, spots, chunk, qkvs, heads)
-    lots[2], local, halo = lax.optimization_barrier((lots[2], local, halo))
-    info = jnp.stack([bound[0], valid_from, first_spot])
+    if lots:
+        lots[2], local, halo, across_x[1] = lax.optimization_barrier((lots[2], local, halo, across_x[1]))
+        corners[1] = lax.ppermute(across_x[1], "seq", xor_pairs(seq_count, 1))
     mixed, *outer = halo_window(info, near, chunk, far, local, first, halo, win_out, heads)
     parts = scatter_rows(outer, lambda: near_chunks(mixed, win_out, near, chunk))
     if seq_count == 4:
@@ -821,20 +861,18 @@
     chunks = gather_rows(units)
     if seq_count == 4:
         across_x[2] = lax.ppermute(lots[2], "seq", xor_pairs(seq_count, 2))
-        corner, _ = lax.optimization_barrier((across_x[2], (chunks[1][0], chunks[-1][0])))
+        corner, _ = lax.optimization_barrier((across_x[2], parts))
         corners[2] = lax.ppermute(corner, "seq", xor_pairs(seq_count, 1))
-        lots = [
-            (marks_at[n], marks_at[n + 1], [vocab_table, beside, across_x[n], corners[n]])
-            for n in range(3)
-        ]
+        shared = [vocab_table, beside]
+        lots = [(marks_at[n], marks_at[n + 1], [across_x[n], corners[n]]) for n in range(3)]
     else:
-        lots = [(0, vocab_rows, [lax.all_gather(vocab_table, "seq", axis=1, tiled=True)])]
+        shared = [lax.all_gather(vocab_table, "seq", axis=1, tiled=True)]
+        lots = [(0, vocab_rows, [])]
         order = jnp.zeros((1,), jnp.int32)
-    goals = (target_ids - vocab_first).reshape(head_count, chunk)
-    goal = jnp.concatenate(
-        [lax.dynamic_index_in_dim(goals, (head_index + k) % head_count, 0, False) for k in slots]
-    ).reshape(1, -1)
-    triple = scores(order, [piece for k in slots for piece in chunks[k]], lots, goal)
+    first = slots[:-1] if chunk % LANES == 0 else []
+    rest = [piece for k in slots[len(first) :] for piece in chunks[k]]
+    first = [turn([piece for k in first for piece in chunks[k]])] if first else []
+    triple = scores(order, first, rest, shared, lots, goal)
     found = {k: triple[:3, at * chunk : (at + 1) * chunk] for at, k in enumerate(slots)}
 
     shares = jnp.stack([found[0]] + [turned(found[k], k) for k in range(1, head_count)])

time: 358 us -> 352 us (0.983)
  waiting for transfers between devices: 135 us -> 116 us
  Pallas kernels: 121 us -> 128 us
  starting transfers between devices: 72.7 us -> 77.6 us
    ppermute x33, waiting for transfers between devices: 127 us -> 106 us  [turned(): lax.ppermute(value, 'head', [(i, (i + step) % size) for i in range(size)])]
    ppermute x33, starting transfers between devices: 52.5 us -> 57.7 us  [turned(): lax.ppermute(value, 'head', [(i, (i + step) % size) for i in range(size)])]
    pallas_call x3 -> x4, Pallas kernels: 32.6 us -> 36.8 us  [lookup(): pl.pallas_call(functools.partial(lookup_kernel, lots), grid=(TABLE_STEPS,...]
    ppermute x1, starting transfers between devices: 0.07 us -> 3.67 us  [shards(): corners[1] = lax.ppermute(across_x[1], 'seq', xor_pairs(seq_count, 1))]
    pallas_call x1 -> x2, Pallas kernels: 23.2 us -> 24.9 us  [the longest x1 22 us: scores(): pl.pallas_call(functools.partial(score_kernel, len(early), len(units), le...]
    unnamed x102 -> x106, local copies, waits for them, and re-layouts: 8.19 us -> 8.62 us
  transfers between devices with their start and end apart: 50 -> 50, of which waited for: 31 -> 29; matrix products, arithmetic and copies ran while one was open for 3% -> 3% of each run, Pallas kernels for 27% -> 30%
where the time goes in v8:
time: 352 us; the launch traced here: 350 us
  Pallas kernels  128 us (36%)
  waiting for transfers between devices  116 us (33%)
  starting transfers between devices  77.6 us (22%)
  local copies, waits for them, and re-layouts  14.9 us (4%)
  other arithmetic  7.38 us (2%)
  between operations  6.78 us (2%)
    ppermute x33, waiting for transfers between devices, turned(): lax.ppermute(value, 'head', [(i, (i + step) % size) for i in range(size)])  106 us
    ppermute x33, starting transfers between devices, turned(): lax.ppermute(value, 'head', [(i, (i + step) % size) for i in range(size)])  57.7 us
    pallas_call x4, Pallas kernels, lookup(): pl.pallas_call(functools.partial(lookup_kernel, lots), grid=(TABLE_STEPS,...  36.8 us
    pallas_call x1, Pallas kernels, scores(): pl.pallas_call(functools.partial(score_kernel, len(early), len(units), le...  22 us
    pallas_call x2, Pallas kernels, matmul(): pl.pallas_call(matmul_kernel, grid=(b.shape[1] // tile,), in_specs=[pl.Bl...  12.5 us
    pallas_call x2, Pallas kernels, project(): pl.pallas_call(functools.partial(project_kernel, heads, slots, chunk, cou...  11.6 us
    unnamed x106, local copies, waits for them, and re-layouts  8.62 us
    pallas_call x2, Pallas kernels, near_chunks(): pl.pallas_call(functools.partial(near_kernel, rows), in_specs=[whole()] *...  7.86 us
  transfers between devices with their start and end apart: 50, of which 29 were waited for; matrix products, arithmetic and copies ran while one was open for 3% of the time, Pallas kernels for 30%

profile of v8, /device:TPU:0, one launch (start us, length us, event | category | flops | bytes accessed | tf_op | source)
XLA Modules:
  0.0 350.4 jit_solution(9049477856876433711)
XLA Ops:
  1.3 2.4 collective-permute-start.2
  8.0 8.6 %lookup.5 = (bf16[256,512]{1,0:T(8,128)(2,1)}, bf16[256,512]{1,0:T(8,128)(2,1)}) custom-call(s32[1,512]{1,0:T(1,128)} %bitcast.49, bf16[6400,512]{1,0:T(8,128)(2,1)} %refs_3_.6), custom_call_target="tpu_custom_call" | custom-call | flops 4800000000 | bytes 24000000 | tf_op jit(solution)/shard_map/lookup/pallas_call | solution.py:152
  21.0 8.6 %lookup.7 = (bf16[256,512]{1,0:T(8,128)(2,1)}, bf16[256,512]{1,0:T(8,128)(2,1)}) custom-call(s32[1,512]{1,0:T(1,128)} %bitcast.51, bf16[6400,512]{1,0:T(8,128)(2,1)} %refs_3_.6), custom_call_target="tpu_custom_call" | custom-call | flops 4800000000 | bytes 24000000 | tf_op jit(solution)/shard_map/lookup/pallas_call | solution.py:152
  32.2 8.6 %lookup.6 = (bf16[256,512]{1,0:T(8,128)(2,1)}, bf16[256,512]{1,0:T(8,128)(2,1)}) custom-call(s32[1,512]{1,0:T(1,128)} %bitcast.52, bf16[6400,512]{1,0:T(8,128)(2,1)} %refs_3_.6), custom_call_target="tpu_custom_call" | custom-call | flops 4800000000 | bytes 24000000 | tf_op jit(solution)/shard_map/lookup/pallas_call | solution.py:152
  43.6 3.8 %collective-permute-start.8 = (bf16[256,512]{1,0:T(8,128)(2,1)}, bf16[256,512]{1,0:T(8,128)(2,1)S(1)}, u32[]{:S(2)}, u32[]{:S(2)}) collective-permute-start(bf16[256,512]{1,0:T(8,128)(2,1)} %get-tuple-element.103), channel_id=1, source_target_pairs={{0,3},{1,0},{2,1},{3,2},{4,7},{5,4},{6,5},{7,6},{8,11},{9,8},{10,9... | collective-permute-start | bytes 786440 | tf_op jit(solution)/shard_map/ppermute | solution.py:56
  47.5 11.1 %lookup.4 = (bf16[256,512]{1,0:T(8,128)(2,1)}, bf16[256,512]{1,0:T(8,128)(2,1)}, bf16[1920,512]{1,0:T(8,128)(2,1)}, bf16[3200,512]{1,0:T(8,128)(2,1)}, bf16[1280,512]{1,0:T(8,128)(2,1)}) custom-call(s32[1,512]{1,0:T(1,128)} %bitcast.45, bf16[6400,512]{1,0:T(8,128)(2,1)} %refs_3_.6), custom_call_target="tpu_custom_call" | custom-call | flops 4800000000 | bytes 24000000 | tf_op jit(solution)/shard_map/lookup/pallas_call | solution.py:152
  63.7 4.7 %collective-permute-done.10.refs_2_ = bf16[128,512]{1,0:T(8,128)(2,1)S(1)} collective-permute-done((bf16[128,512]{1,0:T(8,128)(2,1)}, bf16[128,512]{1,0:T(8,128)(2,1)S(1)}, u32[]{:S(2)}, u32[]{:S(2)}) %collective-permute-start.10) | collective-permute-done | bytes 131104 | tf_op jit(solution)/shard_map/ppermute | solution.py:750
  84.9 6.0 %collective-permute-done.14.refs_1_ = bf16[128,2048]{1,0:T(8,128)(2,1)S(1)} collective-permute-done((bf16[128,2048]{1,0:T(8,128)(2,1)}, bf16[128,2048]{1,0:T(8,128)(2,1)S(1)}, u32[]{:S(2)}, u32[]{:S(2)}) %collective-permute-start.14) | collective-permute-done | bytes 524320 | tf_op jit(solution)/shard_map/ppermute | solution.py:56
  90.9 4.0 %collective-permute-start.15 = (bf16[64,2048]{1,0:T(8,128)(2,1)S(1)}, bf16[64,2048]{1,0:T(8,128)(2,1)S(1)}, u32[]{:S(2)}, u32[]{:S(2)}) collective-permute-start(bf16[64,2048]{1,0:T(8,128)(2,1)S(1)} %slice.119), channel_id=1, source_target_pairs={{0,3},{1,0},{2,1},{3,2},{4,7},{5,4},{6,5},{7,6},{8,11},{9,8},{10,9... | collective-permute-start | bytes 786440 | tf_op jit(solution)/shard_map/ppermute | solution.py:56
  94.9 7.4 %collective-permute-done.12.refs_2_ = bf16[128,2048]{1,0:T(8,128)(2,1)S(1)} collective-permute-done((bf16[128,2048]{1,0:T(8,128)(2,1)}, bf16[128,2048]{1,0:T(8,128)(2,1)S(1)}, u32[]{:S(2)}, u32[]{:S(2)}) %collective-permute-start.12) | collective-permute-done | bytes 524320 | tf_op jit(solution)/shard_map/ppermute | solution.py:56
  104.5 6.5 %project.2 = (bf16[4,384,256]{2,1,0:T(8,128)(2,1)}, bf16[4,384,256]{2,1,0:T(8,128)(2,1)}, bf16[384,512]{1,0:T(8,128)(2,1)}, f32[4,176,128]{2,1,0:T(8,128)}) custom-call(s32[1]{0:T(128)} %copy.35.bound_ref, s32[3]{0:T(128)} %bitcast.53, bf16[128,2048]{1,0:T(8,128)(2,1)} %get-tuple-element.113.refs_0_, bf16[128,2048]{1,0:T(8,128)(2,1)} %copy-done.1, ...), custom_call_target="tpu_custom_call" | custom-call | flops 3000000000 | bytes 15000000 | tf_op jit(solution)/shard_map/project/pallas_call | solution.py:327
  113.5 5.1 %project.3 = (bf16[4,128,256]{2,1,0:T(8,128)(2,1)}, bf16[4,128,256]{2,1,0:T(8,128)(2,1)}, bf16[128,512]{1,0:T(8,128)(2,1)}, bf16[4,176,128]{2,1,0:T(8,128)(2,1)}) custom-call(s32[1]{0:T(128)} %copy.35.bound_ref, s32[1]{0:T(128)} %slice.97.places_ref, bf16[64,2048]{1,0:T(8,128)(2,1)} %copy-done.40, bf16[64,2048]{1,0:T(8,128)(2,1)} %copy-done.35, ...), custom_call_target="tpu_custom_call" | custom-call | flops 3000000000 | bytes 15000000 | tf_op jit(solution)/shard_map/project/pallas_call | solution.py:327
  118.6 2.3 collective-permute-start.19
  124.2 4.6 %within.1 = (f32[4,512,128]{2,1,0:T(8,128)}, f32[4,512,8]{2,1,0:T(8,128)}) custom-call(s32[1]{0:T(128)} %copy.35.bound_ref, s32[4]{0:T(128)} %copy-done.52, bf16[4,384,256]{2,1,0:T(8,128)(2,1)} %get-tuple-element.115.refs_0_, bf16[4,128,256]{2,1,0:T(8,128)(2,1)} %get-tuple-element.119.refs_1_, bf16[4,384,256]{2,1,0:T(8,128)(2,1)} %get-tuple-element.120.refs_2_, ...), custom_call_target="tpu_custom_call" | custom-call | flops 2700000000 | bytes 13500000 | tf_op jit(solution)/shard_map/within/pallas_call | solution.py:366
  130.0 4.8 %across.1 = (bf16[512,512]{1,0:T(8,128)(2,1)}, bf16[64,2048]{1,0:T(8,128)(2,1)}, bf16[64,2048]{1,0:T(8,128)(2,1)}) custom-call(s32[1]{0:T(128)} %copy.35.bound_ref, s32[4]{0:T(128)} %copy-done.52, s32[3]{0:T(128)} %add_convert_fusion.share_ref, bf16[4,384,256]{2,1,0:T(8,128)(2,1)} %get-tuple-element.115.refs_0_, ...), custom_call_target="tpu_custom_call" | custom-call | flops 2700000000 | bytes 13500000 | tf_op jit(solution)/shard_map/across/pallas_call | solution.py:415
  134.8 3.0 collective-permute-start.30
  141.6 4.0 %near.2 = (bf16[64,2048]{1,0:T(8,128)(2,1)}, bf16[64,2048]{1,0:T(8,128)(2,1)}, bf16[64,2048]{1,0:T(8,128)(2,1)}, bf16[64,2048]{1,0:T(8,128)(2,1)}, bf16[64,2048]{1,0:T(8,128)(2,1)}, /*index=5*/bf16[64,2048]{1,0:T(8,128)(2,1)}) custom-call(bf16[512,512]{1,0:T(8,128)(2,1)} %get-tuple-element.129.mixed_ref, bf16[512,2048]{1,0:T(8,128)(2,1)} %weight_ref.3), custom_call_target="tpu_custom_call" | custom-call | flops 2400000000 | bytes 12000000 | tf_op jit(solution)/shard_map/near/pallas_call | solution.py:434
  149.0 6.3 %collective-permute-start.24 = (bf16[64,2048]{1,0:T(8,128)(2,1)}, bf16[64,2048]{1,0:T(8,128)(2,1)S(1)}, u32[]{:S(2)}, u32[]{:S(2)}) collective-permute-start(bf16[64,2048]{1,0:T(8,128)(2,1)} %get-tuple-element.138), channel_id=1, source_target_pairs={{0,1},{1,2},{2,3},{3,0},{4,5},{5,6},{6,7},{7,4},{8,9},{9,10},{10,1... | collective-permute-start | bytes 786440 | tf_op jit(solution)/shard_map/ppermute | solution.py:56
  162.7 2.6 collective-permute-start.25
  166.0 5.0 %collective-permute-done.22.refs_1_ = bf16[64,2048]{1,0:T(8,128)(2,1)S(1)} collective-permute-done((bf16[64,2048]{1,0:T(8,128)(2,1)}, bf16[64,2048]{1,0:T(8,128)(2,1)S(1)}, u32[]{:S(2)}, u32[]{:S(2)}) %collective-permute-start.22) | collective-permute-done | bytes 262176 | tf_op jit(solution)/shard_map/ppermute | solution.py:56
  171.0 3.7 %collective-permute-done.25.refs_5_ = bf16[64,2048]{1,0:T(8,128)(2,1)S(1)} collective-permute-done((bf16[64,2048]{1,0:T(8,128)(2,1)}, bf16[64,2048]{1,0:T(8,128)(2,1)S(1)}, u32[]{:S(2)}, u32[]{:S(2)}) %collective-permute-start.25) | collective-permute-done | bytes 262176 | tf_op jit(solution)/shard_map/ppermute | solution.py:56
  175.4 2.8 finish.2
  178.6 3.5 collective-permute-start.26
  185.2 9.9 %collective-permute-done.27.refs_2_ = bf16[128,2048]{1,0:T(8,128)(2,1)S(1)} collective-permute-done((bf16[128,2048]{1,0:T(8,128)(2,1)}, bf16[128,2048]{1,0:T(8,128)(2,1)S(1)}, u32[]{:S(2)}, u32[]{:S(2)}) %collective-permute-start.27) | collective-permute-done | bytes 524320 | tf_op jit(solution)/shard_map/ppermute | solution.py:56
  195.1 7.9 %collective-permute-done.26.refs_1_ = bf16[128,2048]{1,0:T(8,128)(2,1)S(1)} collective-permute-done((bf16[128,2048]{1,0:T(8,128)(2,1)}, bf16[128,2048]{1,0:T(8,128)(2,1)S(1)}, u32[]{:S(2)}, u32[]{:S(2)}) %collective-permute-start.26) | collective-permute-done | bytes 524320 | tf_op jit(solution)/shard_map/ppermute | solution.py:56
  203.1 3.7 %collective-permute-start.29 = (bf16[64,2048]{1,0:T(8,128)(2,1)S(1)}, bf16[64,2048]{1,0:T(8,128)(2,1)S(1)}, u32[]{:S(2)}, u32[]{:S(2)}) collective-permute-start(bf16[64,2048]{1,0:T(8,128)(2,1)S(1)} %slice.121), channel_id=1, source_target_pairs={{0,3},{1,0},{2,1},{3,2},{4,7},{5,4},{6,5},{7,6},{8,11},{9,8},{10,9... | collective-permute-start | bytes 786440 | tf_op jit(solution)/shard_map/ppermute | solution.py:56
  206.8 7.2 %matmul.2.refs_0_ = bf16[384,1536]{1,0:T(8,128)(2,1)} custom-call(bf16[128,2048]{1,0:T(8,128)(2,1)} %get-tuple-element.143.refs_0_, bf16[128,2048]{1,0:T(8,128)(2,1)} %copy-done.4, bf16[128,2048]{1,0:T(8,128)(2,1)} %copy-done.3, bf16[2048,1536]{1,0:T(8,128)(2,1)} %refs_2_.3), custom_call_target="tpu_custom_call" | custom-call | flops 3000000000 | bytes 15000000 | tf_op jit(solution)/shard_map/matmul/pallas_call | solution.py:453
  215.8 5.2 %matmul.3.refs_1_ = bf16[128,1536]{1,0:T(8,128)(2,1)} custom-call(bf16[64,2048]{1,0:T(8,128)(2,1)} %copy-done.41, bf16[64,2048]{1,0:T(8,128)(2,1)} %copy-done.43, bf16[2048,1536]{1,0:T(8,128)(2,1)} %refs_2_.3), custom_call_target="tpu_custom_call" | custom-call | flops 3000000000 | bytes 15000000 | tf_op jit(solution)/shard_map/matmul/pallas_call | solution.py:453
  223.5 4.8 %local_window.1 = (bf16[512,512]{1,0:T(8,128)(2,1)}, bf16[64,1536]{1,0:T(8,128)(2,1)}) custom-call(s32[1]{0:T(128)} %copy.35.bound_ref, s32[4]{0:T(128)} %copy-done.52, bf16[384,1536]{1,0:T(8,128)(2,1)} %matmul.2.refs_0_, bf16[128,1536]{1,0:T(8,128)(2,1)} %matmul.3.refs_1_), custom_call_target="tpu_custom_call" | custom-call | flops 4800000000 | bytes 24000000 | tf_op jit(solution)/shard_map/local_window/pallas_call | solution.py:521
  228.3 3.7 %collective-permute-start.40 = (bf16[3200,512]{1,0:T(8,128)(2,1)}, bf16[3200,512]{1,0:T(8,128)(2,1)S(1)}, u32[]{:S(2)}, u32[]{:S(2)}) collective-permute-start(bf16[3200,512]{1,0:T(8,128)(2,1)} %collective-permute-done.30.refs_7_), channel_id=1, source_target_pairs={{0,4},{4,0},{8,12},{12,8},{1,5},{5,1},{9,13},{13,9},{2,6},{6,2},{1... | collective-permute-start | bytes 9830408 | tf_op jit(solution)/shard_map/ppermute | solution.py:854
  232.1 3.6 %halo_window.1 = (bf16[512,512]{1,0:T(8,128)(2,1)}, bf16[64,2048]{1,0:T(8,128)(2,1)}, bf16[64,2048]{1,0:T(8,128)(2,1)}) custom-call(s32[3]{0:T(128)} %pad_add_fusion.4.info_ref, bf16[512,512]{1,0:T(8,128)(2,1)} %get-tuple-element.149.local_ref, bf16[64,1536]{1,0:T(8,128)(2,1)} %get-tuple-element.150.first_ref, bf16[64,1536]{1,0:T(8,128)(2,1)} %copy-done.44, ...), custom_call_target="tpu_custom_call" | custom-call | flops 2700000000 | bytes 13500000 | tf_op jit(solution)/shard_map/halo_window/pallas_call | solution.py:558
  236.7 2.9 collective-permute-start.35
  239.6 3.9 %near.3 = (bf16[64,2048]{1,0:T(8,128)(2,1)}, bf16[64,2048]{1,0:T(8,128)(2,1)}, bf16[64,2048]{1,0:T(8,128)(2,1)}, bf16[64,2048]{1,0:T(8,128)(2,1)}, bf16[64,2048]{1,0:T(8,128)(2,1)}, /*index=5*/bf16[64,2048]{1,0:T(8,128)(2,1)}) custom-call(bf16[512,512]{1,0:T(8,128)(2,1)} %get-tuple-element.152.mixed_ref, bf16[512,2048]{1,0:T(8,128)(2,1)} %weight_ref.5), custom_call_target="tpu_custom_call" | custom-call | flops 2400000000 | bytes 12000000 | tf_op jit(solution)/shard_map/near/pallas_call | solution.py:434
  243.5 3.5 collective-permute-done.34.before_ref
  247.0 4.7 %collective-permute-done.35.after_ref = bf16[64,2048]{1,0:T(8,128)(2,1)S(1)} collective-permute-done((bf16[64,2048]{1,0:T(8,128)(2,1)}, bf16[64,2048]{1,0:T(8,128)(2,1)S(1)}, u32[]{:S(2)}, u32[]{:S(2)}) %collective-permute-start.35) | collective-permute-done | bytes 262176 | tf_op jit(solution)/shard_map/ppermute | solution.py:56
  256.5 2.6 collective-permute-start.39
  259.1 4.9 %collective-permute-done.38.refs_4_ = bf16[64,2048]{1,0:T(8,128)(2,1)S(1)} collective-permute-done((bf16[64,2048]{1,0:T(8,128)(2,1)}, bf16[64,2048]{1,0:T(8,128)(2,1)S(1)}, u32[]{:S(2)}, u32[]{:S(2)}) %collective-permute-start.38) | collective-permute-done | bytes 262176 | tf_op jit(solution)/shard_map/ppermute | solution.py:56
  264.0 5.5 %collective-permute-done.36.refs_1_ = bf16[64,2048]{1,0:T(8,128)(2,1)S(1)} collective-permute-done((bf16[64,2048]{1,0:T(8,128)(2,1)}, bf16[64,2048]{1,0:T(8,128)(2,1)S(1)}, u32[]{:S(2)}, u32[]{:S(2)}) %collective-permute-start.36) | collective-permute-done | bytes 262176 | tf_op jit(solution)/shard_map/ppermute | solution.py:56
  269.5 5.1 %collective-permute-done.39.refs_5_ = bf16[64,2048]{1,0:T(8,128)(2,1)S(1)} collective-permute-done((bf16[64,2048]{1,0:T(8,128)(2,1)}, bf16[64,2048]{1,0:T(8,128)(2,1)S(1)}, u32[]{:S(2)}, u32[]{:S(2)}) %collective-permute-start.39) | collective-permute-done | bytes 262176 | tf_op jit(solution)/shard_map/ppermute | solution.py:56
  276.5 2.8 finish.3.refs_0_
  279.9 3.3 collective-permute-start.41
  283.1 13.0 %collective-permute-done.42.refs_2_ = bf16[128,2048]{1,0:T(8,128)(2,1)S(1)} collective-permute-done((bf16[128,2048]{1,0:T(8,128)(2,1)}, bf16[128,2048]{1,0:T(8,128)(2,1)S(1)}, u32[]{:S(2)}, u32[]{:S(2)}) %collective-permute-start.42) | collective-permute-done | bytes 524320 | tf_op jit(solution)/shard_map/ppermute | solution.py:56
  296.2 8.9 %collective-permute-done.41.refs_1_ = bf16[128,2048]{1,0:T(8,128)(2,1)S(1)} collective-permute-done((bf16[128,2048]{1,0:T(8,128)(2,1)}, bf16[128,2048]{1,0:T(8,128)(2,1)S(1)}, u32[]{:S(2)}, u32[]{:S(2)}) %collective-permute-start.41) | collective-permute-done | bytes 524320 | tf_op jit(solution)/shard_map/ppermute | solution.py:56
  305.2 2.8 collective-permute-start.44
  308.0 2.9 turn.1.refs_0_
  313.0 4.6 %collective-permute-done.44.refs_2_ = bf16[64,2048]{1,0:T(8,128)(2,1)S(1)} collective-permute-done((bf16[64,2048]{1,0:T(8,128)(2,1)S(1)}, bf16[64,2048]{1,0:T(8,128)(2,1)S(1)}, u32[]{:S(2)}, u32[]{:S(2)}) %collective-permute-start.44) | collective-permute-done | bytes 262176 | tf_op jit(solution)/shard_map/ppermute | solution.py:56
  319.5 22.0 %scores.1 = f32[8,512]{1,0:T(8,128)} custom-call(s32[4]{0:T(128)} %iota_xor_fusion.order_ref, bf16[2048,384]{1,0:T(8,128)(2,1)} %turn.1.refs_0_, bf16[64,2048]{1,0:T(8,128)(2,1)} %copy-done.33, bf16[64,2048]{1,0:T(8,128)(2,1)} %copy-done.39, bf16[6400,512]{1,0:T(8,128)(2,1)} %refs_3_.6, bf16[6400,512]{1,0:T(8,128)(2,1)} %collective-permute-done.32.refs_4_, ...), custom_call_target="tpu_custom_call" | custom-call | flops 12000000000 | bytes 60000000 | tf_op jit(solution)/shard_map/scores/pallas_call | solution.py:660
  347.5 2.3 collective-permute-done.47
  (221 shorter events, 82.5 us)
Async XLA Ops:
  1.3 3.7 %collective-permute-start.2 = (s32[640]{0:T(1024)S(1)}, s32[640]{0:T(1024)S(1)}, u32[]{:S(2)}, u32[]{:S(2)}) collective-permute-start(s32[640]{0:T(1024)S(1)} %concatenate.12), channel_id=1, source_target_pairs={{0,12},{4,8},{8,4},{12,0},{1,13},{5,9},{9,5},{13,1},{2,14},{6,10},... | collective-permute-start | bytes 7688 | tf_op jit(solution)/shard_map/ppermute | solution.py:711
  3.7 3.6 %collective-permute-start.1 = (s32[640]{0:T(1024)S(1)}, s32[640]{0:T(1024)S(1)}, u32[]{:S(2)}, u32[]{:S(2)}) collective-permute-start(s32[640]{0:T(1024)S(1)} %concatenate.12), channel_id=1, source_target_pairs={{0,8},{4,12},{8,0},{12,4},{1,9},{5,13},{9,1},{13,5},{2,10},{6,14},... | collective-permute-start | bytes 7688 | tf_op jit(solution)/shard_map/ppermute | solution.py:711
  4.4 217.6 %collective-permute-start.32 = (bf16[6400,512]{1,0:T(8,128)(2,1)}, bf16[6400,512]{1,0:T(8,128)(2,1)}, u32[]{:S(2)}, u32[]{:S(2)}) collective-permute-start(bf16[6400,512]{1,0:T(8,128)(2,1)} %refs_3_.6), channel_id=1, source_target_pairs={{0,4},{4,0},{8,12},{12,8},{1,5},{5,1},{9,13},{13,9},{2,6},{6,2},{1... | collective-permute-start | bytes 19660808 | tf_op jit(solution)/shard_map/ppermute | solution.py:834
  16.6 24.2 %collective-permute-start.3 = (bf16[256,512]{1,0:T(8,128)(2,1)}, bf16[256,512]{1,0:T(8,128)(2,1)S(1)}, u32[]{:S(2)}, u32[]{:S(2)}) collective-permute-start(bf16[256,512]{1,0:T(8,128)(2,1)} %get-tuple-element.93), channel_id=1, source_target_pairs={{0,1},{1,2},{2,3},{3,0},{4,5},{5,6},{6,7},{7,4},{8,9},{9,10},{10,1... | collective-permute-start | bytes 786440 | tf_op jit(solution)/shard_map/ppermute | solution.py:56
  18.2 22.6 %collective-permute-start.4 = (bf16[256,512]{1,0:T(8,128)(2,1)}, bf16[256,512]{1,0:T(8,128)(2,1)S(1)}, u32[]{:S(2)}, u32[]{:S(2)}) collective-permute-start(bf16[256,512]{1,0:T(8,128)(2,1)} %get-tuple-element.94), channel_id=1, source_target_pairs={{0,3},{1,0},{2,1},{3,2},{4,7},{5,4},{6,5},{7,6},{8,11},{9,8},{10,9... | collective-permute-start | bytes 786440 | tf_op jit(solution)/shard_map/ppermute | solution.py:56
  29.6 29.0 %collective-permute-start.6 = (bf16[256,512]{1,0:T(8,128)(2,1)}, bf16[256,512]{1,0:T(8,128)(2,1)S(1)}, u32[]{:S(2)}, u32[]{:S(2)}) collective-permute-start(bf16[256,512]{1,0:T(8,128)(2,1)} %get-tuple-element.100), channel_id=1, source_target_pairs={{0,3},{1,0},{2,1},{3,2},{4,7},{5,4},{6,5},{7,6},{8,11},{9,8},{10,9... | collective-permute-start | bytes 786440 | tf_op jit(solution)/shard_map/ppermute | solution.py:56
  31.4 27.2 %collective-permute-start.7 = (bf16[256,512]{1,0:T(8,128)(2,1)}, bf16[256,512]{1,0:T(8,128)(2,1)S(1)}, u32[]{:S(2)}, u32[]{:S(2)}) collective-permute-start(bf16[256,512]{1,0:T(8,128)(2,1)} %get-tuple-element.102), channel_id=1, source_target_pairs={{0,1},{1,2},{2,3},{3,0},{4,5},{5,6},{6,7},{7,4},{8,9},{9,10},{10,1... | collective-permute-start | bytes 786440 | tf_op jit(solution)/shard_map/ppermute | solution.py:56
  43.6 15.0 %collective-permute-start.5 = (bf16[256,512]{1,0:T(8,128)(2,1)}, bf16[256,512]{1,0:T(8,128)(2,1)S(1)}, u32[]{:S(2)}, u32[]{:S(2)}) collective-permute-start(bf16[256,512]{1,0:T(8,128)(2,1)} %get-tuple-element.99), channel_id=1, source_target_pairs={{0,1},{1,2},{2,3},{3,0},{4,5},{5,6},{6,7},{7,4},{8,9},{9,10},{10,1... | collective-permute-start | bytes 786440 | tf_op jit(solution)/shard_map/ppermute | solution.py:56
  43.6 15.0 %collective-permute-start.8 = (bf16[256,512]{1,0:T(8,128)(2,1)}, bf16[256,512]{1,0:T(8,128)(2,1)S(1)}, u32[]{:S(2)}, u32[]{:S(2)}) collective-permute-start(bf16[256,512]{1,0:T(8,128)(2,1)} %get-tuple-element.103), channel_id=1, source_target_pairs={{0,3},{1,0},{2,1},{3,2},{4,7},{5,4},{6,5},{7,6},{8,11},{9,8},{10,9... | collective-permute-start | bytes 786440 | tf_op jit(solution)/shard_map/ppermute | solution.py:56
  61.8 6.5 %collective-permute-start.10 = (bf16[128,512]{1,0:T(8,128)(2,1)}, bf16[128,512]{1,0:T(8,128)(2,1)S(1)}, u32[]{:S(2)}, u32[]{:S(2)}) collective-permute-start(bf16[128,512]{1,0:T(8,128)(2,1)} %get-tuple-element.106), channel_id=1, source_target_pairs={{0,8},{4,12},{8,0},{12,4},{1,9},{5,13},{9,1},{13,5},{2,10},{6,14},... | collective-permute-start | bytes 393224 | tf_op jit(solution)/shard_map/ppermute | solution.py:750
  62.4 7.9 %collective-permute-start.11 = (bf16[128,512]{1,0:T(8,128)(2,1)}, bf16[128,512]{1,0:T(8,128)(2,1)S(1)}, u32[]{:S(2)}, u32[]{:S(2)}) collective-permute-start(bf16[128,512]{1,0:T(8,128)(2,1)} %get-tuple-element.107), channel_id=1, source_target_pairs={{0,12},{4,8},{8,4},{12,0},{1,13},{5,9},{9,5},{13,1},{2,14},{6,10},... | collective-permute-start | bytes 393224 | tf_op jit(solution)/shard_map/ppermute | solution.py:750
  70.3 48.2 %collective-permute-start.16 = (bf16[1920,512]{1,0:T(8,128)(2,1)}, bf16[1920,512]{1,0:T(8,128)(2,1)S(1)}, u32[]{:S(2)}, u32[]{:S(2)}) collective-permute-start(bf16[1920,512]{1,0:T(8,128)(2,1)} %get-tuple-element.127), channel_id=1, source_target_pairs={{0,8},{4,12},{8,0},{12,4},{1,9},{5,13},{9,1},{13,5},{2,10},{6,14},... | collective-permute-start | bytes 5898248 | tf_op jit(solution)/shard_map/ppermute | solution.py:796
  76.2 14.7 %collective-permute-start.14 = (bf16[128,2048]{1,0:T(8,128)(2,1)}, bf16[128,2048]{1,0:T(8,128)(2,1)S(1)}, u32[]{:S(2)}, u32[]{:S(2)}) collective-permute-start(bf16[128,2048]{1,0:T(8,128)(2,1)} %get-tuple-element.113.refs_0_), channel_id=1, source_target_pairs={{0,3},{1,0},{2,1},{3,2},{4,7},{5,4},{6,5},{7,6},{8,11},{9,8},{10,9... | collective-permute-start | bytes 1572872 | tf_op jit(solution)/shard_map/ppermute | solution.py:56
  78.0 24.3 %collective-permute-start.12 = (bf16[128,2048]{1,0:T(8,128)(2,1)}, bf16[128,2048]{1,0:T(8,128)(2,1)S(1)}, u32[]{:S(2)}, u32[]{:S(2)}) collective-permute-start(bf16[128,2048]{1,0:T(8,128)(2,1)} %get-tuple-element.113.refs_0_), channel_id=1, source_target_pairs={{0,1},{1,2},{2,3},{3,0},{4,5},{5,6},{6,7},{7,4},{8,9},{9,10},{10,1... | collective-permute-start | bytes 1572872 | tf_op jit(solution)/shard_map/ppermute | solution.py:56
  90.9 20.1 %collective-permute-start.15 = (bf16[64,2048]{1,0:T(8,128)(2,1)S(1)}, bf16[64,2048]{1,0:T(8,128)(2,1)S(1)}, u32[]{:S(2)}, u32[]{:S(2)}) collective-permute-start(bf16[64,2048]{1,0:T(8,128)(2,1)S(1)} %slice.119), channel_id=1, source_target_pairs={{0,3},{1,0},{2,1},{3,2},{4,7},{5,4},{6,5},{7,6},{8,11},{9,8},{10,9... | collective-permute-start | bytes 786440 | tf_op jit(solution)/shard_map/ppermute | solution.py:56
  102.3 10.5 %collective-permute-start.13 = (bf16[64,2048]{1,0:T(8,128)(2,1)S(1)}, bf16[64,2048]{1,0:T(8,128)(2,1)S(1)}, u32[]{:S(2)}, u32[]{:S(2)}) collective-permute-start(bf16[64,2048]{1,0:T(8,128)(2,1)S(1)} %slice.118), channel_id=1, source_target_pairs={{0,1},{1,2},{2,3},{3,0},{4,5},{5,6},{6,7},{7,4},{8,9},{9,10},{10,1... | collective-permute-start | bytes 786440 | tf_op jit(solution)/shard_map/ppermute | solution.py:56
  118.6 10.3 %collective-permute-start.19 = (bf16[4,176,128]{2,1,0:T(8,128)(2,1)}, bf16[4,176,128]{2,1,0:T(8,128)(2,1)S(1)}, u32[]{:S(2)}, u32[]{:S(2)}) collective-permute-start(bf16[4,176,128]{2,1,0:T(8,128)(2,1)} %get-tuple-element.128), channel_id=1, source_target_pairs={{0,12},{1,13},{2,14},{3,15},{16,28},{17,29},{18,30},{19,31}} | collective-permute-start | bytes 540680 | tf_op jit(solution)/shard_map/ppermute | solution.py:806
  120.9 8.4 %collective-permute-start.18 = (bf16[4,176,128]{2,1,0:T(8,128)(2,1)}, bf16[4,176,128]{2,1,0:T(8,128)(2,1)S(1)}, u32[]{:S(2)}, u32[]{:S(2)}) collective-permute-start(bf16[4,176,128]{2,1,0:T(8,128)(2,1)} %get-tuple-element.128), channel_id=1, source_target_pairs={{0,8},{4,12},{1,9},{5,13},{2,10},{6,14},{3,11},{7,15},{16,24},{20,... | collective-permute-start | bytes 540680 | tf_op jit(solution)/shard_map/ppermute | solution.py:806
  122.6 6.7 %collective-permute-start.17 = (bf16[4,176,128]{2,1,0:T(8,128)(2,1)}, bf16[4,176,128]{2,1,0:T(8,128)(2,1)S(1)}, u32[]{:S(2)}, u32[]{:S(2)}) collective-permute-start(bf16[4,176,128]{2,1,0:T(8,128)(2,1)} %get-tuple-element.128), channel_id=1, source_target_pairs={{0,4},{4,8},{8,12},{1,5},{5,9},{9,13},{2,6},{6,10},{10,14},{3,7},{... | collective-permute-start | bytes 540680 | tf_op jit(solution)/shard_map/ppermute | solution.py:806
  134.8 87.2 %collective-permute-start.30 = (bf16[3200,512]{1,0:T(8,128)(2,1)S(1)}, bf16[3200,512]{1,0:T(8,128)(2,1)}, u32[]{:S(2)}, u32[]{:S(2)}) collective-permute-start(bf16[3200,512]{1,0:T(8,128)(2,1)S(1)} %copy-done.13), channel_id=1, source_target_pairs={{0,8},{4,12},{8,0},{12,4},{1,9},{5,13},{9,1},{13,5},{2,10},{6,14},... | collective-permute-start | bytes 9830408 | tf_op jit(solution)/shard_map/ppermute | solution.py:833
  137.8 11.3 %collective-permute-start.20 = (bf16[64,2048]{1,0:T(8,128)(2,1)}, bf16[64,2048]{1,0:T(8,128)(2,1)S(1)}, u32[]{:S(2)}, u32[]{:S(2)}) collective-permute-start(bf16[64,2048]{1,0:T(8,128)(2,1)} %get-tuple-element.132), channel_id=1, source_target_pairs={{0,1},{1,2},{2,3},{3,0},{4,5},{5,6},{6,7},{7,4},{8,9},{9,10},{10,1... | collective-permute-start | bytes 786440 | tf_op jit(solution)/shard_map/ppermute | solution.py:56
  139.3 16.0 %collective-permute-start.21 = (bf16[64,2048]{1,0:T(8,128)(2,1)}, bf16[64,2048]{1,0:T(8,128)(2,1)S(1)}, u32[]{:S(2)}, u32[]{:S(2)}) collective-permute-start(bf16[64,2048]{1,0:T(8,128)(2,1)} %get-tuple-element.134), channel_id=1, source_target_pairs={{0,3},{1,0},{2,1},{3,2},{4,7},{5,4},{6,5},{7,6},{8,11},{9,8},{10,9... | collective-permute-start | bytes 786440 | tf_op jit(solution)/shard_map/ppermute | solution.py:56
  145.6 14.1 %collective-permute-start.23 = (bf16[64,2048]{1,0:T(8,128)(2,1)}, bf16[64,2048]{1,0:T(8,128)(2,1)S(1)}, u32[]{:S(2)}, u32[]{:S(2)}) collective-permute-start(bf16[64,2048]{1,0:T(8,128)(2,1)} %get-tuple-element.136), channel_id=1, source_target_pairs={{0,3},{1,0},{2,1},{3,2},{4,7},{5,4},{6,5},{7,6},{8,11},{9,8},{10,9... | collective-permute-start | bytes 786440 | tf_op jit(solution)/shard_map/ppermute | solution.py:56
  149.0 13.7 %collective-permute-start.24 = (bf16[64,2048]{1,0:T(8,128)(2,1)}, bf16[64,2048]{1,0:T(8,128)(2,1)S(1)}, u32[]{:S(2)}, u32[]{:S(2)}) collective-permute-start(bf16[64,2048]{1,0:T(8,128)(2,1)} %get-tuple-element.138), channel_id=1, source_target_pairs={{0,1},{1,2},{2,3},{3,0},{4,5},{5,6},{6,7},{7,4},{8,9},{9,10},{10,1... | collective-permute-start | bytes 786440 | tf_op jit(solution)/shard_map/ppermute | solution.py:56
  155.4 66.6 %collective-permute-start.31 = (bf16[1920,512]{1,0:T(8,128)(2,1)S(1)}, bf16[1920,512]{1,0:T(8,128)(2,1)}, u32[]{:S(2)}, u32[]{:S(2)}) collective-permute-start(bf16[1920,512]{1,0:T(8,128)(2,1)S(1)} %copy-done.16), channel_id=1, source_target_pairs={{0,4},{4,0},{8,12},{12,8},{1,5},{5,1},{9,13},{13,9},{2,6},{6,2},{1... | collective-permute-start | bytes 5898248 | tf_op jit(solution)/shard_map/ppermute | solution.py:797
  159.7 11.2 %collective-permute-start.22 = (bf16[64,2048]{1,0:T(8,128)(2,1)}, bf16[64,2048]{1,0:T(8,128)(2,1)S(1)}, u32[]{:S(2)}, u32[]{:S(2)}) collective-permute-start(bf16[64,2048]{1,0:T(8,128)(2,1)} %get-tuple-element.135), channel_id=1, source_target_pairs={{0,1},{1,2},{2,3},{3,0},{4,5},{5,6},{6,7},{7,4},{8,9},{9,10},{10,1... | collective-permute-start | bytes 786440 | tf_op jit(solution)/shard_map/ppermute | solution.py:56
  162.7 11.9 %collective-permute-start.25 = (bf16[64,2048]{1,0:T(8,128)(2,1)}, bf16[64,2048]{1,0:T(8,128)(2,1)S(1)}, u32[]{:S(2)}, u32[]{:S(2)}) collective-permute-start(bf16[64,2048]{1,0:T(8,128)(2,1)} %get-tuple-element.139), channel_id=1, source_target_pairs={{0,3},{1,0},{2,1},{3,2},{4,7},{5,4},{6,5},{7,6},{8,11},{9,8},{10,9... | collective-permute-start | bytes 786440 | tf_op jit(solution)/shard_map/ppermute | solution.py:56
  178.2 16.9 %collective-permute-start.27 = (bf16[128,2048]{1,0:T(8,128)(2,1)}, bf16[128,2048]{1,0:T(8,128)(2,1)S(1)}, u32[]{:S(2)}, u32[]{:S(2)}) collective-permute-start(bf16[128,2048]{1,0:T(8,128)(2,1)} %get-tuple-element.143.refs_0_), channel_id=1, source_target_pairs={{0,1},{1,2},{2,3},{3,0},{4,5},{5,6},{6,7},{7,4},{8,9},{9,10},{10,1... | collective-permute-start | bytes 1572872 | tf_op jit(solution)/shard_map/ppermute | solution.py:56
  178.6 24.5 %collective-permute-start.26 = (bf16[128,2048]{1,0:T(8,128)(2,1)}, bf16[128,2048]{1,0:T(8,128)(2,1)S(1)}, u32[]{:S(2)}, u32[]{:S(2)}) collective-permute-start(bf16[128,2048]{1,0:T(8,128)(2,1)} %get-tuple-element.143.refs_0_), channel_id=1, source_target_pairs={{0,3},{1,0},{2,1},{3,2},{4,7},{5,4},{6,5},{7,6},{8,11},{9,8},{10,9... | collective-permute-start | bytes 1572872 | tf_op jit(solution)/shard_map/ppermute | solution.py:56
  195.1 19.0 %collective-permute-start.28 = (bf16[64,2048]{1,0:T(8,128)(2,1)S(1)}, bf16[64,2048]{1,0:T(8,128)(2,1)S(1)}, u32[]{:S(2)}, u32[]{:S(2)}) collective-permute-start(bf16[64,2048]{1,0:T(8,128)(2,1)S(1)} %slice.120), channel_id=1, source_target_pairs={{0,1},{1,2},{2,3},{3,0},{4,5},{5,6},{6,7},{7,4},{8,9},{9,10},{10,1... | collective-permute-start | bytes 786440 | tf_op jit(solution)/shard_map/ppermute | solution.py:56
  203.1 12.0 %collective-permute-start.29 = (bf16[64,2048]{1,0:T(8,128)(2,1)S(1)}, bf16[64,2048]{1,0:T(8,128)(2,1)S(1)}, u32[]{:S(2)}, u32[]{:S(2)}) collective-permute-start(bf16[64,2048]{1,0:T(8,128)(2,1)S(1)} %slice.121), channel_id=1, source_target_pairs={{0,3},{1,0},{2,1},{3,2},{4,7},{5,4},{6,5},{7,6},{8,11},{9,8},{10,9... | collective-permute-start | bytes 786440 | tf_op jit(solution)/shard_map/ppermute | solution.py:56
  222.1 6.3 %collective-permute-start.33 = (bf16[64,1536]{1,0:T(8,128)(2,1)S(1)}, bf16[64,1536]{1,0:T(8,128)(2,1)S(1)}, u32[]{:S(2)}, u32[]{:S(2)}) collective-permute-start(bf16[64,1536]{1,0:T(8,128)(2,1)S(1)} %fusion.2), channel_id=1, source_target_pairs={{0,4},{4,8},{8,12},{1,5},{5,9},{9,13},{2,6},{6,10},{10,14},{3,7},{... | collective-permute-start | bytes 589832 | tf_op jit(solution)/shard_map/ppermute | solution.py:850
  228.3 46.3 %collective-permute-start.40 = (bf16[3200,512]{1,0:T(8,128)(2,1)}, bf16[3200,512]{1,0:T(8,128)(2,1)S(1)}, u32[]{:S(2)}, u32[]{:S(2)}) collective-permute-start(bf16[3200,512]{1,0:T(8,128)(2,1)} %collective-permute-done.30.refs_7_), channel_id=1, source_target_pairs={{0,4},{4,0},{8,12},{12,8},{1,5},{5,1},{9,13},{13,9},{2,6},{6,2},{1... | collective-permute-start | bytes 9830408 | tf_op jit(solution)/shard_map/ppermute | solution.py:854
  232.0 43.3 %collective-permute-start.45 = (bf16[1280,512]{1,0:T(8,128)(2,1)S(1)}, bf16[1280,512]{1,0:T(8,128)(2,1)S(1)}, u32[]{:S(2)}, u32[]{:S(2)}) collective-permute-start(bf16[1280,512]{1,0:T(8,128)(2,1)S(1)} %copy-done.17), channel_id=1, source_target_pairs={{0,8},{4,12},{8,0},{12,4},{1,9},{5,13},{9,1},{13,5},{2,10},{6,14},... | collective-permute-start | bytes 3932168 | tf_op jit(solution)/shard_map/ppermute | solution.py:863
  235.8 11.2 %collective-permute-start.34 = (bf16[64,2048]{1,0:T(8,128)(2,1)}, bf16[64,2048]{1,0:T(8,128)(2,1)S(1)}, u32[]{:S(2)}, u32[]{:S(2)}) collective-permute-start(bf16[64,2048]{1,0:T(8,128)(2,1)} %get-tuple-element.155), channel_id=1, source_target_pairs={{0,1},{1,2},{2,3},{3,0},{4,5},{5,6},{6,7},{7,4},{8,9},{9,10},{10,1... | collective-permute-start | bytes 786440 | tf_op jit(solution)/shard_map/ppermute | solution.py:56
  236.7 15.0 %collective-permute-start.35 = (bf16[64,2048]{1,0:T(8,128)(2,1)}, bf16[64,2048]{1,0:T(8,128)(2,1)S(1)}, u32[]{:S(2)}, u32[]{:S(2)}) collective-permute-start(bf16[64,2048]{1,0:T(8,128)(2,1)} %get-tuple-element.157), channel_id=1, source_target_pairs={{0,3},{1,0},{2,1},{3,2},{4,7},{5,4},{6,5},{7,6},{8,11},{9,8},{10,9... | collective-permute-start | bytes 786440 | tf_op jit(solution)/shard_map/ppermute | solution.py:56
  243.5 13.0 %collective-permute-start.37 = (bf16[64,2048]{1,0:T(8,128)(2,1)}, bf16[64,2048]{1,0:T(8,128)(2,1)S(1)}, u32[]{:S(2)}, u32[]{:S(2)}) collective-permute-start(bf16[64,2048]{1,0:T(8,128)(2,1)} %get-tuple-element.159), channel_id=1, source_target_pairs={{0,3},{1,0},{2,1},{3,2},{4,7},{5,4},{6,5},{7,6},{8,11},{9,8},{10,9... | collective-permute-start | bytes 786440 | tf_op jit(solution)/shard_map/ppermute | solution.py:56
  247.0 17.0 %collective-permute-start.38 = (bf16[64,2048]{1,0:T(8,128)(2,1)}, bf16[64,2048]{1,0:T(8,128)(2,1)S(1)}, u32[]{:S(2)}, u32[]{:S(2)}) collective-permute-start(bf16[64,2048]{1,0:T(8,128)(2,1)} %get-tuple-element.161), channel_id=1, source_target_pairs={{0,1},{1,2},{2,3},{3,0},{4,5},{5,6},{6,7},{7,4},{8,9},{9,10},{10,1... | collective-permute-start | bytes 786440 | tf_op jit(solution)/shard_map/ppermute | solution.py:56
  254.4 15.1 %collective-permute-start.36 = (bf16[64,2048]{1,0:T(8,128)(2,1)}, bf16[64,2048]{1,0:T(8,128)(2,1)S(1)}, u32[]{:S(2)}, u32[]{:S(2)}) collective-permute-start(bf16[64,2048]{1,0:T(8,128)(2,1)} %get-tuple-element.158), channel_id=1, source_target_pairs={{0,1},{1,2},{2,3},{3,0},{4,5},{5,6},{6,7},{7,4},{8,9},{9,10},{10,1... | collective-permute-start | bytes 786440 | tf_op jit(solution)/shard_map/ppermute | solution.py:56
  256.5 18.1 %collective-permute-start.39 = (bf16[64,2048]{1,0:T(8,128)(2,1)}, bf16[64,2048]{1,0:T(8,128)(2,1)S(1)}, u32[]{:S(2)}, u32[]{:S(2)}) collective-permute-start(bf16[64,2048]{1,0:T(8,128)(2,1)} %get-tuple-element.162), channel_id=1, source_target_pairs={{0,3},{1,0},{2,1},{3,2},{4,7},{5,4},{6,5},{7,6},{8,11},{9,8},{10,9... | collective-permute-start | bytes 786440 | tf_op jit(solution)/shard_map/ppermute | solution.py:56
  275.3 42.4 %collective-permute-start.46 = (bf16[1280,512]{1,0:T(8,128)(2,1)S(1)}, bf16[1280,512]{1,0:T(8,128)(2,1)S(1)}, u32[]{:S(2)}, u32[]{:S(2)}) collective-permute-start(bf16[1280,512]{1,0:T(8,128)(2,1)S(1)} %collective-permute-done.45.refs_9_), channel_id=1, source_target_pairs={{0,4},{4,0},{8,12},{12,8},{1,5},{5,1},{9,13},{13,9},{2,6},{6,2},{1... | collective-permute-start | bytes 3932168 | tf_op jit(solution)/shard_map/ppermute | solution.py:865
  279.3 16.9 %collective-permute-start.42 = (bf16[128,2048]{1,0:T(8,128)(2,1)}, bf16[128,2048]{1,0:T(8,128)(2,1)S(1)}, u32[]{:S(2)}, u32[]{:S(2)}) collective-permute-start(bf16[128,2048]{1,0:T(8,128)(2,1)} %finish.3.refs_0_), channel_id=1, source_target_pairs={{0,1},{1,2},{2,3},{3,0},{4,5},{5,6},{6,7},{7,4},{8,9},{9,10},{10,1... | collective-permute-start | bytes 1572872 | tf_op jit(solution)/shard_map/ppermute | solution.py:56
  279.9 25.3 %collective-permute-start.41 = (bf16[128,2048]{1,0:T(8,128)(2,1)}, bf16[128,2048]{1,0:T(8,128)(2,1)S(1)}, u32[]{:S(2)}, u32[]{:S(2)}) collective-permute-start(bf16[128,2048]{1,0:T(8,128)(2,1)} %finish.3.refs_0_), channel_id=1, source_target_pairs={{0,3},{1,0},{2,1},{3,2},{4,7},{5,4},{6,5},{7,6},{8,11},{9,8},{10,9... | collective-permute-start | bytes 1572872 | tf_op jit(solution)/shard_map/ppermute | solution.py:56
  296.2 16.9 %collective-permute-start.43 = (bf16[64,2048]{1,0:T(8,128)(2,1)S(1)}, bf16[64,2048]{1,0:T(8,128)(2,1)S(1)}, u32[]{:S(2)}, u32[]{:S(2)}) collective-permute-start(bf16[64,2048]{1,0:T(8,128)(2,1)S(1)} %slice.126), channel_id=1, source_target_pairs={{0,1},{1,2},{2,3},{3,0},{4,5},{5,6},{6,7},{7,4},{8,9},{9,10},{10,1... | collective-permute-start | bytes 786440 | tf_op jit(solution)/shard_map/ppermute | solution.py:56
  305.2 12.5 %collective-permute-start.44 = (bf16[64,2048]{1,0:T(8,128)(2,1)S(1)}, bf16[64,2048]{1,0:T(8,128)(2,1)S(1)}, u32[]{:S(2)}, u32[]{:S(2)}) collective-permute-start(bf16[64,2048]{1,0:T(8,128)(2,1)S(1)} %slice.127), channel_id=1, source_target_pairs={{0,3},{1,0},{2,1},{3,2},{4,7},{5,4},{6,5},{7,6},{8,11},{9,8},{10,9... | collective-permute-start | bytes 786440 | tf_op jit(solution)/shard_map/ppermute | solution.py:56
  342.2 3.6 %collective-permute-start.49 = (f32[3,128]{1,0:T(4,128)S(1)}, f32[3,128]{1,0:T(4,128)S(1)}, u32[]{:S(2)}, u32[]{:S(2)}) collective-permute-start(f32[3,128]{1,0:T(4,128)S(1)} %get-tuple-element.184), channel_id=1, source_target_pairs={{0,3},{1,0},{2,1},{3,2},{4,7},{5,4},{6,5},{7,6},{8,11},{9,8},{10,9... | collective-permute-start | bytes 4616 | tf_op jit(solution)/shard_map/ppermute | solution.py:56
  343.0 4.5 %collective-permute-start.48 = (f32[3,128]{1,0:T(4,128)S(1)}, f32[3,128]{1,0:T(4,128)S(1)}, u32[]{:S(2)}, u32[]{:S(2)}) collective-permute-start(f32[3,128]{1,0:T(4,128)S(1)} %get-tuple-element.185), channel_id=1, source_target_pairs={{0,2},{1,3},{2,0},{3,1},{4,6},{5,7},{6,4},{7,5},{8,10},{9,11},{10,... | collective-permute-start | bytes 4616 | tf_op jit(solution)/shard_map/ppermute | solution.py:56
  344.4 5.4 %collective-permute-start.47 = (f32[3,128]{1,0:T(4,128)S(1)}, f32[3,128]{1,0:T(4,128)S(1)}, u32[]{:S(2)}, u32[]{:S(2)}) collective-permute-start(f32[3,128]{1,0:T(4,128)S(1)} %get-tuple-element.186), channel_id=1, source_target_pairs={{0,1},{1,2},{2,3},{3,0},{4,5},{5,6},{6,7},{7,4},{8,9},{9,10},{10,1... | collective-permute-start | bytes 4616 | tf_op jit(solution)/shard_map/ppermute | solution.py:56
  (55 other events, 343.2 us)

commit v9 on v8

--- a/solution.py
+++ b/solution.py
@@ -56,17 +56,25 @@
     return lax.ppermute(value, "head", [(i, (i + step) % size) for i in range(size)])
 
 
-def gather_rows(own):
+def gather_rows(upper, lower):
     size = lax.axis_size("head")
     if size != 4:
-        full = lax.all_gather(own, "head")
+        full = lax.all_gather(jnp.concatenate([upper, lower]), "head")
         here = lax.axis_index("head")
-        return [[own]] + [
+        return [[upper, lower]] + [
             [lax.dynamic_index_in_dim(full, (here + k) % size, 0, False)] for k in range(1, size)
         ]
-    half = own.shape[0] // 2
-    before, after = turned(own, 1), turned(own, -1)
-    return [[own], [after], [turned(before[:half], 1), turned(after[half:], -1)], [before]]
+    before_upper, after_upper = turned(upper, 1), turned(upper, -1)
+    after_lower, before_lower = turned(lower, -1), turned(lower, 1)
+    far = [turned(before_upper, 1), turned(after_lower, -1)]
+    return [[upper, lower], [after_upper, after_lower], far, [before_upper, before_lower]]
+
+
+def in_halves(terms):
+    if len(terms) == 2:
+        return terms
+    half = terms[0][0].shape[0] // 2
+    return [[term[:half] for term in terms[0]], [term[half:] for term in terms[0]]]
 
 
 def scatter_rows(far, near):
@@ -205,23 +213,25 @@
 
 
 def begin_kernel(pieces, order_ref, gain_ref, *refs):
-    ins, (embedded_ref, units_ref, held) = refs[:pieces], refs[pieces:]
-    width = ins[0].shape[1]
+    ins, outs, held = refs[:pieces], refs[pieces:-1], refs[-1]
     for n in range(pieces):
         held[order_ref[n]] = ins[n][...]
     values = jnp.concatenate([held[n] for n in range(pieces)], axis=1)
-    embedded_ref[...] = values
-    units_ref[...] = rms(values.astype(F32), gain_ref[...])
+    units = rms(values.astype(F32), gain_ref[...])
+    half = outs[0].shape[0]
+    for n in range(2):
+        outs[n][...] = values[n * half : (n + 1) * half]
+        outs[2 + n][...] = units[n * half : (n + 1) * half]
 
 
 def begin(order, gain, pieces):
     rows, width = pieces[0].shape
-    full = jax.ShapeDtypeStruct((rows, width * len(pieces)), BF16)
+    half = jax.ShapeDtypeStruct((rows // 2, width * len(pieces)), BF16)
     return pl.pallas_call(
         functools.partial(begin_kernel, len(pieces)),
         in_specs=[smem()] + [whole()] * (1 + len(pieces)),
-        out_specs=[whole()] * 2,
-        out_shape=[full, full],
+        out_specs=[whole()] * 4,
+        out_shape=[half] * 4,
         scratch_shapes=[pltpu.VMEM((len(pieces), rows, width), BF16)],
         compiler_params=params(),
         cost_estimate=cost(2),
@@ -229,9 +239,8 @@
     )(order, gain.reshape(1, -1), *pieces)
 
 
-def finish_kernel(sizes, last, residual_ref, gain_ref, *refs):
-    parts = sum(sizes)
-    total = gathered_sum(refs[:parts], sizes) + residual_ref[...].astype(F32)
+def finish_kernel(parts, last, residual_ref, gain_ref, *refs):
+    total = gathered_sum(refs[:parts], [parts]) + residual_ref[...].astype(F32)
     if not last:
         total = total.astype(BF16)
         refs[parts + 1][...] = total
@@ -240,16 +249,15 @@
 
 def finish(residual, gain, terms, last):
     full = jax.ShapeDtypeStruct(residual.shape, BF16)
-    parts = [term for part in terms for term in part]
-    return pl.pallas_call(
-        functools.partial(finish_kernel, [len(part) for part in terms], last),
-        in_specs=[whole()] * (2 + len(parts)),
+    return pl.pallas_call(
+        functools.partial(finish_kernel, len(terms), last),
+        in_specs=[whole()] * (2 + len(terms)),
         out_specs=[whole()] * (1 if last else 2),
         out_shape=[full] * (1 if last else 2),
         compiler_params=params(),
-        cost_estimate=cost(2.5),
+        cost_estimate=cost(2),
         name="finish",
-    )(residual, gain.reshape(1, -1), *parts)
+    )(residual, gain, *terms)
 
 
 def selectors():
@@ -751,7 +759,7 @@
     ]
     if lots:
         lots[0], gathered = lax.optimization_barrier((lots[0], gathered))
-    embedded, units = begin(order, norm_gain_one, gathered)
+    *embedded, upper, lower = begin(order, norm_gain_one, gathered)
     across_x, corners = [None] * 3, [None] * 3
 
     constants = selectors()
@@ -773,7 +781,7 @@
             heads,
         )
 
-    chunks = gather_rows(units)
+    chunks = gather_rows(upper, lower)
 
     shares = []
     for back in range(1, seq_count):
@@ -791,7 +799,11 @@
     goal = jnp.concatenate(
         [lax.dynamic_index_in_dim(goals, (head_index + k) % head_count, 0, False) for k in slots]
     ).reshape(1, -1)
-    chunks[slots[-1]], shares, info, goal = lax.optimization_barrier((chunks[slots[-1]], shares, info, goal))
+    gain_two, gain_three = norm_gain_two.reshape(1, -1), final_gain.reshape(1, -1)
+    head_gain = lin_head_gain.reshape(1, -1)
+    chunks[slots[-1]], shares, info, goal, gain_two, gain_three, head_gain = lax.optimization_barrier(
+        (chunks[slots[-1]], shares, info, goal, gain_two, gain_three, head_gain)
+    )
     if seq_count == 4:
         across_x[0] = lax.ppermute(lots[0], "seq", xor_pairs(seq_count, 2))
         corners[0] = lax.ppermute(across_x[0], "seq", xor_pairs(seq_count, 1))
@@ -819,21 +831,23 @@
         fqs,
         num,
         den,
-        lin_head_gain.reshape(1, -1),
+        head_gain,
         lin_out,
         states,
         heads,
     )
     far_rows = outer
     parts = scatter_rows(outer, lambda: near_chunks(mixed, lin_out, near, chunk))
-    units, residual = finish(embedded, norm_gain_two, parts, False)
+    parts = in_halves(parts)
+    upper, residual_upper = finish(embedded[0], gain_two, parts[0], False)
+    lower, residual_lower = finish(embedded[1], gain_two, parts[1], False)
 
     if seq_count == 4:
         lots[1], _ = lax.optimization_barrier((lots[1], (states, far_rows)))
         across_x[1] = lax.ppermute(lots[1], "seq", xor_pairs(seq_count, 2))
         beside = lax.ppermute(vocab_table, "seq", xor_pairs(seq_count, 1))
 
-    chunks = gather_rows(units)
+    chunks = gather_rows(upper, lower)
     qkvs = []
     for call in calls:
         qkvs.append(matmul([piece for k in call for piece in chunks[k]], win_qkv, 3 * HEAD_DIM))
@@ -854,14 +868,16 @@
         corners[1] = lax.ppermute(across_x[1], "seq", xor_pairs(seq_count, 1))
     mixed, *outer = halo_window(info, near, chunk, far, local, first, halo, win_out, heads)
     parts = scatter_rows(outer, lambda: near_chunks(mixed, win_out, near, chunk))
+    parts = in_halves(parts)
     if seq_count == 4:
-        parts, corners[1] = lax.optimization_barrier((parts, corners[1]))
-    units = finish(residual, final_gain, parts, True)[0]
-
-    chunks = gather_rows(units)
+        parts[1], corners[1] = lax.optimization_barrier((parts[1], corners[1]))
+    upper = finish(residual_upper, gain_three, parts[0], True)[0]
+    lower = finish(residual_lower, gain_three, parts[1], True)[0]
+
+    chunks = gather_rows(upper, lower)
     if seq_count == 4:
         across_x[2] = lax.ppermute(lots[2], "seq", xor_pairs(seq_count, 2))
-        corner, _ = lax.optimization_barrier((across_x[2], parts))
+        corner, _ = lax.optimization_barrier((across_x[2], parts[1]))
         corners[2] = lax.ppermute(corner, "seq", xor_pairs(seq_count, 1))
         shared = [vocab_table, beside]
         lots = [(marks_at[n], marks_at[n + 1], [across_x[n], corners[n]]) for n in range(3)]

time: 352 us -> 346 us (0.983)
  starting transfers between devices: 77.6 us -> 69.2 us
    ppermute x33 -> x39, starting transfers between devices: 57.7 us -> 51.6 us  [turned(): lax.ppermute(value, 'head', [(i, (i + step) % size) for i in range(size)])]
    pallas_call x2 -> x4, Pallas kernels: 5.62 us -> 8.79 us  [finish(): pl.pallas_call(functools.partial(finish_kernel, len(terms), last), in_spe...]
    unnamed x106 -> x112, local copies, waits for them, and re-layouts: 8.62 us -> 9.93 us
    ppermute x33 -> x39, waiting for transfers between devices: 106 us -> 105 us  [turned(): lax.ppermute(value, 'head', [(i, (i + step) % size) for i in range(size)])]
  transfers between devices with their start and end apart: 50 -> 56, of which waited for: 29 -> 33; matrix products, arithmetic and copies ran while one was open for 3% -> 3% of each run, Pallas kernels for 30% -> 32%
where the time goes in v9:
time: 346 us; the launch traced here: 345 us
  Pallas kernels  131 us (38%)
  waiting for transfers between devices  115 us (33%)
  starting transfers between devices  69.2 us (20%)
  local copies, waits for them, and re-layouts  15.7 us (5%)
  other arithmetic  7.11 us (2%)
  between operations  6.7 us (2%)
    ppermute x39, waiting for transfers between devices, turned(): lax.ppermute(value, 'head', [(i, (i + step) % size) for i in range(size)])  105 us
    ppermute x39, starting transfers between devices, turned(): lax.ppermute(value, 'head', [(i, (i + step) % size) for i in range(size)])  51.6 us
    pallas_call x4, Pallas kernels, lookup(): pl.pallas_call(functools.partial(lookup_kernel, lots), grid=(TABLE_STEPS,...  36.8 us
    pallas_call x1, Pallas kernels, scores(): pl.pallas_call(functools.partial(score_kernel, len(early), len(units), le...  22 us
    pallas_call x2, Pallas kernels, matmul(): pl.pallas_call(matmul_kernel, grid=(b.shape[1] // tile,), in_specs=[pl.Bl...  12.5 us
    pallas_call x2, Pallas kernels, project(): pl.pallas_call(functools.partial(project_kernel, heads, slots, chunk, cou...  11.8 us
    unnamed x112, local copies, waits for them, and re-layouts  9.93 us
    pallas_call x4, Pallas kernels, finish(): pl.pallas_call(functools.partial(finish_kernel, len(terms), last), in_spe...  8.79 us
  transfers between devices with their start and end apart: 56, of which 33 were waited for; matrix products, arithmetic and copies ran while one was open for 3% of the time, Pallas kernels for 32%

profile of v9, /device:TPU:0, one launch (start us, length us, event | category | flops | bytes accessed | tf_op | source)
XLA Modules:
  0.0 344.5 jit_solution(12809858572089101079)
XLA Ops:
  1.3 2.4 collective-permute-start.2
  5.0 2.3 collective-permute-done.1
  8.0 8.6 %lookup.5 = (bf16[256,512]{1,0:T(8,128)(2,1)}, bf16[256,512]{1,0:T(8,128)(2,1)}) custom-call(s32[1,512]{1,0:T(1,128)} %bitcast.49, bf16[6400,512]{1,0:T(8,128)(2,1)} %refs_3_.2), custom_call_target="tpu_custom_call" | custom-call | flops 4800000000 | bytes 24000000 | tf_op jit(solution)/shard_map/lookup/pallas_call | solution.py:160
  21.0 8.5 %lookup.7 = (bf16[256,512]{1,0:T(8,128)(2,1)}, bf16[256,512]{1,0:T(8,128)(2,1)}) custom-call(s32[1,512]{1,0:T(1,128)} %bitcast.51, bf16[6400,512]{1,0:T(8,128)(2,1)} %refs_3_.2), custom_call_target="tpu_custom_call" | custom-call | flops 4800000000 | bytes 24000000 | tf_op jit(solution)/shard_map/lookup/pallas_call | solution.py:160
  32.2 8.6 %lookup.6 = (bf16[256,512]{1,0:T(8,128)(2,1)}, bf16[256,512]{1,0:T(8,128)(2,1)}) custom-call(s32[1,512]{1,0:T(1,128)} %bitcast.52, bf16[6400,512]{1,0:T(8,128)(2,1)} %refs_3_.2), custom_call_target="tpu_custom_call" | custom-call | flops 4800000000 | bytes 24000000 | tf_op jit(solution)/shard_map/lookup/pallas_call | solution.py:160
  43.6 3.8 %collective-permute-start.8 = (bf16[256,512]{1,0:T(8,128)(2,1)}, bf16[256,512]{1,0:T(8,128)(2,1)S(1)}, u32[]{:S(2)}, u32[]{:S(2)}) collective-permute-start(bf16[256,512]{1,0:T(8,128)(2,1)} %get-tuple-element.107), channel_id=1, source_target_pairs={{0,3},{1,0},{2,1},{3,2},{4,7},{5,4},{6,5},{7,6},{8,11},{9,8},{10,9... | collective-permute-start | bytes 786440 | tf_op jit(solution)/shard_map/ppermute | solution.py:56
  47.5 11.1 %lookup.4 = (bf16[256,512]{1,0:T(8,128)(2,1)}, bf16[256,512]{1,0:T(8,128)(2,1)}, bf16[1920,512]{1,0:T(8,128)(2,1)}, bf16[3200,512]{1,0:T(8,128)(2,1)}, bf16[1280,512]{1,0:T(8,128)(2,1)}) custom-call(s32[1,512]{1,0:T(1,128)} %bitcast.45, bf16[6400,512]{1,0:T(8,128)(2,1)} %refs_3_.2), custom_call_target="tpu_custom_call" | custom-call | flops 4800000000 | bytes 24000000 | tf_op jit(solution)/shard_map/lookup/pallas_call | solution.py:160
  63.6 4.7 %collective-permute-done.10.refs_2_ = bf16[128,512]{1,0:T(8,128)(2,1)S(1)} collective-permute-done((bf16[128,512]{1,0:T(8,128)(2,1)}, bf16[128,512]{1,0:T(8,128)(2,1)S(1)}, u32[]{:S(2)}, u32[]{:S(2)}) %collective-permute-start.10) | collective-permute-done | bytes 131104 | tf_op jit(solution)/shard_map/ppermute | solution.py:758
  80.3 2.9 collective-permute-done.16.refs_2_
  83.2 4.2 %collective-permute-start.14 = (bf16[64,2048]{1,0:T(8,128)(2,1)}, bf16[64,2048]{1,0:T(8,128)(2,1)S(1)}, u32[]{:S(2)}, u32[]{:S(2)}) collective-permute-start(bf16[64,2048]{1,0:T(8,128)(2,1)} %get-tuple-element.118.refs_1_), channel_id=1, source_target_pairs={{0,3},{1,0},{2,1},{3,2},{4,7},{5,4},{6,5},{7,6},{8,11},{9,8},{10,9... | collective-permute-start | bytes 786440 | tf_op jit(solution)/shard_map/ppermute | solution.py:56
  92.9 9.5 %collective-permute-done.14.refs_3_ = bf16[64,2048]{1,0:T(8,128)(2,1)S(1)} collective-permute-done((bf16[64,2048]{1,0:T(8,128)(2,1)}, bf16[64,2048]{1,0:T(8,128)(2,1)S(1)}, u32[]{:S(2)}, u32[]{:S(2)}) %collective-permute-start.14) | collective-permute-done | bytes 262176 | tf_op jit(solution)/shard_map/ppermute | solution.py:56
  105.0 6.7 %project.2 = (bf16[4,384,256]{2,1,0:T(8,128)(2,1)}, bf16[4,384,256]{2,1,0:T(8,128)(2,1)}, bf16[384,512]{1,0:T(8,128)(2,1)}, f32[4,176,128]{2,1,0:T(8,128)}) custom-call(s32[1]{0:T(128)} %copy.35.bound_ref, s32[3]{0:T(128)} %bitcast.53, bf16[64,2048]{1,0:T(8,128)(2,1)} %get-tuple-element.117.refs_0_, bf16[64,2048]{1,0:T(8,128)(2,1)} %get-tuple-element.118.refs_1_, ...), custom_call_target="tpu_custom_call" | custom-call | flops 3000000000 | bytes 15000000 | tf_op jit(solution)/shard_map/project/pallas_call | solution.py:335
  113.2 5.1 %project.3 = (bf16[4,128,256]{2,1,0:T(8,128)(2,1)}, bf16[4,128,256]{2,1,0:T(8,128)(2,1)}, bf16[128,512]{1,0:T(8,128)(2,1)}, bf16[4,176,128]{2,1,0:T(8,128)(2,1)}) custom-call(s32[1]{0:T(128)} %copy.35.bound_ref, s32[1]{0:T(128)} %slice.77.places_ref, bf16[64,2048]{1,0:T(8,128)(2,1)} %copy-done.36, bf16[64,2048]{1,0:T(8,128)(2,1)} %copy-done.40, ...), custom_call_target="tpu_custom_call" | custom-call | flops 3000000000 | bytes 15000000 | tf_op jit(solution)/shard_map/project/pallas_call | solution.py:335
  118.3 2.8 collective-permute-start.21
  124.4 4.6 %within.1 = (f32[4,512,128]{2,1,0:T(8,128)}, f32[4,512,8]{2,1,0:T(8,128)}) custom-call(s32[1]{0:T(128)} %copy.35.bound_ref, s32[4]{0:T(128)} %copy-done.6, bf16[4,384,256]{2,1,0:T(8,128)(2,1)} %get-tuple-element.121.refs_0_, bf16[4,128,256]{2,1,0:T(8,128)(2,1)} %get-tuple-element.125.refs_1_, bf16[4,384,256]{2,1,0:T(8,128)(2,1)} %get-tuple-element.126.refs_2_, ...), custom_call_target="tpu_custom_call" | custom-call | flops 2700000000 | bytes 13500000 | tf_op jit(solution)/shard_map/within/pallas_call | solution.py:374
  130.2 4.8 %across.1 = (bf16[512,512]{1,0:T(8,128)(2,1)}, bf16[64,2048]{1,0:T(8,128)(2,1)}, bf16[64,2048]{1,0:T(8,128)(2,1)}) custom-call(s32[1]{0:T(128)} %copy.35.bound_ref, s32[4]{0:T(128)} %copy-done.6, s32[3]{0:T(128)} %add_convert_fusion.share_ref, bf16[4,384,256]{2,1,0:T(8,128)(2,1)} %get-tuple-element.121.refs_0_, ...), custom_call_target="tpu_custom_call" | custom-call | flops 2700000000 | bytes 13500000 | tf_op jit(solution)/shard_map/across/pallas_call | solution.py:423
  135.0 3.0 collective-permute-start.34
  138.6 3.3 collective-permute-start.23
  141.9 3.8 %near.2 = (bf16[64,2048]{1,0:T(8,128)(2,1)}, bf16[64,2048]{1,0:T(8,128)(2,1)}, bf16[64,2048]{1,0:T(8,128)(2,1)}, bf16[64,2048]{1,0:T(8,128)(2,1)}, bf16[64,2048]{1,0:T(8,128)(2,1)}, /*index=5*/bf16[64,2048]{1,0:T(8,128)(2,1)}) custom-call(bf16[512,512]{1,0:T(8,128)(2,1)} %get-tuple-element.136.mixed_ref, bf16[512,2048]{1,0:T(8,128)(2,1)} %weight_ref.3), custom_call_target="tpu_custom_call" | custom-call | flops 2400000000 | bytes 12000000 | tf_op jit(solution)/shard_map/near/pallas_call | solution.py:442
  145.7 3.6 %collective-permute-done.22.before_ref = bf16[64,2048]{1,0:T(8,128)(2,1)S(1)} collective-permute-done((bf16[64,2048]{1,0:T(8,128)(2,1)}, bf16[64,2048]{1,0:T(8,128)(2,1)S(1)}, u32[]{:S(2)}, u32[]{:S(2)}) %collective-permute-start.22) | collective-permute-done | bytes 262176 | tf_op jit(solution)/shard_map/ppermute | solution.py:56
  149.3 2.6 collective-permute-done.23.after_ref
  158.5 7.5 %collective-permute-done.24.refs_1_ = bf16[64,2048]{1,0:T(8,128)(2,1)S(1)} collective-permute-done((bf16[64,2048]{1,0:T(8,128)(2,1)}, bf16[64,2048]{1,0:T(8,128)(2,1)S(1)}, u32[]{:S(2)}, u32[]{:S(2)}) %collective-permute-start.24) | collective-permute-done | bytes 262176 | tf_op jit(solution)/shard_map/ppermute | solution.py:56
  171.6 2.7 collective-permute-start.30
  174.3 3.7 %collective-permute-done.27.refs_2_ = bf16[64,2048]{1,0:T(8,128)(2,1)S(1)} collective-permute-done((bf16[64,2048]{1,0:T(8,128)(2,1)}, bf16[64,2048]{1,0:T(8,128)(2,1)S(1)}, u32[]{:S(2)}, u32[]{:S(2)}) %collective-permute-start.27) | collective-permute-done | bytes 262176 | tf_op jit(solution)/shard_map/ppermute | solution.py:56
  182.9 2.3 collective-permute-start.31
  185.1 5.0 %collective-permute-done.28.refs_2_ = bf16[64,2048]{1,0:T(8,128)(2,1)S(1)} collective-permute-done((bf16[64,2048]{1,0:T(8,128)(2,1)}, bf16[64,2048]{1,0:T(8,128)(2,1)S(1)}, u32[]{:S(2)}, u32[]{:S(2)}) %collective-permute-start.28) | collective-permute-done | bytes 262176 | tf_op jit(solution)/shard_map/ppermute | solution.py:56
  195.4 7.0 %collective-permute-done.29.refs_3_ = bf16[64,2048]{1,0:T(8,128)(2,1)S(1)} collective-permute-done((bf16[64,2048]{1,0:T(8,128)(2,1)}, bf16[64,2048]{1,0:T(8,128)(2,1)S(1)}, u32[]{:S(2)}, u32[]{:S(2)}) %collective-permute-start.29) | collective-permute-done | bytes 262176 | tf_op jit(solution)/shard_map/ppermute | solution.py:56
  203.1 7.2 %matmul.2.refs_0_ = bf16[384,1536]{1,0:T(8,128)(2,1)} custom-call(bf16[64,2048]{1,0:T(8,128)(2,1)} %get-tuple-element.148.refs_0_, bf16[64,2048]{1,0:T(8,128)(2,1)} %get-tuple-element.153.refs_1_, bf16[64,2048]{1,0:T(8,128)(2,1)} %copy-done.22, bf16[64,2048]{1,0:T(8,128)(2,1)} %copy-done.32, bf16[64,2048]{1,0:T(8,128)(2,1)} %copy-done.20, ...), custom_call_target="tpu_custom_call" | custom-call | flops 3000000000 | bytes 15000000 | tf_op jit(solution)/shard_map/matmul/pallas_call | solution.py:461
  210.3 5.3 %matmul.3.refs_1_ = bf16[128,1536]{1,0:T(8,128)(2,1)} custom-call(bf16[64,2048]{1,0:T(8,128)(2,1)} %collective-permute-done.32.refs_0_, bf16[64,2048]{1,0:T(8,128)(2,1)} %collective-permute-done.33.refs_1_, bf16[2048,1536]{1,0:T(8,128)(2,1)} %refs_2_.3), custom_call_target="tpu_custom_call" | custom-call | flops 3000000000 | bytes 15000000 | tf_op jit(solution)/shard_map/matmul/pallas_call | solution.py:461
  218.0 4.8 %local_window.1 = (bf16[512,512]{1,0:T(8,128)(2,1)}, bf16[64,1536]{1,0:T(8,128)(2,1)}) custom-call(s32[1]{0:T(128)} %copy.35.bound_ref, s32[4]{0:T(128)} %copy-done.6, bf16[384,1536]{1,0:T(8,128)(2,1)} %matmul.2.refs_0_, bf16[128,1536]{1,0:T(8,128)(2,1)} %matmul.3.refs_1_), custom_call_target="tpu_custom_call" | custom-call | flops 4800000000 | bytes 24000000 | tf_op jit(solution)/shard_map/local_window/pallas_call | solution.py:529
  224.1 3.6 %halo_window.1 = (bf16[512,512]{1,0:T(8,128)(2,1)}, bf16[64,2048]{1,0:T(8,128)(2,1)}, bf16[64,2048]{1,0:T(8,128)(2,1)}) custom-call(s32[3]{0:T(128)} %pad_add_fusion.4.info_ref, bf16[512,512]{1,0:T(8,128)(2,1)} %get-tuple-element.159.local_ref, bf16[64,1536]{1,0:T(8,128)(2,1)} %get-tuple-element.160.first_ref, bf16[64,1536]{1,0:T(8,128)(2,1)} %copy-done.48, ...), custom_call_target="tpu_custom_call" | custom-call | flops 2700000000 | bytes 13500000 | tf_op jit(solution)/shard_map/halo_window/pallas_call | solution.py:566
  229.0 2.5 collective-permute-start.39
  231.5 3.9 %near.3 = (bf16[64,2048]{1,0:T(8,128)(2,1)}, bf16[64,2048]{1,0:T(8,128)(2,1)}, bf16[64,2048]{1,0:T(8,128)(2,1)}, bf16[64,2048]{1,0:T(8,128)(2,1)}, bf16[64,2048]{1,0:T(8,128)(2,1)}, /*index=5*/bf16[64,2048]{1,0:T(8,128)(2,1)}) custom-call(bf16[512,512]{1,0:T(8,128)(2,1)} %get-tuple-element.162.mixed_ref, bf16[512,2048]{1,0:T(8,128)(2,1)} %weight_ref.5), custom_call_target="tpu_custom_call" | custom-call | flops 2400000000 | bytes 12000000 | tf_op jit(solution)/shard_map/near/pallas_call | solution.py:442
  235.4 3.5 %collective-permute-done.38.before_ref = bf16[64,2048]{1,0:T(8,128)(2,1)} collective-permute-done((bf16[64,2048]{1,0:T(8,128)(2,1)}, bf16[64,2048]{1,0:T(8,128)(2,1)}, u32[]{:S(2)}, u32[]{:S(2)}) %collective-permute-start.38) | collective-permute-done | bytes 262176 | tf_op jit(solution)/shard_map/ppermute | solution.py:56
  238.9 4.4 %collective-permute-done.39.after_ref = bf16[64,2048]{1,0:T(8,128)(2,1)} collective-permute-done((bf16[64,2048]{1,0:T(8,128)(2,1)}, bf16[64,2048]{1,0:T(8,128)(2,1)}, u32[]{:S(2)}, u32[]{:S(2)}) %collective-permute-start.39) | collective-permute-done | bytes 262176 | tf_op jit(solution)/shard_map/ppermute | solution.py:56
  245.4 2.6 collective-permute-start.43
  250.1 5.2 %collective-permute-done.43.refs_2_ = bf16[64,2048]{1,0:T(8,128)(2,1)S(1)} collective-permute-done((bf16[64,2048]{1,0:T(8,128)(2,1)}, bf16[64,2048]{1,0:T(8,128)(2,1)S(1)}, u32[]{:S(2)}, u32[]{:S(2)}) %collective-permute-start.43) | collective-permute-done | bytes 262176 | tf_op jit(solution)/shard_map/ppermute | solution.py:56
  258.2 7.0 %collective-permute-done.41.refs_2_ = bf16[64,2048]{1,0:T(8,128)(2,1)S(1)} collective-permute-done((bf16[64,2048]{1,0:T(8,128)(2,1)}, bf16[64,2048]{1,0:T(8,128)(2,1)S(1)}, u32[]{:S(2)}, u32[]{:S(2)}) %collective-permute-start.41) | collective-permute-done | bytes 262176 | tf_op jit(solution)/shard_map/ppermute | solution.py:56
  265.1 5.8 %collective-permute-done.40.refs_1_ = bf16[64,2048]{1,0:T(8,128)(2,1)S(1)} collective-permute-done((bf16[64,2048]{1,0:T(8,128)(2,1)}, bf16[64,2048]{1,0:T(8,128)(2,1)S(1)}, u32[]{:S(2)}, u32[]{:S(2)}) %collective-permute-start.40) | collective-permute-done | bytes 262176 | tf_op jit(solution)/shard_map/ppermute | solution.py:56
  281.9 3.2 collective-permute-done.47.refs_4_
  285.1 4.7 %collective-permute-done.46.refs_3_ = bf16[64,2048]{1,0:T(8,128)(2,1)S(1)} collective-permute-done((bf16[64,2048]{1,0:T(8,128)(2,1)}, bf16[64,2048]{1,0:T(8,128)(2,1)S(1)}, u32[]{:S(2)}, u32[]{:S(2)}) %collective-permute-start.46) | collective-permute-done | bytes 262176 | tf_op jit(solution)/shard_map/ppermute | solution.py:56
  289.7 2.9 collective-permute-start.50
  292.6 3.9 %collective-permute-done.45.refs_2_ = bf16[64,2048]{1,0:T(8,128)(2,1)S(1)} collective-permute-done((bf16[64,2048]{1,0:T(8,128)(2,1)S(1)}, bf16[64,2048]{1,0:T(8,128)(2,1)S(1)}, u32[]{:S(2)}, u32[]{:S(2)}) %collective-permute-start.45) | collective-permute-done | bytes 262176 | tf_op jit(solution)/shard_map/ppermute | solution.py:56
  296.5 5.6 %collective-permute-done.48.refs_5_ = bf16[64,2048]{1,0:T(8,128)(2,1)S(1)} collective-permute-done((bf16[64,2048]{1,0:T(8,128)(2,1)}, bf16[64,2048]{1,0:T(8,128)(2,1)S(1)}, u32[]{:S(2)}, u32[]{:S(2)}) %collective-permute-start.48) | collective-permute-done | bytes 262176 | tf_op jit(solution)/shard_map/ppermute | solution.py:56
  302.8 3.0 turn.1.refs_0_
  307.6 4.5 %collective-permute-done.50.refs_2_ = bf16[64,2048]{1,0:T(8,128)(2,1)S(1)} collective-permute-done((bf16[64,2048]{1,0:T(8,128)(2,1)S(1)}, bf16[64,2048]{1,0:T(8,128)(2,1)S(1)}, u32[]{:S(2)}, u32[]{:S(2)}) %collective-permute-start.50) | collective-permute-done | bytes 262176 | tf_op jit(solution)/shard_map/ppermute | solution.py:56
  313.9 22.0 %scores.1 = f32[8,512]{1,0:T(8,128)} custom-call(s32[4]{0:T(128)} %iota_xor_fusion.order_ref, bf16[2048,384]{1,0:T(8,128)(2,1)} %turn.1.refs_0_, bf16[64,2048]{1,0:T(8,128)(2,1)} %copy-done.33, bf16[64,2048]{1,0:T(8,128)(2,1)} %copy-done.37, bf16[6400,512]{1,0:T(8,128)(2,1)} %refs_3_.2, bf16[6400,512]{1,0:T(8,128)(2,1)} %collective-permute-done.36.refs_4_, ...), custom_call_target="tpu_custom_call" | custom-call | flops 12000000000 | bytes 60000000 | tf_op jit(solution)/shard_map/scores/pallas_call | solution.py:668
  340.1 2.5 collective-permute-done.54
  (235 shorter events, 94.9 us)
Async XLA Ops:
  4.4 212.2 %collective-permute-start.36 = (bf16[6400,512]{1,0:T(8,128)(2,1)}, bf16[6400,512]{1,0:T(8,128)(2,1)}, u32[]{:S(2)}, u32[]{:S(2)}) collective-permute-start(bf16[6400,512]{1,0:T(8,128)(2,1)} %refs_3_.2), channel_id=1, source_target_pairs={{0,4},{4,0},{8,12},{12,8},{1,5},{5,1},{9,13},{13,9},{2,6},{6,2},{1... | collective-permute-start | bytes 19660808 | tf_op jit(solution)/shard_map/ppermute | solution.py:848
  16.6 24.1 %collective-permute-start.3 = (bf16[256,512]{1,0:T(8,128)(2,1)}, bf16[256,512]{1,0:T(8,128)(2,1)S(1)}, u32[]{:S(2)}, u32[]{:S(2)}) collective-permute-start(bf16[256,512]{1,0:T(8,128)(2,1)} %get-tuple-element.97), channel_id=1, source_target_pairs={{0,1},{1,2},{2,3},{3,0},{4,5},{5,6},{6,7},{7,4},{8,9},{9,10},{10,1... | collective-permute-start | bytes 786440 | tf_op jit(solution)/shard_map/ppermute | solution.py:56
  18.2 22.6 %collective-permute-start.4 = (bf16[256,512]{1,0:T(8,128)(2,1)}, bf16[256,512]{1,0:T(8,128)(2,1)S(1)}, u32[]{:S(2)}, u32[]{:S(2)}) collective-permute-start(bf16[256,512]{1,0:T(8,128)(2,1)} %get-tuple-element.98), channel_id=1, source_target_pairs={{0,3},{1,0},{2,1},{3,2},{4,7},{5,4},{6,5},{7,6},{8,11},{9,8},{10,9... | collective-permute-start | bytes 786440 | tf_op jit(solution)/shard_map/ppermute | solution.py:56
  29.5 29.0 %collective-permute-start.6 = (bf16[256,512]{1,0:T(8,128)(2,1)}, bf16[256,512]{1,0:T(8,128)(2,1)S(1)}, u32[]{:S(2)}, u32[]{:S(2)}) collective-permute-start(bf16[256,512]{1,0:T(8,128)(2,1)} %get-tuple-element.104), channel_id=1, source_target_pairs={{0,3},{1,0},{2,1},{3,2},{4,7},{5,4},{6,5},{7,6},{8,11},{9,8},{10,9... | collective-permute-start | bytes 786440 | tf_op jit(solution)/shard_map/ppermute | solution.py:56
  31.4 27.2 %collective-permute-start.7 = (bf16[256,512]{1,0:T(8,128)(2,1)}, bf16[256,512]{1,0:T(8,128)(2,1)S(1)}, u32[]{:S(2)}, u32[]{:S(2)}) collective-permute-start(bf16[256,512]{1,0:T(8,128)(2,1)} %get-tuple-element.106), channel_id=1, source_target_pairs={{0,1},{1,2},{2,3},{3,0},{4,5},{5,6},{6,7},{7,4},{8,9},{9,10},{10,1... | collective-permute-start | bytes 786440 | tf_op jit(solution)/shard_map/ppermute | solution.py:56
  43.6 14.9 %collective-permute-start.5 = (bf16[256,512]{1,0:T(8,128)(2,1)}, bf16[256,512]{1,0:T(8,128)(2,1)S(1)}, u32[]{:S(2)}, u32[]{:S(2)}) collective-permute-start(bf16[256,512]{1,0:T(8,128)(2,1)} %get-tuple-element.103), channel_id=1, source_target_pairs={{0,1},{1,2},{2,3},{3,0},{4,5},{5,6},{6,7},{7,4},{8,9},{9,10},{10,1... | collective-permute-start | bytes 786440 | tf_op jit(solution)/shard_map/ppermute | solution.py:56
  43.6 14.9 %collective-permute-start.8 = (bf16[256,512]{1,0:T(8,128)(2,1)}, bf16[256,512]{1,0:T(8,128)(2,1)S(1)}, u32[]{:S(2)}, u32[]{:S(2)}) collective-permute-start(bf16[256,512]{1,0:T(8,128)(2,1)} %get-tuple-element.107), channel_id=1, source_target_pairs={{0,3},{1,0},{2,1},{3,2},{4,7},{5,4},{6,5},{7,6},{8,11},{9,8},{10,9... | collective-permute-start | bytes 786440 | tf_op jit(solution)/shard_map/ppermute | solution.py:56
  61.7 6.5 %collective-permute-start.10 = (bf16[128,512]{1,0:T(8,128)(2,1)}, bf16[128,512]{1,0:T(8,128)(2,1)S(1)}, u32[]{:S(2)}, u32[]{:S(2)}) collective-permute-start(bf16[128,512]{1,0:T(8,128)(2,1)} %get-tuple-element.110), channel_id=1, source_target_pairs={{0,8},{4,12},{8,0},{12,4},{1,9},{5,13},{9,1},{13,5},{2,10},{6,14},... | collective-permute-start | bytes 393224 | tf_op jit(solution)/shard_map/ppermute | solution.py:758
  62.4 7.9 %collective-permute-start.11 = (bf16[128,512]{1,0:T(8,128)(2,1)}, bf16[128,512]{1,0:T(8,128)(2,1)S(1)}, u32[]{:S(2)}, u32[]{:S(2)}) collective-permute-start(bf16[128,512]{1,0:T(8,128)(2,1)} %get-tuple-element.111), channel_id=1, source_target_pairs={{0,12},{4,8},{8,4},{12,0},{1,13},{5,9},{9,5},{13,1},{2,14},{6,10},... | collective-permute-start | bytes 393224 | tf_op jit(solution)/shard_map/ppermute | solution.py:758
  70.3 48.0 %collective-permute-start.18 = (bf16[1920,512]{1,0:T(8,128)(2,1)}, bf16[1920,512]{1,0:T(8,128)(2,1)S(1)}, u32[]{:S(2)}, u32[]{:S(2)}) collective-permute-start(bf16[1920,512]{1,0:T(8,128)(2,1)} %get-tuple-element.134), channel_id=1, source_target_pairs={{0,8},{4,12},{8,0},{12,4},{1,9},{5,13},{9,1},{13,5},{2,10},{6,14},... | collective-permute-start | bytes 5898248 | tf_op jit(solution)/shard_map/ppermute | solution.py:808
  74.3 8.9 %collective-permute-start.16 = (bf16[64,2048]{1,0:T(8,128)(2,1)}, bf16[64,2048]{1,0:T(8,128)(2,1)S(1)}, u32[]{:S(2)}, u32[]{:S(2)}) collective-permute-start(bf16[64,2048]{1,0:T(8,128)(2,1)} %get-tuple-element.117.refs_0_), channel_id=1, source_target_pairs={{0,3},{1,0},{2,1},{3,2},{4,7},{5,4},{6,5},{7,6},{8,11},{9,8},{10,9... | collective-permute-start | bytes 786440 | tf_op jit(solution)/shard_map/ppermute | solution.py:56
  80.0 12.9 %collective-permute-start.12 = (bf16[64,2048]{1,0:T(8,128)(2,1)}, bf16[64,2048]{1,0:T(8,128)(2,1)S(1)}, u32[]{:S(2)}, u32[]{:S(2)}) collective-permute-start(bf16[64,2048]{1,0:T(8,128)(2,1)} %get-tuple-element.117.refs_0_), channel_id=1, source_target_pairs={{0,1},{1,2},{2,3},{3,0},{4,5},{5,6},{6,7},{7,4},{8,9},{9,10},{10,1... | collective-permute-start | bytes 786440 | tf_op jit(solution)/shard_map/ppermute | solution.py:56
  80.3 24.0 %collective-permute-start.17 = (bf16[64,2048]{1,0:T(8,128)(2,1)}, bf16[64,2048]{1,0:T(8,128)(2,1)S(1)}, u32[]{:S(2)}, u32[]{:S(2)}) collective-permute-start(bf16[64,2048]{1,0:T(8,128)(2,1)} %get-tuple-element.118.refs_1_), channel_id=1, source_target_pairs={{0,1},{1,2},{2,3},{3,0},{4,5},{5,6},{6,7},{7,4},{8,9},{9,10},{10,1... | collective-permute-start | bytes 786440 | tf_op jit(solution)/shard_map/ppermute | solution.py:56
  83.2 19.3 %collective-permute-start.14 = (bf16[64,2048]{1,0:T(8,128)(2,1)}, bf16[64,2048]{1,0:T(8,128)(2,1)S(1)}, u32[]{:S(2)}, u32[]{:S(2)}) collective-permute-start(bf16[64,2048]{1,0:T(8,128)(2,1)} %get-tuple-element.118.refs_1_), channel_id=1, source_target_pairs={{0,3},{1,0},{2,1},{3,2},{4,7},{5,4},{6,5},{7,6},{8,11},{9,8},{10,9... | collective-permute-start | bytes 786440 | tf_op jit(solution)/shard_map/ppermute | solution.py:56
  92.9 18.7 %collective-permute-start.13 = (bf16[64,2048]{1,0:T(8,128)(2,1)S(1)}, bf16[64,2048]{1,0:T(8,128)(2,1)S(1)}, u32[]{:S(2)}, u32[]{:S(2)}) collective-permute-start(bf16[64,2048]{1,0:T(8,128)(2,1)S(1)} %collective-permute-done.12.refs_4_), channel_id=1, source_target_pairs={{0,1},{1,2},{2,3},{3,0},{4,5},{5,6},{6,7},{7,4},{8,9},{9,10},{10,1... | collective-permute-start | bytes 786440 | tf_op jit(solution)/shard_map/ppermute | solution.py:56
  102.5 10.0 %collective-permute-start.15 = (bf16[64,2048]{1,0:T(8,128)(2,1)S(1)}, bf16[64,2048]{1,0:T(8,128)(2,1)S(1)}, u32[]{:S(2)}, u32[]{:S(2)}) collective-permute-start(bf16[64,2048]{1,0:T(8,128)(2,1)S(1)} %collective-permute-done.14.refs_3_), channel_id=1, source_target_pairs={{0,3},{1,0},{2,1},{3,2},{4,7},{5,4},{6,5},{7,6},{8,11},{9,8},{10,9... | collective-permute-start | bytes 786440 | tf_op jit(solution)/shard_map/ppermute | solution.py:56
  118.3 10.8 %collective-permute-start.21 = (bf16[4,176,128]{2,1,0:T(8,128)(2,1)}, bf16[4,176,128]{2,1,0:T(8,128)(2,1)S(1)}, u32[]{:S(2)}, u32[]{:S(2)}) collective-permute-start(bf16[4,176,128]{2,1,0:T(8,128)(2,1)} %get-tuple-element.135), channel_id=1, source_target_pairs={{0,12},{1,13},{2,14},{3,15},{16,28},{17,29},{18,30},{19,31}} | collective-permute-start | bytes 540680 | tf_op jit(solution)/shard_map/ppermute | solution.py:818
  121.1 8.4 %collective-permute-start.20 = (bf16[4,176,128]{2,1,0:T(8,128)(2,1)}, bf16[4,176,128]{2,1,0:T(8,128)(2,1)S(1)}, u32[]{:S(2)}, u32[]{:S(2)}) collective-permute-start(bf16[4,176,128]{2,1,0:T(8,128)(2,1)} %get-tuple-element.135), channel_id=1, source_target_pairs={{0,8},{4,12},{1,9},{5,13},{2,10},{6,14},{3,11},{7,15},{16,24},{20,... | collective-permute-start | bytes 540680 | tf_op jit(solution)/shard_map/ppermute | solution.py:818
  122.4 7.1 %collective-permute-start.19 = (bf16[4,176,128]{2,1,0:T(8,128)(2,1)}, bf16[4,176,128]{2,1,0:T(8,128)(2,1)S(1)}, u32[]{:S(2)}, u32[]{:S(2)}) collective-permute-start(bf16[4,176,128]{2,1,0:T(8,128)(2,1)} %get-tuple-element.135), channel_id=1, source_target_pairs={{0,4},{4,8},{8,12},{1,5},{5,9},{9,13},{2,6},{6,10},{10,14},{3,7},{... | collective-permute-start | bytes 540680 | tf_op jit(solution)/shard_map/ppermute | solution.py:818
  135.0 81.6 %collective-permute-start.34 = (bf16[3200,512]{1,0:T(8,128)(2,1)S(1)}, bf16[3200,512]{1,0:T(8,128)(2,1)S(1)}, u32[]{:S(2)}, u32[]{:S(2)}) collective-permute-start(bf16[3200,512]{1,0:T(8,128)(2,1)S(1)} %copy-done.8), channel_id=1, source_target_pairs={{0,8},{4,12},{8,0},{12,4},{1,9},{5,13},{9,1},{13,5},{2,10},{6,14},... | collective-permute-start | bytes 9830408 | tf_op jit(solution)/shard_map/ppermute | solution.py:847
  138.0 11.3 %collective-permute-start.22 = (bf16[64,2048]{1,0:T(8,128)(2,1)}, bf16[64,2048]{1,0:T(8,128)(2,1)S(1)}, u32[]{:S(2)}, u32[]{:S(2)}) collective-permute-start(bf16[64,2048]{1,0:T(8,128)(2,1)} %get-tuple-element.139), channel_id=1, source_target_pairs={{0,1},{1,2},{2,3},{3,0},{4,5},{5,6},{6,7},{7,4},{8,9},{9,10},{10,1... | collective-permute-start | bytes 786440 | tf_op jit(solution)/shard_map/ppermute | solution.py:56
  138.6 13.3 %collective-permute-start.23 = (bf16[64,2048]{1,0:T(8,128)(2,1)}, bf16[64,2048]{1,0:T(8,128)(2,1)S(1)}, u32[]{:S(2)}, u32[]{:S(2)}) collective-permute-start(bf16[64,2048]{1,0:T(8,128)(2,1)} %get-tuple-element.141), channel_id=1, source_target_pairs={{0,3},{1,0},{2,1},{3,2},{4,7},{5,4},{6,5},{7,6},{8,11},{9,8},{10,9... | collective-permute-start | bytes 786440 | tf_op jit(solution)/shard_map/ppermute | solution.py:56
  145.7 10.9 %collective-permute-start.25 = (bf16[64,2048]{1,0:T(8,128)(2,1)}, bf16[64,2048]{1,0:T(8,128)(2,1)S(1)}, u32[]{:S(2)}, u32[]{:S(2)}) collective-permute-start(bf16[64,2048]{1,0:T(8,128)(2,1)} %get-tuple-element.143), channel_id=1, source_target_pairs={{0,3},{1,0},{2,1},{3,2},{4,7},{5,4},{6,5},{7,6},{8,11},{9,8},{10,9... | collective-permute-start | bytes 786440 | tf_op jit(solution)/shard_map/ppermute | solution.py:56
  154.6 11.3 %collective-permute-start.24 = (bf16[64,2048]{1,0:T(8,128)(2,1)}, bf16[64,2048]{1,0:T(8,128)(2,1)S(1)}, u32[]{:S(2)}, u32[]{:S(2)}) collective-permute-start(bf16[64,2048]{1,0:T(8,128)(2,1)} %get-tuple-element.142), channel_id=1, source_target_pairs={{0,1},{1,2},{2,3},{3,0},{4,5},{5,6},{6,7},{7,4},{8,9},{9,10},{10,1... | collective-permute-start | bytes 786440 | tf_op jit(solution)/shard_map/ppermute | solution.py:56
  155.1 61.5 %collective-permute-start.35 = (bf16[1920,512]{1,0:T(8,128)(2,1)}, bf16[1920,512]{1,0:T(8,128)(2,1)}, u32[]{:S(2)}, u32[]{:S(2)}) collective-permute-start(bf16[1920,512]{1,0:T(8,128)(2,1)} %copy-done.11), channel_id=1, source_target_pairs={{0,4},{4,0},{8,12},{12,8},{1,5},{5,1},{9,13},{13,9},{2,6},{6,2},{1... | collective-permute-start | bytes 5898248 | tf_op jit(solution)/shard_map/ppermute | solution.py:809
  156.5 15.1 %collective-permute-start.26 = (bf16[64,2048]{1,0:T(8,128)(2,1)S(1)}, bf16[64,2048]{1,0:T(8,128)(2,1)S(1)}, u32[]{:S(2)}, u32[]{:S(2)}) collective-permute-start(bf16[64,2048]{1,0:T(8,128)(2,1)S(1)} %copy-done.23), channel_id=1, source_target_pairs={{0,1},{1,2},{2,3},{3,0},{4,5},{5,6},{6,7},{7,4},{8,9},{9,10},{10,1... | collective-permute-start | bytes 786440 | tf_op jit(solution)/shard_map/ppermute | solution.py:56
  166.0 12.1 %collective-permute-start.27 = (bf16[64,2048]{1,0:T(8,128)(2,1)}, bf16[64,2048]{1,0:T(8,128)(2,1)S(1)}, u32[]{:S(2)}, u32[]{:S(2)}) collective-permute-start(bf16[64,2048]{1,0:T(8,128)(2,1)} %get-tuple-element.152), channel_id=1, source_target_pairs={{0,3},{1,0},{2,1},{3,2},{4,7},{5,4},{6,5},{7,6},{8,11},{9,8},{10,9... | collective-permute-start | bytes 786440 | tf_op jit(solution)/shard_map/ppermute | solution.py:56
  171.6 11.2 %collective-permute-start.30 = (bf16[64,2048]{1,0:T(8,128)(2,1)}, bf16[64,2048]{1,0:T(8,128)(2,1)S(1)}, u32[]{:S(2)}, u32[]{:S(2)}) collective-permute-start(bf16[64,2048]{1,0:T(8,128)(2,1)} %get-tuple-element.148.refs_0_), channel_id=1, source_target_pairs={{0,1},{1,2},{2,3},{3,0},{4,5},{5,6},{6,7},{7,4},{8,9},{9,10},{10,1... | collective-permute-start | bytes 786440 | tf_op jit(solution)/shard_map/ppermute | solution.py:56
  178.1 12.1 %collective-permute-start.28 = (bf16[64,2048]{1,0:T(8,128)(2,1)}, bf16[64,2048]{1,0:T(8,128)(2,1)S(1)}, u32[]{:S(2)}, u32[]{:S(2)}) collective-permute-start(bf16[64,2048]{1,0:T(8,128)(2,1)} %get-tuple-element.148.refs_0_), channel_id=1, source_target_pairs={{0,3},{1,0},{2,1},{3,2},{4,7},{5,4},{6,5},{7,6},{8,11},{9,8},{10,9... | collective-permute-start | bytes 786440 | tf_op jit(solution)/shard_map/ppermute | solution.py:56
  182.9 11.2 %collective-permute-start.31 = (bf16[64,2048]{1,0:T(8,128)(2,1)}, bf16[64,2048]{1,0:T(8,128)(2,1)S(1)}, u32[]{:S(2)}, u32[]{:S(2)}) collective-permute-start(bf16[64,2048]{1,0:T(8,128)(2,1)} %get-tuple-element.153.refs_1_), channel_id=1, source_target_pairs={{0,1},{1,2},{2,3},{3,0},{4,5},{5,6},{6,7},{7,4},{8,9},{9,10},{10,1... | collective-permute-start | bytes 786440 | tf_op jit(solution)/shard_map/ppermute | solution.py:56
  190.2 12.2 %collective-permute-start.29 = (bf16[64,2048]{1,0:T(8,128)(2,1)}, bf16[64,2048]{1,0:T(8,128)(2,1)S(1)}, u32[]{:S(2)}, u32[]{:S(2)}) collective-permute-start(bf16[64,2048]{1,0:T(8,128)(2,1)} %get-tuple-element.153.refs_1_), channel_id=1, source_target_pairs={{0,3},{1,0},{2,1},{3,2},{4,7},{5,4},{6,5},{7,6},{8,11},{9,8},{10,9... | collective-permute-start | bytes 786440 | tf_op jit(solution)/shard_map/ppermute | solution.py:56
  194.1 16.2 %collective-permute-start.32 = (bf16[64,2048]{1,0:T(8,128)(2,1)S(1)}, bf16[64,2048]{1,0:T(8,128)(2,1)}, u32[]{:S(2)}, u32[]{:S(2)}) collective-permute-start(bf16[64,2048]{1,0:T(8,128)(2,1)S(1)} %collective-permute-done.30.refs_4_), channel_id=1, source_target_pairs={{0,1},{1,2},{2,3},{3,0},{4,5},{5,6},{6,7},{7,4},{8,9},{9,10},{10,1... | collective-permute-start | bytes 786440 | tf_op jit(solution)/shard_map/ppermute | solution.py:56
  202.4 7.9 %collective-permute-start.33 = (bf16[64,2048]{1,0:T(8,128)(2,1)S(1)}, bf16[64,2048]{1,0:T(8,128)(2,1)}, u32[]{:S(2)}, u32[]{:S(2)}) collective-permute-start(bf16[64,2048]{1,0:T(8,128)(2,1)S(1)} %collective-permute-done.29.refs_3_), channel_id=1, source_target_pairs={{0,3},{1,0},{2,1},{3,2},{4,7},{5,4},{6,5},{7,6},{8,11},{9,8},{10,9... | collective-permute-start | bytes 786440 | tf_op jit(solution)/shard_map/ppermute | solution.py:56
  222.8 32.5 %collective-permute-start.44 = (bf16[3200,512]{1,0:T(8,128)(2,1)S(1)}, bf16[3200,512]{1,0:T(8,128)(2,1)S(1)}, u32[]{:S(2)}, u32[]{:S(2)}) collective-permute-start(bf16[3200,512]{1,0:T(8,128)(2,1)S(1)} %collective-permute-done.34.refs_7_), channel_id=1, source_target_pairs={{0,4},{4,0},{8,12},{12,8},{1,5},{5,1},{9,13},{13,9},{2,6},{6,2},{1... | collective-permute-start | bytes 9830408 | tf_op jit(solution)/shard_map/ppermute | solution.py:868
  223.9 31.4 %collective-permute-start.51 = (bf16[1280,512]{1,0:T(8,128)(2,1)}, bf16[1280,512]{1,0:T(8,128)(2,1)S(1)}, u32[]{:S(2)}, u32[]{:S(2)}) collective-permute-start(bf16[1280,512]{1,0:T(8,128)(2,1)} %get-tuple-element.182), channel_id=1, source_target_pairs={{0,8},{4,12},{8,0},{12,4},{1,9},{5,13},{9,1},{13,5},{2,10},{6,14},... | collective-permute-start | bytes 3932168 | tf_op jit(solution)/shard_map/ppermute | solution.py:879
  227.7 11.3 %collective-permute-start.38 = (bf16[64,2048]{1,0:T(8,128)(2,1)}, bf16[64,2048]{1,0:T(8,128)(2,1)}, u32[]{:S(2)}, u32[]{:S(2)}) collective-permute-start(bf16[64,2048]{1,0:T(8,128)(2,1)} %get-tuple-element.165), channel_id=1, source_target_pairs={{0,1},{1,2},{2,3},{3,0},{4,5},{5,6},{6,7},{7,4},{8,9},{9,10},{10,1... | collective-permute-start | bytes 786440 | tf_op jit(solution)/shard_map/ppermute | solution.py:56
  229.0 14.3 %collective-permute-start.39 = (bf16[64,2048]{1,0:T(8,128)(2,1)}, bf16[64,2048]{1,0:T(8,128)(2,1)}, u32[]{:S(2)}, u32[]{:S(2)}) collective-permute-start(bf16[64,2048]{1,0:T(8,128)(2,1)} %get-tuple-element.167), channel_id=1, source_target_pairs={{0,3},{1,0},{2,1},{3,2},{4,7},{5,4},{6,5},{7,6},{8,11},{9,8},{10,9... | collective-permute-start | bytes 786440 | tf_op jit(solution)/shard_map/ppermute | solution.py:56
  235.4 14.7 %collective-permute-start.42 = (bf16[64,2048]{1,0:T(8,128)(2,1)}, bf16[64,2048]{1,0:T(8,128)(2,1)S(1)}, u32[]{:S(2)}, u32[]{:S(2)}) collective-permute-start(bf16[64,2048]{1,0:T(8,128)(2,1)} %get-tuple-element.172), channel_id=1, source_target_pairs={{0,1},{1,2},{2,3},{3,0},{4,5},{5,6},{6,7},{7,4},{8,9},{9,10},{10,1... | collective-permute-start | bytes 786440 | tf_op jit(solution)/shard_map/ppermute | solution.py:56
  245.4 9.9 %collective-permute-start.43 = (bf16[64,2048]{1,0:T(8,128)(2,1)}, bf16[64,2048]{1,0:T(8,128)(2,1)S(1)}, u32[]{:S(2)}, u32[]{:S(2)}) collective-permute-start(bf16[64,2048]{1,0:T(8,128)(2,1)} %get-tuple-element.173), channel_id=1, source_target_pairs={{0,3},{1,0},{2,1},{3,2},{4,7},{5,4},{6,5},{7,6},{8,11},{9,8},{10,9... | collective-permute-start | bytes 786440 | tf_op jit(solution)/shard_map/ppermute | solution.py:56
  256.0 56.1 %collective-permute-start.52 = (bf16[1280,512]{1,0:T(8,128)(2,1)S(1)}, bf16[1280,512]{1,0:T(8,128)(2,1)S(1)}, u32[]{:S(2)}, u32[]{:S(2)}) collective-permute-start(bf16[1280,512]{1,0:T(8,128)(2,1)S(1)} %collective-permute-done.51.refs_9_), channel_id=1, source_target_pairs={{0,4},{4,0},{8,12},{12,8},{1,5},{5,1},{9,13},{13,9},{2,6},{6,2},{1... | collective-permute-start | bytes 3932168 | tf_op jit(solution)/shard_map/ppermute | solution.py:881
  256.0 9.1 %collective-permute-start.41 = (bf16[64,2048]{1,0:T(8,128)(2,1)}, bf16[64,2048]{1,0:T(8,128)(2,1)S(1)}, u32[]{:S(2)}, u32[]{:S(2)}) collective-permute-start(bf16[64,2048]{1,0:T(8,128)(2,1)} %get-tuple-element.169), channel_id=1, source_target_pairs={{0,3},{1,0},{2,1},{3,2},{4,7},{5,4},{6,5},{7,6},{8,11},{9,8},{10,9... | collective-permute-start | bytes 786440 | tf_op jit(solution)/shard_map/ppermute | solution.py:56
  258.2 12.8 %collective-permute-start.40 = (bf16[64,2048]{1,0:T(8,128)(2,1)}, bf16[64,2048]{1,0:T(8,128)(2,1)S(1)}, u32[]{:S(2)}, u32[]{:S(2)}) collective-permute-start(bf16[64,2048]{1,0:T(8,128)(2,1)} %get-tuple-element.168), channel_id=1, source_target_pairs={{0,1},{1,2},{2,3},{3,0},{4,5},{5,6},{6,7},{7,4},{8,9},{9,10},{10,1... | collective-permute-start | bytes 786440 | tf_op jit(solution)/shard_map/ppermute | solution.py:56
  273.8 11.2 %collective-permute-start.47 = (bf16[64,2048]{1,0:T(8,128)(2,1)}, bf16[64,2048]{1,0:T(8,128)(2,1)S(1)}, u32[]{:S(2)}, u32[]{:S(2)}) collective-permute-start(bf16[64,2048]{1,0:T(8,128)(2,1)} %finish.6.refs_0_), channel_id=1, source_target_pairs={{0,1},{1,2},{2,3},{3,0},{4,5},{5,6},{6,7},{7,4},{8,9},{9,10},{10,1... | collective-permute-start | bytes 786440 | tf_op jit(solution)/shard_map/ppermute | solution.py:56
  277.8 11.9 %collective-permute-start.46 = (bf16[64,2048]{1,0:T(8,128)(2,1)}, bf16[64,2048]{1,0:T(8,128)(2,1)S(1)}, u32[]{:S(2)}, u32[]{:S(2)}) collective-permute-start(bf16[64,2048]{1,0:T(8,128)(2,1)} %finish.7.refs_1_), channel_id=1, source_target_pairs={{0,3},{1,0},{2,1},{3,2},{4,7},{5,4},{6,5},{7,6},{8,11},{9,8},{10,9... | collective-permute-start | bytes 786440 | tf_op jit(solution)/shard_map/ppermute | solution.py:56
  279.9 16.6 %collective-permute-start.45 = (bf16[64,2048]{1,0:T(8,128)(2,1)S(1)}, bf16[64,2048]{1,0:T(8,128)(2,1)S(1)}, u32[]{:S(2)}, u32[]{:S(2)}) collective-permute-start(bf16[64,2048]{1,0:T(8,128)(2,1)S(1)} %copy-done.26), channel_id=1, source_target_pairs={{0,3},{1,0},{2,1},{3,2},{4,7},{5,4},{6,5},{7,6},{8,11},{9,8},{10,9... | collective-permute-start | bytes 786440 | tf_op jit(solution)/shard_map/ppermute | solution.py:56
  279.9 22.2 %collective-permute-start.48 = (bf16[64,2048]{1,0:T(8,128)(2,1)}, bf16[64,2048]{1,0:T(8,128)(2,1)S(1)}, u32[]{:S(2)}, u32[]{:S(2)}) collective-permute-start(bf16[64,2048]{1,0:T(8,128)(2,1)} %finish.7.refs_1_), channel_id=1, source_target_pairs={{0,1},{1,2},{2,3},{3,0},{4,5},{5,6},{6,7},{7,4},{8,9},{9,10},{10,1... | collective-permute-start | bytes 786440 | tf_op jit(solution)/shard_map/ppermute | solution.py:56
  285.1 22.5 %collective-permute-start.49 = (bf16[64,2048]{1,0:T(8,128)(2,1)S(1)}, bf16[64,2048]{1,0:T(8,128)(2,1)S(1)}, u32[]{:S(2)}, u32[]{:S(2)}) collective-permute-start(bf16[64,2048]{1,0:T(8,128)(2,1)S(1)} %collective-permute-done.47.refs_4_), channel_id=1, source_target_pairs={{0,1},{1,2},{2,3},{3,0},{4,5},{5,6},{6,7},{7,4},{8,9},{9,10},{10,1... | collective-permute-start | bytes 786440 | tf_op jit(solution)/shard_map/ppermute | solution.py:56
  289.7 22.3 %collective-permute-start.50 = (bf16[64,2048]{1,0:T(8,128)(2,1)S(1)}, bf16[64,2048]{1,0:T(8,128)(2,1)S(1)}, u32[]{:S(2)}, u32[]{:S(2)}) collective-permute-start(bf16[64,2048]{1,0:T(8,128)(2,1)S(1)} %collective-permute-done.46.refs_3_), channel_id=1, source_target_pairs={{0,3},{1,0},{2,1},{3,2},{4,7},{5,4},{6,5},{7,6},{8,11},{9,8},{10,9... | collective-permute-start | bytes 786440 | tf_op jit(solution)/shard_map/ppermute | solution.py:56
  (64 other events, 404.1 us)

commit v10 on v9

--- a/solution.py
+++ b/solution.py
@@ -867,17 +867,17 @@
         lots[2], local, halo, across_x[1] = lax.optimization_barrier((lots[2], local, halo, across_x[1]))
         corners[1] = lax.ppermute(across_x[1], "seq", xor_pairs(seq_count, 1))
     mixed, *outer = halo_window(info, near, chunk, far, local, first, halo, win_out, heads)
+    if seq_count == 4:
+        mixed, corners[1] = lax.optimization_barrier((mixed, corners[1]))
     parts = scatter_rows(outer, lambda: near_chunks(mixed, win_out, near, chunk))
     parts = in_halves(parts)
-    if seq_count == 4:
-        parts[1], corners[1] = lax.optimization_barrier((parts[1], corners[1]))
     upper = finish(residual_upper, gain_three, parts[0], True)[0]
     lower = finish(residual_lower, gain_three, parts[1], True)[0]
 
     chunks = gather_rows(upper, lower)
     if seq_count == 4:
         across_x[2] = lax.ppermute(lots[2], "seq", xor_pairs(seq_count, 2))
-        corner, _ = lax.optimization_barrier((across_x[2], parts[1]))
+        corner, _ = lax.optimization_barrier((across_x[2], chunks[1:]))
         corners[2] = lax.ppermute(corner, "seq", xor_pairs(seq_count, 1))
         shared = [vocab_table, beside]
         lots = [(marks_at[n], marks_at[n + 1], [across_x[n], corners[n]]) for n in range(3)]

time: 346 us -> 346 us (level)
  waiting for transfers between devices: 115 us -> 102 us
  starting transfers between devices: 69.2 us -> 81.5 us
    ppermute x39, starting transfers between devices: 51.6 us -> 65 us  [turned(): lax.ppermute(value, 'head', [(i, (i + step) % size) for i in range(size)])]
    ppermute x39, waiting for transfers between devices: 105 us -> 92.5 us  [turned(): lax.ppermute(value, 'head', [(i, (i + step) % size) for i in range(size)])]
    unnamed x112 -> x118, local copies, waits for them, and re-layouts: 9.93 us -> 8.61 us
  transfers between devices with their start and end apart: 56 -> 56, of which waited for: 33 -> 30; matrix products, arithmetic and copies ran while one was open for 3% -> 3% of each run, Pallas kernels for 32% -> 32%
where the time goes in v10:
time: 346 us; the launch traced here: 345 us
  Pallas kernels  133 us (38%)
  waiting for transfers between devices  102 us (29%)
  starting transfers between devices  81.5 us (24%)
  local copies, waits for them, and re-layouts  14.2 us (4%)
  other arithmetic  7.31 us (2%)
  between operations  6.71 us (2%)
    ppermute x39, waiting for transfers between devices, turned(): lax.ppermute(value, 'head', [(i, (i + step) % size) for i in range(size)])  92.5 us
    ppermute x39, starting transfers between devices, turned(): lax.ppermute(value, 'head', [(i, (i + step) % size) for i in range(size)])  65 us
    pallas_call x4, Pallas kernels, lookup(): pl.pallas_call(functools.partial(lookup_kernel, lots), grid=(TABLE_STEPS,...  36.8 us
    pallas_call x1, Pallas kernels, scores(): pl.pallas_call(functools.partial(score_kernel, len(early), len(units), le...  22 us
    pallas_call x2, Pallas kernels, matmul(): pl.pallas_call(matmul_kernel, grid=(b.shape[1] // tile,), in_specs=[pl.Bl...  12.6 us
    pallas_call x2, Pallas kernels, project(): pl.pallas_call(functools.partial(project_kernel, heads, slots, chunk, cou...  11.8 us
    pallas_call x2, Pallas kernels, near_chunks(): pl.pallas_call(functools.partial(near_kernel, rows), in_specs=[whole()] *...  8.87 us
    pallas_call x4, Pallas kernels, finish(): pl.pallas_call(functools.partial(finish_kernel, len(terms), last), in_spe...  8.82 us
  transfers between devices with their start and end apart: 56, of which 30 were waited for; matrix products, arithmetic and copies ran while one was open for 3% of the time, Pallas kernels for 32%

profile of v10, /device:TPU:0, one launch (start us, length us, event | category | flops | bytes accessed | tf_op | source)
XLA Modules:
  0.0 344.6 jit_solution(4557172828053943285)
XLA Ops:
  1.3 2.4 collective-permute-start.2
  5.0 2.3 collective-permute-done.1
  8.0 8.6 %lookup.5 = (bf16[256,512]{1,0:T(8,128)(2,1)}, bf16[256,512]{1,0:T(8,128)(2,1)}) custom-call(s32[1,512]{1,0:T(1,128)} %bitcast.49, bf16[6400,512]{1,0:T(8,128)(2,1)} %refs_3_.2), custom_call_target="tpu_custom_call" | custom-call | flops 4800000000 | bytes 24000000 | tf_op jit(solution)/shard_map/lookup/pallas_call | solution.py:160
  20.9 8.6 %lookup.7 = (bf16[256,512]{1,0:T(8,128)(2,1)}, bf16[256,512]{1,0:T(8,128)(2,1)}) custom-call(s32[1,512]{1,0:T(1,128)} %bitcast.51, bf16[6400,512]{1,0:T(8,128)(2,1)} %refs_3_.2), custom_call_target="tpu_custom_call" | custom-call | flops 4800000000 | bytes 24000000 | tf_op jit(solution)/shard_map/lookup/pallas_call | solution.py:160
  32.0 8.6 %lookup.6 = (bf16[256,512]{1,0:T(8,128)(2,1)}, bf16[256,512]{1,0:T(8,128)(2,1)}) custom-call(s32[1,512]{1,0:T(1,128)} %bitcast.52, bf16[6400,512]{1,0:T(8,128)(2,1)} %refs_3_.2), custom_call_target="tpu_custom_call" | custom-call | flops 4800000000 | bytes 24000000 | tf_op jit(solution)/shard_map/lookup/pallas_call | solution.py:160
  43.5 3.8 %collective-permute-start.8 = (bf16[256,512]{1,0:T(8,128)(2,1)}, bf16[256,512]{1,0:T(8,128)(2,1)S(1)}, u32[]{:S(2)}, u32[]{:S(2)}) collective-permute-start(bf16[256,512]{1,0:T(8,128)(2,1)} %get-tuple-element.105), channel_id=1, source_target_pairs={{0,3},{1,0},{2,1},{3,2},{4,7},{5,4},{6,5},{7,6},{8,11},{9,8},{10,9... | collective-permute-start | bytes 786440 | tf_op jit(solution)/shard_map/ppermute | solution.py:56
  47.3 11.1 %lookup.4 = (bf16[256,512]{1,0:T(8,128)(2,1)}, bf16[256,512]{1,0:T(8,128)(2,1)}, bf16[1920,512]{1,0:T(8,128)(2,1)}, bf16[3200,512]{1,0:T(8,128)(2,1)}, bf16[1280,512]{1,0:T(8,128)(2,1)}) custom-call(s32[1,512]{1,0:T(1,128)} %bitcast.45, bf16[6400,512]{1,0:T(8,128)(2,1)} %refs_3_.2), custom_call_target="tpu_custom_call" | custom-call | flops 4800000000 | bytes 24000000 | tf_op jit(solution)/shard_map/lookup/pallas_call | solution.py:160
  59.5 2.2 collect.1
  63.6 4.6 %collective-permute-done.10.refs_2_ = bf16[128,512]{1,0:T(8,128)(2,1)S(1)} collective-permute-done((bf16[128,512]{1,0:T(8,128)(2,1)}, bf16[128,512]{1,0:T(8,128)(2,1)S(1)}, u32[]{:S(2)}, u32[]{:S(2)}) %collective-permute-start.10) | collective-permute-done | bytes 131104 | tf_op jit(solution)/shard_map/ppermute | solution.py:758
  72.1 2.2 begin.1
  80.5 2.7 collective-permute-done.16.refs_2_
  83.2 4.2 %collective-permute-start.14 = (bf16[64,2048]{1,0:T(8,128)(2,1)}, bf16[64,2048]{1,0:T(8,128)(2,1)S(1)}, u32[]{:S(2)}, u32[]{:S(2)}) collective-permute-start(bf16[64,2048]{1,0:T(8,128)(2,1)} %get-tuple-element.116.refs_1_), channel_id=1, source_target_pairs={{0,3},{1,0},{2,1},{3,2},{4,7},{5,4},{6,5},{7,6},{8,11},{9,8},{10,9... | collective-permute-start | bytes 786440 | tf_op jit(solution)/shard_map/ppermute | solution.py:56
  93.0 9.6 %collective-permute-done.14.refs_3_ = bf16[64,2048]{1,0:T(8,128)(2,1)S(1)} collective-permute-done((bf16[64,2048]{1,0:T(8,128)(2,1)}, bf16[64,2048]{1,0:T(8,128)(2,1)S(1)}, u32[]{:S(2)}, u32[]{:S(2)}) %collective-permute-start.14) | collective-permute-done | bytes 262176 | tf_op jit(solution)/shard_map/ppermute | solution.py:56
  105.0 6.7 %project.2 = (bf16[4,384,256]{2,1,0:T(8,128)(2,1)}, bf16[4,384,256]{2,1,0:T(8,128)(2,1)}, bf16[384,512]{1,0:T(8,128)(2,1)}, f32[4,176,128]{2,1,0:T(8,128)}) custom-call(s32[1]{0:T(128)} %copy.35.bound_ref, s32[3]{0:T(128)} %bitcast.53, bf16[64,2048]{1,0:T(8,128)(2,1)} %get-tuple-element.115.refs_0_, bf16[64,2048]{1,0:T(8,128)(2,1)} %get-tuple-element.116.refs_1_, ...), custom_call_target="tpu_custom_call" | custom-call | flops 3000000000 | bytes 15000000 | tf_op jit(solution)/shard_map/project/pallas_call | solution.py:335
  113.2 5.1 %project.3 = (bf16[4,128,256]{2,1,0:T(8,128)(2,1)}, bf16[4,128,256]{2,1,0:T(8,128)(2,1)}, bf16[128,512]{1,0:T(8,128)(2,1)}, bf16[4,176,128]{2,1,0:T(8,128)(2,1)}) custom-call(s32[1]{0:T(128)} %copy.35.bound_ref, s32[1]{0:T(128)} %slice.77.places_ref, bf16[64,2048]{1,0:T(8,128)(2,1)} %copy-done.40, bf16[64,2048]{1,0:T(8,128)(2,1)} %copy-done.45, ...), custom_call_target="tpu_custom_call" | custom-call | flops 3000000000 | bytes 15000000 | tf_op jit(solution)/shard_map/project/pallas_call | solution.py:335
  118.3 2.8 collective-permute-start.21
  124.5 4.6 %within.1 = (f32[4,512,128]{2,1,0:T(8,128)}, f32[4,512,8]{2,1,0:T(8,128)}) custom-call(s32[1]{0:T(128)} %copy.35.bound_ref, s32[4]{0:T(128)} %copy-done.6, bf16[4,384,256]{2,1,0:T(8,128)(2,1)} %get-tuple-element.119.refs_0_, bf16[4,128,256]{2,1,0:T(8,128)(2,1)} %get-tuple-element.123.refs_1_, bf16[4,384,256]{2,1,0:T(8,128)(2,1)} %get-tuple-element.124.refs_2_, ...), custom_call_target="tpu_custom_call" | custom-call | flops 2700000000 | bytes 13500000 | tf_op jit(solution)/shard_map/within/pallas_call | solution.py:374
  130.3 4.8 %across.1 = (bf16[512,512]{1,0:T(8,128)(2,1)}, bf16[64,2048]{1,0:T(8,128)(2,1)}, bf16[64,2048]{1,0:T(8,128)(2,1)}) custom-call(s32[1]{0:T(128)} %copy.35.bound_ref, s32[4]{0:T(128)} %copy-done.6, s32[3]{0:T(128)} %add_convert_fusion.share_ref, bf16[4,384,256]{2,1,0:T(8,128)(2,1)} %get-tuple-element.119.refs_0_, ...), custom_call_target="tpu_custom_call" | custom-call | flops 2700000000 | bytes 13500000 | tf_op jit(solution)/shard_map/across/pallas_call | solution.py:423
  135.1 3.0 collective-permute-start.34
  138.6 3.3 collective-permute-start.23
  141.9 3.9 %near.2 = (bf16[64,2048]{1,0:T(8,128)(2,1)}, bf16[64,2048]{1,0:T(8,128)(2,1)}, bf16[64,2048]{1,0:T(8,128)(2,1)}, bf16[64,2048]{1,0:T(8,128)(2,1)}, bf16[64,2048]{1,0:T(8,128)(2,1)}, /*index=5*/bf16[64,2048]{1,0:T(8,128)(2,1)}) custom-call(bf16[512,512]{1,0:T(8,128)(2,1)} %get-tuple-element.134.mixed_ref, bf16[512,2048]{1,0:T(8,128)(2,1)} %weight_ref.3), custom_call_target="tpu_custom_call" | custom-call | flops 2400000000 | bytes 12000000 | tf_op jit(solution)/shard_map/near/pallas_call | solution.py:442
  145.8 3.6 %collective-permute-done.22.before_ref = bf16[64,2048]{1,0:T(8,128)(2,1)S(1)} collective-permute-done((bf16[64,2048]{1,0:T(8,128)(2,1)}, bf16[64,2048]{1,0:T(8,128)(2,1)S(1)}, u32[]{:S(2)}, u32[]{:S(2)}) %collective-permute-start.22) | collective-permute-done | bytes 262176 | tf_op jit(solution)/shard_map/ppermute | solution.py:56
  149.3 2.6 collective-permute-done.23.after_ref
  158.6 7.5 %collective-permute-done.24.refs_1_ = bf16[64,2048]{1,0:T(8,128)(2,1)S(1)} collective-permute-done((bf16[64,2048]{1,0:T(8,128)(2,1)}, bf16[64,2048]{1,0:T(8,128)(2,1)S(1)}, u32[]{:S(2)}, u32[]{:S(2)}) %collective-permute-start.24) | collective-permute-done | bytes 262176 | tf_op jit(solution)/shard_map/ppermute | solution.py:56
  171.7 2.7 collective-permute-start.30
  174.4 3.7 %collective-permute-done.27.refs_2_ = bf16[64,2048]{1,0:T(8,128)(2,1)S(1)} collective-permute-done((bf16[64,2048]{1,0:T(8,128)(2,1)}, bf16[64,2048]{1,0:T(8,128)(2,1)S(1)}, u32[]{:S(2)}, u32[]{:S(2)}) %collective-permute-start.27) | collective-permute-done | bytes 262176 | tf_op jit(solution)/shard_map/ppermute | solution.py:56
  183.0 8.8 %collective-permute-start.31 = (bf16[64,2048]{1,0:T(8,128)(2,1)}, bf16[64,2048]{1,0:T(8,128)(2,1)S(1)}, u32[]{:S(2)}, u32[]{:S(2)}) collective-permute-start(bf16[64,2048]{1,0:T(8,128)(2,1)} %get-tuple-element.151.refs_1_), channel_id=1, source_target_pairs={{0,1},{1,2},{2,3},{3,0},{4,5},{5,6},{6,7},{7,4},{8,9},{9,10},{10,1... | collective-permute-start | bytes 786440 | tf_op jit(solution)/shard_map/ppermute | solution.py:56
  195.8 3.8 %collective-permute-done.31.refs_5_ = bf16[64,2048]{1,0:T(8,128)(2,1)S(1)} collective-permute-done((bf16[64,2048]{1,0:T(8,128)(2,1)}, bf16[64,2048]{1,0:T(8,128)(2,1)S(1)}, u32[]{:S(2)}, u32[]{:S(2)}) %collective-permute-start.31) | collective-permute-done | bytes 262176 | tf_op jit(solution)/shard_map/ppermute | solution.py:56
  199.6 6.6 %collective-permute-start.32 = (bf16[64,2048]{1,0:T(8,128)(2,1)S(1)}, bf16[64,2048]{1,0:T(8,128)(2,1)}, u32[]{:S(2)}, u32[]{:S(2)}) collective-permute-start(bf16[64,2048]{1,0:T(8,128)(2,1)S(1)} %collective-permute-done.30.refs_4_), channel_id=1, source_target_pairs={{0,1},{1,2},{2,3},{3,0},{4,5},{5,6},{6,7},{7,4},{8,9},{9,10},{10,1... | collective-permute-start | bytes 786440 | tf_op jit(solution)/shard_map/ppermute | solution.py:56
  208.1 7.2 %matmul.2.refs_0_ = bf16[384,1536]{1,0:T(8,128)(2,1)} custom-call(bf16[64,2048]{1,0:T(8,128)(2,1)} %get-tuple-element.146.refs_0_, bf16[64,2048]{1,0:T(8,128)(2,1)} %get-tuple-element.151.refs_1_, bf16[64,2048]{1,0:T(8,128)(2,1)} %copy-done.24, bf16[64,2048]{1,0:T(8,128)(2,1)} %copy-done.37, bf16[64,2048]{1,0:T(8,128)(2,1)} %copy-done.20, ...), custom_call_target="tpu_custom_call" | custom-call | flops 3000000000 | bytes 15000000 | tf_op jit(solution)/shard_map/matmul/pallas_call | solution.py:461
  215.4 5.4 %matmul.3.refs_1_ = bf16[128,1536]{1,0:T(8,128)(2,1)} custom-call(bf16[64,2048]{1,0:T(8,128)(2,1)} %collective-permute-done.32.refs_0_, bf16[64,2048]{1,0:T(8,128)(2,1)} %collective-permute-done.33.refs_1_, bf16[2048,1536]{1,0:T(8,128)(2,1)} %refs_2_.3), custom_call_target="tpu_custom_call" | custom-call | flops 3000000000 | bytes 15000000 | tf_op jit(solution)/shard_map/matmul/pallas_call | solution.py:461
  223.0 4.8 %local_window.1 = (bf16[512,512]{1,0:T(8,128)(2,1)}, bf16[64,1536]{1,0:T(8,128)(2,1)}) custom-call(s32[1]{0:T(128)} %copy.35.bound_ref, s32[4]{0:T(128)} %copy-done.6, bf16[384,1536]{1,0:T(8,128)(2,1)} %matmul.2.refs_0_, bf16[128,1536]{1,0:T(8,128)(2,1)} %matmul.3.refs_1_), custom_call_target="tpu_custom_call" | custom-call | flops 4800000000 | bytes 24000000 | tf_op jit(solution)/shard_map/local_window/pallas_call | solution.py:529
  228.5 3.7 %halo_window.1 = (bf16[512,512]{1,0:T(8,128)(2,1)}, bf16[64,2048]{1,0:T(8,128)(2,1)}, bf16[64,2048]{1,0:T(8,128)(2,1)}) custom-call(s32[3]{0:T(128)} %pad_add_fusion.4.info_ref, bf16[512,512]{1,0:T(8,128)(2,1)} %get-tuple-element.157.local_ref, bf16[64,1536]{1,0:T(8,128)(2,1)} %get-tuple-element.158.first_ref, bf16[64,1536]{1,0:T(8,128)(2,1)} %copy-done.51, ...), custom_call_target="tpu_custom_call" | custom-call | flops 2700000000 | bytes 13500000 | tf_op jit(solution)/shard_map/halo_window/pallas_call | solution.py:566
  233.4 2.6 collective-permute-start.40
  236.1 5.0 %near.3 = (bf16[64,2048]{1,0:T(8,128)(2,1)}, bf16[64,2048]{1,0:T(8,128)(2,1)}, bf16[64,2048]{1,0:T(8,128)(2,1)}, bf16[64,2048]{1,0:T(8,128)(2,1)}, bf16[64,2048]{1,0:T(8,128)(2,1)}, /*index=5*/bf16[64,2048]{1,0:T(8,128)(2,1)}) custom-call(bf16[512,512]{1,0:T(8,128)(2,1)} %get-tuple-element.162.mixed_ref, bf16[512,2048]{1,0:T(8,128)(2,1)} %weight_ref.5), custom_call_target="tpu_custom_call" | custom-call | flops 2400000000 | bytes 12000000 | tf_op jit(solution)/shard_map/near/pallas_call | solution.py:442
  241.1 2.3 collective-permute-done.39.before_ref
  243.5 3.8 %collective-permute-done.40.after_ref = bf16[64,2048]{1,0:T(8,128)(2,1)} collective-permute-done((bf16[64,2048]{1,0:T(8,128)(2,1)}, bf16[64,2048]{1,0:T(8,128)(2,1)}, u32[]{:S(2)}, u32[]{:S(2)}) %collective-permute-start.40) | collective-permute-done | bytes 262176 | tf_op jit(solution)/shard_map/ppermute | solution.py:56
  250.6 2.5 collective-permute-start.42
  255.1 5.4 %collective-permute-done.41.refs_1_ = bf16[64,2048]{1,0:T(8,128)(2,1)S(1)} collective-permute-done((bf16[64,2048]{1,0:T(8,128)(2,1)}, bf16[64,2048]{1,0:T(8,128)(2,1)S(1)}, u32[]{:S(2)}, u32[]{:S(2)}) %collective-permute-start.41) | collective-permute-done | bytes 262176 | tf_op jit(solution)/shard_map/ppermute | solution.py:56
  260.5 3.8 %collective-permute-done.42.refs_2_ = bf16[64,2048]{1,0:T(8,128)(2,1)S(1)} collective-permute-done((bf16[64,2048]{1,0:T(8,128)(2,1)S(1)}, bf16[64,2048]{1,0:T(8,128)(2,1)S(1)}, u32[]{:S(2)}, u32[]{:S(2)}) %collective-permute-start.42) | collective-permute-done | bytes 262176 | tf_op jit(solution)/shard_map/ppermute | solution.py:56
  267.8 3.7 %collective-permute-done.44.refs_2_ = bf16[64,2048]{1,0:T(8,128)(2,1)S(1)} collective-permute-done((bf16[64,2048]{1,0:T(8,128)(2,1)}, bf16[64,2048]{1,0:T(8,128)(2,1)S(1)}, u32[]{:S(2)}, u32[]{:S(2)}) %collective-permute-start.44) | collective-permute-done | bytes 262176 | tf_op jit(solution)/shard_map/ppermute | solution.py:56
  271.4 6.0 %collective-permute-done.43.refs_1_ = bf16[64,2048]{1,0:T(8,128)(2,1)S(1)} collective-permute-done((bf16[64,2048]{1,0:T(8,128)(2,1)S(1)}, bf16[64,2048]{1,0:T(8,128)(2,1)S(1)}, u32[]{:S(2)}, u32[]{:S(2)}) %collective-permute-start.43) | collective-permute-done | bytes 262176 | tf_op jit(solution)/shard_map/ppermute | solution.py:56
  284.4 5.4 %collective-permute-done.46.refs_3_ = bf16[64,2048]{1,0:T(8,128)(2,1)S(1)} collective-permute-done((bf16[64,2048]{1,0:T(8,128)(2,1)}, bf16[64,2048]{1,0:T(8,128)(2,1)S(1)}, u32[]{:S(2)}, u32[]{:S(2)}) %collective-permute-start.46) | collective-permute-done | bytes 262176 | tf_op jit(solution)/shard_map/ppermute | solution.py:56
  291.9 14.5 %collective-permute-done.45.refs_2_ = bf16[64,2048]{1,0:T(8,128)(2,1)S(1)} collective-permute-done((bf16[64,2048]{1,0:T(8,128)(2,1)S(1)}, bf16[64,2048]{1,0:T(8,128)(2,1)S(1)}, u32[]{:S(2)}, u32[]{:S(2)}) %collective-permute-start.45) | collective-permute-done | bytes 262176 | tf_op jit(solution)/shard_map/ppermute | solution.py:56
  306.4 2.8 collective-permute-done.50.refs_2_
  309.3 3.0 turn.1.refs_0_
  313.6 22.0 %scores.1 = f32[8,512]{1,0:T(8,128)} custom-call(s32[4]{0:T(128)} %iota_xor_fusion.order_ref, bf16[2048,384]{1,0:T(8,128)(2,1)} %turn.1.refs_0_, bf16[64,2048]{1,0:T(8,128)(2,1)} %copy-done.28, bf16[64,2048]{1,0:T(8,128)(2,1)} %copy-done.36, bf16[6400,512]{1,0:T(8,128)(2,1)} %refs_3_.2, bf16[6400,512]{1,0:T(8,128)(2,1)} %collective-permute-done.36.refs_4_, ...), custom_call_target="tpu_custom_call" | custom-call | flops 12000000000 | bytes 60000000 | tf_op jit(solution)/shard_map/scores/pallas_call | solution.py:668
  339.8 3.0 collective-permute-done.54
  (241 shorter events, 86.6 us)
Async XLA Ops:
  4.4 217.3 %collective-permute-start.36 = (bf16[6400,512]{1,0:T(8,128)(2,1)}, bf16[6400,512]{1,0:T(8,128)(2,1)}, u32[]{:S(2)}, u32[]{:S(2)}) collective-permute-start(bf16[6400,512]{1,0:T(8,128)(2,1)} %refs_3_.2), channel_id=1, source_target_pairs={{0,4},{4,0},{8,12},{12,8},{1,5},{5,1},{9,13},{13,9},{2,6},{6,2},{1... | collective-permute-start | bytes 19660808 | tf_op jit(solution)/shard_map/ppermute | solution.py:848
  16.5 24.1 %collective-permute-start.3 = (bf16[256,512]{1,0:T(8,128)(2,1)}, bf16[256,512]{1,0:T(8,128)(2,1)S(1)}, u32[]{:S(2)}, u32[]{:S(2)}) collective-permute-start(bf16[256,512]{1,0:T(8,128)(2,1)} %get-tuple-element.95), channel_id=1, source_target_pairs={{0,1},{1,2},{2,3},{3,0},{4,5},{5,6},{6,7},{7,4},{8,9},{9,10},{10,1... | collective-permute-start | bytes 786440 | tf_op jit(solution)/shard_map/ppermute | solution.py:56
  18.1 22.5 %collective-permute-start.4 = (bf16[256,512]{1,0:T(8,128)(2,1)}, bf16[256,512]{1,0:T(8,128)(2,1)S(1)}, u32[]{:S(2)}, u32[]{:S(2)}) collective-permute-start(bf16[256,512]{1,0:T(8,128)(2,1)} %get-tuple-element.96), channel_id=1, source_target_pairs={{0,3},{1,0},{2,1},{3,2},{4,7},{5,4},{6,5},{7,6},{8,11},{9,8},{10,9... | collective-permute-start | bytes 786440 | tf_op jit(solution)/shard_map/ppermute | solution.py:56
  29.5 29.0 %collective-permute-start.6 = (bf16[256,512]{1,0:T(8,128)(2,1)}, bf16[256,512]{1,0:T(8,128)(2,1)S(1)}, u32[]{:S(2)}, u32[]{:S(2)}) collective-permute-start(bf16[256,512]{1,0:T(8,128)(2,1)} %get-tuple-element.102), channel_id=1, source_target_pairs={{0,3},{1,0},{2,1},{3,2},{4,7},{5,4},{6,5},{7,6},{8,11},{9,8},{10,9... | collective-permute-start | bytes 786440 | tf_op jit(solution)/shard_map/ppermute | solution.py:56
  31.3 27.2 %collective-permute-start.7 = (bf16[256,512]{1,0:T(8,128)(2,1)}, bf16[256,512]{1,0:T(8,128)(2,1)S(1)}, u32[]{:S(2)}, u32[]{:S(2)}) collective-permute-start(bf16[256,512]{1,0:T(8,128)(2,1)} %get-tuple-element.104), channel_id=1, source_target_pairs={{0,1},{1,2},{2,3},{3,0},{4,5},{5,6},{6,7},{7,4},{8,9},{9,10},{10,1... | collective-permute-start | bytes 786440 | tf_op jit(solution)/shard_map/ppermute | solution.py:56
  43.5 15.0 %collective-permute-start.5 = (bf16[256,512]{1,0:T(8,128)(2,1)}, bf16[256,512]{1,0:T(8,128)(2,1)S(1)}, u32[]{:S(2)}, u32[]{:S(2)}) collective-permute-start(bf16[256,512]{1,0:T(8,128)(2,1)} %get-tuple-element.101), channel_id=1, source_target_pairs={{0,1},{1,2},{2,3},{3,0},{4,5},{5,6},{6,7},{7,4},{8,9},{9,10},{10,1... | collective-permute-start | bytes 786440 | tf_op jit(solution)/shard_map/ppermute | solution.py:56
  43.5 15.0 %collective-permute-start.8 = (bf16[256,512]{1,0:T(8,128)(2,1)}, bf16[256,512]{1,0:T(8,128)(2,1)S(1)}, u32[]{:S(2)}, u32[]{:S(2)}) collective-permute-start(bf16[256,512]{1,0:T(8,128)(2,1)} %get-tuple-element.105), channel_id=1, source_target_pairs={{0,3},{1,0},{2,1},{3,2},{4,7},{5,4},{6,5},{7,6},{8,11},{9,8},{10,9... | collective-permute-start | bytes 786440 | tf_op jit(solution)/shard_map/ppermute | solution.py:56
  61.7 6.5 %collective-permute-start.10 = (bf16[128,512]{1,0:T(8,128)(2,1)}, bf16[128,512]{1,0:T(8,128)(2,1)S(1)}, u32[]{:S(2)}, u32[]{:S(2)}) collective-permute-start(bf16[128,512]{1,0:T(8,128)(2,1)} %get-tuple-element.108), channel_id=1, source_target_pairs={{0,8},{4,12},{8,0},{12,4},{1,9},{5,13},{9,1},{13,5},{2,10},{6,14},... | collective-permute-start | bytes 393224 | tf_op jit(solution)/shard_map/ppermute | solution.py:758
  62.3 7.9 %collective-permute-start.11 = (bf16[128,512]{1,0:T(8,128)(2,1)}, bf16[128,512]{1,0:T(8,128)(2,1)S(1)}, u32[]{:S(2)}, u32[]{:S(2)}) collective-permute-start(bf16[128,512]{1,0:T(8,128)(2,1)} %get-tuple-element.109), channel_id=1, source_target_pairs={{0,12},{4,8},{8,4},{12,0},{1,13},{5,9},{9,5},{13,1},{2,14},{6,10},... | collective-permute-start | bytes 393224 | tf_op jit(solution)/shard_map/ppermute | solution.py:758
  70.3 48.0 %collective-permute-start.18 = (bf16[1920,512]{1,0:T(8,128)(2,1)}, bf16[1920,512]{1,0:T(8,128)(2,1)S(1)}, u32[]{:S(2)}, u32[]{:S(2)}) collective-permute-start(bf16[1920,512]{1,0:T(8,128)(2,1)} %get-tuple-element.132), channel_id=1, source_target_pairs={{0,8},{4,12},{8,0},{12,4},{1,9},{5,13},{9,1},{13,5},{2,10},{6,14},... | collective-permute-start | bytes 5898248 | tf_op jit(solution)/shard_map/ppermute | solution.py:808
  74.4 8.8 %collective-permute-start.16 = (bf16[64,2048]{1,0:T(8,128)(2,1)}, bf16[64,2048]{1,0:T(8,128)(2,1)S(1)}, u32[]{:S(2)}, u32[]{:S(2)}) collective-permute-start(bf16[64,2048]{1,0:T(8,128)(2,1)} %get-tuple-element.115.refs_0_), channel_id=1, source_target_pairs={{0,3},{1,0},{2,1},{3,2},{4,7},{5,4},{6,5},{7,6},{8,11},{9,8},{10,9... | collective-permute-start | bytes 786440 | tf_op jit(solution)/shard_map/ppermute | solution.py:56
  80.1 12.9 %collective-permute-start.12 = (bf16[64,2048]{1,0:T(8,128)(2,1)}, bf16[64,2048]{1,0:T(8,128)(2,1)S(1)}, u32[]{:S(2)}, u32[]{:S(2)}) collective-permute-start(bf16[64,2048]{1,0:T(8,128)(2,1)} %get-tuple-element.115.refs_0_), channel_id=1, source_target_pairs={{0,1},{1,2},{2,3},{3,0},{4,5},{5,6},{6,7},{7,4},{8,9},{9,10},{10,1... | collective-permute-start | bytes 786440 | tf_op jit(solution)/shard_map/ppermute | solution.py:56
  80.4 23.8 %collective-permute-start.17 = (bf16[64,2048]{1,0:T(8,128)(2,1)}, bf16[64,2048]{1,0:T(8,128)(2,1)S(1)}, u32[]{:S(2)}, u32[]{:S(2)}) collective-permute-start(bf16[64,2048]{1,0:T(8,128)(2,1)} %get-tuple-element.116.refs_1_), channel_id=1, source_target_pairs={{0,1},{1,2},{2,3},{3,0},{4,5},{5,6},{6,7},{7,4},{8,9},{9,10},{10,1... | collective-permute-start | bytes 786440 | tf_op jit(solution)/shard_map/ppermute | solution.py:56
  83.2 19.4 %collective-permute-start.14 = (bf16[64,2048]{1,0:T(8,128)(2,1)}, bf16[64,2048]{1,0:T(8,128)(2,1)S(1)}, u32[]{:S(2)}, u32[]{:S(2)}) collective-permute-start(bf16[64,2048]{1,0:T(8,128)(2,1)} %get-tuple-element.116.refs_1_), channel_id=1, source_target_pairs={{0,3},{1,0},{2,1},{3,2},{4,7},{5,4},{6,5},{7,6},{8,11},{9,8},{10,9... | collective-permute-start | bytes 786440 | tf_op jit(solution)/shard_map/ppermute | solution.py:56
  93.0 18.7 %collective-permute-start.13 = (bf16[64,2048]{1,0:T(8,128)(2,1)S(1)}, bf16[64,2048]{1,0:T(8,128)(2,1)S(1)}, u32[]{:S(2)}, u32[]{:S(2)}) collective-permute-start(bf16[64,2048]{1,0:T(8,128)(2,1)S(1)} %collective-permute-done.12.refs_4_), channel_id=1, source_target_pairs={{0,1},{1,2},{2,3},{3,0},{4,5},{5,6},{6,7},{7,4},{8,9},{9,10},{10,1... | collective-permute-start | bytes 786440 | tf_op jit(solution)/shard_map/ppermute | solution.py:56
  102.5 10.0 %collective-permute-start.15 = (bf16[64,2048]{1,0:T(8,128)(2,1)S(1)}, bf16[64,2048]{1,0:T(8,128)(2,1)S(1)}, u32[]{:S(2)}, u32[]{:S(2)}) collective-permute-start(bf16[64,2048]{1,0:T(8,128)(2,1)S(1)} %collective-permute-done.14.refs_3_), channel_id=1, source_target_pairs={{0,3},{1,0},{2,1},{3,2},{4,7},{5,4},{6,5},{7,6},{8,11},{9,8},{10,9... | collective-permute-start | bytes 786440 | tf_op jit(solution)/shard_map/ppermute | solution.py:56
  118.3 10.8 %collective-permute-start.21 = (bf16[4,176,128]{2,1,0:T(8,128)(2,1)}, bf16[4,176,128]{2,1,0:T(8,128)(2,1)S(1)}, u32[]{:S(2)}, u32[]{:S(2)}) collective-permute-start(bf16[4,176,128]{2,1,0:T(8,128)(2,1)} %get-tuple-element.133), channel_id=1, source_target_pairs={{0,12},{1,13},{2,14},{3,15},{16,28},{17,29},{18,30},{19,31}} | collective-permute-start | bytes 540680 | tf_op jit(solution)/shard_map/ppermute | solution.py:818
  121.1 8.4 %collective-permute-start.20 = (bf16[4,176,128]{2,1,0:T(8,128)(2,1)}, bf16[4,176,128]{2,1,0:T(8,128)(2,1)S(1)}, u32[]{:S(2)}, u32[]{:S(2)}) collective-permute-start(bf16[4,176,128]{2,1,0:T(8,128)(2,1)} %get-tuple-element.133), channel_id=1, source_target_pairs={{0,8},{4,12},{1,9},{5,13},{2,10},{6,14},{3,11},{7,15},{16,24},{20,... | collective-permute-start | bytes 540680 | tf_op jit(solution)/shard_map/ppermute | solution.py:818
  122.4 7.1 %collective-permute-start.19 = (bf16[4,176,128]{2,1,0:T(8,128)(2,1)}, bf16[4,176,128]{2,1,0:T(8,128)(2,1)S(1)}, u32[]{:S(2)}, u32[]{:S(2)}) collective-permute-start(bf16[4,176,128]{2,1,0:T(8,128)(2,1)} %get-tuple-element.133), channel_id=1, source_target_pairs={{0,4},{4,8},{8,12},{1,5},{5,9},{9,13},{2,6},{6,10},{10,14},{3,7},{... | collective-permute-start | bytes 540680 | tf_op jit(solution)/shard_map/ppermute | solution.py:818
  135.1 86.6 %collective-permute-start.34 = (bf16[3200,512]{1,0:T(8,128)(2,1)S(1)}, bf16[3200,512]{1,0:T(8,128)(2,1)S(1)}, u32[]{:S(2)}, u32[]{:S(2)}) collective-permute-start(bf16[3200,512]{1,0:T(8,128)(2,1)S(1)} %copy-done.8), channel_id=1, source_target_pairs={{0,8},{4,12},{8,0},{12,4},{1,9},{5,13},{9,1},{13,5},{2,10},{6,14},... | collective-permute-start | bytes 9830408 | tf_op jit(solution)/shard_map/ppermute | solution.py:847
  138.1 11.3 %collective-permute-start.22 = (bf16[64,2048]{1,0:T(8,128)(2,1)}, bf16[64,2048]{1,0:T(8,128)(2,1)S(1)}, u32[]{:S(2)}, u32[]{:S(2)}) collective-permute-start(bf16[64,2048]{1,0:T(8,128)(2,1)} %get-tuple-element.137), channel_id=1, source_target_pairs={{0,1},{1,2},{2,3},{3,0},{4,5},{5,6},{6,7},{7,4},{8,9},{9,10},{10,1... | collective-permute-start | bytes 786440 | tf_op jit(solution)/shard_map/ppermute | solution.py:56
  138.6 13.3 %collective-permute-start.23 = (bf16[64,2048]{1,0:T(8,128)(2,1)}, bf16[64,2048]{1,0:T(8,128)(2,1)S(1)}, u32[]{:S(2)}, u32[]{:S(2)}) collective-permute-start(bf16[64,2048]{1,0:T(8,128)(2,1)} %get-tuple-element.139), channel_id=1, source_target_pairs={{0,3},{1,0},{2,1},{3,2},{4,7},{5,4},{6,5},{7,6},{8,11},{9,8},{10,9... | collective-permute-start | bytes 786440 | tf_op jit(solution)/shard_map/ppermute | solution.py:56
  145.8 10.7 %collective-permute-start.25 = (bf16[64,2048]{1,0:T(8,128)(2,1)}, bf16[64,2048]{1,0:T(8,128)(2,1)S(1)}, u32[]{:S(2)}, u32[]{:S(2)}) collective-permute-start(bf16[64,2048]{1,0:T(8,128)(2,1)} %get-tuple-element.141), channel_id=1, source_target_pairs={{0,3},{1,0},{2,1},{3,2},{4,7},{5,4},{6,5},{7,6},{8,11},{9,8},{10,9... | collective-permute-start | bytes 786440 | tf_op jit(solution)/shard_map/ppermute | solution.py:56
  154.7 11.3 %collective-permute-start.24 = (bf16[64,2048]{1,0:T(8,128)(2,1)}, bf16[64,2048]{1,0:T(8,128)(2,1)S(1)}, u32[]{:S(2)}, u32[]{:S(2)}) collective-permute-start(bf16[64,2048]{1,0:T(8,128)(2,1)} %get-tuple-element.140), channel_id=1, source_target_pairs={{0,1},{1,2},{2,3},{3,0},{4,5},{5,6},{6,7},{7,4},{8,9},{9,10},{10,1... | collective-permute-start | bytes 786440 | tf_op jit(solution)/shard_map/ppermute | solution.py:56
  155.2 66.5 %collective-permute-start.35 = (bf16[1920,512]{1,0:T(8,128)(2,1)}, bf16[1920,512]{1,0:T(8,128)(2,1)}, u32[]{:S(2)}, u32[]{:S(2)}) collective-permute-start(bf16[1920,512]{1,0:T(8,128)(2,1)} %copy-done.11), channel_id=1, source_target_pairs={{0,4},{4,0},{8,12},{12,8},{1,5},{5,1},{9,13},{13,9},{2,6},{6,2},{1... | collective-permute-start | bytes 5898248 | tf_op jit(solution)/shard_map/ppermute | solution.py:809
  156.5 15.2 %collective-permute-start.26 = (bf16[64,2048]{1,0:T(8,128)(2,1)S(1)}, bf16[64,2048]{1,0:T(8,128)(2,1)S(1)}, u32[]{:S(2)}, u32[]{:S(2)}) collective-permute-start(bf16[64,2048]{1,0:T(8,128)(2,1)S(1)} %copy-done.25), channel_id=1, source_target_pairs={{0,1},{1,2},{2,3},{3,0},{4,5},{5,6},{6,7},{7,4},{8,9},{9,10},{10,1... | collective-permute-start | bytes 786440 | tf_op jit(solution)/shard_map/ppermute | solution.py:56
  166.1 12.1 %collective-permute-start.27 = (bf16[64,2048]{1,0:T(8,128)(2,1)}, bf16[64,2048]{1,0:T(8,128)(2,1)S(1)}, u32[]{:S(2)}, u32[]{:S(2)}) collective-permute-start(bf16[64,2048]{1,0:T(8,128)(2,1)} %get-tuple-element.150), channel_id=1, source_target_pairs={{0,3},{1,0},{2,1},{3,2},{4,7},{5,4},{6,5},{7,6},{8,11},{9,8},{10,9... | collective-permute-start | bytes 786440 | tf_op jit(solution)/shard_map/ppermute | solution.py:56
  171.7 11.2 %collective-permute-start.30 = (bf16[64,2048]{1,0:T(8,128)(2,1)}, bf16[64,2048]{1,0:T(8,128)(2,1)S(1)}, u32[]{:S(2)}, u32[]{:S(2)}) collective-permute-start(bf16[64,2048]{1,0:T(8,128)(2,1)} %get-tuple-element.146.refs_0_), channel_id=1, source_target_pairs={{0,1},{1,2},{2,3},{3,0},{4,5},{5,6},{6,7},{7,4},{8,9},{9,10},{10,1... | collective-permute-start | bytes 786440 | tf_op jit(solution)/shard_map/ppermute | solution.py:56
  178.2 13.6 %collective-permute-start.28 = (bf16[64,2048]{1,0:T(8,128)(2,1)}, bf16[64,2048]{1,0:T(8,128)(2,1)S(1)}, u32[]{:S(2)}, u32[]{:S(2)}) collective-permute-start(bf16[64,2048]{1,0:T(8,128)(2,1)} %get-tuple-element.146.refs_0_), channel_id=1, source_target_pairs={{0,3},{1,0},{2,1},{3,2},{4,7},{5,4},{6,5},{7,6},{8,11},{9,8},{10,9... | collective-permute-start | bytes 786440 | tf_op jit(solution)/shard_map/ppermute | solution.py:56
  183.0 16.6 %collective-permute-start.31 = (bf16[64,2048]{1,0:T(8,128)(2,1)}, bf16[64,2048]{1,0:T(8,128)(2,1)S(1)}, u32[]{:S(2)}, u32[]{:S(2)}) collective-permute-start(bf16[64,2048]{1,0:T(8,128)(2,1)} %get-tuple-element.151.refs_1_), channel_id=1, source_target_pairs={{0,1},{1,2},{2,3},{3,0},{4,5},{5,6},{6,7},{7,4},{8,9},{9,10},{10,1... | collective-permute-start | bytes 786440 | tf_op jit(solution)/shard_map/ppermute | solution.py:56
  191.8 14.4 %collective-permute-start.29 = (bf16[64,2048]{1,0:T(8,128)(2,1)}, bf16[64,2048]{1,0:T(8,128)(2,1)S(1)}, u32[]{:S(2)}, u32[]{:S(2)}) collective-permute-start(bf16[64,2048]{1,0:T(8,128)(2,1)} %get-tuple-element.151.refs_1_), channel_id=1, source_target_pairs={{0,3},{1,0},{2,1},{3,2},{4,7},{5,4},{6,5},{7,6},{8,11},{9,8},{10,9... | collective-permute-start | bytes 786440 | tf_op jit(solution)/shard_map/ppermute | solution.py:56
  199.6 15.8 %collective-permute-start.32 = (bf16[64,2048]{1,0:T(8,128)(2,1)S(1)}, bf16[64,2048]{1,0:T(8,128)(2,1)}, u32[]{:S(2)}, u32[]{:S(2)}) collective-permute-start(bf16[64,2048]{1,0:T(8,128)(2,1)S(1)} %collective-permute-done.30.refs_4_), channel_id=1, source_target_pairs={{0,1},{1,2},{2,3},{3,0},{4,5},{5,6},{6,7},{7,4},{8,9},{9,10},{10,1... | collective-permute-start | bytes 786440 | tf_op jit(solution)/shard_map/ppermute | solution.py:56
  206.2 9.1 %collective-permute-start.33 = (bf16[64,2048]{1,0:T(8,128)(2,1)S(1)}, bf16[64,2048]{1,0:T(8,128)(2,1)}, u32[]{:S(2)}, u32[]{:S(2)}) collective-permute-start(bf16[64,2048]{1,0:T(8,128)(2,1)S(1)} %collective-permute-done.29.refs_3_), channel_id=1, source_target_pairs={{0,3},{1,0},{2,1},{3,2},{4,7},{5,4},{6,5},{7,6},{8,11},{9,8},{10,9... | collective-permute-start | bytes 786440 | tf_op jit(solution)/shard_map/ppermute | solution.py:56
  221.7 6.1 %collective-permute-start.37 = (bf16[64,1536]{1,0:T(8,128)(2,1)S(1)}, bf16[64,1536]{1,0:T(8,128)(2,1)S(1)}, u32[]{:S(2)}, u32[]{:S(2)}) collective-permute-start(bf16[64,1536]{1,0:T(8,128)(2,1)S(1)} %fusion.2), channel_id=1, source_target_pairs={{0,4},{4,8},{8,12},{1,5},{5,9},{9,13},{2,6},{6,10},{10,14},{3,7},{... | collective-permute-start | bytes 589832 | tf_op jit(solution)/shard_map/ppermute | solution.py:864
  227.9 8.2 %collective-permute-start.38 = (bf16[3200,512]{1,0:T(8,128)(2,1)S(1)}, bf16[3200,512]{1,0:T(8,128)(2,1)S(1)}, u32[]{:S(2)}, u32[]{:S(2)}) collective-permute-start(bf16[3200,512]{1,0:T(8,128)(2,1)S(1)} %collective-permute-done.34.refs_7_), channel_id=1, source_target_pairs={{0,4},{4,0},{8,12},{12,8},{1,5},{5,1},{9,13},{13,9},{2,6},{6,2},{1... | collective-permute-start | bytes 9830408 | tf_op jit(solution)/shard_map/ppermute | solution.py:868
  232.3 11.2 %collective-permute-start.39 = (bf16[64,2048]{1,0:T(8,128)(2,1)}, bf16[64,2048]{1,0:T(8,128)(2,1)S(1)}, u32[]{:S(2)}, u32[]{:S(2)}) collective-permute-start(bf16[64,2048]{1,0:T(8,128)(2,1)} %get-tuple-element.165), channel_id=1, source_target_pairs={{0,1},{1,2},{2,3},{3,0},{4,5},{5,6},{6,7},{7,4},{8,9},{9,10},{10,1... | collective-permute-start | bytes 786440 | tf_op jit(solution)/shard_map/ppermute | solution.py:56
  233.4 13.8 %collective-permute-start.40 = (bf16[64,2048]{1,0:T(8,128)(2,1)}, bf16[64,2048]{1,0:T(8,128)(2,1)}, u32[]{:S(2)}, u32[]{:S(2)}) collective-permute-start(bf16[64,2048]{1,0:T(8,128)(2,1)} %get-tuple-element.167), channel_id=1, source_target_pairs={{0,3},{1,0},{2,1},{3,2},{4,7},{5,4},{6,5},{7,6},{8,11},{9,8},{10,9... | collective-permute-start | bytes 786440 | tf_op jit(solution)/shard_map/ppermute | solution.py:56
  236.1 55.8 %collective-permute-start.51 = (bf16[1280,512]{1,0:T(8,128)(2,1)S(1)}, bf16[1280,512]{1,0:T(8,128)(2,1)}, u32[]{:S(2)}, u32[]{:S(2)}) collective-permute-start(bf16[1280,512]{1,0:T(8,128)(2,1)S(1)} %copy-done.12), channel_id=1, source_target_pairs={{0,8},{4,12},{8,0},{12,4},{1,9},{5,13},{9,1},{13,5},{2,10},{6,14},... | collective-permute-start | bytes 3932168 | tf_op jit(solution)/shard_map/ppermute | solution.py:879
  249.3 11.3 %collective-permute-start.41 = (bf16[64,2048]{1,0:T(8,128)(2,1)}, bf16[64,2048]{1,0:T(8,128)(2,1)S(1)}, u32[]{:S(2)}, u32[]{:S(2)}) collective-permute-start(bf16[64,2048]{1,0:T(8,128)(2,1)} %get-tuple-element.168), channel_id=1, source_target_pairs={{0,1},{1,2},{2,3},{3,0},{4,5},{5,6},{6,7},{7,4},{8,9},{9,10},{10,1... | collective-permute-start | bytes 786440 | tf_op jit(solution)/shard_map/ppermute | solution.py:56
  250.6 13.7 %collective-permute-start.42 = (bf16[64,2048]{1,0:T(8,128)(2,1)S(1)}, bf16[64,2048]{1,0:T(8,128)(2,1)S(1)}, u32[]{:S(2)}, u32[]{:S(2)}) collective-permute-start(bf16[64,2048]{1,0:T(8,128)(2,1)S(1)} %copy-done.33), channel_id=1, source_target_pairs={{0,3},{1,0},{2,1},{3,2},{4,7},{5,4},{6,5},{7,6},{8,11},{9,8},{10,9... | collective-permute-start | bytes 786440 | tf_op jit(solution)/shard_map/ppermute | solution.py:56
  253.1 18.3 %collective-permute-start.44 = (bf16[64,2048]{1,0:T(8,128)(2,1)}, bf16[64,2048]{1,0:T(8,128)(2,1)S(1)}, u32[]{:S(2)}, u32[]{:S(2)}) collective-permute-start(bf16[64,2048]{1,0:T(8,128)(2,1)} %get-tuple-element.173), channel_id=1, source_target_pairs={{0,3},{1,0},{2,1},{3,2},{4,7},{5,4},{6,5},{7,6},{8,11},{9,8},{10,9... | collective-permute-start | bytes 786440 | tf_op jit(solution)/shard_map/ppermute | solution.py:56
  253.4 24.0 %collective-permute-start.43 = (bf16[64,2048]{1,0:T(8,128)(2,1)S(1)}, bf16[64,2048]{1,0:T(8,128)(2,1)S(1)}, u32[]{:S(2)}, u32[]{:S(2)}) collective-permute-start(bf16[64,2048]{1,0:T(8,128)(2,1)S(1)} %copy-done.23), channel_id=1, source_target_pairs={{0,1},{1,2},{2,3},{3,0},{4,5},{5,6},{6,7},{7,4},{8,9},{9,10},{10,1... | collective-permute-start | bytes 786440 | tf_op jit(solution)/shard_map/ppermute | solution.py:56
  267.2 15.7 %collective-permute-start.47 = (bf16[64,2048]{1,0:T(8,128)(2,1)}, bf16[64,2048]{1,0:T(8,128)(2,1)S(1)}, u32[]{:S(2)}, u32[]{:S(2)}) collective-permute-start(bf16[64,2048]{1,0:T(8,128)(2,1)} %finish.6.refs_0_), channel_id=1, source_target_pairs={{0,1},{1,2},{2,3},{3,0},{4,5},{5,6},{6,7},{7,4},{8,9},{9,10},{10,1... | collective-permute-start | bytes 786440 | tf_op jit(solution)/shard_map/ppermute | solution.py:56
  280.3 9.5 %collective-permute-start.46 = (bf16[64,2048]{1,0:T(8,128)(2,1)}, bf16[64,2048]{1,0:T(8,128)(2,1)S(1)}, u32[]{:S(2)}, u32[]{:S(2)}) collective-permute-start(bf16[64,2048]{1,0:T(8,128)(2,1)} %finish.7.refs_1_), channel_id=1, source_target_pairs={{0,3},{1,0},{2,1},{3,2},{4,7},{5,4},{6,5},{7,6},{8,11},{9,8},{10,9... | collective-permute-start | bytes 786440 | tf_op jit(solution)/shard_map/ppermute | solution.py:56
  280.6 25.8 %collective-permute-start.45 = (bf16[64,2048]{1,0:T(8,128)(2,1)S(1)}, bf16[64,2048]{1,0:T(8,128)(2,1)S(1)}, u32[]{:S(2)}, u32[]{:S(2)}) collective-permute-start(bf16[64,2048]{1,0:T(8,128)(2,1)S(1)} %copy-done.18), channel_id=1, source_target_pairs={{0,3},{1,0},{2,1},{3,2},{4,7},{5,4},{6,5},{7,6},{8,11},{9,8},{10,9... | collective-permute-start | bytes 786440 | tf_op jit(solution)/shard_map/ppermute | solution.py:56
  281.5 24.9 %collective-permute-start.48 = (bf16[64,2048]{1,0:T(8,128)(2,1)}, bf16[64,2048]{1,0:T(8,128)(2,1)S(1)}, u32[]{:S(2)}, u32[]{:S(2)}) collective-permute-start(bf16[64,2048]{1,0:T(8,128)(2,1)} %finish.7.refs_1_), channel_id=1, source_target_pairs={{0,1},{1,2},{2,3},{3,0},{4,5},{5,6},{6,7},{7,4},{8,9},{9,10},{10,1... | collective-permute-start | bytes 786440 | tf_op jit(solution)/shard_map/ppermute | solution.py:56
  282.9 23.5 %collective-permute-start.49 = (bf16[64,2048]{1,0:T(8,128)(2,1)S(1)}, bf16[64,2048]{1,0:T(8,128)(2,1)S(1)}, u32[]{:S(2)}, u32[]{:S(2)}) collective-permute-start(bf16[64,2048]{1,0:T(8,128)(2,1)S(1)} %collective-permute-done.47.refs_4_), channel_id=1, source_target_pairs={{0,1},{1,2},{2,3},{3,0},{4,5},{5,6},{6,7},{7,4},{8,9},{9,10},{10,1... | collective-permute-start | bytes 786440 | tf_op jit(solution)/shard_map/ppermute | solution.py:56
  289.8 19.4 %collective-permute-start.50 = (bf16[64,2048]{1,0:T(8,128)(2,1)S(1)}, bf16[64,2048]{1,0:T(8,128)(2,1)S(1)}, u32[]{:S(2)}, u32[]{:S(2)}) collective-permute-start(bf16[64,2048]{1,0:T(8,128)(2,1)S(1)} %collective-permute-done.46.refs_3_), channel_id=1, source_target_pairs={{0,3},{1,0},{2,1},{3,2},{4,7},{5,4},{6,5},{7,6},{8,11},{9,8},{10,9... | collective-permute-start | bytes 786440 | tf_op jit(solution)/shard_map/ppermute | solution.py:56
  (67 other events, 379.7 us)

commit v11 on v10

--- a/solution.py
+++ b/solution.py
@@ -877,8 +877,7 @@
     chunks = gather_rows(upper, lower)
     if seq_count == 4:
         across_x[2] = lax.ppermute(lots[2], "seq", xor_pairs(seq_count, 2))
-        corner, _ = lax.optimization_barrier((across_x[2], chunks[1:]))
-        corners[2] = lax.ppermute(corner, "seq", xor_pairs(seq_count, 1))
+        corners[2] = lax.ppermute(lots[2], "seq", xor_pairs(seq_count, 3))
         shared = [vocab_table, beside]
         lots = [(marks_at[n], marks_at[n + 1], [across_x[n], corners[n]]) for n in range(3)]
     else:

time: 346 us -> 339 us (0.980)
  starting transfers between devices: 81.5 us -> 68.1 us
  waiting for transfers between devices: 102 us -> 108 us
    ppermute x39, starting transfers between devices: 65 us -> 49 us  [turned(): lax.ppermute(value, 'head', [(i, (i + step) % size) for i in range(size)])]
    ppermute x39, waiting for transfers between devices: 92.5 us -> 98.4 us  [turned(): lax.ppermute(value, 'head', [(i, (i + step) % size) for i in range(size)])]
    unnamed x118 -> x114, local copies, waits for them, and re-layouts: 8.61 us -> 8.99 us
  transfers between devices with their start and end apart: 56 -> 56, of which waited for: 30 -> 33; matrix products, arithmetic and copies ran while one was open for 3% -> 3% of each run, Pallas kernels for 32% -> 33%
where the time goes in v11:
time: 339 us; the launch traced here: 337 us
  Pallas kernels  132 us (39%)
  waiting for transfers between devices  108 us (32%)
  starting transfers between devices  68.1 us (20%)
  local copies, waits for them, and re-layouts  14.7 us (4%)
  other arithmetic  7.41 us (2%)
  between operations  6.92 us (2%)
    ppermute x39, waiting for transfers between devices, turned(): lax.ppermute(value, 'head', [(i, (i + step) % size) for i in range(size)])  98.4 us
    ppermute x39, starting transfers between devices, turned(): lax.ppermute(value, 'head', [(i, (i + step) % size) for i in range(size)])  49 us
    pallas_call x4, Pallas kernels, lookup(): pl.pallas_call(functools.partial(lookup_kernel, lots), grid=(TABLE_STEPS,...  36.8 us
    pallas_call x1, Pallas kernels, scores(): pl.pallas_call(functools.partial(score_kernel, len(early), len(units), le...  22 us
    pallas_call x2, Pallas kernels, matmul(): pl.pallas_call(matmul_kernel, grid=(b.shape[1] // tile,), in_specs=[pl.Bl...  12.5 us
    pallas_call x2, Pallas kernels, project(): pl.pallas_call(functools.partial(project_kernel, heads, slots, chunk, cou...  11.8 us
    unnamed x114, local copies, waits for them, and re-layouts  8.99 us
    pallas_call x2, Pallas kernels, near_chunks(): pl.pallas_call(functools.partial(near_kernel, rows), in_specs=[whole()] *...  8.81 us
  transfers between devices with their start and end apart: 56, of which 33 were waited for; matrix products, arithmetic and copies ran while one was open for 3% of the time, Pallas kernels for 33%

profile of v11, /device:TPU:0, one launch (start us, length us, event | category | flops | bytes accessed | tf_op | source)
XLA Modules:
  0.0 337.4 jit_solution(3692393027741129745)
XLA Ops:
  1.3 2.4 collective-permute-start.2
  5.0 2.3 collective-permute-done.1
  8.0 8.6 %lookup.5 = (bf16[256,512]{1,0:T(8,128)(2,1)}, bf16[256,512]{1,0:T(8,128)(2,1)}) custom-call(s32[1,512]{1,0:T(1,128)} %bitcast.49, bf16[6400,512]{1,0:T(8,128)(2,1)} %refs_3_.2), custom_call_target="tpu_custom_call" | custom-call | flops 4800000000 | bytes 24000000 | tf_op jit(solution)/shard_map/lookup/pallas_call | solution.py:160
  18.2 2.3 collective-permute-start.4
  21.0 8.5 %lookup.7 = (bf16[256,512]{1,0:T(8,128)(2,1)}, bf16[256,512]{1,0:T(8,128)(2,1)}) custom-call(s32[1,512]{1,0:T(1,128)} %bitcast.51, bf16[6400,512]{1,0:T(8,128)(2,1)} %refs_3_.2), custom_call_target="tpu_custom_call" | custom-call | flops 4800000000 | bytes 24000000 | tf_op jit(solution)/shard_map/lookup/pallas_call | solution.py:160
  32.1 8.6 %lookup.6 = (bf16[256,512]{1,0:T(8,128)(2,1)}, bf16[256,512]{1,0:T(8,128)(2,1)}) custom-call(s32[1,512]{1,0:T(1,128)} %bitcast.52, bf16[6400,512]{1,0:T(8,128)(2,1)} %refs_3_.2), custom_call_target="tpu_custom_call" | custom-call | flops 4800000000 | bytes 24000000 | tf_op jit(solution)/shard_map/lookup/pallas_call | solution.py:160
  43.6 3.8 %collective-permute-start.8 = (bf16[256,512]{1,0:T(8,128)(2,1)}, bf16[256,512]{1,0:T(8,128)(2,1)S(1)}, u32[]{:S(2)}, u32[]{:S(2)}) collective-permute-start(bf16[256,512]{1,0:T(8,128)(2,1)} %get-tuple-element.104), channel_id=1, source_target_pairs={{0,3},{1,0},{2,1},{3,2},{4,7},{5,4},{6,5},{7,6},{8,11},{9,8},{10,9... | collective-permute-start | bytes 786440 | tf_op jit(solution)/shard_map/ppermute | solution.py:56
  47.4 11.1 %lookup.4 = (bf16[256,512]{1,0:T(8,128)(2,1)}, bf16[256,512]{1,0:T(8,128)(2,1)}, bf16[1920,512]{1,0:T(8,128)(2,1)}, bf16[3200,512]{1,0:T(8,128)(2,1)}, bf16[1280,512]{1,0:T(8,128)(2,1)}) custom-call(s32[1,512]{1,0:T(1,128)} %bitcast.45, bf16[6400,512]{1,0:T(8,128)(2,1)} %refs_3_.2), custom_call_target="tpu_custom_call" | custom-call | flops 4800000000 | bytes 24000000 | tf_op jit(solution)/shard_map/lookup/pallas_call | solution.py:160
  59.5 2.3 collect.1
  63.7 4.6 %collective-permute-done.10.refs_2_ = bf16[128,512]{1,0:T(8,128)(2,1)S(1)} collective-permute-done((bf16[128,512]{1,0:T(8,128)(2,1)}, bf16[128,512]{1,0:T(8,128)(2,1)S(1)}, u32[]{:S(2)}, u32[]{:S(2)}) %collective-permute-start.10) | collective-permute-done | bytes 131104 | tf_op jit(solution)/shard_map/ppermute | solution.py:758
  80.6 2.8 collective-permute-done.16.refs_2_
  83.3 4.2 %collective-permute-start.14 = (bf16[64,2048]{1,0:T(8,128)(2,1)}, bf16[64,2048]{1,0:T(8,128)(2,1)S(1)}, u32[]{:S(2)}, u32[]{:S(2)}) collective-permute-start(bf16[64,2048]{1,0:T(8,128)(2,1)} %get-tuple-element.115.refs_1_), channel_id=1, source_target_pairs={{0,3},{1,0},{2,1},{3,2},{4,7},{5,4},{6,5},{7,6},{8,11},{9,8},{10,9... | collective-permute-start | bytes 786440 | tf_op jit(solution)/shard_map/ppermute | solution.py:56
  93.5 9.2 %collective-permute-done.14.refs_3_ = bf16[64,2048]{1,0:T(8,128)(2,1)S(1)} collective-permute-done((bf16[64,2048]{1,0:T(8,128)(2,1)}, bf16[64,2048]{1,0:T(8,128)(2,1)S(1)}, u32[]{:S(2)}, u32[]{:S(2)}) %collective-permute-start.14) | collective-permute-done | bytes 262176 | tf_op jit(solution)/shard_map/ppermute | solution.py:56
  105.1 6.7 %project.2 = (bf16[4,384,256]{2,1,0:T(8,128)(2,1)}, bf16[4,384,256]{2,1,0:T(8,128)(2,1)}, bf16[384,512]{1,0:T(8,128)(2,1)}, f32[4,176,128]{2,1,0:T(8,128)}) custom-call(s32[1]{0:T(128)} %copy.35.bound_ref, s32[3]{0:T(128)} %bitcast.53, bf16[64,2048]{1,0:T(8,128)(2,1)} %get-tuple-element.114.refs_0_, bf16[64,2048]{1,0:T(8,128)(2,1)} %get-tuple-element.115.refs_1_, ...), custom_call_target="tpu_custom_call" | custom-call | flops 3000000000 | bytes 15000000 | tf_op jit(solution)/shard_map/project/pallas_call | solution.py:335
  113.4 5.1 %project.3 = (bf16[4,128,256]{2,1,0:T(8,128)(2,1)}, bf16[4,128,256]{2,1,0:T(8,128)(2,1)}, bf16[128,512]{1,0:T(8,128)(2,1)}, bf16[4,176,128]{2,1,0:T(8,128)(2,1)}) custom-call(s32[1]{0:T(128)} %copy.35.bound_ref, s32[1]{0:T(128)} %slice.77.places_ref, bf16[64,2048]{1,0:T(8,128)(2,1)} %copy-done.36, bf16[64,2048]{1,0:T(8,128)(2,1)} %copy-done.42, ...), custom_call_target="tpu_custom_call" | custom-call | flops 3000000000 | bytes 15000000 | tf_op jit(solution)/shard_map/project/pallas_call | solution.py:335
  118.5 2.8 collective-permute-start.21
  124.6 4.6 %within.1 = (f32[4,512,128]{2,1,0:T(8,128)}, f32[4,512,8]{2,1,0:T(8,128)}) custom-call(s32[1]{0:T(128)} %copy.35.bound_ref, s32[4]{0:T(128)} %copy-done.6, bf16[4,384,256]{2,1,0:T(8,128)(2,1)} %get-tuple-element.118.refs_0_, bf16[4,128,256]{2,1,0:T(8,128)(2,1)} %get-tuple-element.122.refs_1_, bf16[4,384,256]{2,1,0:T(8,128)(2,1)} %get-tuple-element.123.refs_2_, ...), custom_call_target="tpu_custom_call" | custom-call | flops 2700000000 | bytes 13500000 | tf_op jit(solution)/shard_map/within/pallas_call | solution.py:374
  130.4 4.8 %across.1 = (bf16[512,512]{1,0:T(8,128)(2,1)}, bf16[64,2048]{1,0:T(8,128)(2,1)}, bf16[64,2048]{1,0:T(8,128)(2,1)}) custom-call(s32[1]{0:T(128)} %copy.35.bound_ref, s32[4]{0:T(128)} %copy-done.6, s32[3]{0:T(128)} %add_convert_fusion.share_ref, bf16[4,384,256]{2,1,0:T(8,128)(2,1)} %get-tuple-element.118.refs_0_, ...), custom_call_target="tpu_custom_call" | custom-call | flops 2700000000 | bytes 13500000 | tf_op jit(solution)/shard_map/across/pallas_call | solution.py:423
  135.2 3.0 collective-permute-start.34
  138.8 3.3 collective-permute-start.23
  142.0 3.8 %near.2 = (bf16[64,2048]{1,0:T(8,128)(2,1)}, bf16[64,2048]{1,0:T(8,128)(2,1)}, bf16[64,2048]{1,0:T(8,128)(2,1)}, bf16[64,2048]{1,0:T(8,128)(2,1)}, bf16[64,2048]{1,0:T(8,128)(2,1)}, /*index=5*/bf16[64,2048]{1,0:T(8,128)(2,1)}) custom-call(bf16[512,512]{1,0:T(8,128)(2,1)} %get-tuple-element.133.mixed_ref, bf16[512,2048]{1,0:T(8,128)(2,1)} %weight_ref.3), custom_call_target="tpu_custom_call" | custom-call | flops 2400000000 | bytes 12000000 | tf_op jit(solution)/shard_map/near/pallas_call | solution.py:442
  145.9 3.6 %collective-permute-done.22.before_ref = bf16[64,2048]{1,0:T(8,128)(2,1)S(1)} collective-permute-done((bf16[64,2048]{1,0:T(8,128)(2,1)}, bf16[64,2048]{1,0:T(8,128)(2,1)S(1)}, u32[]{:S(2)}, u32[]{:S(2)}) %collective-permute-start.22) | collective-permute-done | bytes 262176 | tf_op jit(solution)/shard_map/ppermute | solution.py:56
  149.5 2.6 collective-permute-done.23.after_ref
  158.6 7.5 %collective-permute-done.24.refs_1_ = bf16[64,2048]{1,0:T(8,128)(2,1)S(1)} collective-permute-done((bf16[64,2048]{1,0:T(8,128)(2,1)}, bf16[64,2048]{1,0:T(8,128)(2,1)S(1)}, u32[]{:S(2)}, u32[]{:S(2)}) %collective-permute-start.24) | collective-permute-done | bytes 262176 | tf_op jit(solution)/shard_map/ppermute | solution.py:56
  171.8 2.7 collective-permute-start.30
  174.5 3.7 %collective-permute-done.27.refs_2_ = bf16[64,2048]{1,0:T(8,128)(2,1)S(1)} collective-permute-done((bf16[64,2048]{1,0:T(8,128)(2,1)}, bf16[64,2048]{1,0:T(8,128)(2,1)S(1)}, u32[]{:S(2)}, u32[]{:S(2)}) %collective-permute-start.27) | collective-permute-done | bytes 262176 | tf_op jit(solution)/shard_map/ppermute | solution.py:56
  183.0 2.3 collective-permute-start.31
  185.3 5.0 %collective-permute-done.28.refs_2_ = bf16[64,2048]{1,0:T(8,128)(2,1)S(1)} collective-permute-done((bf16[64,2048]{1,0:T(8,128)(2,1)}, bf16[64,2048]{1,0:T(8,128)(2,1)S(1)}, u32[]{:S(2)}, u32[]{:S(2)}) %collective-permute-start.28) | collective-permute-done | bytes 262176 | tf_op jit(solution)/shard_map/ppermute | solution.py:56
  195.7 6.9 %collective-permute-done.29.refs_3_ = bf16[64,2048]{1,0:T(8,128)(2,1)S(1)} collective-permute-done((bf16[64,2048]{1,0:T(8,128)(2,1)}, bf16[64,2048]{1,0:T(8,128)(2,1)S(1)}, u32[]{:S(2)}, u32[]{:S(2)}) %collective-permute-start.29) | collective-permute-done | bytes 262176 | tf_op jit(solution)/shard_map/ppermute | solution.py:56
  203.3 7.2 %matmul.2.refs_0_ = bf16[384,1536]{1,0:T(8,128)(2,1)} custom-call(bf16[64,2048]{1,0:T(8,128)(2,1)} %get-tuple-element.145.refs_0_, bf16[64,2048]{1,0:T(8,128)(2,1)} %get-tuple-element.150.refs_1_, bf16[64,2048]{1,0:T(8,128)(2,1)} %copy-done.22, bf16[64,2048]{1,0:T(8,128)(2,1)} %copy-done.34, bf16[64,2048]{1,0:T(8,128)(2,1)} %copy-done.18, ...), custom_call_target="tpu_custom_call" | custom-call | flops 3000000000 | bytes 15000000 | tf_op jit(solution)/shard_map/matmul/pallas_call | solution.py:461
  210.5 5.3 %matmul.3.refs_1_ = bf16[128,1536]{1,0:T(8,128)(2,1)} custom-call(bf16[64,2048]{1,0:T(8,128)(2,1)} %collective-permute-done.32.refs_0_, bf16[64,2048]{1,0:T(8,128)(2,1)} %collective-permute-done.33.refs_1_, bf16[2048,1536]{1,0:T(8,128)(2,1)} %refs_2_.3), custom_call_target="tpu_custom_call" | custom-call | flops 3000000000 | bytes 15000000 | tf_op jit(solution)/shard_map/matmul/pallas_call | solution.py:461
  218.1 4.8 %local_window.1 = (bf16[512,512]{1,0:T(8,128)(2,1)}, bf16[64,1536]{1,0:T(8,128)(2,1)}) custom-call(s32[1]{0:T(128)} %copy.35.bound_ref, s32[4]{0:T(128)} %copy-done.6, bf16[384,1536]{1,0:T(8,128)(2,1)} %matmul.2.refs_0_, bf16[128,1536]{1,0:T(8,128)(2,1)} %matmul.3.refs_1_), custom_call_target="tpu_custom_call" | custom-call | flops 4800000000 | bytes 24000000 | tf_op jit(solution)/shard_map/local_window/pallas_call | solution.py:529
  224.1 3.7 %halo_window.1 = (bf16[512,512]{1,0:T(8,128)(2,1)}, bf16[64,2048]{1,0:T(8,128)(2,1)}, bf16[64,2048]{1,0:T(8,128)(2,1)}) custom-call(s32[3]{0:T(128)} %pad_add_fusion.4.info_ref, bf16[512,512]{1,0:T(8,128)(2,1)} %get-tuple-element.156.local_ref, bf16[64,1536]{1,0:T(8,128)(2,1)} %get-tuple-element.157.first_ref, bf16[64,1536]{1,0:T(8,128)(2,1)} %copy-done.49, ...), custom_call_target="tpu_custom_call" | custom-call | flops 2700000000 | bytes 13500000 | tf_op jit(solution)/shard_map/halo_window/pallas_call | solution.py:566
  229.1 2.5 collective-permute-start.40
  233.3 5.0 %near.3 = (bf16[64,2048]{1,0:T(8,128)(2,1)}, bf16[64,2048]{1,0:T(8,128)(2,1)}, bf16[64,2048]{1,0:T(8,128)(2,1)}, bf16[64,2048]{1,0:T(8,128)(2,1)}, bf16[64,2048]{1,0:T(8,128)(2,1)}, /*index=5*/bf16[64,2048]{1,0:T(8,128)(2,1)}) custom-call(bf16[512,512]{1,0:T(8,128)(2,1)} %get-tuple-element.161.mixed_ref, bf16[512,2048]{1,0:T(8,128)(2,1)} %weight_ref.5), custom_call_target="tpu_custom_call" | custom-call | flops 2400000000 | bytes 12000000 | tf_op jit(solution)/shard_map/near/pallas_call | solution.py:442
  238.9 4.7 %collective-permute-done.40.after_ref = bf16[64,2048]{1,0:T(8,128)(2,1)} collective-permute-done((bf16[64,2048]{1,0:T(8,128)(2,1)}, bf16[64,2048]{1,0:T(8,128)(2,1)}, u32[]{:S(2)}, u32[]{:S(2)}) %collective-permute-start.40) | collective-permute-done | bytes 262176 | tf_op jit(solution)/shard_map/ppermute | solution.py:56
  246.4 3.1 collective-permute-start.42
  249.8 7.1 %collective-permute-done.41.refs_1_ = bf16[64,2048]{1,0:T(8,128)(2,1)S(1)} collective-permute-done((bf16[64,2048]{1,0:T(8,128)(2,1)}, bf16[64,2048]{1,0:T(8,128)(2,1)S(1)}, u32[]{:S(2)}, u32[]{:S(2)}) %collective-permute-start.41) | collective-permute-done | bytes 262176 | tf_op jit(solution)/shard_map/ppermute | solution.py:56
  256.9 4.2 %collective-permute-done.42.refs_2_ = bf16[64,2048]{1,0:T(8,128)(2,1)S(1)} collective-permute-done((bf16[64,2048]{1,0:T(8,128)(2,1)S(1)}, bf16[64,2048]{1,0:T(8,128)(2,1)S(1)}, u32[]{:S(2)}, u32[]{:S(2)}) %collective-permute-start.42) | collective-permute-done | bytes 262176 | tf_op jit(solution)/shard_map/ppermute | solution.py:56
  265.1 3.9 %collective-permute-start.45 = (bf16[64,2048]{1,0:T(8,128)(2,1)}, bf16[64,2048]{1,0:T(8,128)(2,1)S(1)}, u32[]{:S(2)}, u32[]{:S(2)}) collective-permute-start(bf16[64,2048]{1,0:T(8,128)(2,1)} %finish.6.refs_0_), channel_id=1, source_target_pairs={{0,3},{1,0},{2,1},{3,2},{4,7},{5,4},{6,5},{7,6},{8,11},{9,8},{10,9... | collective-permute-start | bytes 786440 | tf_op jit(solution)/shard_map/ppermute | solution.py:56
  268.9 5.0 %collective-permute-done.43.refs_1_ = bf16[64,2048]{1,0:T(8,128)(2,1)S(1)} collective-permute-done((bf16[64,2048]{1,0:T(8,128)(2,1)S(1)}, bf16[64,2048]{1,0:T(8,128)(2,1)S(1)}, u32[]{:S(2)}, u32[]{:S(2)}) %collective-permute-start.43) | collective-permute-done | bytes 262176 | tf_op jit(solution)/shard_map/ppermute | solution.py:56
  276.8 2.7 collective-permute-done.47.refs_4_
  279.4 4.3 %collective-permute-done.45.refs_2_ = bf16[64,2048]{1,0:T(8,128)(2,1)S(1)} collective-permute-done((bf16[64,2048]{1,0:T(8,128)(2,1)}, bf16[64,2048]{1,0:T(8,128)(2,1)S(1)}, u32[]{:S(2)}, u32[]{:S(2)}) %collective-permute-start.45) | collective-permute-done | bytes 262176 | tf_op jit(solution)/shard_map/ppermute | solution.py:56
  284.2 5.5 %collective-permute-done.46.refs_3_ = bf16[64,2048]{1,0:T(8,128)(2,1)S(1)} collective-permute-done((bf16[64,2048]{1,0:T(8,128)(2,1)}, bf16[64,2048]{1,0:T(8,128)(2,1)S(1)}, u32[]{:S(2)}, u32[]{:S(2)}) %collective-permute-start.46) | collective-permute-done | bytes 262176 | tf_op jit(solution)/shard_map/ppermute | solution.py:56
  291.4 5.0 %collective-permute-done.48.refs_5_ = bf16[64,2048]{1,0:T(8,128)(2,1)S(1)} collective-permute-done((bf16[64,2048]{1,0:T(8,128)(2,1)}, bf16[64,2048]{1,0:T(8,128)(2,1)S(1)}, u32[]{:S(2)}, u32[]{:S(2)}) %collective-permute-start.48) | collective-permute-done | bytes 262176 | tf_op jit(solution)/shard_map/ppermute | solution.py:56
  297.1 3.0 turn.1.refs_0_
  301.9 4.1 %collective-permute-done.50.refs_2_ = bf16[64,2048]{1,0:T(8,128)(2,1)S(1)} collective-permute-done((bf16[64,2048]{1,0:T(8,128)(2,1)S(1)}, bf16[64,2048]{1,0:T(8,128)(2,1)S(1)}, u32[]{:S(2)}, u32[]{:S(2)}) %collective-permute-start.50) | collective-permute-done | bytes 262176 | tf_op jit(solution)/shard_map/ppermute | solution.py:56
  306.7 22.0 %scores.1 = f32[8,512]{1,0:T(8,128)} custom-call(s32[4]{0:T(128)} %iota_xor_fusion.order_ref, bf16[2048,384]{1,0:T(8,128)(2,1)} %turn.1.refs_0_, bf16[64,2048]{1,0:T(8,128)(2,1)} %copy-done.33, bf16[64,2048]{1,0:T(8,128)(2,1)} %copy-done.38, bf16[6400,512]{1,0:T(8,128)(2,1)} %refs_3_.2, bf16[6400,512]{1,0:T(8,128)(2,1)} %collective-permute-done.36.refs_4_, ...), custom_call_target="tpu_custom_call" | custom-call | flops 12000000000 | bytes 60000000 | tf_op jit(solution)/shard_map/scores/pallas_call | solution.py:668
  (237 shorter events, 88.6 us)
Async XLA Ops:
  4.4 212.4 %collective-permute-start.36 = (bf16[6400,512]{1,0:T(8,128)(2,1)}, bf16[6400,512]{1,0:T(8,128)(2,1)}, u32[]{:S(2)}, u32[]{:S(2)}) collective-permute-start(bf16[6400,512]{1,0:T(8,128)(2,1)} %refs_3_.2), channel_id=1, source_target_pairs={{0,4},{4,0},{8,12},{12,8},{1,5},{5,1},{9,13},{13,9},{2,6},{6,2},{1... | collective-permute-start | bytes 19660808 | tf_op jit(solution)/shard_map/ppermute | solution.py:848
  16.6 24.0 %collective-permute-start.3 = (bf16[256,512]{1,0:T(8,128)(2,1)}, bf16[256,512]{1,0:T(8,128)(2,1)S(1)}, u32[]{:S(2)}, u32[]{:S(2)}) collective-permute-start(bf16[256,512]{1,0:T(8,128)(2,1)} %get-tuple-element.94), channel_id=1, source_target_pairs={{0,1},{1,2},{2,3},{3,0},{4,5},{5,6},{6,7},{7,4},{8,9},{9,10},{10,1... | collective-permute-start | bytes 786440 | tf_op jit(solution)/shard_map/ppermute | solution.py:56
  18.2 22.5 %collective-permute-start.4 = (bf16[256,512]{1,0:T(8,128)(2,1)}, bf16[256,512]{1,0:T(8,128)(2,1)S(1)}, u32[]{:S(2)}, u32[]{:S(2)}) collective-permute-start(bf16[256,512]{1,0:T(8,128)(2,1)} %get-tuple-element.95), channel_id=1, source_target_pairs={{0,3},{1,0},{2,1},{3,2},{4,7},{5,4},{6,5},{7,6},{8,11},{9,8},{10,9... | collective-permute-start | bytes 786440 | tf_op jit(solution)/shard_map/ppermute | solution.py:56
  29.5 29.0 %collective-permute-start.6 = (bf16[256,512]{1,0:T(8,128)(2,1)}, bf16[256,512]{1,0:T(8,128)(2,1)S(1)}, u32[]{:S(2)}, u32[]{:S(2)}) collective-permute-start(bf16[256,512]{1,0:T(8,128)(2,1)} %get-tuple-element.101), channel_id=1, source_target_pairs={{0,3},{1,0},{2,1},{3,2},{4,7},{5,4},{6,5},{7,6},{8,11},{9,8},{10,9... | collective-permute-start | bytes 786440 | tf_op jit(solution)/shard_map/ppermute | solution.py:56
  31.3 27.2 %collective-permute-start.7 = (bf16[256,512]{1,0:T(8,128)(2,1)}, bf16[256,512]{1,0:T(8,128)(2,1)S(1)}, u32[]{:S(2)}, u32[]{:S(2)}) collective-permute-start(bf16[256,512]{1,0:T(8,128)(2,1)} %get-tuple-element.103), channel_id=1, source_target_pairs={{0,1},{1,2},{2,3},{3,0},{4,5},{5,6},{6,7},{7,4},{8,9},{9,10},{10,1... | collective-permute-start | bytes 786440 | tf_op jit(solution)/shard_map/ppermute | solution.py:56
  43.6 15.0 %collective-permute-start.5 = (bf16[256,512]{1,0:T(8,128)(2,1)}, bf16[256,512]{1,0:T(8,128)(2,1)S(1)}, u32[]{:S(2)}, u32[]{:S(2)}) collective-permute-start(bf16[256,512]{1,0:T(8,128)(2,1)} %get-tuple-element.100), channel_id=1, source_target_pairs={{0,1},{1,2},{2,3},{3,0},{4,5},{5,6},{6,7},{7,4},{8,9},{9,10},{10,1... | collective-permute-start | bytes 786440 | tf_op jit(solution)/shard_map/ppermute | solution.py:56
  43.6 15.0 %collective-permute-start.8 = (bf16[256,512]{1,0:T(8,128)(2,1)}, bf16[256,512]{1,0:T(8,128)(2,1)S(1)}, u32[]{:S(2)}, u32[]{:S(2)}) collective-permute-start(bf16[256,512]{1,0:T(8,128)(2,1)} %get-tuple-element.104), channel_id=1, source_target_pairs={{0,3},{1,0},{2,1},{3,2},{4,7},{5,4},{6,5},{7,6},{8,11},{9,8},{10,9... | collective-permute-start | bytes 786440 | tf_op jit(solution)/shard_map/ppermute | solution.py:56
  61.8 6.5 %collective-permute-start.10 = (bf16[128,512]{1,0:T(8,128)(2,1)}, bf16[128,512]{1,0:T(8,128)(2,1)S(1)}, u32[]{:S(2)}, u32[]{:S(2)}) collective-permute-start(bf16[128,512]{1,0:T(8,128)(2,1)} %get-tuple-element.107), channel_id=1, source_target_pairs={{0,8},{4,12},{8,0},{12,4},{1,9},{5,13},{9,1},{13,5},{2,10},{6,14},... | collective-permute-start | bytes 393224 | tf_op jit(solution)/shard_map/ppermute | solution.py:758
  62.4 7.9 %collective-permute-start.11 = (bf16[128,512]{1,0:T(8,128)(2,1)}, bf16[128,512]{1,0:T(8,128)(2,1)S(1)}, u32[]{:S(2)}, u32[]{:S(2)}) collective-permute-start(bf16[128,512]{1,0:T(8,128)(2,1)} %get-tuple-element.108), channel_id=1, source_target_pairs={{0,12},{4,8},{8,4},{12,0},{1,13},{5,9},{9,5},{13,1},{2,14},{6,10},... | collective-permute-start | bytes 393224 | tf_op jit(solution)/shard_map/ppermute | solution.py:758
  70.4 48.1 %collective-permute-start.18 = (bf16[1920,512]{1,0:T(8,128)(2,1)}, bf16[1920,512]{1,0:T(8,128)(2,1)S(1)}, u32[]{:S(2)}, u32[]{:S(2)}) collective-permute-start(bf16[1920,512]{1,0:T(8,128)(2,1)} %get-tuple-element.131), channel_id=1, source_target_pairs={{0,8},{4,12},{8,0},{12,4},{1,9},{5,13},{9,1},{13,5},{2,10},{6,14},... | collective-permute-start | bytes 5898248 | tf_op jit(solution)/shard_map/ppermute | solution.py:808
  74.5 8.9 %collective-permute-start.16 = (bf16[64,2048]{1,0:T(8,128)(2,1)}, bf16[64,2048]{1,0:T(8,128)(2,1)S(1)}, u32[]{:S(2)}, u32[]{:S(2)}) collective-permute-start(bf16[64,2048]{1,0:T(8,128)(2,1)} %get-tuple-element.114.refs_0_), channel_id=1, source_target_pairs={{0,3},{1,0},{2,1},{3,2},{4,7},{5,4},{6,5},{7,6},{8,11},{9,8},{10,9... | collective-permute-start | bytes 786440 | tf_op jit(solution)/shard_map/ppermute | solution.py:56
  80.2 13.2 %collective-permute-start.12 = (bf16[64,2048]{1,0:T(8,128)(2,1)}, bf16[64,2048]{1,0:T(8,128)(2,1)S(1)}, u32[]{:S(2)}, u32[]{:S(2)}) collective-permute-start(bf16[64,2048]{1,0:T(8,128)(2,1)} %get-tuple-element.114.refs_0_), channel_id=1, source_target_pairs={{0,1},{1,2},{2,3},{3,0},{4,5},{5,6},{6,7},{7,4},{8,9},{9,10},{10,1... | collective-permute-start | bytes 786440 | tf_op jit(solution)/shard_map/ppermute | solution.py:56
  80.5 23.9 %collective-permute-start.17 = (bf16[64,2048]{1,0:T(8,128)(2,1)}, bf16[64,2048]{1,0:T(8,128)(2,1)S(1)}, u32[]{:S(2)}, u32[]{:S(2)}) collective-permute-start(bf16[64,2048]{1,0:T(8,128)(2,1)} %get-tuple-element.115.refs_1_), channel_id=1, source_target_pairs={{0,1},{1,2},{2,3},{3,0},{4,5},{5,6},{6,7},{7,4},{8,9},{9,10},{10,1... | collective-permute-start | bytes 786440 | tf_op jit(solution)/shard_map/ppermute | solution.py:56
  83.3 19.4 %collective-permute-start.14 = (bf16[64,2048]{1,0:T(8,128)(2,1)}, bf16[64,2048]{1,0:T(8,128)(2,1)S(1)}, u32[]{:S(2)}, u32[]{:S(2)}) collective-permute-start(bf16[64,2048]{1,0:T(8,128)(2,1)} %get-tuple-element.115.refs_1_), channel_id=1, source_target_pairs={{0,3},{1,0},{2,1},{3,2},{4,7},{5,4},{6,5},{7,6},{8,11},{9,8},{10,9... | collective-permute-start | bytes 786440 | tf_op jit(solution)/shard_map/ppermute | solution.py:56
  93.5 18.4 %collective-permute-start.13 = (bf16[64,2048]{1,0:T(8,128)(2,1)S(1)}, bf16[64,2048]{1,0:T(8,128)(2,1)S(1)}, u32[]{:S(2)}, u32[]{:S(2)}) collective-permute-start(bf16[64,2048]{1,0:T(8,128)(2,1)S(1)} %collective-permute-done.12.refs_4_), channel_id=1, source_target_pairs={{0,1},{1,2},{2,3},{3,0},{4,5},{5,6},{6,7},{7,4},{8,9},{9,10},{10,1... | collective-permute-start | bytes 786440 | tf_op jit(solution)/shard_map/ppermute | solution.py:56
  102.7 10.0 %collective-permute-start.15 = (bf16[64,2048]{1,0:T(8,128)(2,1)S(1)}, bf16[64,2048]{1,0:T(8,128)(2,1)S(1)}, u32[]{:S(2)}, u32[]{:S(2)}) collective-permute-start(bf16[64,2048]{1,0:T(8,128)(2,1)S(1)} %collective-permute-done.14.refs_3_), channel_id=1, source_target_pairs={{0,3},{1,0},{2,1},{3,2},{4,7},{5,4},{6,5},{7,6},{8,11},{9,8},{10,9... | collective-permute-start | bytes 786440 | tf_op jit(solution)/shard_map/ppermute | solution.py:56
  118.5 10.7 %collective-permute-start.21 = (bf16[4,176,128]{2,1,0:T(8,128)(2,1)}, bf16[4,176,128]{2,1,0:T(8,128)(2,1)S(1)}, u32[]{:S(2)}, u32[]{:S(2)}) collective-permute-start(bf16[4,176,128]{2,1,0:T(8,128)(2,1)} %get-tuple-element.132), channel_id=1, source_target_pairs={{0,12},{1,13},{2,14},{3,15},{16,28},{17,29},{18,30},{19,31}} | collective-permute-start | bytes 540680 | tf_op jit(solution)/shard_map/ppermute | solution.py:818
  121.2 8.4 %collective-permute-start.20 = (bf16[4,176,128]{2,1,0:T(8,128)(2,1)}, bf16[4,176,128]{2,1,0:T(8,128)(2,1)S(1)}, u32[]{:S(2)}, u32[]{:S(2)}) collective-permute-start(bf16[4,176,128]{2,1,0:T(8,128)(2,1)} %get-tuple-element.132), channel_id=1, source_target_pairs={{0,8},{4,12},{1,9},{5,13},{2,10},{6,14},{3,11},{7,15},{16,24},{20,... | collective-permute-start | bytes 540680 | tf_op jit(solution)/shard_map/ppermute | solution.py:818
  122.5 7.1 %collective-permute-start.19 = (bf16[4,176,128]{2,1,0:T(8,128)(2,1)}, bf16[4,176,128]{2,1,0:T(8,128)(2,1)S(1)}, u32[]{:S(2)}, u32[]{:S(2)}) collective-permute-start(bf16[4,176,128]{2,1,0:T(8,128)(2,1)} %get-tuple-element.132), channel_id=1, source_target_pairs={{0,4},{4,8},{8,12},{1,5},{5,9},{9,13},{2,6},{6,10},{10,14},{3,7},{... | collective-permute-start | bytes 540680 | tf_op jit(solution)/shard_map/ppermute | solution.py:818
  135.2 81.6 %collective-permute-start.34 = (bf16[3200,512]{1,0:T(8,128)(2,1)S(1)}, bf16[3200,512]{1,0:T(8,128)(2,1)S(1)}, u32[]{:S(2)}, u32[]{:S(2)}) collective-permute-start(bf16[3200,512]{1,0:T(8,128)(2,1)S(1)} %copy-done.8), channel_id=1, source_target_pairs={{0,8},{4,12},{8,0},{12,4},{1,9},{5,13},{9,1},{13,5},{2,10},{6,14},... | collective-permute-start | bytes 9830408 | tf_op jit(solution)/shard_map/ppermute | solution.py:847
  138.2 11.3 %collective-permute-start.22 = (bf16[64,2048]{1,0:T(8,128)(2,1)}, bf16[64,2048]{1,0:T(8,128)(2,1)S(1)}, u32[]{:S(2)}, u32[]{:S(2)}) collective-permute-start(bf16[64,2048]{1,0:T(8,128)(2,1)} %get-tuple-element.136), channel_id=1, source_target_pairs={{0,1},{1,2},{2,3},{3,0},{4,5},{5,6},{6,7},{7,4},{8,9},{9,10},{10,1... | collective-permute-start | bytes 786440 | tf_op jit(solution)/shard_map/ppermute | solution.py:56
  138.8 13.3 %collective-permute-start.23 = (bf16[64,2048]{1,0:T(8,128)(2,1)}, bf16[64,2048]{1,0:T(8,128)(2,1)S(1)}, u32[]{:S(2)}, u32[]{:S(2)}) collective-permute-start(bf16[64,2048]{1,0:T(8,128)(2,1)} %get-tuple-element.138), channel_id=1, source_target_pairs={{0,3},{1,0},{2,1},{3,2},{4,7},{5,4},{6,5},{7,6},{8,11},{9,8},{10,9... | collective-permute-start | bytes 786440 | tf_op jit(solution)/shard_map/ppermute | solution.py:56
  145.9 10.8 %collective-permute-start.25 = (bf16[64,2048]{1,0:T(8,128)(2,1)}, bf16[64,2048]{1,0:T(8,128)(2,1)S(1)}, u32[]{:S(2)}, u32[]{:S(2)}) collective-permute-start(bf16[64,2048]{1,0:T(8,128)(2,1)} %get-tuple-element.140), channel_id=1, source_target_pairs={{0,3},{1,0},{2,1},{3,2},{4,7},{5,4},{6,5},{7,6},{8,11},{9,8},{10,9... | collective-permute-start | bytes 786440 | tf_op jit(solution)/shard_map/ppermute | solution.py:56
  154.8 11.3 %collective-permute-start.24 = (bf16[64,2048]{1,0:T(8,128)(2,1)}, bf16[64,2048]{1,0:T(8,128)(2,1)S(1)}, u32[]{:S(2)}, u32[]{:S(2)}) collective-permute-start(bf16[64,2048]{1,0:T(8,128)(2,1)} %get-tuple-element.139), channel_id=1, source_target_pairs={{0,1},{1,2},{2,3},{3,0},{4,5},{5,6},{6,7},{7,4},{8,9},{9,10},{10,1... | collective-permute-start | bytes 786440 | tf_op jit(solution)/shard_map/ppermute | solution.py:56
  155.3 61.5 %collective-permute-start.35 = (bf16[1920,512]{1,0:T(8,128)(2,1)}, bf16[1920,512]{1,0:T(8,128)(2,1)}, u32[]{:S(2)}, u32[]{:S(2)}) collective-permute-start(bf16[1920,512]{1,0:T(8,128)(2,1)} %copy-done.11), channel_id=1, source_target_pairs={{0,4},{4,0},{8,12},{12,8},{1,5},{5,1},{9,13},{13,9},{2,6},{6,2},{1... | collective-permute-start | bytes 5898248 | tf_op jit(solution)/shard_map/ppermute | solution.py:809
  156.7 15.1 %collective-permute-start.26 = (bf16[64,2048]{1,0:T(8,128)(2,1)S(1)}, bf16[64,2048]{1,0:T(8,128)(2,1)S(1)}, u32[]{:S(2)}, u32[]{:S(2)}) collective-permute-start(bf16[64,2048]{1,0:T(8,128)(2,1)S(1)} %copy-done.23), channel_id=1, source_target_pairs={{0,1},{1,2},{2,3},{3,0},{4,5},{5,6},{6,7},{7,4},{8,9},{9,10},{10,1... | collective-permute-start | bytes 786440 | tf_op jit(solution)/shard_map/ppermute | solution.py:56
  166.1 12.1 %collective-permute-start.27 = (bf16[64,2048]{1,0:T(8,128)(2,1)}, bf16[64,2048]{1,0:T(8,128)(2,1)S(1)}, u32[]{:S(2)}, u32[]{:S(2)}) collective-permute-start(bf16[64,2048]{1,0:T(8,128)(2,1)} %get-tuple-element.149), channel_id=1, source_target_pairs={{0,3},{1,0},{2,1},{3,2},{4,7},{5,4},{6,5},{7,6},{8,11},{9,8},{10,9... | collective-permute-start | bytes 786440 | tf_op jit(solution)/shard_map/ppermute | solution.py:56
  171.8 11.2 %collective-permute-start.30 = (bf16[64,2048]{1,0:T(8,128)(2,1)}, bf16[64,2048]{1,0:T(8,128)(2,1)S(1)}, u32[]{:S(2)}, u32[]{:S(2)}) collective-permute-start(bf16[64,2048]{1,0:T(8,128)(2,1)} %get-tuple-element.145.refs_0_), channel_id=1, source_target_pairs={{0,1},{1,2},{2,3},{3,0},{4,5},{5,6},{6,7},{7,4},{8,9},{9,10},{10,1... | collective-permute-start | bytes 786440 | tf_op jit(solution)/shard_map/ppermute | solution.py:56
  178.2 12.1 %collective-permute-start.28 = (bf16[64,2048]{1,0:T(8,128)(2,1)}, bf16[64,2048]{1,0:T(8,128)(2,1)S(1)}, u32[]{:S(2)}, u32[]{:S(2)}) collective-permute-start(bf16[64,2048]{1,0:T(8,128)(2,1)} %get-tuple-element.145.refs_0_), channel_id=1, source_target_pairs={{0,3},{1,0},{2,1},{3,2},{4,7},{5,4},{6,5},{7,6},{8,11},{9,8},{10,9... | collective-permute-start | bytes 786440 | tf_op jit(solution)/shard_map/ppermute | solution.py:56
  183.0 11.2 %collective-permute-start.31 = (bf16[64,2048]{1,0:T(8,128)(2,1)}, bf16[64,2048]{1,0:T(8,128)(2,1)S(1)}, u32[]{:S(2)}, u32[]{:S(2)}) collective-permute-start(bf16[64,2048]{1,0:T(8,128)(2,1)} %get-tuple-element.150.refs_1_), channel_id=1, source_target_pairs={{0,1},{1,2},{2,3},{3,0},{4,5},{5,6},{6,7},{7,4},{8,9},{9,10},{10,1... | collective-permute-start | bytes 786440 | tf_op jit(solution)/shard_map/ppermute | solution.py:56
  190.3 12.2 %collective-permute-start.29 = (bf16[64,2048]{1,0:T(8,128)(2,1)}, bf16[64,2048]{1,0:T(8,128)(2,1)S(1)}, u32[]{:S(2)}, u32[]{:S(2)}) collective-permute-start(bf16[64,2048]{1,0:T(8,128)(2,1)} %get-tuple-element.150.refs_1_), channel_id=1, source_target_pairs={{0,3},{1,0},{2,1},{3,2},{4,7},{5,4},{6,5},{7,6},{8,11},{9,8},{10,9... | collective-permute-start | bytes 786440 | tf_op jit(solution)/shard_map/ppermute | solution.py:56
  194.3 16.2 %collective-permute-start.32 = (bf16[64,2048]{1,0:T(8,128)(2,1)S(1)}, bf16[64,2048]{1,0:T(8,128)(2,1)}, u32[]{:S(2)}, u32[]{:S(2)}) collective-permute-start(bf16[64,2048]{1,0:T(8,128)(2,1)S(1)} %collective-permute-done.30.refs_4_), channel_id=1, source_target_pairs={{0,1},{1,2},{2,3},{3,0},{4,5},{5,6},{6,7},{7,4},{8,9},{9,10},{10,1... | collective-permute-start | bytes 786440 | tf_op jit(solution)/shard_map/ppermute | solution.py:56
  202.6 7.9 %collective-permute-start.33 = (bf16[64,2048]{1,0:T(8,128)(2,1)S(1)}, bf16[64,2048]{1,0:T(8,128)(2,1)}, u32[]{:S(2)}, u32[]{:S(2)}) collective-permute-start(bf16[64,2048]{1,0:T(8,128)(2,1)S(1)} %collective-permute-done.29.refs_3_), channel_id=1, source_target_pairs={{0,3},{1,0},{2,1},{3,2},{4,7},{5,4},{6,5},{7,6},{8,11},{9,8},{10,9... | collective-permute-start | bytes 786440 | tf_op jit(solution)/shard_map/ppermute | solution.py:56
  222.9 10.3 %collective-permute-start.38 = (bf16[3200,512]{1,0:T(8,128)(2,1)S(1)}, bf16[3200,512]{1,0:T(8,128)(2,1)S(1)}, u32[]{:S(2)}, u32[]{:S(2)}) collective-permute-start(bf16[3200,512]{1,0:T(8,128)(2,1)S(1)} %collective-permute-done.34.refs_7_), channel_id=1, source_target_pairs={{0,4},{4,0},{8,12},{12,8},{1,5},{5,1},{9,13},{13,9},{2,6},{6,2},{1... | collective-permute-start | bytes 9830408 | tf_op jit(solution)/shard_map/ppermute | solution.py:868
  227.8 11.1 %collective-permute-start.39 = (bf16[64,2048]{1,0:T(8,128)(2,1)}, bf16[64,2048]{1,0:T(8,128)(2,1)S(1)}, u32[]{:S(2)}, u32[]{:S(2)}) collective-permute-start(bf16[64,2048]{1,0:T(8,128)(2,1)} %get-tuple-element.164), channel_id=1, source_target_pairs={{0,1},{1,2},{2,3},{3,0},{4,5},{5,6},{6,7},{7,4},{8,9},{9,10},{10,1... | collective-permute-start | bytes 786440 | tf_op jit(solution)/shard_map/ppermute | solution.py:56
  229.1 14.4 %collective-permute-start.40 = (bf16[64,2048]{1,0:T(8,128)(2,1)}, bf16[64,2048]{1,0:T(8,128)(2,1)}, u32[]{:S(2)}, u32[]{:S(2)}) collective-permute-start(bf16[64,2048]{1,0:T(8,128)(2,1)} %get-tuple-element.166), channel_id=1, source_target_pairs={{0,3},{1,0},{2,1},{3,2},{4,7},{5,4},{6,5},{7,6},{8,11},{9,8},{10,9... | collective-permute-start | bytes 786440 | tf_op jit(solution)/shard_map/ppermute | solution.py:56
  231.6 68.5 %collective-permute-start.52 = (bf16[1280,512]{1,0:T(8,128)(2,1)S(1)}, bf16[1280,512]{1,0:T(8,128)(2,1)}, u32[]{:S(2)}, u32[]{:S(2)}) collective-permute-start(bf16[1280,512]{1,0:T(8,128)(2,1)S(1)} %copy-done.12), channel_id=1, source_target_pairs={{0,12},{4,8},{8,4},{12,0},{1,13},{5,9},{9,5},{13,1},{2,14},{6,10},... | collective-permute-start | bytes 3932168 | tf_op jit(solution)/shard_map/ppermute | solution.py:880
  231.6 68.5 %collective-permute-start.51 = (bf16[1280,512]{1,0:T(8,128)(2,1)S(1)}, bf16[1280,512]{1,0:T(8,128)(2,1)}, u32[]{:S(2)}, u32[]{:S(2)}) collective-permute-start(bf16[1280,512]{1,0:T(8,128)(2,1)S(1)} %copy-done.12), channel_id=1, source_target_pairs={{0,8},{4,12},{8,0},{12,4},{1,9},{5,13},{9,1},{13,5},{2,10},{6,14},... | collective-permute-start | bytes 3932168 | tf_op jit(solution)/shard_map/ppermute | solution.py:879
  245.7 11.3 %collective-permute-start.41 = (bf16[64,2048]{1,0:T(8,128)(2,1)}, bf16[64,2048]{1,0:T(8,128)(2,1)S(1)}, u32[]{:S(2)}, u32[]{:S(2)}) collective-permute-start(bf16[64,2048]{1,0:T(8,128)(2,1)} %get-tuple-element.167), channel_id=1, source_target_pairs={{0,1},{1,2},{2,3},{3,0},{4,5},{5,6},{6,7},{7,4},{8,9},{9,10},{10,1... | collective-permute-start | bytes 786440 | tf_op jit(solution)/shard_map/ppermute | solution.py:56
  246.4 14.8 %collective-permute-start.42 = (bf16[64,2048]{1,0:T(8,128)(2,1)S(1)}, bf16[64,2048]{1,0:T(8,128)(2,1)S(1)}, u32[]{:S(2)}, u32[]{:S(2)}) collective-permute-start(bf16[64,2048]{1,0:T(8,128)(2,1)S(1)} %copy-done.29), channel_id=1, source_target_pairs={{0,3},{1,0},{2,1},{3,2},{4,7},{5,4},{6,5},{7,6},{8,11},{9,8},{10,9... | collective-permute-start | bytes 786440 | tf_op jit(solution)/shard_map/ppermute | solution.py:56
  249.5 15.6 %collective-permute-start.44 = (bf16[64,2048]{1,0:T(8,128)(2,1)}, bf16[64,2048]{1,0:T(8,128)(2,1)S(1)}, u32[]{:S(2)}, u32[]{:S(2)}) collective-permute-start(bf16[64,2048]{1,0:T(8,128)(2,1)} %get-tuple-element.172), channel_id=1, source_target_pairs={{0,3},{1,0},{2,1},{3,2},{4,7},{5,4},{6,5},{7,6},{8,11},{9,8},{10,9... | collective-permute-start | bytes 786440 | tf_op jit(solution)/shard_map/ppermute | solution.py:56
  256.9 17.0 %collective-permute-start.43 = (bf16[64,2048]{1,0:T(8,128)(2,1)S(1)}, bf16[64,2048]{1,0:T(8,128)(2,1)S(1)}, u32[]{:S(2)}, u32[]{:S(2)}) collective-permute-start(bf16[64,2048]{1,0:T(8,128)(2,1)S(1)} %copy-done.20), channel_id=1, source_target_pairs={{0,1},{1,2},{2,3},{3,0},{4,5},{5,6},{6,7},{7,4},{8,9},{9,10},{10,1... | collective-permute-start | bytes 786440 | tf_op jit(solution)/shard_map/ppermute | solution.py:56
  264.0 15.4 %collective-permute-start.47 = (bf16[64,2048]{1,0:T(8,128)(2,1)}, bf16[64,2048]{1,0:T(8,128)(2,1)S(1)}, u32[]{:S(2)}, u32[]{:S(2)}) collective-permute-start(bf16[64,2048]{1,0:T(8,128)(2,1)} %finish.6.refs_0_), channel_id=1, source_target_pairs={{0,1},{1,2},{2,3},{3,0},{4,5},{5,6},{6,7},{7,4},{8,9},{9,10},{10,1... | collective-permute-start | bytes 786440 | tf_op jit(solution)/shard_map/ppermute | solution.py:56
  265.1 18.6 %collective-permute-start.45 = (bf16[64,2048]{1,0:T(8,128)(2,1)}, bf16[64,2048]{1,0:T(8,128)(2,1)S(1)}, u32[]{:S(2)}, u32[]{:S(2)}) collective-permute-start(bf16[64,2048]{1,0:T(8,128)(2,1)} %finish.6.refs_0_), channel_id=1, source_target_pairs={{0,3},{1,0},{2,1},{3,2},{4,7},{5,4},{6,5},{7,6},{8,11},{9,8},{10,9... | collective-permute-start | bytes 786440 | tf_op jit(solution)/shard_map/ppermute | solution.py:56
  276.8 12.9 %collective-permute-start.46 = (bf16[64,2048]{1,0:T(8,128)(2,1)}, bf16[64,2048]{1,0:T(8,128)(2,1)S(1)}, u32[]{:S(2)}, u32[]{:S(2)}) collective-permute-start(bf16[64,2048]{1,0:T(8,128)(2,1)} %finish.7.refs_1_), channel_id=1, source_target_pairs={{0,3},{1,0},{2,1},{3,2},{4,7},{5,4},{6,5},{7,6},{8,11},{9,8},{10,9... | collective-permute-start | bytes 786440 | tf_op jit(solution)/shard_map/ppermute | solution.py:56
  279.4 17.0 %collective-permute-start.48 = (bf16[64,2048]{1,0:T(8,128)(2,1)}, bf16[64,2048]{1,0:T(8,128)(2,1)S(1)}, u32[]{:S(2)}, u32[]{:S(2)}) collective-permute-start(bf16[64,2048]{1,0:T(8,128)(2,1)} %finish.7.refs_1_), channel_id=1, source_target_pairs={{0,1},{1,2},{2,3},{3,0},{4,5},{5,6},{6,7},{7,4},{8,9},{9,10},{10,1... | collective-permute-start | bytes 786440 | tf_op jit(solution)/shard_map/ppermute | solution.py:56
  283.7 18.2 %collective-permute-start.49 = (bf16[64,2048]{1,0:T(8,128)(2,1)S(1)}, bf16[64,2048]{1,0:T(8,128)(2,1)S(1)}, u32[]{:S(2)}, u32[]{:S(2)}) collective-permute-start(bf16[64,2048]{1,0:T(8,128)(2,1)S(1)} %collective-permute-done.47.refs_4_), channel_id=1, source_target_pairs={{0,1},{1,2},{2,3},{3,0},{4,5},{5,6},{6,7},{7,4},{8,9},{9,10},{10,1... | collective-permute-start | bytes 786440 | tf_op jit(solution)/shard_map/ppermute | solution.py:56
  289.6 16.4 %collective-permute-start.50 = (bf16[64,2048]{1,0:T(8,128)(2,1)S(1)}, bf16[64,2048]{1,0:T(8,128)(2,1)S(1)}, u32[]{:S(2)}, u32[]{:S(2)}) collective-permute-start(bf16[64,2048]{1,0:T(8,128)(2,1)S(1)} %collective-permute-done.46.refs_3_), channel_id=1, source_target_pairs={{0,3},{1,0},{2,1},{3,2},{4,7},{5,4},{6,5},{7,6},{8,11},{9,8},{10,9... | collective-permute-start | bytes 786440 | tf_op jit(solution)/shard_map/ppermute | solution.py:56
  (65 other events, 359.1 us)

commit v12 on v11

--- a/solution.py
+++ b/solution.py
@@ -865,10 +865,10 @@
     local, first = local_window(bound, places, slots, spots, chunk, qkvs, heads)
     if lots:
         lots[2], local, halo, across_x[1] = lax.optimization_barrier((lots[2], local, halo, across_x[1]))
-        corners[1] = lax.ppermute(across_x[1], "seq", xor_pairs(seq_count, 1))
     mixed, *outer = halo_window(info, near, chunk, far, local, first, halo, win_out, heads)
     if seq_count == 4:
-        mixed, corners[1] = lax.optimization_barrier((mixed, corners[1]))
+        across_x[1], lots[2], _ = lax.optimization_barrier((across_x[1], lots[2], outer))
+        corners[1] = lax.ppermute(across_x[1], "seq", xor_pairs(seq_count, 1))
     parts = scatter_rows(outer, lambda: near_chunks(mixed, win_out, near, chunk))
     parts = in_halves(parts)
     upper = finish(residual_upper, gain_three, parts[0], True)[0]

time: 339 us -> 343 us (1.012)
  starting transfers between devices: 68.1 us -> 75 us
    ppermute x39, starting transfers between devices: 49 us -> 57.7 us  [turned(): lax.ppermute(value, 'head', [(i, (i + step) % size) for i in range(size)])]
    ppermute x39, waiting for transfers between devices: 98.4 us -> 93.7 us  [turned(): lax.ppermute(value, 'head', [(i, (i + step) % size) for i in range(size)])]
    ppermute x1, waiting for transfers between devices: 0.01 us -> 4.6 us  [shards(): across_x[2] = lax.ppermute(lots[2], 'seq', xor_pairs(seq_count, 2))]
    unnamed x114 -> x92, local copies, waits for them, and re-layouts: 8.99 us -> 7.78 us
  transfers between devices with their start and end apart: 56 -> 56, of which waited for: 33 -> 32; matrix products, arithmetic and copies ran while one was open for 3% -> 3% of each run, Pallas kernels for 33% -> 31%
where the time goes in v12:
time: 343 us; the launch traced here: 342 us
  Pallas kernels  131 us (38%)
  waiting for transfers between devices  108 us (31%)
  starting transfers between devices  75 us (22%)
  local copies, waits for them, and re-layouts  13.5 us (4%)
  other arithmetic  7.51 us (2%)
  between operations  6.8 us (2%)
    ppermute x39, waiting for transfers between devices, turned(): lax.ppermute(value, 'head', [(i, (i + step) % size) for i in range(size)])  93.7 us
    ppermute x39, starting transfers between devices, turned(): lax.ppermute(value, 'head', [(i, (i + step) % size) for i in range(size)])  57.7 us
    pallas_call x4, Pallas kernels, lookup(): pl.pallas_call(functools.partial(lookup_kernel, lots), grid=(TABLE_STEPS,...  36.8 us
    pallas_call x1, Pallas kernels, scores(): pl.pallas_call(functools.partial(score_kernel, len(early), len(units), le...  22 us
    pallas_call x2, Pallas kernels, matmul(): pl.pallas_call(matmul_kernel, grid=(b.shape[1] // tile,), in_specs=[pl.Bl...  12.6 us
    pallas_call x2, Pallas kernels, project(): pl.pallas_call(functools.partial(project_kernel, heads, slots, chunk, cou...  11.9 us
    pallas_call x4, Pallas kernels, finish(): pl.pallas_call(functools.partial(finish_kernel, len(terms), last), in_spe...  8.72 us
    unnamed x92, local copies, waits for them, and re-layouts  7.78 us
  transfers between devices with their start and end apart: 56, of which 32 were waited for; matrix products, arithmetic and copies ran while one was open for 3% of the time, Pallas kernels for 31%

profile of v12, /device:TPU:0, one launch (start us, length us, event | category | flops | bytes accessed | tf_op | source)
XLA Modules:
  0.0 341.9 jit_solution(8045867769178582441)
XLA Ops:
  1.3 2.4 collective-permute-start.2
  5.0 2.3 collective-permute-done.1
  8.0 8.6 %lookup.5 = (bf16[256,512]{1,0:T(8,128)(2,1)}, bf16[256,512]{1,0:T(8,128)(2,1)}) custom-call(s32[1,512]{1,0:T(1,128)} %bitcast.49, bf16[6400,512]{1,0:T(8,128)(2,1)} %refs_3_.2), custom_call_target="tpu_custom_call" | custom-call | flops 4800000000 | bytes 24000000 | tf_op jit(solution)/shard_map/lookup/pallas_call | solution.py:160
  18.2 2.2 collective-permute-start.4
  21.0 8.6 %lookup.7 = (bf16[256,512]{1,0:T(8,128)(2,1)}, bf16[256,512]{1,0:T(8,128)(2,1)}) custom-call(s32[1,512]{1,0:T(1,128)} %bitcast.51, bf16[6400,512]{1,0:T(8,128)(2,1)} %refs_3_.2), custom_call_target="tpu_custom_call" | custom-call | flops 4800000000 | bytes 24000000 | tf_op jit(solution)/shard_map/lookup/pallas_call | solution.py:160
  32.2 8.6 %lookup.6 = (bf16[256,512]{1,0:T(8,128)(2,1)}, bf16[256,512]{1,0:T(8,128)(2,1)}) custom-call(s32[1,512]{1,0:T(1,128)} %bitcast.52, bf16[6400,512]{1,0:T(8,128)(2,1)} %refs_3_.2), custom_call_target="tpu_custom_call" | custom-call | flops 4800000000 | bytes 24000000 | tf_op jit(solution)/shard_map/lookup/pallas_call | solution.py:160
  43.6 3.8 %collective-permute-start.8 = (bf16[256,512]{1,0:T(8,128)(2,1)}, bf16[256,512]{1,0:T(8,128)(2,1)S(1)}, u32[]{:S(2)}, u32[]{:S(2)}) collective-permute-start(bf16[256,512]{1,0:T(8,128)(2,1)} %get-tuple-element.104), channel_id=1, source_target_pairs={{0,3},{1,0},{2,1},{3,2},{4,7},{5,4},{6,5},{7,6},{8,11},{9,8},{10,9... | collective-permute-start | bytes 786440 | tf_op jit(solution)/shard_map/ppermute | solution.py:56
  47.5 11.1 %lookup.4 = (bf16[256,512]{1,0:T(8,128)(2,1)}, bf16[256,512]{1,0:T(8,128)(2,1)}, bf16[1920,512]{1,0:T(8,128)(2,1)}, bf16[3200,512]{1,0:T(8,128)(2,1)}, bf16[1280,512]{1,0:T(8,128)(2,1)}) custom-call(s32[1,512]{1,0:T(1,128)} %bitcast.45, bf16[6400,512]{1,0:T(8,128)(2,1)} %refs_3_.2), custom_call_target="tpu_custom_call" | custom-call | flops 4800000000 | bytes 24000000 | tf_op jit(solution)/shard_map/lookup/pallas_call | solution.py:160
  59.5 2.2 collect.1
  63.7 4.7 %collective-permute-done.10.refs_2_ = bf16[128,512]{1,0:T(8,128)(2,1)S(1)} collective-permute-done((bf16[128,512]{1,0:T(8,128)(2,1)}, bf16[128,512]{1,0:T(8,128)(2,1)S(1)}, u32[]{:S(2)}, u32[]{:S(2)}) %collective-permute-start.10) | collective-permute-done | bytes 131104 | tf_op jit(solution)/shard_map/ppermute | solution.py:758
  80.5 2.7 collective-permute-done.16.refs_2_
  83.2 4.2 %collective-permute-start.14 = (bf16[64,2048]{1,0:T(8,128)(2,1)}, bf16[64,2048]{1,0:T(8,128)(2,1)S(1)}, u32[]{:S(2)}, u32[]{:S(2)}) collective-permute-start(bf16[64,2048]{1,0:T(8,128)(2,1)} %get-tuple-element.115.refs_1_), channel_id=1, source_target_pairs={{0,3},{1,0},{2,1},{3,2},{4,7},{5,4},{6,5},{7,6},{8,11},{9,8},{10,9... | collective-permute-start | bytes 786440 | tf_op jit(solution)/shard_map/ppermute | solution.py:56
  93.3 9.3 %collective-permute-done.14.refs_3_ = bf16[64,2048]{1,0:T(8,128)(2,1)S(1)} collective-permute-done((bf16[64,2048]{1,0:T(8,128)(2,1)}, bf16[64,2048]{1,0:T(8,128)(2,1)S(1)}, u32[]{:S(2)}, u32[]{:S(2)}) %collective-permute-start.14) | collective-permute-done | bytes 262176 | tf_op jit(solution)/shard_map/ppermute | solution.py:56
  105.0 6.7 %project.2 = (bf16[4,384,256]{2,1,0:T(8,128)(2,1)}, bf16[4,384,256]{2,1,0:T(8,128)(2,1)}, bf16[384,512]{1,0:T(8,128)(2,1)}, f32[4,176,128]{2,1,0:T(8,128)}) custom-call(s32[1]{0:T(128)} %copy.35.bound_ref, s32[3]{0:T(128)} %bitcast.53, bf16[64,2048]{1,0:T(8,128)(2,1)} %get-tuple-element.114.refs_0_, bf16[64,2048]{1,0:T(8,128)(2,1)} %get-tuple-element.115.refs_1_, ...), custom_call_target="tpu_custom_call" | custom-call | flops 3000000000 | bytes 15000000 | tf_op jit(solution)/shard_map/project/pallas_call | solution.py:335
  113.3 5.2 %project.3 = (bf16[4,128,256]{2,1,0:T(8,128)(2,1)}, bf16[4,128,256]{2,1,0:T(8,128)(2,1)}, bf16[128,512]{1,0:T(8,128)(2,1)}, bf16[4,176,128]{2,1,0:T(8,128)(2,1)}) custom-call(s32[1]{0:T(128)} %copy.35.bound_ref, s32[1]{0:T(128)} %slice.77.places_ref, bf16[64,2048]{1,0:T(8,128)(2,1)} %copy-done.31, bf16[64,2048]{1,0:T(8,128)(2,1)} %copy-done.34, ...), custom_call_target="tpu_custom_call" | custom-call | flops 3000000000 | bytes 15000000 | tf_op jit(solution)/shard_map/project/pallas_call | solution.py:335
  118.5 2.8 collective-permute-start.21
  124.6 4.6 %within.1 = (f32[4,512,128]{2,1,0:T(8,128)}, f32[4,512,8]{2,1,0:T(8,128)}) custom-call(s32[1]{0:T(128)} %copy.35.bound_ref, s32[4]{0:T(128)} %copy-done.6, bf16[4,384,256]{2,1,0:T(8,128)(2,1)} %get-tuple-element.118.refs_0_, bf16[4,128,256]{2,1,0:T(8,128)(2,1)} %get-tuple-element.122.refs_1_, bf16[4,384,256]{2,1,0:T(8,128)(2,1)} %get-tuple-element.123.refs_2_, ...), custom_call_target="tpu_custom_call" | custom-call | flops 2700000000 | bytes 13500000 | tf_op jit(solution)/shard_map/within/pallas_call | solution.py:374
  130.4 4.8 %across.1 = (bf16[512,512]{1,0:T(8,128)(2,1)}, bf16[64,2048]{1,0:T(8,128)(2,1)}, bf16[64,2048]{1,0:T(8,128)(2,1)}) custom-call(s32[1]{0:T(128)} %copy.35.bound_ref, s32[4]{0:T(128)} %copy-done.6, s32[3]{0:T(128)} %add_convert_fusion.share_ref, bf16[4,384,256]{2,1,0:T(8,128)(2,1)} %get-tuple-element.118.refs_0_, ...), custom_call_target="tpu_custom_call" | custom-call | flops 2700000000 | bytes 13500000 | tf_op jit(solution)/shard_map/across/pallas_call | solution.py:423
  135.3 3.0 collective-permute-start.34
  138.8 3.2 collective-permute-start.23
  142.1 3.9 %near.2 = (bf16[64,2048]{1,0:T(8,128)(2,1)}, bf16[64,2048]{1,0:T(8,128)(2,1)}, bf16[64,2048]{1,0:T(8,128)(2,1)}, bf16[64,2048]{1,0:T(8,128)(2,1)}, bf16[64,2048]{1,0:T(8,128)(2,1)}, /*index=5*/bf16[64,2048]{1,0:T(8,128)(2,1)}) custom-call(bf16[512,512]{1,0:T(8,128)(2,1)} %get-tuple-element.133.mixed_ref, bf16[512,2048]{1,0:T(8,128)(2,1)} %weight_ref.3), custom_call_target="tpu_custom_call" | custom-call | flops 2400000000 | bytes 12000000 | tf_op jit(solution)/shard_map/near/pallas_call | solution.py:442
  145.9 3.6 %collective-permute-done.22.before_ref = bf16[64,2048]{1,0:T(8,128)(2,1)S(1)} collective-permute-done((bf16[64,2048]{1,0:T(8,128)(2,1)}, bf16[64,2048]{1,0:T(8,128)(2,1)S(1)}, u32[]{:S(2)}, u32[]{:S(2)}) %collective-permute-start.22) | collective-permute-done | bytes 262176 | tf_op jit(solution)/shard_map/ppermute | solution.py:56
  149.5 2.6 collective-permute-done.23.after_ref
  158.7 7.5 %collective-permute-done.24.refs_1_ = bf16[64,2048]{1,0:T(8,128)(2,1)S(1)} collective-permute-done((bf16[64,2048]{1,0:T(8,128)(2,1)}, bf16[64,2048]{1,0:T(8,128)(2,1)S(1)}, u32[]{:S(2)}, u32[]{:S(2)}) %collective-permute-start.24) | collective-permute-done | bytes 262176 | tf_op jit(solution)/shard_map/ppermute | solution.py:56
  171.9 2.7 collective-permute-start.30
  174.6 3.7 %collective-permute-done.27.refs_2_ = bf16[64,2048]{1,0:T(8,128)(2,1)S(1)} collective-permute-done((bf16[64,2048]{1,0:T(8,128)(2,1)}, bf16[64,2048]{1,0:T(8,128)(2,1)S(1)}, u32[]{:S(2)}, u32[]{:S(2)}) %collective-permute-start.27) | collective-permute-done | bytes 262176 | tf_op jit(solution)/shard_map/ppermute | solution.py:56
  183.1 8.8 %collective-permute-start.31 = (bf16[64,2048]{1,0:T(8,128)(2,1)}, bf16[64,2048]{1,0:T(8,128)(2,1)S(1)}, u32[]{:S(2)}, u32[]{:S(2)}) collective-permute-start(bf16[64,2048]{1,0:T(8,128)(2,1)} %get-tuple-element.150.refs_1_), channel_id=1, source_target_pairs={{0,1},{1,2},{2,3},{3,0},{4,5},{5,6},{6,7},{7,4},{8,9},{9,10},{10,1... | collective-permute-start | bytes 786440 | tf_op jit(solution)/shard_map/ppermute | solution.py:56
  195.9 3.7 %collective-permute-done.31.refs_5_ = bf16[64,2048]{1,0:T(8,128)(2,1)S(1)} collective-permute-done((bf16[64,2048]{1,0:T(8,128)(2,1)}, bf16[64,2048]{1,0:T(8,128)(2,1)S(1)}, u32[]{:S(2)}, u32[]{:S(2)}) %collective-permute-start.31) | collective-permute-done | bytes 262176 | tf_op jit(solution)/shard_map/ppermute | solution.py:56
  199.6 6.8 %collective-permute-start.32 = (bf16[64,2048]{1,0:T(8,128)(2,1)S(1)}, bf16[64,2048]{1,0:T(8,128)(2,1)}, u32[]{:S(2)}, u32[]{:S(2)}) collective-permute-start(bf16[64,2048]{1,0:T(8,128)(2,1)S(1)} %collective-permute-done.30.refs_4_), channel_id=1, source_target_pairs={{0,1},{1,2},{2,3},{3,0},{4,5},{5,6},{6,7},{7,4},{8,9},{9,10},{10,1... | collective-permute-start | bytes 786440 | tf_op jit(solution)/shard_map/ppermute | solution.py:56
  208.3 7.2 %matmul.2.refs_0_ = bf16[384,1536]{1,0:T(8,128)(2,1)} custom-call(bf16[64,2048]{1,0:T(8,128)(2,1)} %get-tuple-element.145.refs_0_, bf16[64,2048]{1,0:T(8,128)(2,1)} %get-tuple-element.150.refs_1_, bf16[64,2048]{1,0:T(8,128)(2,1)} %copy-done.21, bf16[64,2048]{1,0:T(8,128)(2,1)} %copy-done.29, bf16[64,2048]{1,0:T(8,128)(2,1)} %copy-done.18, ...), custom_call_target="tpu_custom_call" | custom-call | flops 3000000000 | bytes 15000000 | tf_op jit(solution)/shard_map/matmul/pallas_call | solution.py:461
  215.5 5.4 %matmul.3.refs_1_ = bf16[128,1536]{1,0:T(8,128)(2,1)} custom-call(bf16[64,2048]{1,0:T(8,128)(2,1)} %collective-permute-done.32.refs_0_, bf16[64,2048]{1,0:T(8,128)(2,1)} %collective-permute-done.33.refs_1_, bf16[2048,1536]{1,0:T(8,128)(2,1)} %refs_2_.3), custom_call_target="tpu_custom_call" | custom-call | flops 3000000000 | bytes 15000000 | tf_op jit(solution)/shard_map/matmul/pallas_call | solution.py:461
  223.2 4.8 %local_window.1 = (bf16[512,512]{1,0:T(8,128)(2,1)}, bf16[64,1536]{1,0:T(8,128)(2,1)}) custom-call(s32[1]{0:T(128)} %copy.35.bound_ref, s32[4]{0:T(128)} %copy-done.6, bf16[384,1536]{1,0:T(8,128)(2,1)} %matmul.2.refs_0_, bf16[128,1536]{1,0:T(8,128)(2,1)} %matmul.3.refs_1_), custom_call_target="tpu_custom_call" | custom-call | flops 4800000000 | bytes 24000000 | tf_op jit(solution)/shard_map/local_window/pallas_call | solution.py:529
  228.7 3.7 %halo_window.1 = (bf16[512,512]{1,0:T(8,128)(2,1)}, bf16[64,2048]{1,0:T(8,128)(2,1)}, bf16[64,2048]{1,0:T(8,128)(2,1)}) custom-call(s32[3]{0:T(128)} %pad_add_fusion.4.info_ref, bf16[512,512]{1,0:T(8,128)(2,1)} %get-tuple-element.156.local_ref, bf16[64,1536]{1,0:T(8,128)(2,1)} %get-tuple-element.157.first_ref, bf16[64,1536]{1,0:T(8,128)(2,1)} %copy-done.38, ...), custom_call_target="tpu_custom_call" | custom-call | flops 2700000000 | bytes 13500000 | tf_op jit(solution)/shard_map/halo_window/pallas_call | solution.py:566
  233.6 2.6 collective-permute-start.39
  236.2 3.8 %near.3 = (bf16[64,2048]{1,0:T(8,128)(2,1)}, bf16[64,2048]{1,0:T(8,128)(2,1)}, bf16[64,2048]{1,0:T(8,128)(2,1)}, bf16[64,2048]{1,0:T(8,128)(2,1)}, bf16[64,2048]{1,0:T(8,128)(2,1)}, /*index=5*/bf16[64,2048]{1,0:T(8,128)(2,1)}) custom-call(bf16[512,512]{1,0:T(8,128)(2,1)} %get-tuple-element.159.mixed_ref, bf16[512,2048]{1,0:T(8,128)(2,1)} %weight_ref.5), custom_call_target="tpu_custom_call" | custom-call | flops 2400000000 | bytes 12000000 | tf_op jit(solution)/shard_map/near/pallas_call | solution.py:442
  240.2 3.5 %collective-permute-done.38.before_ref = bf16[64,2048]{1,0:T(8,128)(2,1)} collective-permute-done((bf16[64,2048]{1,0:T(8,128)(2,1)}, bf16[64,2048]{1,0:T(8,128)(2,1)}, u32[]{:S(2)}, u32[]{:S(2)}) %collective-permute-start.38) | collective-permute-done | bytes 262176 | tf_op jit(solution)/shard_map/ppermute | solution.py:56
  243.7 5.0 %collective-permute-done.39.after_ref = bf16[64,2048]{1,0:T(8,128)(2,1)} collective-permute-done((bf16[64,2048]{1,0:T(8,128)(2,1)}, bf16[64,2048]{1,0:T(8,128)(2,1)}, u32[]{:S(2)}, u32[]{:S(2)}) %collective-permute-start.39) | collective-permute-done | bytes 262176 | tf_op jit(solution)/shard_map/ppermute | solution.py:56
  255.1 7.2 %collective-permute-done.40.refs_1_ = bf16[64,2048]{1,0:T(8,128)(2,1)} collective-permute-done((bf16[64,2048]{1,0:T(8,128)(2,1)}, bf16[64,2048]{1,0:T(8,128)(2,1)}, u32[]{:S(2)}, u32[]{:S(2)}) %collective-permute-start.40) | collective-permute-done | bytes 262176 | tf_op jit(solution)/shard_map/ppermute | solution.py:56
  264.4 3.3 collective-permute-done.42.refs_1_
  267.7 5.6 %collective-permute-done.43.refs_2_ = bf16[64,2048]{1,0:T(8,128)(2,1)} collective-permute-done((bf16[64,2048]{1,0:T(8,128)(2,1)}, bf16[64,2048]{1,0:T(8,128)(2,1)}, u32[]{:S(2)}, u32[]{:S(2)}) %collective-permute-start.43) | collective-permute-done | bytes 262176 | tf_op jit(solution)/shard_map/ppermute | solution.py:56
  276.3 2.7 collective-permute-done.46.refs_4_
  279.0 5.7 %collective-permute-done.44.refs_2_ = bf16[64,2048]{1,0:T(8,128)(2,1)} collective-permute-done((bf16[64,2048]{1,0:T(8,128)(2,1)}, bf16[64,2048]{1,0:T(8,128)(2,1)}, u32[]{:S(2)}, u32[]{:S(2)}) %collective-permute-start.44) | collective-permute-done | bytes 262176 | tf_op jit(solution)/shard_map/ppermute | solution.py:56
  285.5 4.9 %collective-permute-done.47.refs_5_ = bf16[64,2048]{1,0:T(8,128)(2,1)} collective-permute-done((bf16[64,2048]{1,0:T(8,128)(2,1)}, bf16[64,2048]{1,0:T(8,128)(2,1)}, u32[]{:S(2)}, u32[]{:S(2)}) %collective-permute-start.47) | collective-permute-done | bytes 262176 | tf_op jit(solution)/shard_map/ppermute | solution.py:56
  290.4 5.7 %collective-permute-done.45.refs_3_ = bf16[64,2048]{1,0:T(8,128)(2,1)} collective-permute-done((bf16[64,2048]{1,0:T(8,128)(2,1)}, bf16[64,2048]{1,0:T(8,128)(2,1)}, u32[]{:S(2)}, u32[]{:S(2)}) %collective-permute-start.45) | collective-permute-done | bytes 262176 | tf_op jit(solution)/shard_map/ppermute | solution.py:56
  296.9 2.9 turn.1.refs_0_
  301.7 3.6 %collective-permute-done.49.refs_2_ = bf16[64,2048]{1,0:T(8,128)(2,1)} collective-permute-done((bf16[64,2048]{1,0:T(8,128)(2,1)}, bf16[64,2048]{1,0:T(8,128)(2,1)}, u32[]{:S(2)}, u32[]{:S(2)}) %collective-permute-start.49) | collective-permute-done | bytes 262176 | tf_op jit(solution)/shard_map/ppermute | solution.py:56
  305.2 4.6 %collective-permute-done.51.refs_9_ = bf16[1280,512]{1,0:T(8,128)(2,1)} collective-permute-done((bf16[1280,512]{1,0:T(8,128)(2,1)S(1)}, bf16[1280,512]{1,0:T(8,128)(2,1)}, u32[]{:S(2)}, u32[]{:S(2)}) %collective-permute-start.51) | collective-permute-done | bytes 1310752 | tf_op jit(solution)/shard_map/ppermute | solution.py:879
  311.6 22.0 %scores.1 = f32[8,512]{1,0:T(8,128)} custom-call(s32[4]{0:T(128)} %iota_xor_fusion.order_ref, bf16[2048,384]{1,0:T(8,128)(2,1)} %turn.1.refs_0_, bf16[64,2048]{1,0:T(8,128)(2,1)} %collective-permute-done.48.refs_1_, bf16[64,2048]{1,0:T(8,128)(2,1)} %collective-permute-done.49.refs_2_, bf16[6400,512]{1,0:T(8,128)(2,1)} %refs_3_.2, ...), custom_call_target="tpu_custom_call" | custom-call | flops 12000000000 | bytes 60000000 | tf_op jit(solution)/shard_map/scores/pallas_call | solution.py:668
  (215 shorter events, 86.7 us)
Async XLA Ops:
  4.4 217.5 %collective-permute-start.36 = (bf16[6400,512]{1,0:T(8,128)(2,1)}, bf16[6400,512]{1,0:T(8,128)(2,1)}, u32[]{:S(2)}, u32[]{:S(2)}) collective-permute-start(bf16[6400,512]{1,0:T(8,128)(2,1)} %refs_3_.2), channel_id=1, source_target_pairs={{0,4},{4,0},{8,12},{12,8},{1,5},{5,1},{9,13},{13,9},{2,6},{6,2},{1... | collective-permute-start | bytes 19660808 | tf_op jit(solution)/shard_map/ppermute | solution.py:848
  16.6 24.2 %collective-permute-start.3 = (bf16[256,512]{1,0:T(8,128)(2,1)}, bf16[256,512]{1,0:T(8,128)(2,1)S(1)}, u32[]{:S(2)}, u32[]{:S(2)}) collective-permute-start(bf16[256,512]{1,0:T(8,128)(2,1)} %get-tuple-element.94), channel_id=1, source_target_pairs={{0,1},{1,2},{2,3},{3,0},{4,5},{5,6},{6,7},{7,4},{8,9},{9,10},{10,1... | collective-permute-start | bytes 786440 | tf_op jit(solution)/shard_map/ppermute | solution.py:56
  18.2 22.6 %collective-permute-start.4 = (bf16[256,512]{1,0:T(8,128)(2,1)}, bf16[256,512]{1,0:T(8,128)(2,1)S(1)}, u32[]{:S(2)}, u32[]{:S(2)}) collective-permute-start(bf16[256,512]{1,0:T(8,128)(2,1)} %get-tuple-element.95), channel_id=1, source_target_pairs={{0,3},{1,0},{2,1},{3,2},{4,7},{5,4},{6,5},{7,6},{8,11},{9,8},{10,9... | collective-permute-start | bytes 786440 | tf_op jit(solution)/shard_map/ppermute | solution.py:56
  29.6 29.0 %collective-permute-start.6 = (bf16[256,512]{1,0:T(8,128)(2,1)}, bf16[256,512]{1,0:T(8,128)(2,1)S(1)}, u32[]{:S(2)}, u32[]{:S(2)}) collective-permute-start(bf16[256,512]{1,0:T(8,128)(2,1)} %get-tuple-element.101), channel_id=1, source_target_pairs={{0,3},{1,0},{2,1},{3,2},{4,7},{5,4},{6,5},{7,6},{8,11},{9,8},{10,9... | collective-permute-start | bytes 786440 | tf_op jit(solution)/shard_map/ppermute | solution.py:56
  31.4 27.2 %collective-permute-start.7 = (bf16[256,512]{1,0:T(8,128)(2,1)}, bf16[256,512]{1,0:T(8,128)(2,1)S(1)}, u32[]{:S(2)}, u32[]{:S(2)}) collective-permute-start(bf16[256,512]{1,0:T(8,128)(2,1)} %get-tuple-element.103), channel_id=1, source_target_pairs={{0,1},{1,2},{2,3},{3,0},{4,5},{5,6},{6,7},{7,4},{8,9},{9,10},{10,1... | collective-permute-start | bytes 786440 | tf_op jit(solution)/shard_map/ppermute | solution.py:56
  43.6 15.0 %collective-permute-start.5 = (bf16[256,512]{1,0:T(8,128)(2,1)}, bf16[256,512]{1,0:T(8,128)(2,1)S(1)}, u32[]{:S(2)}, u32[]{:S(2)}) collective-permute-start(bf16[256,512]{1,0:T(8,128)(2,1)} %get-tuple-element.100), channel_id=1, source_target_pairs={{0,1},{1,2},{2,3},{3,0},{4,5},{5,6},{6,7},{7,4},{8,9},{9,10},{10,1... | collective-permute-start | bytes 786440 | tf_op jit(solution)/shard_map/ppermute | solution.py:56
  43.6 15.0 %collective-permute-start.8 = (bf16[256,512]{1,0:T(8,128)(2,1)}, bf16[256,512]{1,0:T(8,128)(2,1)S(1)}, u32[]{:S(2)}, u32[]{:S(2)}) collective-permute-start(bf16[256,512]{1,0:T(8,128)(2,1)} %get-tuple-element.104), channel_id=1, source_target_pairs={{0,3},{1,0},{2,1},{3,2},{4,7},{5,4},{6,5},{7,6},{8,11},{9,8},{10,9... | collective-permute-start | bytes 786440 | tf_op jit(solution)/shard_map/ppermute | solution.py:56
  61.8 6.5 %collective-permute-start.10 = (bf16[128,512]{1,0:T(8,128)(2,1)}, bf16[128,512]{1,0:T(8,128)(2,1)S(1)}, u32[]{:S(2)}, u32[]{:S(2)}) collective-permute-start(bf16[128,512]{1,0:T(8,128)(2,1)} %get-tuple-element.107), channel_id=1, source_target_pairs={{0,8},{4,12},{8,0},{12,4},{1,9},{5,13},{9,1},{13,5},{2,10},{6,14},... | collective-permute-start | bytes 393224 | tf_op jit(solution)/shard_map/ppermute | solution.py:758
  62.4 7.9 %collective-permute-start.11 = (bf16[128,512]{1,0:T(8,128)(2,1)}, bf16[128,512]{1,0:T(8,128)(2,1)S(1)}, u32[]{:S(2)}, u32[]{:S(2)}) collective-permute-start(bf16[128,512]{1,0:T(8,128)(2,1)} %get-tuple-element.108), channel_id=1, source_target_pairs={{0,12},{4,8},{8,4},{12,0},{1,13},{5,9},{9,5},{13,1},{2,14},{6,10},... | collective-permute-start | bytes 393224 | tf_op jit(solution)/shard_map/ppermute | solution.py:758
  70.3 48.1 %collective-permute-start.18 = (bf16[1920,512]{1,0:T(8,128)(2,1)}, bf16[1920,512]{1,0:T(8,128)(2,1)S(1)}, u32[]{:S(2)}, u32[]{:S(2)}) collective-permute-start(bf16[1920,512]{1,0:T(8,128)(2,1)} %get-tuple-element.131), channel_id=1, source_target_pairs={{0,8},{4,12},{8,0},{12,4},{1,9},{5,13},{9,1},{13,5},{2,10},{6,14},... | collective-permute-start | bytes 5898248 | tf_op jit(solution)/shard_map/ppermute | solution.py:808
  74.4 8.8 %collective-permute-start.16 = (bf16[64,2048]{1,0:T(8,128)(2,1)}, bf16[64,2048]{1,0:T(8,128)(2,1)S(1)}, u32[]{:S(2)}, u32[]{:S(2)}) collective-permute-start(bf16[64,2048]{1,0:T(8,128)(2,1)} %get-tuple-element.114.refs_0_), channel_id=1, source_target_pairs={{0,3},{1,0},{2,1},{3,2},{4,7},{5,4},{6,5},{7,6},{8,11},{9,8},{10,9... | collective-permute-start | bytes 786440 | tf_op jit(solution)/shard_map/ppermute | solution.py:56
  80.1 13.2 %collective-permute-start.12 = (bf16[64,2048]{1,0:T(8,128)(2,1)}, bf16[64,2048]{1,0:T(8,128)(2,1)S(1)}, u32[]{:S(2)}, u32[]{:S(2)}) collective-permute-start(bf16[64,2048]{1,0:T(8,128)(2,1)} %get-tuple-element.114.refs_0_), channel_id=1, source_target_pairs={{0,1},{1,2},{2,3},{3,0},{4,5},{5,6},{6,7},{7,4},{8,9},{9,10},{10,1... | collective-permute-start | bytes 786440 | tf_op jit(solution)/shard_map/ppermute | solution.py:56
  80.4 23.9 %collective-permute-start.17 = (bf16[64,2048]{1,0:T(8,128)(2,1)}, bf16[64,2048]{1,0:T(8,128)(2,1)S(1)}, u32[]{:S(2)}, u32[]{:S(2)}) collective-permute-start(bf16[64,2048]{1,0:T(8,128)(2,1)} %get-tuple-element.115.refs_1_), channel_id=1, source_target_pairs={{0,1},{1,2},{2,3},{3,0},{4,5},{5,6},{6,7},{7,4},{8,9},{9,10},{10,1... | collective-permute-start | bytes 786440 | tf_op jit(solution)/shard_map/ppermute | solution.py:56
  83.2 19.4 %collective-permute-start.14 = (bf16[64,2048]{1,0:T(8,128)(2,1)}, bf16[64,2048]{1,0:T(8,128)(2,1)S(1)}, u32[]{:S(2)}, u32[]{:S(2)}) collective-permute-start(bf16[64,2048]{1,0:T(8,128)(2,1)} %get-tuple-element.115.refs_1_), channel_id=1, source_target_pairs={{0,3},{1,0},{2,1},{3,2},{4,7},{5,4},{6,5},{7,6},{8,11},{9,8},{10,9... | collective-permute-start | bytes 786440 | tf_op jit(solution)/shard_map/ppermute | solution.py:56
  93.3 18.4 %collective-permute-start.13 = (bf16[64,2048]{1,0:T(8,128)(2,1)S(1)}, bf16[64,2048]{1,0:T(8,128)(2,1)S(1)}, u32[]{:S(2)}, u32[]{:S(2)}) collective-permute-start(bf16[64,2048]{1,0:T(8,128)(2,1)S(1)} %collective-permute-done.12.refs_4_), channel_id=1, source_target_pairs={{0,1},{1,2},{2,3},{3,0},{4,5},{5,6},{6,7},{7,4},{8,9},{9,10},{10,1... | collective-permute-start | bytes 786440 | tf_op jit(solution)/shard_map/ppermute | solution.py:56
  102.6 10.0 %collective-permute-start.15 = (bf16[64,2048]{1,0:T(8,128)(2,1)S(1)}, bf16[64,2048]{1,0:T(8,128)(2,1)S(1)}, u32[]{:S(2)}, u32[]{:S(2)}) collective-permute-start(bf16[64,2048]{1,0:T(8,128)(2,1)S(1)} %collective-permute-done.14.refs_3_), channel_id=1, source_target_pairs={{0,3},{1,0},{2,1},{3,2},{4,7},{5,4},{6,5},{7,6},{8,11},{9,8},{10,9... | collective-permute-start | bytes 786440 | tf_op jit(solution)/shard_map/ppermute | solution.py:56
  118.5 10.8 %collective-permute-start.21 = (bf16[4,176,128]{2,1,0:T(8,128)(2,1)}, bf16[4,176,128]{2,1,0:T(8,128)(2,1)S(1)}, u32[]{:S(2)}, u32[]{:S(2)}) collective-permute-start(bf16[4,176,128]{2,1,0:T(8,128)(2,1)} %get-tuple-element.132), channel_id=1, source_target_pairs={{0,12},{1,13},{2,14},{3,15},{16,28},{17,29},{18,30},{19,31}} | collective-permute-start | bytes 540680 | tf_op jit(solution)/shard_map/ppermute | solution.py:818
  121.3 8.4 %collective-permute-start.20 = (bf16[4,176,128]{2,1,0:T(8,128)(2,1)}, bf16[4,176,128]{2,1,0:T(8,128)(2,1)S(1)}, u32[]{:S(2)}, u32[]{:S(2)}) collective-permute-start(bf16[4,176,128]{2,1,0:T(8,128)(2,1)} %get-tuple-element.132), channel_id=1, source_target_pairs={{0,8},{4,12},{1,9},{5,13},{2,10},{6,14},{3,11},{7,15},{16,24},{20,... | collective-permute-start | bytes 540680 | tf_op jit(solution)/shard_map/ppermute | solution.py:818
  122.6 7.1 %collective-permute-start.19 = (bf16[4,176,128]{2,1,0:T(8,128)(2,1)}, bf16[4,176,128]{2,1,0:T(8,128)(2,1)S(1)}, u32[]{:S(2)}, u32[]{:S(2)}) collective-permute-start(bf16[4,176,128]{2,1,0:T(8,128)(2,1)} %get-tuple-element.132), channel_id=1, source_target_pairs={{0,4},{4,8},{8,12},{1,5},{5,9},{9,13},{2,6},{6,10},{10,14},{3,7},{... | collective-permute-start | bytes 540680 | tf_op jit(solution)/shard_map/ppermute | solution.py:818
  135.3 86.6 %collective-permute-start.34 = (bf16[3200,512]{1,0:T(8,128)(2,1)S(1)}, bf16[3200,512]{1,0:T(8,128)(2,1)S(1)}, u32[]{:S(2)}, u32[]{:S(2)}) collective-permute-start(bf16[3200,512]{1,0:T(8,128)(2,1)S(1)} %copy-done.8), channel_id=1, source_target_pairs={{0,8},{4,12},{8,0},{12,4},{1,9},{5,13},{9,1},{13,5},{2,10},{6,14},... | collective-permute-start | bytes 9830408 | tf_op jit(solution)/shard_map/ppermute | solution.py:847
  138.2 11.3 %collective-permute-start.22 = (bf16[64,2048]{1,0:T(8,128)(2,1)}, bf16[64,2048]{1,0:T(8,128)(2,1)S(1)}, u32[]{:S(2)}, u32[]{:S(2)}) collective-permute-start(bf16[64,2048]{1,0:T(8,128)(2,1)} %get-tuple-element.136), channel_id=1, source_target_pairs={{0,1},{1,2},{2,3},{3,0},{4,5},{5,6},{6,7},{7,4},{8,9},{9,10},{10,1... | collective-permute-start | bytes 786440 | tf_op jit(solution)/shard_map/ppermute | solution.py:56
  138.8 13.3 %collective-permute-start.23 = (bf16[64,2048]{1,0:T(8,128)(2,1)}, bf16[64,2048]{1,0:T(8,128)(2,1)S(1)}, u32[]{:S(2)}, u32[]{:S(2)}) collective-permute-start(bf16[64,2048]{1,0:T(8,128)(2,1)} %get-tuple-element.138), channel_id=1, source_target_pairs={{0,3},{1,0},{2,1},{3,2},{4,7},{5,4},{6,5},{7,6},{8,11},{9,8},{10,9... | collective-permute-start | bytes 786440 | tf_op jit(solution)/shard_map/ppermute | solution.py:56
  145.9 10.7 %collective-permute-start.25 = (bf16[64,2048]{1,0:T(8,128)(2,1)}, bf16[64,2048]{1,0:T(8,128)(2,1)S(1)}, u32[]{:S(2)}, u32[]{:S(2)}) collective-permute-start(bf16[64,2048]{1,0:T(8,128)(2,1)} %get-tuple-element.140), channel_id=1, source_target_pairs={{0,3},{1,0},{2,1},{3,2},{4,7},{5,4},{6,5},{7,6},{8,11},{9,8},{10,9... | collective-permute-start | bytes 786440 | tf_op jit(solution)/shard_map/ppermute | solution.py:56
  154.9 11.3 %collective-permute-start.24 = (bf16[64,2048]{1,0:T(8,128)(2,1)}, bf16[64,2048]{1,0:T(8,128)(2,1)S(1)}, u32[]{:S(2)}, u32[]{:S(2)}) collective-permute-start(bf16[64,2048]{1,0:T(8,128)(2,1)} %get-tuple-element.139), channel_id=1, source_target_pairs={{0,1},{1,2},{2,3},{3,0},{4,5},{5,6},{6,7},{7,4},{8,9},{9,10},{10,1... | collective-permute-start | bytes 786440 | tf_op jit(solution)/shard_map/ppermute | solution.py:56
  155.4 66.5 %collective-permute-start.35 = (bf16[1920,512]{1,0:T(8,128)(2,1)}, bf16[1920,512]{1,0:T(8,128)(2,1)}, u32[]{:S(2)}, u32[]{:S(2)}) collective-permute-start(bf16[1920,512]{1,0:T(8,128)(2,1)} %copy-done.11), channel_id=1, source_target_pairs={{0,4},{4,0},{8,12},{12,8},{1,5},{5,1},{9,13},{13,9},{2,6},{6,2},{1... | collective-permute-start | bytes 5898248 | tf_op jit(solution)/shard_map/ppermute | solution.py:809
  156.7 15.2 %collective-permute-start.26 = (bf16[64,2048]{1,0:T(8,128)(2,1)S(1)}, bf16[64,2048]{1,0:T(8,128)(2,1)S(1)}, u32[]{:S(2)}, u32[]{:S(2)}) collective-permute-start(bf16[64,2048]{1,0:T(8,128)(2,1)S(1)} %copy-done.22), channel_id=1, source_target_pairs={{0,1},{1,2},{2,3},{3,0},{4,5},{5,6},{6,7},{7,4},{8,9},{9,10},{10,1... | collective-permute-start | bytes 786440 | tf_op jit(solution)/shard_map/ppermute | solution.py:56
  166.2 12.1 %collective-permute-start.27 = (bf16[64,2048]{1,0:T(8,128)(2,1)}, bf16[64,2048]{1,0:T(8,128)(2,1)S(1)}, u32[]{:S(2)}, u32[]{:S(2)}) collective-permute-start(bf16[64,2048]{1,0:T(8,128)(2,1)} %get-tuple-element.149), channel_id=1, source_target_pairs={{0,3},{1,0},{2,1},{3,2},{4,7},{5,4},{6,5},{7,6},{8,11},{9,8},{10,9... | collective-permute-start | bytes 786440 | tf_op jit(solution)/shard_map/ppermute | solution.py:56
  171.9 11.2 %collective-permute-start.30 = (bf16[64,2048]{1,0:T(8,128)(2,1)}, bf16[64,2048]{1,0:T(8,128)(2,1)S(1)}, u32[]{:S(2)}, u32[]{:S(2)}) collective-permute-start(bf16[64,2048]{1,0:T(8,128)(2,1)} %get-tuple-element.145.refs_0_), channel_id=1, source_target_pairs={{0,1},{1,2},{2,3},{3,0},{4,5},{5,6},{6,7},{7,4},{8,9},{9,10},{10,1... | collective-permute-start | bytes 786440 | tf_op jit(solution)/shard_map/ppermute | solution.py:56
  178.3 13.6 %collective-permute-start.28 = (bf16[64,2048]{1,0:T(8,128)(2,1)}, bf16[64,2048]{1,0:T(8,128)(2,1)S(1)}, u32[]{:S(2)}, u32[]{:S(2)}) collective-permute-start(bf16[64,2048]{1,0:T(8,128)(2,1)} %get-tuple-element.145.refs_0_), channel_id=1, source_target_pairs={{0,3},{1,0},{2,1},{3,2},{4,7},{5,4},{6,5},{7,6},{8,11},{9,8},{10,9... | collective-permute-start | bytes 786440 | tf_op jit(solution)/shard_map/ppermute | solution.py:56
  183.1 16.5 %collective-permute-start.31 = (bf16[64,2048]{1,0:T(8,128)(2,1)}, bf16[64,2048]{1,0:T(8,128)(2,1)S(1)}, u32[]{:S(2)}, u32[]{:S(2)}) collective-permute-start(bf16[64,2048]{1,0:T(8,128)(2,1)} %get-tuple-element.150.refs_1_), channel_id=1, source_target_pairs={{0,1},{1,2},{2,3},{3,0},{4,5},{5,6},{6,7},{7,4},{8,9},{9,10},{10,1... | collective-permute-start | bytes 786440 | tf_op jit(solution)/shard_map/ppermute | solution.py:56
  191.9 14.4 %collective-permute-start.29 = (bf16[64,2048]{1,0:T(8,128)(2,1)}, bf16[64,2048]{1,0:T(8,128)(2,1)S(1)}, u32[]{:S(2)}, u32[]{:S(2)}) collective-permute-start(bf16[64,2048]{1,0:T(8,128)(2,1)} %get-tuple-element.150.refs_1_), channel_id=1, source_target_pairs={{0,3},{1,0},{2,1},{3,2},{4,7},{5,4},{6,5},{7,6},{8,11},{9,8},{10,9... | collective-permute-start | bytes 786440 | tf_op jit(solution)/shard_map/ppermute | solution.py:56
  199.6 15.9 %collective-permute-start.32 = (bf16[64,2048]{1,0:T(8,128)(2,1)S(1)}, bf16[64,2048]{1,0:T(8,128)(2,1)}, u32[]{:S(2)}, u32[]{:S(2)}) collective-permute-start(bf16[64,2048]{1,0:T(8,128)(2,1)S(1)} %collective-permute-done.30.refs_4_), channel_id=1, source_target_pairs={{0,1},{1,2},{2,3},{3,0},{4,5},{5,6},{6,7},{7,4},{8,9},{9,10},{10,1... | collective-permute-start | bytes 786440 | tf_op jit(solution)/shard_map/ppermute | solution.py:56
  206.4 9.2 %collective-permute-start.33 = (bf16[64,2048]{1,0:T(8,128)(2,1)S(1)}, bf16[64,2048]{1,0:T(8,128)(2,1)}, u32[]{:S(2)}, u32[]{:S(2)}) collective-permute-start(bf16[64,2048]{1,0:T(8,128)(2,1)S(1)} %collective-permute-done.29.refs_3_), channel_id=1, source_target_pairs={{0,3},{1,0},{2,1},{3,2},{4,7},{5,4},{6,5},{7,6},{8,11},{9,8},{10,9... | collective-permute-start | bytes 786440 | tf_op jit(solution)/shard_map/ppermute | solution.py:56
  232.3 77.5 %collective-permute-start.50 = (bf16[3200,512]{1,0:T(8,128)(2,1)S(1)}, bf16[3200,512]{1,0:T(8,128)(2,1)S(1)}, u32[]{:S(2)}, u32[]{:S(2)}) collective-permute-start(bf16[3200,512]{1,0:T(8,128)(2,1)S(1)} %collective-permute-done.34.refs_7_), channel_id=1, source_target_pairs={{0,4},{4,0},{8,12},{12,8},{1,5},{5,1},{9,13},{13,9},{2,6},{6,2},{1... | collective-permute-start | bytes 9830408 | tf_op jit(solution)/shard_map/ppermute | solution.py:871
  232.4 11.3 %collective-permute-start.38 = (bf16[64,2048]{1,0:T(8,128)(2,1)}, bf16[64,2048]{1,0:T(8,128)(2,1)}, u32[]{:S(2)}, u32[]{:S(2)}) collective-permute-start(bf16[64,2048]{1,0:T(8,128)(2,1)} %get-tuple-element.162), channel_id=1, source_target_pairs={{0,1},{1,2},{2,3},{3,0},{4,5},{5,6},{6,7},{7,4},{8,9},{9,10},{10,1... | collective-permute-start | bytes 786440 | tf_op jit(solution)/shard_map/ppermute | solution.py:56
  233.6 15.1 %collective-permute-start.39 = (bf16[64,2048]{1,0:T(8,128)(2,1)}, bf16[64,2048]{1,0:T(8,128)(2,1)}, u32[]{:S(2)}, u32[]{:S(2)}) collective-permute-start(bf16[64,2048]{1,0:T(8,128)(2,1)} %get-tuple-element.164), channel_id=1, source_target_pairs={{0,3},{1,0},{2,1},{3,2},{4,7},{5,4},{6,5},{7,6},{8,11},{9,8},{10,9... | collective-permute-start | bytes 786440 | tf_op jit(solution)/shard_map/ppermute | solution.py:56
  240.1 13.4 %collective-permute-start.41 = (bf16[64,2048]{1,0:T(8,128)(2,1)}, bf16[64,2048]{1,0:T(8,128)(2,1)}, u32[]{:S(2)}, u32[]{:S(2)}) collective-permute-start(bf16[64,2048]{1,0:T(8,128)(2,1)} %get-tuple-element.166), channel_id=1, source_target_pairs={{0,3},{1,0},{2,1},{3,2},{4,7},{5,4},{6,5},{7,6},{8,11},{9,8},{10,9... | collective-permute-start | bytes 786440 | tf_op jit(solution)/shard_map/ppermute | solution.py:56
  250.7 11.5 %collective-permute-start.40 = (bf16[64,2048]{1,0:T(8,128)(2,1)}, bf16[64,2048]{1,0:T(8,128)(2,1)}, u32[]{:S(2)}, u32[]{:S(2)}) collective-permute-start(bf16[64,2048]{1,0:T(8,128)(2,1)} %get-tuple-element.165), channel_id=1, source_target_pairs={{0,1},{1,2},{2,3},{3,0},{4,5},{5,6},{6,7},{7,4},{8,9},{9,10},{10,1... | collective-permute-start | bytes 786440 | tf_op jit(solution)/shard_map/ppermute | solution.py:56
  251.5 53.7 %collective-permute-start.52 = (bf16[1280,512]{1,0:T(8,128)(2,1)S(1)}, bf16[1280,512]{1,0:T(8,128)(2,1)}, u32[]{:S(2)}, u32[]{:S(2)}) collective-permute-start(bf16[1280,512]{1,0:T(8,128)(2,1)S(1)} %copy-done.12), channel_id=1, source_target_pairs={{0,12},{4,8},{8,4},{12,0},{1,13},{5,9},{9,5},{13,1},{2,14},{6,10},... | collective-permute-start | bytes 3932168 | tf_op jit(solution)/shard_map/ppermute | solution.py:880
  251.5 58.3 %collective-permute-start.51 = (bf16[1280,512]{1,0:T(8,128)(2,1)S(1)}, bf16[1280,512]{1,0:T(8,128)(2,1)}, u32[]{:S(2)}, u32[]{:S(2)}) collective-permute-start(bf16[1280,512]{1,0:T(8,128)(2,1)S(1)} %copy-done.12), channel_id=1, source_target_pairs={{0,8},{4,12},{8,0},{12,4},{1,9},{5,13},{9,1},{13,5},{2,10},{6,14},... | collective-permute-start | bytes 3932168 | tf_op jit(solution)/shard_map/ppermute | solution.py:879
  253.5 14.2 %collective-permute-start.42 = (bf16[64,2048]{1,0:T(8,128)(2,1)S(1)}, bf16[64,2048]{1,0:T(8,128)(2,1)}, u32[]{:S(2)}, u32[]{:S(2)}) collective-permute-start(bf16[64,2048]{1,0:T(8,128)(2,1)S(1)} %copy-done.20), channel_id=1, source_target_pairs={{0,1},{1,2},{2,3},{3,0},{4,5},{5,6},{6,7},{7,4},{8,9},{9,10},{10,1... | collective-permute-start | bytes 786440 | tf_op jit(solution)/shard_map/ppermute | solution.py:56
  262.2 11.1 %collective-permute-start.43 = (bf16[64,2048]{1,0:T(8,128)(2,1)}, bf16[64,2048]{1,0:T(8,128)(2,1)}, u32[]{:S(2)}, u32[]{:S(2)}) collective-permute-start(bf16[64,2048]{1,0:T(8,128)(2,1)} %get-tuple-element.170), channel_id=1, source_target_pairs={{0,3},{1,0},{2,1},{3,2},{4,7},{5,4},{6,5},{7,6},{8,11},{9,8},{10,9... | collective-permute-start | bytes 786440 | tf_op jit(solution)/shard_map/ppermute | solution.py:56
  267.7 11.3 %collective-permute-start.46 = (bf16[64,2048]{1,0:T(8,128)(2,1)}, bf16[64,2048]{1,0:T(8,128)(2,1)S(1)}, u32[]{:S(2)}, u32[]{:S(2)}) collective-permute-start(bf16[64,2048]{1,0:T(8,128)(2,1)} %finish.6.refs_0_), channel_id=1, source_target_pairs={{0,1},{1,2},{2,3},{3,0},{4,5},{5,6},{6,7},{7,4},{8,9},{9,10},{10,1... | collective-permute-start | bytes 786440 | tf_op jit(solution)/shard_map/ppermute | solution.py:56
  273.4 11.4 %collective-permute-start.44 = (bf16[64,2048]{1,0:T(8,128)(2,1)}, bf16[64,2048]{1,0:T(8,128)(2,1)}, u32[]{:S(2)}, u32[]{:S(2)}) collective-permute-start(bf16[64,2048]{1,0:T(8,128)(2,1)} %finish.6.refs_0_), channel_id=1, source_target_pairs={{0,3},{1,0},{2,1},{3,2},{4,7},{5,4},{6,5},{7,6},{8,11},{9,8},{10,9... | collective-permute-start | bytes 786440 | tf_op jit(solution)/shard_map/ppermute | solution.py:56
  279.0 11.4 %collective-permute-start.47 = (bf16[64,2048]{1,0:T(8,128)(2,1)}, bf16[64,2048]{1,0:T(8,128)(2,1)}, u32[]{:S(2)}, u32[]{:S(2)}) collective-permute-start(bf16[64,2048]{1,0:T(8,128)(2,1)} %finish.7.refs_1_), channel_id=1, source_target_pairs={{0,1},{1,2},{2,3},{3,0},{4,5},{5,6},{6,7},{7,4},{8,9},{9,10},{10,1... | collective-permute-start | bytes 786440 | tf_op jit(solution)/shard_map/ppermute | solution.py:56
  284.7 11.4 %collective-permute-start.45 = (bf16[64,2048]{1,0:T(8,128)(2,1)}, bf16[64,2048]{1,0:T(8,128)(2,1)}, u32[]{:S(2)}, u32[]{:S(2)}) collective-permute-start(bf16[64,2048]{1,0:T(8,128)(2,1)} %finish.7.refs_1_), channel_id=1, source_target_pairs={{0,3},{1,0},{2,1},{3,2},{4,7},{5,4},{6,5},{7,6},{8,11},{9,8},{10,9... | collective-permute-start | bytes 786440 | tf_op jit(solution)/shard_map/ppermute | solution.py:56
  290.4 11.3 %collective-permute-start.48 = (bf16[64,2048]{1,0:T(8,128)(2,1)S(1)}, bf16[64,2048]{1,0:T(8,128)(2,1)}, u32[]{:S(2)}, u32[]{:S(2)}) collective-permute-start(bf16[64,2048]{1,0:T(8,128)(2,1)S(1)} %collective-permute-done.46.refs_4_), channel_id=1, source_target_pairs={{0,1},{1,2},{2,3},{3,0},{4,5},{5,6},{6,7},{7,4},{8,9},{9,10},{10,1... | collective-permute-start | bytes 786440 | tf_op jit(solution)/shard_map/ppermute | solution.py:56
  296.1 9.2 %collective-permute-start.49 = (bf16[64,2048]{1,0:T(8,128)(2,1)}, bf16[64,2048]{1,0:T(8,128)(2,1)}, u32[]{:S(2)}, u32[]{:S(2)}) collective-permute-start(bf16[64,2048]{1,0:T(8,128)(2,1)} %collective-permute-done.45.refs_3_), channel_id=1, source_target_pairs={{0,3},{1,0},{2,1},{3,2},{4,7},{5,4},{6,5},{7,6},{8,11},{9,8},{10,9... | collective-permute-start | bytes 786440 | tf_op jit(solution)/shard_map/ppermute | solution.py:56
  (54 other events, 317.8 us)
